TPU v7x, 32 devices: a whole 2x2x4 slice. The times are simulated.
32 devices in a mesh: exp: 8 (over z, y), fsdp: 4 (over x, core).
Axes of the slice: x: 2, y: 2, z: 4, core: 2. Of those that a mesh axis runs over, the one named last changes fastest.
Arguments:
- tokens: bfloat16 [4096, 2048], P(('exp', 'fsdp')), may hold values from -6 to 6
- lengths: int32 [32, 4], P(('exp', 'fsdp')), may hold values from 1 to 64, 128 in all within a row
- routes: int32 [4096, 8], P(('exp', 'fsdp')), may hold values from 0 to 31, all different within a row; in each aligned block of 128 rows (0 to 127, 128 to 255, ...) at most 64 rows name the same one
- attn_gain: bfloat16 [2048], P('fsdp'), may hold values from 0.099609375 to 1.8984375
- w_query: bfloat16 [2048, 4096], P('fsdp'), may hold values from -0.125 to 0.125
- key_weight: bfloat16 [2048, 512], P('fsdp'), may hold values from -0.125 to 0.125
- value_weight: bfloat16 [2048, 512], P('fsdp'), may hold values from -0.125 to 0.125
- q_gain: bfloat16 [128], P('fsdp'), may hold values from 0.5 to 2
- k_gain: bfloat16 [128], P('fsdp'), may hold values from 0.5 to 2
- w_out: bfloat16 [4096, 2048], P('fsdp'), may hold values from -0.75 to 0.75
- mlp_gain: bfloat16 [2048], P('fsdp'), may hold values from 0.099609375 to 1.8984375
- w_router: bfloat16 [2048, 32], P('fsdp'), may hold values from -4 to 4
- expert_gate: bfloat16 [32, 2048, 768], P(('exp', 'fsdp')), may hold values from -0.125 to 0.125
- expert_up: bfloat16 [32, 2048, 768], P(('exp', 'fsdp')), may hold values from -0.125 to 0.125
- expert_down: bfloat16 [32, 768, 2048], P(('exp', 'fsdp')), may hold values from -0.875 to 0.875
- cotangent: bfloat16 [4096, 2048], P(('exp', 'fsdp')), may hold values from -6 to 6
Outputs:
- layer_out: bfloat16 [4096, 2048], P(('exp', 'fsdp'))
- grad_tokens: bfloat16 [4096, 2048], P(('exp', 'fsdp'))
- grad_attn_gain: float32 [2048], P('fsdp')
- grad_query: float32 [2048, 4096], P('fsdp')
- grad_key: float32 [2048, 512], P('fsdp')
- grad_value: float32 [2048, 512], P('fsdp')
- grad_q_gain: float32 [128], P('fsdp')
- grad_k_gain: float32 [128], P('fsdp')
- grad_out_proj: float32 [4096, 2048], P('fsdp')
- grad_mlp_gain: float32 [2048], P('fsdp')
- grad_router: float32 [2048, 32], P('fsdp')
- grad_expert_gate: float32 [32, 2048, 768], P(('exp', 'fsdp'))
- grad_expert_up: float32 [32, 2048, 768], P(('exp', 'fsdp'))
- grad_expert_down: float32 [32, 768, 2048], P(('exp', 'fsdp'))
Inputs may be any that keep to these rules, and one draw needn't show every extreme that they name: `lengths`: each row packs the sequences of one device; they sum to 128, and the longest is 64. `routes`: each token names 8 different experts. Among the tokens of one device no expert is named more than 64 times, a bound that some block reaches.
All inputs are finite; a program needn't handle non-finite values.
Results may differ from a plain program's by a relative error of at most 0.023.
Values may be sent and summed in bfloat16 or wider, within the bound.
A program may use at most 320 MiB of HBM per device.

v0:
```python
import math

import jax
import jax.numpy as jnp
from jax import lax
from jax.sharding import PartitionSpec as P

MODEL_WIDTH = 2048
QUERY_HEADS = 32
KEY_VALUE_HEADS = 4
HEAD_WIDTH = 128


EPSILON = 1e-06
THETA = 1000000.0
MASKED = -1e30


def as_sent(x):
    return jax.tree.map(lambda a: a.astype(jnp.bfloat16) if a.dtype == jnp.float32 else a, x)


def matrix_product(left, right):
    return jnp.dot(left, right, preferred_element_type=jnp.float32)


def left_trans(left, right):
    return lax.dot_general(
        left, right, (((0,), (0,)), ((), ())), preferred_element_type=jnp.float32
    )


def right_transposed(left, right):
    return lax.dot_general(
        left, right, (((1,), (1,)), ((), ())), preferred_element_type=jnp.float32
    )


def rms_scale(values):
    return lax.rsqrt(jnp.mean(values * values, axis=-1, keepdims=True) + EPSILON)


def rms_back(grad_hat, values, scale):
    normal = values * scale
    return scale * (grad_hat - normal * jnp.mean(grad_hat * normal, axis=-1, keepdims=True))


def seq_layout(length_row, token_count):
    ends = jnp.cumsum(length_row)
    starts = ends - length_row
    places = jnp.arange(token_count, dtype=jnp.int32)
    member = (places[:, None] >= starts[None, :]) & (places[:, None] < ends[None, :])
    numbers = jnp.arange(length_row.shape[0], dtype=jnp.int32)
    segment = jnp.sum(jnp.where(member, numbers[None, :], 0), axis=1)
    position = places - jnp.sum(jnp.where(member, starts[None, :], 0), axis=1)
    allowed = (segment[:, None] == segment[None, :]) & (places[None, :] <= places[:, None])
    return (position, allowed)


def rotary_tables(position, head_size):
    half = head_size // 2
    index = jnp.arange(head_size, dtype=jnp.int32) % half
    inverse = jnp.exp(index.astype(jnp.float32) * (-2.0 * math.log(THETA) / head_size))
    angles = position.astype(jnp.float32)[:, None] * inverse[None, :]
    return (jnp.cos(angles)[:, None, :], jnp.sin(angles)[:, None, :])


def rotate(values, cosine, sine):
    half = values.shape[-1] // 2
    turned = jnp.concatenate([-values[..., half:], values[..., :half]], axis=-1)
    return values * cosine + turned * sine


def rotate_back(grads, cosine, sine):
    half = grads.shape[-1] // 2
    moved = grads * sine
    return grads * cosine + jnp.concatenate([moved[..., half:], -moved[..., :half]], axis=-1)


def slot_table(route_rows, experts, capacity):
    flat = route_rows.reshape(-1)
    onehot = (flat[:, None] == jnp.arange(experts, dtype=jnp.int32)[None, :]).astype(jnp.int32)
    ranks = jnp.cumsum(onehot, axis=0) - 1
    rank = jnp.sum(ranks * onehot, axis=1)
    return flat * capacity + rank


def dispatch_rows(buffer):
    return lax.all_to_all(buffer, ("exp", "fsdp"), split_axis=0, concat_axis=0, tiled=True)


def combine_rows(buffer):
    return lax.all_to_all(buffer, ("exp", "fsdp"), split_axis=0, concat_axis=0, tiled=True)


def output_grad_rows(buffer):
    return lax.all_to_all(buffer, ("exp", "fsdp"), split_axis=0, concat_axis=0, tiled=True)


def input_grad_rows(buffer):
    return lax.all_to_all(buffer, ("exp", "fsdp"), split_axis=0, concat_axis=0, tiled=True)


def score_table(query_low, key_low, allowed):
    scores = jnp.einsum("qkgd,pkd->kgqp", query_low, key_low, preferred_element_type=jnp.float32)
    return jnp.where(allowed[None, None], scores * HEAD_WIDTH ** (-0.5), MASKED)


def local(
    tokens,
    lengths,
    routes,
    attn_gain,
    w_query,
    key_weight,
    value_weight,
    q_gain,
    k_gain,
    w_out,
    mlp_gain,
    w_router,
    expert_gate,
    expert_up,
    expert_down,
    cotangent,
):
    fetched = (
        lax.all_gather(w_query, "fsdp", axis=0, tiled=True),
        lax.all_gather(key_weight, "fsdp", axis=0, tiled=True),
        lax.all_gather(value_weight, "fsdp", axis=0, tiled=True),
        lax.all_gather(w_out, "fsdp", axis=0, tiled=True),
        lax.all_gather(w_router, "fsdp", axis=0, tiled=True),
        lax.all_gather(attn_gain, "fsdp", axis=0, tiled=True),
        lax.all_gather(mlp_gain, "fsdp", axis=0, tiled=True),
        lax.all_gather(q_gain, "fsdp", axis=0, tiled=True),
        lax.all_gather(k_gain, "fsdp", axis=0, tiled=True),
    )
    query_full, key_complete, value_complete, output_complete, router_full = fetched[:5]
    gain_attn = fetched[5].astype(jnp.float32)
    gain_mlp = fetched[6].astype(jnp.float32)
    gain_query = fetched[7].astype(jnp.float32)
    gain_key = fetched[8].astype(jnp.float32)
    token_count = tokens.shape[0]
    topk = routes.shape[1]
    experts = lax.axis_size("exp") * lax.axis_size("fsdp")
    capacity = 2 * token_count * topk // experts
    head_group = QUERY_HEADS // KEY_VALUE_HEADS
    inputs = tokens.astype(jnp.float32)
    position, allowed = seq_layout(lengths[0], token_count)
    cosine, sine = rotary_tables(position, HEAD_WIDTH)
    scale_one = rms_scale(inputs)
    first_normed = (inputs * scale_one * gain_attn).astype(jnp.bfloat16)
    query_raw = matrix_product(first_normed, query_full).reshape(
        token_count, QUERY_HEADS, HEAD_WIDTH
    )
    key_unscaled = matrix_product(first_normed, key_complete).reshape(
        token_count, KEY_VALUE_HEADS, HEAD_WIDTH
    )
    value_lower = (
        matrix_product(first_normed, value_complete)
        .astype(jnp.bfloat16)
        .reshape(token_count, KEY_VALUE_HEADS, HEAD_WIDTH)
    )
    query_scale = rms_scale(query_raw)
    query_hat = query_raw * query_scale
    key_scale = rms_scale(key_unscaled)
    key_hat = key_unscaled * key_scale
    query_low = (
        rotate(query_hat * gain_query, cosine, sine)
        .astype(jnp.bfloat16)
        .reshape(token_count, KEY_VALUE_HEADS, head_group, HEAD_WIDTH)
    )
    key_low = rotate(key_hat * gain_key, cosine, sine).astype(jnp.bfloat16)
    scores = score_table(query_low, key_low, allowed)
    top = jnp.max(scores, axis=-1, keepdims=True)
    raised = jnp.exp(scores - top)
    total = jnp.sum(raised, axis=-1, keepdims=True)
    probs = raised / total
    log_total = top + jnp.log(total)
    probs_low = probs.astype(jnp.bfloat16)
    attended = jnp.einsum(
        "kgqp,pkd->qkgd", probs_low, value_lower, preferred_element_type=jnp.float32
    )
    attended_low = attended.reshape(token_count, QUERY_HEADS * HEAD_WIDTH).astype(jnp.bfloat16)
    middle = inputs + matrix_product(attended_low, output_complete)
    scale_two = rms_scale(middle)
    normed_two = (middle * scale_two * gain_mlp).astype(jnp.bfloat16)
    logits = matrix_product(normed_two, router_full)
    picked = jnp.take_along_axis(logits, routes, axis=1)
    peak = jnp.max(picked, axis=1, keepdims=True)
    lifted = jnp.exp(picked - peak)
    gates = lifted / jnp.sum(lifted, axis=1, keepdims=True)
    slots = slot_table(routes, experts, capacity)
    rows = jnp.repeat(normed_two, topk, axis=0)
    packed = (
        jnp.zeros((experts * capacity, MODEL_WIDTH), jnp.bfloat16)
        .at[slots]
        .set(rows)
        .reshape(experts, capacity, MODEL_WIDTH)
    )
    arrived = dispatch_rows(packed).reshape(experts * capacity, MODEL_WIDTH)
    gate_pre = matrix_product(arrived, expert_gate[0])
    up_pre = matrix_product(arrived, expert_up[0])
    sigma = jax.nn.sigmoid(gate_pre)
    silu_value = gate_pre * sigma
    active_low = (silu_value * up_pre).astype(jnp.bfloat16)
    produced = (
        matrix_product(active_low, expert_down[0])
        .astype(jnp.bfloat16)
        .reshape(experts, capacity, MODEL_WIDTH)
    )
    returned = (
        combine_rows(produced)
        .reshape(experts * capacity, MODEL_WIDTH)[slots]
        .reshape(token_count, topk, MODEL_WIDTH)
    )
    mixed = jnp.einsum("tk,tkd->td", gates, returned.astype(jnp.float32))
    layer_out = (middle + mixed).astype(jnp.bfloat16)
    upstream = cotangent.astype(jnp.float32)
    gate_grad = jnp.einsum("td,tkd->tk", cotangent, returned, preferred_element_type=jnp.float32)
    out_rows = (
        (gates[:, :, None] * upstream[:, None, :])
        .astype(jnp.bfloat16)
        .reshape(token_count * topk, MODEL_WIDTH)
    )
    packed_grad = jnp.zeros((experts * capacity, MODEL_WIDTH), jnp.bfloat16).at[slots].set(out_rows)
    arrived_grad = output_grad_rows(packed_grad.reshape(experts, capacity, MODEL_WIDTH)).reshape(
        experts * capacity, MODEL_WIDTH
    )
    active_grad = right_transposed(arrived_grad, expert_down[0])
    down_grad = left_trans(active_low, arrived_grad)
    gate_pre_grad = (active_grad * up_pre * (sigma * (1.0 + gate_pre * (1.0 - sigma)))).astype(
        jnp.bfloat16
    )
    up_pre_grad = (active_grad * silu_value).astype(jnp.bfloat16)
    gate_w_grad = left_trans(arrived, gate_pre_grad)
    up_w_grad = left_trans(arrived, up_pre_grad)
    rows_back = right_transposed(gate_pre_grad, expert_gate[0]) + right_transposed(
        up_pre_grad, expert_up[0]
    )
    rows_back = rows_back.astype(jnp.bfloat16).reshape(experts, capacity, MODEL_WIDTH)
    back_rows = (
        input_grad_rows(rows_back)
        .reshape(experts * capacity, MODEL_WIDTH)[slots]
        .reshape(token_count, topk, MODEL_WIDTH)
    )
    picked_grad = gates * (gate_grad - jnp.sum(gates * gate_grad, axis=1, keepdims=True))
    onehot = routes[:, :, None] == jnp.arange(experts, dtype=jnp.int32)[None, None, :]
    logit_grad = jnp.sum(jnp.where(onehot, picked_grad[:, :, None], 0.0), axis=1).astype(
        jnp.bfloat16
    )
    normed_two_grad = jnp.sum(back_rows, axis=1, dtype=jnp.float32) + right_transposed(
        logit_grad, router_full
    )
    mlp_gain_grad = jnp.sum(normed_two_grad * middle * scale_two, axis=0)
    middle_grad = upstream + rms_back(normed_two_grad * gain_mlp, middle, scale_two)
    branch_gradient = middle_grad.astype(jnp.bfloat16)
    attended_grad = (
        right_transposed(branch_gradient, output_complete)
        .astype(jnp.bfloat16)
        .reshape(token_count, KEY_VALUE_HEADS, head_group, HEAD_WIDTH)
    )
    scores = score_table(query_low, key_low, allowed)
    probs = jnp.exp(scores - log_total)
    probs_low = probs.astype(jnp.bfloat16)
    prob_grad = jnp.einsum(
        "qkgd,pkd->kgqp", attended_grad, value_lower, preferred_element_type=jnp.float32
    )
    value_gradient = jnp.einsum(
        "kgqp,qkgd->pkd", probs_low, attended_grad, preferred_element_type=jnp.float32
    )
    value_gradient = value_gradient.astype(jnp.bfloat16).reshape(
        token_count, KEY_VALUE_HEADS * HEAD_WIDTH
    )
    balance = jnp.sum(probs * prob_grad, axis=-1, keepdims=True)
    score_grad = (probs * (prob_grad - balance)).astype(jnp.bfloat16)
    query_low_grad = jnp.einsum(
        "kgqp,pkd->qkgd", score_grad, key_low, preferred_element_type=jnp.float32
    )
    query_low_grad = query_low_grad.reshape(token_count, QUERY_HEADS, HEAD_WIDTH) * HEAD_WIDTH ** (
        -0.5
    )
    key_low_grad = jnp.einsum(
        "kgqp,qkgd->pkd", score_grad, query_low, preferred_element_type=jnp.float32
    )
    key_low_grad = key_low_grad * HEAD_WIDTH ** (-0.5)
    query_norm_grad = rotate_back(query_low_grad, cosine, sine)
    key_norm_grad = rotate_back(key_low_grad, cosine, sine)
    q_gain_grad = jnp.sum(query_norm_grad * query_hat, axis=(0, 1))
    k_gain_grad = jnp.sum(key_norm_grad * key_hat, axis=(0, 1))
    query_grad = rms_back(query_norm_grad * gain_query, query_raw, query_scale)
    query_grad = query_grad.astype(jnp.bfloat16).reshape(token_count, QUERY_HEADS * HEAD_WIDTH)
    key_gradient = rms_back(key_norm_grad * gain_key, key_unscaled, key_scale)
    key_gradient = key_gradient.astype(jnp.bfloat16).reshape(
        token_count, KEY_VALUE_HEADS * HEAD_WIDTH
    )
    normed_one_grad = right_transposed(query_grad, query_full) + right_transposed(
        key_gradient, key_complete
    )
    normed_one_grad = normed_one_grad + right_transposed(value_gradient, value_complete)
    attn_gain_grad = jnp.sum(normed_one_grad * inputs * scale_one, axis=0)
    input_grad = (middle_grad + rms_back(normed_one_grad * gain_attn, inputs, scale_one)).astype(
        jnp.bfloat16
    )
    query_w_grad = left_trans(first_normed, query_grad)
    key_w_grad = left_trans(first_normed, key_gradient)
    value_w_grad = left_trans(first_normed, value_gradient)
    out_w_grad = left_trans(attended_low, branch_gradient)
    router_grad = left_trans(normed_two, logit_grad)
    shard_grads = (
        lax.psum_scatter(
            query_w_grad.astype(jnp.bfloat16), "fsdp", scatter_dimension=0, tiled=True
        ).astype(jnp.float32),
        lax.psum_scatter(
            key_w_grad.astype(jnp.bfloat16), "fsdp", scatter_dimension=0, tiled=True
        ).astype(jnp.float32),
        lax.psum_scatter(
            value_w_grad.astype(jnp.bfloat16), "fsdp", scatter_dimension=0, tiled=True
        ).astype(jnp.float32),
        lax.psum_scatter(
            out_w_grad.astype(jnp.bfloat16), "fsdp", scatter_dimension=0, tiled=True
        ).astype(jnp.float32),
        lax.psum_scatter(
            router_grad.astype(jnp.bfloat16), "fsdp", scatter_dimension=0, tiled=True
        ).astype(jnp.float32),
        lax.psum_scatter(
            attn_gain_grad.astype(jnp.bfloat16), "fsdp", scatter_dimension=0, tiled=True
        ).astype(jnp.float32),
        lax.psum_scatter(
            mlp_gain_grad.astype(jnp.bfloat16), "fsdp", scatter_dimension=0, tiled=True
        ).astype(jnp.float32),
        lax.psum_scatter(
            q_gain_grad.astype(jnp.bfloat16), "fsdp", scatter_dimension=0, tiled=True
        ).astype(jnp.float32),
        lax.psum_scatter(
            k_gain_grad.astype(jnp.bfloat16), "fsdp", scatter_dimension=0, tiled=True
        ).astype(jnp.float32),
    )
    summed = jax.tree.map(
        lambda part: part.astype(jnp.float32), lax.psum(as_sent(tuple(shard_grads)), "exp")
    )
    return (
        layer_out,
        input_grad,
        summed[5],
        summed[0],
        summed[1],
        summed[2],
        summed[7],
        summed[8],
        summed[3],
        summed[6],
        summed[4],
        gate_w_grad[None],
        up_w_grad[None],
        down_grad[None],
    )


def solution(mesh):
    in_specs = (
        P(("exp", "fsdp"), None),
        P(("exp", "fsdp"), None),
        P(("exp", "fsdp"), None),
        P("fsdp"),
        P("fsdp", None),
        P("fsdp", None),
        P("fsdp", None),
        P("fsdp"),
        P("fsdp"),
        P("fsdp", None),
        P("fsdp"),
        P("fsdp", None),
        P(("exp", "fsdp"), None, None),
        P(("exp", "fsdp"), None, None),
        P(("exp", "fsdp"), None, None),
        P(("exp", "fsdp"), None),
    )
    out_specs = (
        P(("exp", "fsdp"), None),
        P(("exp", "fsdp"), None),
        P("fsdp"),
        P("fsdp", None),
        P("fsdp", None),
        P("fsdp", None),
        P("fsdp"),
        P("fsdp"),
        P("fsdp", None),
        P("fsdp"),
        P("fsdp", None),
        P(("exp", "fsdp"), None, None),
        P(("exp", "fsdp"), None, None),
        P(("exp", "fsdp"), None, None),
    )
    return jax.shard_map(local, mesh=mesh, in_specs=in_specs, out_specs=out_specs, check_vma=False)
```

profile of v0, /device:TPU:8, one launch (start us, length us, event | category | flops | bytes accessed | tf_op | source)
XLA Modules:
  0.0 1858.2 jit_solution(11151721271283755918)
XLA Ops:
  47.6 10.1 all-gather.9.cloned.1.call-done
  65.0 100.3 %all-gather.11.cloned.1.call-done = bf16[2048,4096]{1,0:T(8,128)(2,1)} async-done(((bf16[512,4096]{1,0:T(8,128)(2,1)}), bf16[2048,4096]{1,0:T(8,128)(2,1)}) %all-gather.11.cloned.1.call-update) | async-done | bytes 16777232 | tf_op jit(solution)/shard_map/all_gather | solution.py:128
  165.3 9.8 fusion.81
  187.5 85.1 %all-gather.13.cloned.1.call-done = bf16[4096,2048]{1,0:T(8,128)(2,1)} async-done(((bf16[1024,2048]{1,0:T(8,128)(2,1)}), bf16[4096,2048]{1,0:T(8,128)(2,1)}) %all-gather.13.cloned.1.call-update) | async-done | bytes 16777232 | tf_op jit(solution)/shard_map/all_gather | solution.py:131
  283.1 12.2 scatter_custom_fusion
  295.4 187.4 %all_to_all.20 = bf16[32,64,2048]{2,1,0:T(8,128)(2,1)S(1)} all-to-all(bf16[32,64,2048]{2,1,0:T(8,128)(2,1)} %bitcast.233), channel_id=1, replica_groups=mesh['exp'=8,'fsdp'=4] {'exp','fsdp'}, dimensions={0} | all-to-all | bytes 16777216 | tf_op jit(solution)/shard_map/all_to_all | solution.py:89
  515.1 47.2 %all_gather.35 = bf16[2048,32]{0,1:T(8,128)(2,1)S(1)} all-gather(bf16[512,32]{0,1:T(8,128)(2,1)S(1)} %copy-done.59), channel_id=1, replica_groups=mesh['exp'=8,'fsdp'=4] {'fsdp'}, dimensions={0}, use_global_device_ids=true | all-gather | bytes 163840 | tf_op jit(solution)/shard_map/all_gather | solution.py:132
  570.9 122.9 %all-to-all-done.1 = bf16[32,64,2048]{2,1,0:T(8,128)(2,1)} async-done(((bf16[32,64,2048]{2,1,0:T(8,128)(2,1)}), bf16[32,64,2048]{2,1,0:T(8,128)(2,1)}, u32[]{:S(2)}, u32[]{:S(2)}) %all-to-all-start.1) | async-done | bytes 8388640 | tf_op jit(solution)/shard_map/all_to_all | solution.py:93
  693.8 13.3 gather_fusion
  712.4 12.6 scatter_custom_fusion.1
  725.0 190.3 %all_to_all.21 = bf16[32,64,2048]{2,1,0:T(8,128)(2,1)S(1)} all-to-all(bf16[32,64,2048]{2,1,0:T(8,128)(2,1)} %bitcast.232), channel_id=1, replica_groups=mesh['exp'=8,'fsdp'=4] {'exp','fsdp'}, dimensions={0} | all-to-all | bytes 16777216 | tf_op jit(solution)/shard_map/all_to_all | solution.py:97
  915.3 16.4 multiply_convert_fusion
  931.7 12.4 fusion.20
  944.0 12.4 add_convert_fusion
  966.1 176.4 %all-to-all-done.3 = bf16[32,64,2048]{2,1,0:T(8,128)(2,1)} async-done(((bf16[32,64,2048]{2,1,0:T(8,128)(2,1)}), bf16[32,64,2048]{2,1,0:T(8,128)(2,1)}, u32[]{:S(2)}, u32[]{:S(2)}) %all-to-all-start.3) | async-done | bytes 8388640 | tf_op jit(solution)/shard_map/all_to_all | solution.py:101
  1142.5 13.3 gather_fusion.1
  1164.2 11.5 fusion.39
  1250.9 128.7 %reduce-scatter.12.cloned.1.call-done = bf16[1024,2048]{1,0:T(8,128)(2,1)} async-done(((bf16[4096,2048]{1,0:T(8,128)(2,1)}), bf16[1024,2048]{1,0:T(8,128)(2,1)}) %reduce-scatter.12.cloned.1.call-update) | async-done | bytes 4194320 | tf_op jit(solution)/shard_map/reduce_scatter | solution.py:320
  1379.6 128.9 %reduce-scatter.6.cloned.1.call-done = bf16[512,4096]{1,0:T(8,128)(2,1)} async-done(((bf16[2048,4096]{1,0:T(8,128)(2,1)}), bf16[512,4096]{1,0:T(8,128)(2,1)}) %reduce-scatter.6.cloned.1.call-update) | async-done | bytes 4194320 | tf_op jit(solution)/shard_map/reduce_scatter | solution.py:311
  1509.8 11.9 convolution_bitcast_fusion
  1521.8 11.1 convolution_bitcast_fusion.1
  1542.1 11.7 fusion.93
  1564.7 37.8 %all-reduce.6 = (bf16[512]{0:T(512)(128)(2,1)S(1)}, bf16[32]{0:T(256)(128)(2,1)S(1)}, bf16[32]{0:T(256)(128)(2,1)S(1)}, bf16[512]{0:T(512)(128)(2,1)S(1)}, bf16[512,32]{0,1:T(8,128)(2,1)S(1)}) all-reduce(bf16[512]{0:T(512)(128)(2,1)S(1)} %dynamic-slice.3, ...), channel_id=1, replica_groups=mesh['exp'=8,'fsdp'=4] {'exp'}, use_global_device_ids=true, to_apply=%region_26.27 | all-reduce | flops 17472 | bytes 69888 | tf_op jit(solution)/shard_map/psum | solution.py:340
  1606.4 229.1 %all-reduce.12.cloned.1.call-done = (bf16[512,4096]{1,0:T(8,128)(2,1)}, bf16[512,512]{1,0:T(8,128)(2,1)}, bf16[512,512]{1,0:T(8,128)(2,1)}, bf16[1024,2048]{1,0:T(8,128)(2,1)}) async-done(((bf16[512,4096]{1,0:T(8,128)(2,1)}, bf16[512,512]{1,0:T(8,128)(2,1)}, bf16[512,512]{1,0:T(8,128)(2,1)}, bf16[1024,2048]{1,0:T(8,128)(2,1)}), (bf16[512,4096]{1,0:T(8,128)(2,1)}, bf16[512,512]{1,0:T(8,128)(2,1)}, ...) | async-done | bytes 9437200 | tf_op jit(solution)/shard_map/psum | solution.py:340
  (336 shorter events, 248.0 us)
Async XLA Ops:
  7.2 491.4 %copy-start = (bf16[1,768,2048]{2,1,0:T(8,128)(2,1)S(1)}, bf16[1,768,2048]{2,1,0:T(8,128)(2,1)}, u32[]{:S(2)}) copy-start(bf16[1,768,2048]{2,1,0:T(8,128)(2,1)} %param.30) | copy-start | bytes 9437188
  7.2 37.5 %all-gather.7.cloned.1.call-start = ((), (), s32[]{:S(2)}) async-start(), calls=%async_computation.9 | async-start | bytes 2621440 | tf_op jit(solution)/shard_map/all_gather | solution.py:130
  7.9 49.8 %all-gather.9.cloned.1.call-start = ((), (), s32[]{:S(2)}) async-start(), calls=%async_computation.10 | async-start | bytes 2621440 | tf_op jit(solution)/shard_map/all_gather | solution.py:129
  8.7 156.6 %all-gather.11.cloned.1.call-start = ((), (), s32[]{:S(2)}) async-start(), calls=%async_computation.11 | async-start | bytes 20971520 | tf_op jit(solution)/shard_map/all_gather | solution.py:128
  9.5 21.8 %copy-start.75 = (s32[1,4]{1,0:T(1,128)S(1)}, s32[1,4]{1,0:T(1,128)}, u32[]{:S(2)}) copy-start(s32[1,4]{1,0:T(1,128)} %param.17) | copy-start | bytes 52
  9.5 263.1 %all-gather.13.cloned.1.call-start = ((), (), s32[]{:S(2)}) async-start(), calls=%async_computation.12 | async-start | bytes 20971520 | tf_op jit(solution)/shard_map/all_gather | solution.py:131
  31.1 134.2 %copy-start.33 = (f32[4,1,512]{2,1,0:T(1,128)}, f32[4,1,512]{2,1,0:T(1,128)S(1)}, u32[]{:S(2)}) copy-start(f32[4,1,512]{2,1,0:T(1,128)S(1)} %convert_element_type.253) | copy-start | bytes 24580
  42.4 122.9 %copy-start.57 = (f32[128]{0:T(128)}, f32[128]{0:T(128)S(1)}, u32[]{:S(2)}) copy-start(f32[128]{0:T(128)S(1)} %add_rsqrt_fusion.3) | copy-start | bytes 1540
  61.8 113.2 %copy-start.24 = (f32[128,4,128]{0,2,1:T(8,128)}, f32[128,4,128]{0,2,1:T(8,128)S(1)}, u32[]{:S(2)}) copy-start(f32[128,4,128]{0,2,1:T(8,128)S(1)} %copy.189) | copy-start | bytes 786436
  65.0 118.2 %copy-start.35 = (bf16[128,4,128,1]{0,2,3,1:T(8,128)(2,1)}, bf16[128,4,128,1]{0,2,3,1:T(8,128)(2,1)S(1)}, u32[]{:S(2)}) copy-start(bf16[128,4,128,1]{0,2,3,1:T(8,128)(2,1)S(1)} %fusion.58) | copy-start | bytes 393220
  281.2 14.1 copy-start.64
  295.4 187.4 %copy-start.69 = (bf16[1,2048,768]{2,1,0:T(8,128)(2,1)S(1)}, bf16[1,2048,768]{2,1,0:T(8,128)(2,1)}, u32[]{:S(2)}) copy-start(bf16[1,2048,768]{2,1,0:T(8,128)(2,1)} %param.28) | copy-start | bytes 9437188
  507.5 186.3 %all-to-all-start.1 = ((bf16[32,64,2048]{2,1,0:T(8,128)(2,1)}), bf16[32,64,2048]{2,1,0:T(8,128)(2,1)}, u32[]{:S(2)}, u32[]{:S(2)}) async-start(bf16[32,64,2048]{2,1,0:T(8,128)(2,1)} %bitcast.242), calls=%async_computation.1 | async-start | bytes 16777216 | tf_op jit(solution)/shard_map/all_to_all | solution.py:93
  915.3 16.4 copy-start.20
  915.3 16.4 copy-start.70
  956.4 186.1 %all-to-all-start.3 = ((bf16[32,64,2048]{2,1,0:T(8,128)(2,1)}), bf16[32,64,2048]{2,1,0:T(8,128)(2,1)}, u32[]{:S(2)}, u32[]{:S(2)}) async-start(bf16[32,64,2048]{2,1,0:T(8,128)(2,1)} %bitcast.243), calls=%async_computation.3 | async-start | bytes 16777216 | tf_op jit(solution)/shard_map/all_to_all | solution.py:101
  961.2 282.7 %reduce-scatter.8.cloned.1.call-start = ((), (), s32[]{:S(2)}) async-start(), calls=%async_computation.14 | async-start | bytes 2621440 | tf_op jit(solution)/shard_map/reduce_scatter | solution.py:314
  1183.8 67.1 %reduce-scatter.10.cloned.1.call-start = ((), (), s32[]{:S(2)}) async-start(), calls=%async_computation.15 | async-start | bytes 2621440 | tf_op jit(solution)/shard_map/reduce_scatter | solution.py:317
  1189.9 189.7 %reduce-scatter.12.cloned.1.call-start = ((), (), s32[]{:S(2)}) async-start(), calls=%async_computation.16 | async-start | bytes 20971520 | tf_op jit(solution)/shard_map/reduce_scatter | solution.py:320
  1198.3 310.2 %reduce-scatter.6.cloned.1.call-start = ((), (), s32[]{:S(2)}) async-start(), calls=%async_computation.13 | async-start | bytes 20971520 | tf_op jit(solution)/shard_map/reduce_scatter | solution.py:311
  1242.0 322.7 %reduce-scatter.14.cloned.1.call-start = ((), (), s32[]{:S(2)}) async-start(), calls=%async_computation.17 | async-start | bytes 163840 | tf_op jit(solution)/shard_map/reduce_scatter | solution.py:323
  1243.9 591.7 %all-reduce.12.cloned.1.call-start = ((), (), s32[]{:S(2)}) async-start(), calls=%async_computation.18 | async-start | bytes 18874368 | tf_op jit(solution)/shard_map/psum | solution.py:340
  1509.8 23.1 %slice-start = ((s8[8388608]{0:T(1024)(128)(4,1)}), s8[4194304]{0:T(1024)(128)(4,1)S(1)}, s32[]{:S(2)}) async-start(s8[8388608]{0:T(1024)(128)(4,1)} %bitcast.237), calls=%async_computation.19 | async-start | bytes 8388608
  1556.4 48.9 %copy-start.11 = (f32[128,2048]{1,0:T(8,128)S(1)}, f32[128,2048]{1,0:T(8,128)}, u32[]{:S(2)}) copy-start(f32[128,2048]{1,0:T(8,128)} %copy-done.9) | copy-start | bytes 3145732
  (71 other events, 302.7 us)
Sparse Core Ops, SparseCore 0:
  9.6 23.8 all-gather.6
  35.0 22.6 all-gather.8
  59.3 105.9 all-gather.10
  166.7 105.9 all-gather.12
  1183.9 32.9 reduce-scatter.7
  1219.4 31.3 reduce-scatter.9
  1253.4 126.1 reduce-scatter.11
  1382.4 126.0 reduce-scatter.5
  1511.5 19.5 reduce-scatter.13
  1536.1 299.4 all-reduce.11
where the time goes:
time: 1870 us; the launch traced here: 1860 us
  waiting for transfers between devices  991 us (53%)
  blocking collectives  487 us (26%)
  matrix products  189 us (10%)
  local copies, waits for them, and re-layouts  82.1 us (4%)
  other arithmetic  81.5 us (4%)
    psum x1, waiting for transfers between devices, local(): lax.psum(as_sent(tuple(shard_grads)), 'exp')  229 us
    all_to_all x1, blocking collectives, output_grad_rows(): lax.all_to_all(buffer, ('exp', 'fsdp'), split_axis=0, concat_axis=0, tile...  190 us
    all_to_all x1, blocking collectives, dispatch_rows(): lax.all_to_all(buffer, ('exp', 'fsdp'), split_axis=0, concat_axis=0, tile...  187 us
    all_to_all x1, waiting for transfers between devices, input_grad_rows(): lax.all_to_all(buffer, ('exp', 'fsdp'), split_axis=0, concat_axis=0, tile...  176 us
    reduce_scatter x1, waiting for transfers between devices, local(): lax.psum_scatter(query_w_grad.astype(jnp.bfloat16), 'fsdp', scatter_dimen...  129 us
    reduce_scatter x1, waiting for transfers between devices, local(): lax.psum_scatter(out_w_grad.astype(jnp.bfloat16), 'fsdp', scatter_dimensi...  129 us
    all_to_all x1, waiting for transfers between devices, combine_rows(): lax.all_to_all(buffer, ('exp', 'fsdp'), split_axis=0, concat_axis=0, tile...  123 us
    all_gather x1, waiting for transfers between devices, local(): lax.all_gather(w_query, 'fsdp', axis=0, tiled=True)  100 us
  transfers between devices with their start and end apart: 12, of which 9 were waited for; matrix products, arithmetic and copies ran while one was open for 9% of the time, Pallas kernels for 0%

commit v1 on v0

v1 whole, which is shorter than its diff:
```python
import math

import jax
import jax.numpy as jnp
from jax import lax
from jax.sharding import PartitionSpec as P

MODEL_WIDTH = 2048
QUERY_HEADS = 32
KEY_VALUE_HEADS = 4
HEAD_WIDTH = 128


EPSILON = 1e-06
THETA = 1000000.0
MASKED = -1e30
BOTH = ("exp", "fsdp")


def matrix_product(left, right):
    return jnp.dot(left, right, preferred_element_type=jnp.float32)


def left_trans(left, right):
    return lax.dot_general(
        left, right, (((0,), (0,)), ((), ())), preferred_element_type=jnp.float32
    )


def right_transposed(left, right):
    return lax.dot_general(
        left, right, (((1,), (1,)), ((), ())), preferred_element_type=jnp.float32
    )


def contract(spec, left, right):
    return jnp.einsum(spec, left, right, preferred_element_type=jnp.float32)


def rms_scale(values):
    return lax.rsqrt(jnp.mean(values * values, axis=-1, keepdims=True) + EPSILON)


def rms_back(grad_hat, values, scale):
    normal = values * scale
    return scale * (grad_hat - normal * jnp.mean(grad_hat * normal, axis=-1, keepdims=True))


def seq_layout(length_row, token_count):
    ends = jnp.cumsum(length_row)
    starts = ends - length_row
    places = jnp.arange(token_count, dtype=jnp.int32)
    member = (places[:, None] >= starts[None, :]) & (places[:, None] < ends[None, :])
    numbers = jnp.arange(length_row.shape[0], dtype=jnp.int32)
    segment = jnp.sum(jnp.where(member, numbers[None, :], 0), axis=1)
    position = places - jnp.sum(jnp.where(member, starts[None, :], 0), axis=1)
    allowed = (segment[:, None] == segment[None, :]) & (places[None, :] <= places[:, None])
    return (position, allowed)


def rotary_tables(position, head_size):
    half = head_size // 2
    index = jnp.arange(head_size, dtype=jnp.int32) % half
    inverse = jnp.exp(index.astype(jnp.float32) * (-2.0 * math.log(THETA) / head_size))
    angles = position.astype(jnp.float32)[..., None] * inverse
    return (jnp.cos(angles)[..., None, :], jnp.sin(angles)[..., None, :])


def rotate(values, cosine, sine):
    half = values.shape[-1] // 2
    turned = jnp.concatenate([-values[..., half:], values[..., :half]], axis=-1)
    return values * cosine + turned * sine


def rotate_back(grads, cosine, sine):
    half = grads.shape[-1] // 2
    moved = grads * sine
    return grads * cosine + jnp.concatenate([moved[..., half:], -moved[..., :half]], axis=-1)


def slot_table(route_rows, experts, capacity):
    flat = route_rows.reshape(-1)
    onehot = (flat[:, None] == jnp.arange(experts, dtype=jnp.int32)[None, :]).astype(jnp.int32)
    ranks = jnp.cumsum(onehot, axis=0) - 1
    rank = jnp.sum(ranks * onehot, axis=1)
    return flat * capacity + rank


def exchange(buffer):
    return lax.all_to_all(buffer, BOTH, split_axis=0, concat_axis=0, tiled=True)


def two_halves(values):
    high = values.astype(jnp.bfloat16)
    low = (values - high.astype(jnp.float32)).astype(jnp.bfloat16)
    return high, low


def expert_forward(arrived, gate_w, up_w):
    gate_pre = matrix_product(arrived, gate_w)
    up_pre = matrix_product(arrived, up_w)
    sigma = jax.nn.sigmoid(gate_pre)
    active = (gate_pre * sigma * up_pre).astype(jnp.bfloat16)
    return gate_pre, up_pre, sigma, active


def expert_back(arrived, out_rows, hidden, gate_w, up_w, down_w):
    gate_pre, up_pre, sigma, active = hidden
    active_grad = right_transposed(out_rows, down_w)
    gate_pre_grad = (active_grad * up_pre * (sigma * (1.0 + gate_pre * (1.0 - sigma)))).astype(
        jnp.bfloat16
    )
    up_pre_grad = (active_grad * (gate_pre * sigma)).astype(jnp.bfloat16)
    rows_back = right_transposed(gate_pre_grad, gate_w) + right_transposed(up_pre_grad, up_w)
    return (
        rows_back.astype(jnp.bfloat16),
        left_trans(arrived, gate_pre_grad),
        left_trans(arrived, up_pre_grad),
        left_trans(active, out_rows),
    )


def gates_of(logits, routes, experts):
    picked = jnp.take_along_axis(logits, routes, axis=1)
    peak = jnp.max(picked, axis=1, keepdims=True)
    lifted = jnp.exp(picked - peak)
    return lifted / jnp.sum(lifted, axis=1, keepdims=True)


def moe_gathered(normed, router, routes, capacity, cotangent, weights):
    gate_w, up_w, down_w = weights
    token_count = normed.shape[0]
    experts = router.shape[1]
    mine = lax.axis_index("exp") * lax.axis_size("fsdp") + lax.axis_index("fsdp")
    all_routes = lax.all_gather(routes, BOTH, axis=0, tiled=True)
    all_grads = lax.all_gather(cotangent, BOTH, axis=0, tiled=True)
    columns = jnp.arange(experts, dtype=jnp.int32)
    named = jnp.any(all_routes[:, :, None] == columns[None, None, :], axis=1)
    own = jnp.any(all_routes == mine, axis=1).reshape(experts, token_count)
    before = jnp.tril(jnp.ones((token_count, token_count), jnp.bfloat16), -1)
    rank = right_transposed(own.astype(jnp.bfloat16), before).astype(jnp.int32)
    places = jnp.arange(capacity, dtype=jnp.int32)
    select = (own[:, None, :] & (rank[:, None, :] == places[None, :, None])).astype(jnp.bfloat16)
    grad_rows = contract(
        "bcj,bjd->bcd", select, all_grads.reshape(experts, token_count, MODEL_WIDTH)
    ).astype(jnp.bfloat16)
    grad_rows = grad_rows.reshape(experts * capacity, MODEL_WIDTH)

    all_normed = lax.all_gather(normed, BOTH, axis=0, tiled=True)
    logits = matrix_product(all_normed, router)
    masked = jnp.where(named, logits, MASKED)
    peak = jnp.max(masked, axis=1, keepdims=True)
    lifted = jnp.exp(masked - peak)
    own_gate = jnp.sum(jnp.where(columns[None, :] == mine, lifted, 0.0), axis=1) / jnp.sum(
        lifted, axis=1
    )
    row_gate = jnp.sum(
        jnp.where(select > 0, own_gate.reshape(experts, 1, token_count), 0.0), axis=2
    ).reshape(experts * capacity, 1)
    arrived = (
        contract("bcj,bjd->bcd", select, all_normed.reshape(experts, token_count, MODEL_WIDTH))
        .astype(jnp.bfloat16)
        .reshape(experts * capacity, MODEL_WIDTH)
    )
    hidden = expert_forward(arrived, gate_w, up_w)
    out_rows = (row_gate * grad_rows.astype(jnp.float32)).astype(jnp.bfloat16)
    rows_back, gate_w_grad, up_w_grad, down_grad = expert_back(
        arrived, out_rows, hidden, gate_w, up_w, down_w
    )
    produced = matrix_product(hidden[3], down_w).astype(jnp.bfloat16)
    row_grad = jnp.sum(produced.astype(jnp.float32) * grad_rows.astype(jnp.float32), axis=1)
    weighted = (row_gate * produced.astype(jnp.float32)).astype(jnp.bfloat16)

    def spread(rows):
        rows = rows.reshape(experts, capacity, rows.shape[1])
        return (
            contract("bcj,bcd->bjd", select, rows)
            .astype(jnp.bfloat16)
            .reshape(experts * token_count, rows.shape[2])
        )

    own_grad = jnp.sum(
        jnp.where(select > 0, row_grad.reshape(experts, capacity, 1), 0.0), axis=1
    ).reshape(experts * token_count, 1)
    placed = jnp.where(columns[None, :] == mine, own_grad, 0.0)
    high, low = two_halves(placed)
    back = lax.psum_scatter(
        jnp.concatenate([spread(rows_back), high, low], axis=1),
        BOTH,
        scatter_dimension=0,
        tiled=True,
    )
    mixed = lax.psum_scatter(spread(weighted), BOTH, scatter_dimension=0, tiled=True)
    summed = back[:, :MODEL_WIDTH].astype(jnp.float32)
    high = back[:, MODEL_WIDTH : MODEL_WIDTH + experts].astype(jnp.float32)
    low = back[:, MODEL_WIDTH + experts :].astype(jnp.float32)
    gate_grad = jnp.take_along_axis(high + low, routes, axis=1)
    gates = gates_of(matrix_product(normed, router), routes, experts)
    return mixed.astype(jnp.float32), summed, gates, gate_grad, gate_w_grad, up_w_grad, down_grad


def moe_exchanged(normed, router, routes, capacity, cotangent, weights):
    gate_w, up_w, down_w = weights
    token_count, topk = routes.shape
    experts = router.shape[1]
    gates = gates_of(matrix_product(normed, router), routes, experts)
    slots = slot_table(routes, experts, capacity)

    def send(rows):
        packed = jnp.zeros((experts * capacity, MODEL_WIDTH), jnp.bfloat16).at[slots].set(rows)
        return exchange(packed.reshape(experts, capacity, MODEL_WIDTH)).reshape(
            experts * capacity, MODEL_WIDTH
        )

    def bring(rows):
        rows = exchange(rows.reshape(experts, capacity, MODEL_WIDTH))
        return rows.reshape(experts * capacity, MODEL_WIDTH)[slots].reshape(
            token_count, topk, MODEL_WIDTH
        )

    arrived = send(jnp.repeat(normed, topk, axis=0))
    hidden = expert_forward(arrived, gate_w, up_w)
    scaled = (gates[:, :, None] * cotangent.astype(jnp.float32)[:, None, :]).astype(jnp.bfloat16)
    out_rows = send(scaled.reshape(token_count * topk, MODEL_WIDTH))
    rows_back, gate_w_grad, up_w_grad, down_grad = expert_back(
        arrived, out_rows, hidden, gate_w, up_w, down_w
    )
    returned = bring(matrix_product(hidden[3], down_w).astype(jnp.bfloat16))
    mixed = jnp.einsum("tk,tkd->td", gates, returned.astype(jnp.float32))
    gate_grad = jnp.einsum("td,tkd->tk", cotangent, returned, preferred_element_type=jnp.float32)
    summed = jnp.sum(bring(rows_back), axis=1, dtype=jnp.float32)
    return mixed, summed, gates, gate_grad, gate_w_grad, up_w_grad, down_grad


def local(
    tokens,
    lengths,
    routes,
    attn_gain,
    w_query,
    key_weight,
    value_weight,
    q_gain,
    k_gain,
    w_out,
    mlp_gain,
    w_router,
    expert_gate,
    expert_up,
    expert_down,
    cotangent,
):
    shards, members = lax.axis_size("fsdp"), lax.axis_size("exp")
    experts = shards * members
    token_count, topk = routes.shape
    capacity = 2 * token_count * topk // experts
    group = shards * token_count
    depth = w_query.shape[0]
    heads = QUERY_HEADS // shards
    kv_heads = max(1, KEY_VALUE_HEADS // shards)
    copies = shards * kv_heads // KEY_VALUE_HEADS
    head_group = heads // kv_heads
    wide, narrow = heads * HEAD_WIDTH, kv_heads * HEAD_WIDTH
    place = lax.axis_index("fsdp")

    gathered = lax.all_gather(
        jnp.concatenate([w_router.reshape(-1), attn_gain, mlp_gain, q_gain, k_gain]), "fsdp"
    )
    cuts, start = [], 0
    for leaf in (w_router, attn_gain, mlp_gain, q_gain, k_gain):
        cuts.append(gathered[:, start : start + leaf.size])
        start += leaf.size
    router = cuts[0].reshape(MODEL_WIDTH, experts)
    gain_attn, gain_mlp, gain_query, gain_key = [
        cut.reshape(-1).astype(jnp.float32) for cut in cuts[1:]
    ]
    all_lengths = lax.all_gather(lengths[0], "fsdp")

    def by_shard(weight):
        weight = weight.reshape(depth, KEY_VALUE_HEADS, HEAD_WIDTH)
        return jnp.repeat(weight, copies, axis=1).reshape(depth, shards, narrow)

    joined = jnp.concatenate(
        [w_query.reshape(depth, shards, wide), by_shard(key_weight), by_shard(value_weight)], axis=2
    ).transpose(1, 0, 2)

    inputs = tokens.astype(jnp.float32)
    scale_one = rms_scale(inputs)
    first_normed = (inputs * scale_one * gain_attn).astype(jnp.bfloat16)
    hidden = lax.all_to_all(first_normed, "fsdp", split_axis=1, concat_axis=0, tiled=True)
    partial = contract("gk,nkc->ngc", hidden, joined).astype(jnp.bfloat16)
    raw = lax.psum_scatter(partial, "fsdp", scatter_dimension=0, tiled=True)[0].astype(jnp.float32)
    raw = raw.reshape(shards, token_count, wide + 2 * narrow)
    query_raw = raw[:, :, :wide].reshape(shards, token_count, heads, HEAD_WIDTH)
    key_raw = raw[:, :, wide : wide + narrow].reshape(shards, token_count, kv_heads, HEAD_WIDTH)
    value = (
        raw[:, :, wide + narrow :]
        .astype(jnp.bfloat16)
        .reshape(shards, token_count, kv_heads, HEAD_WIDTH)
    )
    position, allowed = jax.vmap(lambda row: seq_layout(row, token_count))(all_lengths)
    cosine, sine = rotary_tables(position, HEAD_WIDTH)
    query_scale = rms_scale(query_raw)
    query_hat = query_raw * query_scale
    key_scale = rms_scale(key_raw)
    key_hat = key_raw * key_scale
    query = (
        rotate(query_hat * gain_query, cosine, sine)
        .astype(jnp.bfloat16)
        .reshape(shards, token_count, kv_heads, head_group, HEAD_WIDTH)
    )
    key = rotate(key_hat * gain_key, cosine, sine).astype(jnp.bfloat16)
    scores = contract("bqkgd,bpkd->bkgqp", query, key) * HEAD_WIDTH ** (-0.5)
    scores = jnp.where(allowed[:, None, None], scores, MASKED)
    top = jnp.max(scores, axis=-1, keepdims=True)
    raised = jnp.exp(scores - top)
    probs = raised / jnp.sum(raised, axis=-1, keepdims=True)
    probs_low = probs.astype(jnp.bfloat16)
    attended = contract("bkgqp,bpkd->bqkgd", probs_low, value).astype(jnp.bfloat16)
    attended = attended.reshape(group, wide)
    mixed_heads = lax.psum_scatter(
        matrix_product(attended, w_out).astype(jnp.bfloat16), "fsdp", scatter_dimension=0, tiled=True
    )
    middle = inputs + mixed_heads.astype(jnp.float32)
    scale_two = rms_scale(middle)
    normed = (middle * scale_two * gain_mlp).astype(jnp.bfloat16)

    moe = moe_gathered if capacity * experts * 2 >= token_count * experts else moe_exchanged
    mixed, summed, gates, gate_grad, gate_w_grad, up_w_grad, down_grad = moe(
        normed,
        router,
        routes,
        capacity,
        cotangent,
        (expert_gate[0], expert_up[0], expert_down[0]),
    )
    layer_out = (middle + mixed).astype(jnp.bfloat16)

    upstream = cotangent.astype(jnp.float32)
    picked_grad = gates * (gate_grad - jnp.sum(gates * gate_grad, axis=1, keepdims=True))
    onehot = routes[:, :, None] == jnp.arange(experts, dtype=jnp.int32)[None, None, :]
    logit_grad = jnp.sum(jnp.where(onehot, picked_grad[:, :, None], 0.0), axis=1).astype(
        jnp.bfloat16
    )
    normed_grad = summed + right_transposed(logit_grad, router)
    mlp_gain_grad = jnp.sum(normed_grad * middle * scale_two, axis=0)
    router_grad = left_trans(normed, logit_grad)
    middle_grad = upstream + rms_back(normed_grad * gain_mlp, middle, scale_two)
    branch_grad = lax.all_gather(middle_grad.astype(jnp.bfloat16), "fsdp", axis=0, tiled=True)
    out_w_grad = left_trans(attended, branch_grad)
    attended_grad = (
        right_transposed(branch_grad, w_out)
        .astype(jnp.bfloat16)
        .reshape(shards, token_count, kv_heads, head_group, HEAD_WIDTH)
    )
    prob_grad = contract("bqkgd,bpkd->bkgqp", attended_grad, value)
    value_grad = contract("bkgqp,bqkgd->bpkd", probs_low, attended_grad)
    balance = jnp.sum(probs * prob_grad, axis=-1, keepdims=True)
    score_grad = (probs * (prob_grad - balance)).astype(jnp.bfloat16)
    query_norm_grad = contract("bkgqp,bpkd->bqkgd", score_grad, key) * HEAD_WIDTH ** (-0.5)
    query_norm_grad = query_norm_grad.reshape(shards, token_count, heads, HEAD_WIDTH)
    key_norm_grad = contract("bkgqp,bqkgd->bpkd", score_grad, query) * HEAD_WIDTH ** (-0.5)
    query_norm_grad = rotate_back(query_norm_grad, cosine, sine)
    key_norm_grad = rotate_back(key_norm_grad, cosine, sine)
    q_gain_grad = jnp.sum(query_norm_grad * query_hat, axis=(0, 1, 2))
    k_gain_grad = jnp.sum(key_norm_grad * key_hat, axis=(0, 1, 2))
    query_grad = rms_back(query_norm_grad * gain_query, query_raw, query_scale)
    key_grad = rms_back(key_norm_grad * gain_key, key_raw, key_scale)
    head_grads = jnp.concatenate(
        [
            query_grad.reshape(group, wide),
            key_grad.reshape(group, narrow),
            value_grad.reshape(group, narrow),
        ],
        axis=1,
    ).astype(jnp.bfloat16)
    head_grads = lax.all_gather(head_grads, "fsdp")
    hidden_grad = contract("ngc,nkc->gk", head_grads, joined).astype(jnp.bfloat16)
    first_grad = lax.all_to_all(
        hidden_grad, "fsdp", split_axis=0, concat_axis=1, tiled=True
    ).astype(jnp.float32)
    attn_gain_grad = jnp.sum(first_grad * inputs * scale_one, axis=0)
    input_grad = (middle_grad + rms_back(first_grad * gain_attn, inputs, scale_one)).astype(
        jnp.bfloat16
    )
    joined_grad = contract("gk,ngc->nkc", hidden, head_grads).astype(jnp.bfloat16)

    out_sum = lax.psum(out_w_grad.astype(jnp.bfloat16), "exp").astype(jnp.float32)
    joined_sum = lax.psum(joined_grad, "exp").astype(jnp.float32)
    vectors = jnp.concatenate(
        [router_grad.reshape(-1), attn_gain_grad, mlp_gain_grad, q_gain_grad, k_gain_grad]
    )
    vectors = lax.psum(vectors, BOTH)
    sums, start = [], 0
    for leaf in (w_router, attn_gain, mlp_gain, q_gain, k_gain):
        sums.append(
            lax.dynamic_slice_in_dim(vectors, start + place * leaf.size, leaf.size).reshape(
                leaf.shape
            )
        )
        start += leaf.size * shards

    def gather_heads(part):
        return part.transpose(1, 0, 2).reshape(depth, KEY_VALUE_HEADS, copies, HEAD_WIDTH).sum(
            axis=2
        ).reshape(depth, KEY_VALUE_HEADS * HEAD_WIDTH)

    return (
        layer_out,
        input_grad,
        sums[1],
        joined_sum[:, :, :wide].transpose(1, 0, 2).reshape(depth, QUERY_HEADS * HEAD_WIDTH),
        gather_heads(joined_sum[:, :, wide : wide + narrow]),
        gather_heads(joined_sum[:, :, wide + narrow :]),
        sums[3],
        sums[4],
        out_sum,
        sums[2],
        sums[0],
        gate_w_grad[None],
        up_w_grad[None],
        down_grad[None],
    )


def solution(mesh):
    in_specs = (
        P(("exp", "fsdp"), None),
        P(("exp", "fsdp"), None),
        P(("exp", "fsdp"), None),
        P("fsdp"),
        P("fsdp", None),
        P("fsdp", None),
        P("fsdp", None),
        P("fsdp"),
        P("fsdp"),
        P("fsdp", None),
        P("fsdp"),
        P("fsdp", None),
        P(("exp", "fsdp"), None, None),
        P(("exp", "fsdp"), None, None),
        P(("exp", "fsdp"), None, None),
        P(("exp", "fsdp"), None),
    )
    out_specs = (
        P(("exp", "fsdp"), None),
        P(("exp", "fsdp"), None),
        P("fsdp"),
        P("fsdp", None),
        P("fsdp", None),
        P("fsdp", None),
        P("fsdp"),
        P("fsdp"),
        P("fsdp", None),
        P("fsdp"),
        P("fsdp", None),
        P(("exp", "fsdp"), None, None),
        P(("exp", "fsdp"), None, None),
        P(("exp", "fsdp"), None, None),
    )
    return jax.shard_map(local, mesh=mesh, in_specs=in_specs, out_specs=out_specs, check_vma=False)
```

time: 1870 us -> 1500 us (0.80)
  blocking collectives: 487 us -> 40.1 us
  local copies, waits for them, and re-layouts: 82.1 us -> 124 us
  waiting for transfers between devices: 991 us -> 1020 us
  matrix products: 189 us -> 216 us
    all_to_all x2 -> x0, blocking collectives: 378 us -> none  [the longest x1 190 us: output_grad_rows(): lax.all_to_all(buffer, ('exp', 'fsdp'), split_axis=0, concat_axis=0, tile...]
    all_to_all x2, waiting for transfers between devices: 299 us -> 8.89 us  [the longest x1 8.88 us: local(): lax.all_to_all(hidden_grad, 'fsdp', split_axis=0, concat_axis=1, tiled=True)]
    psum x1 -> x2, waiting for transfers between devices: 229 us -> 433 us  [the longest x1 295 us: local(): joined_sum = lax.psum(joined_grad, 'exp').astype(jnp.float32)]
    reduce_scatter x5 -> x4, waiting for transfers between devices: 265 us -> 364 us  [the longest x1 180 us: moe_gathered(): lax.psum_scatter(jnp.concatenate([spread(rows_back), high, low], axis=1),...]
    dot_general x8 -> x13, matrix products: 16 us -> 82 us  [contract(): return jnp.einsum(spec, left, right, preferred_element_type=jnp.float32)]
    psum x1 -> x0, blocking collectives: 37.8 us -> none  [local(): lax.psum(as_sent(tuple(shard_grads)), 'exp')]
    concatenate x0 -> x4, local copies, waits for them, and re-layouts: none -> 31.4 us  [the longest x1 25.7 us: moe_gathered(): jnp.concatenate([spread(rows_back), high, low], axis=1)]
    unnamed x10 -> x12, waiting for transfers between devices: 2.68 us -> 30.9 us
  transfers between devices with their start and end apart: 12 -> 13, of which waited for: 9 -> 12; matrix products, arithmetic and copies ran while one was open for 9% -> 9% of each run, Pallas kernels for 0% -> 0%
where the time goes in v1:
time: 1500 us; the launch traced here: 1490 us
  waiting for transfers between devices  1020 us (68%)
  matrix products  216 us (14%)
  local copies, waits for them, and re-layouts  124 us (8%)
  other arithmetic  63.8 us (4%)
  blocking collectives  40.1 us (3%)
  between operations  17.4 us (1%)
    psum x1, waiting for transfers between devices, local(): joined_sum = lax.psum(joined_grad, 'exp').astype(jnp.float32)  295 us
    reduce_scatter x1, waiting for transfers between devices, moe_gathered(): lax.psum_scatter(jnp.concatenate([spread(rows_back), high, low], axis=1),...  180 us
    psum x1, waiting for transfers between devices, local(): vectors = lax.psum(vectors, BOTH)  138 us
    reduce_scatter x1, waiting for transfers between devices, moe_gathered(): lax.psum_scatter(spread(weighted), BOTH, scatter_dimension=0, tiled=True)  106 us
    all_gather x1, waiting for transfers between devices, moe_gathered(): all_normed = lax.all_gather(normed, BOTH, axis=0, tiled=True)  105 us
    dot_general x13, matrix products, contract(): return jnp.einsum(spec, left, right, preferred_element_type=jnp.float32)  82 us
    dot_general x6, matrix products, matrix_product(): return jnp.dot(left, right, preferred_element_type=jnp.float32)  51 us
    reduce_scatter x1, waiting for transfers between devices, local(): lax.psum_scatter(partial, 'fsdp', scatter_dimension=0, tiled=True)[0]  46.4 us
  transfers between devices with their start and end apart: 13, of which 12 were waited for; matrix products, arithmetic and copies ran while one was open for 9% of the time, Pallas kernels for 0%

profile of v1, /device:TPU:8, one launch (start us, length us, event | category | flops | bytes accessed | tf_op | source)
XLA Modules:
  0.0 1487.9 jit_solution(401731751144188976)
XLA Ops:
  16.5 30.2 %all-reduce.8.cloned.1.call-done = bf16[69888]{0:T(1024)(128)(2,1)} async-done(((bf16[69888]{0:T(1024)(128)(2,1)}), bf16[69888]{0:T(1024)(128)(2,1)}) %all-reduce.8.cloned.1.call-update) | async-done | bytes 139792
  79.2 46.4 %reduce-scatter.5.cloned.1.call-done = bf16[1,512,1280]{1,2,0:T(8,128)(2,1)} async-done(((bf16[4,512,1280]{1,2,0:T(8,128)(2,1)}), bf16[1,512,1280]{1,2,0:T(8,128)(2,1)}) %reduce-scatter.5.cloned.1.call-update) | async-done | bytes 1310736 | tf_op jit(solution)/shard_map/reduce_scatter | solution.py:292
  147.9 30.9 %reduce-scatter.7.cloned.1.call-done = bf16[128,2048]{1,0:T(8,128)(2,1)} async-done(((bf16[512,2048]{1,0:T(8,128)(2,1)}), bf16[128,2048]{1,0:T(8,128)(2,1)}) %reduce-scatter.7.cloned.1.call-update) | async-done | bytes 524304 | tf_op jit(solution)/shard_map/reduce_scatter | solution.py:321
  182.9 34.8 %all_gather.28 = s32[4096,8]{0,1:T(8,128)S(1)} all-gather(s32[128,8]{0,1:T(8,128)S(1)} %copy-done.53), channel_id=1, replica_groups=mesh['exp'=8,'fsdp'=4] {'exp','fsdp'}, dimensions={0}, use_global_device_ids=true | all-gather | bytes 135168 | tf_op jit(solution)/shard_map/all_gather | solution.py:135
  219.8 45.9 %all-gather.9.cloned.1.call-done = bf16[4096,2048]{1,0:T(8,128)(2,1)} async-done(((bf16[128,2048]{1,0:T(8,128)(2,1)}), bf16[4096,2048]{1,0:T(8,128)(2,1)}) %all-gather.9.cloned.1.call-update) | async-done | bytes 16777232 | tf_op jit(solution)/shard_map/all_gather | solution.py:136
  265.7 11.5 convolution_convert_fusion.4
  277.2 105.2 %all-gather.7.cloned.1.call-done = bf16[4096,2048]{1,0:T(8,128)(2,1)} async-done(((bf16[128,2048]{1,0:T(8,128)(2,1)}), bf16[4096,2048]{1,0:T(8,128)(2,1)}) %all-gather.7.cloned.1.call-update) | async-done | bytes 16777232 | tf_op jit(solution)/shard_map/all_gather | solution.py:149
  382.4 11.6 convolution_convert_fusion.5
  394.0 11.8 fusion.16
  405.9 11.5 multiply_convert_fusion.2
  426.9 11.7 fusion.117
  449.7 14.1 multiply_convert_fusion
  473.4 12.7 add_convert_fusion
  486.1 13.7 convolution_convert_fusion
  500.8 25.7 %concatenate.57 = bf16[4096,2112]{1,0:T(8,128)(2,1)} concatenate(bf16[4096,2048]{1,0:T(8,128)(2,1)} %bitcast.312, bf16[4096,32]{1,0:T(8,128)(2,1)S(1)} %copy.198, bf16[4096,32]{1,0:T(8,128)(2,1)S(1)} %copy.199), dimensions={1} | concatenate | bytes 34603008 | tf_op jit(solution)/shard_map/concatenate | solution.py:188
  535.2 180.3 %reduce-scatter.11.cloned.1.call-done = bf16[128,2112]{1,0:T(8,128)(2,1)} async-done(((bf16[4096,2112]{1,0:T(8,128)(2,1)}), bf16[128,2112]{1,0:T(8,128)(2,1)}) %reduce-scatter.11.cloned.1.call-update) | async-done | bytes 540688 | tf_op jit(solution)/shard_map/reduce_scatter | solution.py:187
  738.3 19.4 %all-gather.11.cloned.1.call-done = bf16[512,2048]{1,0:T(8,128)(2,1)} async-done(((bf16[128,2048]{1,0:T(8,128)(2,1)}), bf16[512,2048]{1,0:T(8,128)(2,1)}) %all-gather.11.cloned.1.call-update) | async-done | bytes 2097168 | tf_op jit(solution)/shard_map/all_gather | solution.py:349
  793.2 14.9 %fusion.3 = (bf16[2048,2048]{1,0:T(8,128)(2,1)}, bf16[2048,2048]{1,0:T(8,128)(2,1)}) fusion(bf16[32,64,2048]{2,1,0:T(8,128)(2,1)} %convolution_convert_fusion.4, f32[2048]{0:T(1024)S(1)} %mul.518, bf16[2048,2048]{1,0:T(8,128)(2,1)} %get-tuple-element.139), kind=kLoop, calls=%fused_computation.9 | loop fusion | flops 25165824 | bytes 33562624 | tf_op jit(solution)/shard_map/convert_element_type | solution.py:166
  808.1 13.7 convolution_convert_fusion.1
  870.5 12.2 convolution_bitcast_fusion
  882.7 11.2 convolution_bitcast_fusion.1
  902.9 106.3 %reduce-scatter.9.cloned.1.call-done = bf16[128,2048]{1,0:T(8,128)(2,1)} async-done(((bf16[4096,2048]{1,0:T(8,128)(2,1)}), bf16[128,2048]{1,0:T(8,128)(2,1)}) %reduce-scatter.9.cloned.1.call-update) | async-done | bytes 524304 | tf_op jit(solution)/shard_map/reduce_scatter | solution.py:193
  1012.4 137.7 %all-reduce.6.cloned.1.call-done = f32[69888]{0:T(1024)} async-done(((f32[69888]{0:T(1024)}), f32[69888]{0:T(1024)}) %all-reduce.6.cloned.1.call-update) | async-done | bytes 279568 | tf_op jit(solution)/shard_map/psum | solution.py:393
  1154.7 295.5 %all-reduce.10.cloned.1.call-done = (bf16[4,512,1280]{1,2,0:T(8,128)(2,1)}, bf16[1024,2048]{1,0:T(8,128)(2,1)}) async-done(((bf16[4,512,1280]{1,2,0:T(8,128)(2,1)}, bf16[1024,2048]{1,0:T(8,128)(2,1)}), (bf16[4,512,1280]{1,2,0:T(8,128)(2,1)}, bf16[1024,2048]{1,0:T(8,128)(2,1)})) %all-reduce.10.cloned.1.call-update) | async-done | bytes 9437200 | tf_op jit(solution)/shard_map/psum | solution.py:389
  (337 shorter events, 261.5 us)
Async XLA Ops:
  8.0 409.4 %copy-start = (bf16[1,768,2048]{2,1,0:T(8,128)(2,1)S(1)}, bf16[1,768,2048]{2,1,0:T(8,128)(2,1)}, u32[]{:S(2)}) copy-start(bf16[1,768,2048]{2,1,0:T(8,128)(2,1)} %param.32) | copy-start | bytes 9437188
  8.0 38.7 %all-reduce.8.cloned.1.call-start = ((), (), s32[]{:S(2)}) async-start(), calls=%async_computation.15 | async-start | bytes 282624
  16.5 44.1 %copy-start.61 = (f32[128]{0:T(128)}, f32[128]{0:T(128)S(1)}, u32[]{:S(2)}) copy-start(f32[128]{0:T(128)S(1)} %add_rsqrt_fusion.3) | copy-start | bytes 1540
  50.0 14.7 all-to-all-start
  54.2 71.5 %reduce-scatter.5.cloned.1.call-start = ((), (), s32[]{:S(2)}) async-start(), calls=%async_computation.6 | async-start | bytes 6553600 | tf_op jit(solution)/shard_map/reduce_scatter | solution.py:292
  72.6 106.2 %reduce-scatter.7.cloned.1.call-start = ((), (), s32[]{:S(2)}) async-start(), calls=%async_computation.7 | async-start | bytes 2621440 | tf_op jit(solution)/shard_map/reduce_scatter | solution.py:321
  78.7 53.2 %copy-start.65 = (f32[128]{0:T(128)}, f32[128]{0:T(128)S(1)}, u32[]{:S(2)}) copy-start(f32[128]{0:T(128)S(1)} %fusion.101) | copy-start | bytes 1540
  78.8 53.1 %copy-start.55 = (f32[4,128]{1,0:T(4,128)}, f32[4,128]{1,0:T(4,128)S(1)}, u32[]{:S(2)}) copy-start(f32[4,128]{1,0:T(4,128)S(1)} %subtract_convert_fusion) | copy-start | bytes 6148
  79.1 52.8 %copy-start.59 = (f32[128]{0:T(128)}, f32[128]{0:T(128)S(1)}, u32[]{:S(2)}) copy-start(f32[128]{0:T(128)S(1)} %reshape.523) | copy-start | bytes 1540
  79.2 54.1 %copy-start.57 = (f32[128]{0:T(128)}, f32[128]{0:T(128)S(1)}, u32[]{:S(2)}) copy-start(f32[128]{0:T(128)S(1)} %reshape.524) | copy-start | bytes 1540
  147.2 71.5 %slice-start.4 = ((bf16[4,17472]{1,0:T(4,128)(2,1)}), bf16[4,16384]{1,0:T(4,128)(2,1)S(1)}, s32[]{:S(2)}) async-start(bf16[4,17472]{1,0:T(4,128)(2,1)} %copy-done.35), calls=%async_computation.21 | async-start | bytes 262144 | tf_op jit(solution)/shard_map/slice | solution.py:271
  147.2 118.4 %all-gather.9.cloned.1.call-start = ((), (), s32[]{:S(2)}) async-start(), calls=%async_computation.10 | async-start | bytes 17301504 | tf_op jit(solution)/shard_map/all_gather | solution.py:136
  147.8 234.5 %all-gather.7.cloned.1.call-start = ((), (), s32[]{:S(2)}) async-start(), calls=%async_computation.8 | async-start | bytes 17301504 | tf_op jit(solution)/shard_map/all_gather | solution.py:149
  147.9 69.9 %copy-start.49 = (f32[1,4,4,128]{3,1,2,0:T(4,128)}, f32[1,4,4,128]{3,1,2,0:T(4,128)S(1)}, u32[]{:S(2)}) copy-start(f32[1,4,4,128]{3,1,2,0:T(4,128)S(1)} %copy.248) | copy-start | bytes 24580
  180.3 37.5 %copy-start.63 = (f32[128]{0:T(128)}, f32[128]{0:T(128)S(1)}, u32[]{:S(2)}) copy-start(f32[128]{0:T(128)S(1)} %add_rsqrt_fusion.2) | copy-start | bytes 1540
  182.8 532.6 %reduce-scatter.11.cloned.1.call-start = ((), (), s32[]{:S(2)}) async-start(), calls=%async_computation.11 | async-start | bytes 18382848 | tf_op jit(solution)/shard_map/reduce_scatter | solution.py:187
  526.5 231.2 %all-gather.11.cloned.1.call-start = ((), (), s32[]{:S(2)}) async-start(), calls=%async_computation.12 | async-start | bytes 2621440 | tf_op jit(solution)/shard_map/all_gather | solution.py:349
  729.5 104.5 %all-gather.13.cloned.1.call-start = ((), (), s32[]{:S(2)}) async-start(), calls=%async_computation.13 | async-start | bytes 6553600 | tf_op jit(solution)/shard_map/all_gather | solution.py:377
  793.1 216.2 %reduce-scatter.9.cloned.1.call-start = ((), (), s32[]{:S(2)}) async-start(), calls=%async_computation.9 | async-start | bytes 17301504 | tf_op jit(solution)/shard_map/reduce_scatter | solution.py:193
  841.5 19.5 %all-to-all-start.1 = ((bf16[4,128,512]{2,1,0:T(8,128)(2,1)}), bf16[4,128,512]{2,1,0:T(8,128)(2,1)S(1)}, u32[]{:S(2)}, u32[]{:S(2)}) async-start(bf16[4,128,512]{2,1,0:T(8,128)(2,1)} %bitcast.69), calls=%async_computation.5 | async-start | bytes 1048576 | tf_op jit(solution)/shard_map/all_to_all | solution.py:379
  846.0 304.2 %all-reduce.6.cloned.1.call-start = ((), (), s32[]{:S(2)}) async-start(), calls=%async_computation.14 | async-start | bytes 565248 | tf_op jit(solution)/shard_map/psum | solution.py:393
  862.4 587.8 %all-reduce.10.cloned.1.call-start = ((), (), s32[]{:S(2)}) async-start(), calls=%async_computation.16 | async-start | bytes 18874368 | tf_op jit(solution)/shard_map/psum | solution.py:389
  893.9 115.3 %copy-start.17 = (bf16[128,2048]{1,0:T(8,128)(2,1)S(1)}, bf16[128,2048]{1,0:T(8,128)(2,1)}, u32[]{:S(2)}) copy-start(bf16[128,2048]{1,0:T(8,128)(2,1)} %reduce-scatter.7.cloned.1.call-done) | copy-start | bytes 1572868
  893.9 115.3 %copy-start.19 = (bf16[128,2048]{1,0:T(8,128)(2,1)S(1)}, bf16[128,2048]{1,0:T(8,128)(2,1)}, u32[]{:S(2)}) copy-start(bf16[128,2048]{1,0:T(8,128)(2,1)} %param.33) | copy-start | bytes 1572868
  (71 other events, 509.3 us)
Sparse Core Ops, SparseCore 0:
  15.4 31.2 all-reduce.7
  72.7 52.8 reduce-scatter.4
  147.4 31.4 reduce-scatter.6
  729.6 28.0 all-gather.10
  793.2 40.7 all-gather.12
Sparse Core Ops, SparseCore 1:
  151.0 114.6 all-gather.8
  269.4 112.9 all-gather.6
  526.6 188.8 reduce-scatter.10
  821.9 187.3 reduce-scatter.8
  1016.1 134.0 all-reduce.5
  1154.7 295.4 all-reduce.9

commit v2 on v1

--- a/solution.py
+++ b/solution.py
@@ -3,6 +3,8 @@
 import jax
 import jax.numpy as jnp
 from jax import lax
+from jax.experimental import pallas as pl
+from jax.experimental.pallas import tpu as pltpu
 from jax.sharding import PartitionSpec as P
 
 MODEL_WIDTH = 2048
@@ -15,6 +17,7 @@
 THETA = 1000000.0
 MASKED = -1e30
 BOTH = ("exp", "fsdp")
+MESH = pl.DeviceIdType.MESH
 
 
 def matrix_product(left, right):
@@ -104,20 +107,15 @@
     return gate_pre, up_pre, sigma, active
 
 
-def expert_back(arrived, out_rows, hidden, gate_w, up_w, down_w):
-    gate_pre, up_pre, sigma, active = hidden
+def expert_back(out_rows, hidden, gate_w, up_w, down_w):
+    gate_pre, up_pre, sigma, _ = hidden
     active_grad = right_transposed(out_rows, down_w)
     gate_pre_grad = (active_grad * up_pre * (sigma * (1.0 + gate_pre * (1.0 - sigma)))).astype(
         jnp.bfloat16
     )
     up_pre_grad = (active_grad * (gate_pre * sigma)).astype(jnp.bfloat16)
     rows_back = right_transposed(gate_pre_grad, gate_w) + right_transposed(up_pre_grad, up_w)
-    return (
-        rows_back.astype(jnp.bfloat16),
-        left_trans(arrived, gate_pre_grad),
-        left_trans(arrived, up_pre_grad),
-        left_trans(active, out_rows),
-    )
+    return rows_back.astype(jnp.bfloat16), gate_pre_grad, up_pre_grad
 
 
 def gates_of(logits, routes, experts):
@@ -125,6 +123,418 @@
     peak = jnp.max(picked, axis=1, keepdims=True)
     lifted = jnp.exp(picked - peak)
     return lifted / jnp.sum(lifted, axis=1, keepdims=True)
+
+
+def spot():
+    member, shard = lax.axis_index("exp"), lax.axis_index("fsdp")
+    return member // 2, member % 2, shard // 2, shard % 2
+
+def where_is(z, y, x, c):
+    return (z * 2 + y, x * 2 + c)
+
+def number(z, y, x, c):
+    return z * 8 + y * 4 + x * 2 + c
+
+def greet(peers):
+    barrier = pltpu.get_barrier_semaphore()
+    for peer in peers:
+        pl.semaphore_signal(barrier, inc=1, device_id=peer, device_id_type=MESH)
+    pl.semaphore_wait(barrier, len(peers))
+
+def gather_kernel(x_ref, select_ref, out_ref, held, arrive, to_z, to_y, to_x, to_core):
+    z, y, x, c = spot()
+    half = x_ref.shape[0] // 2
+    y_peer, x_peer, core_peer = (
+        where_is(z, 1 - y, x, c), where_is(z, y, 1 - x, c), where_is(z, y, x, 1 - c))
+    z_peers = [where_is((z + k) % 4, y, x, c) for k in range(1, 4)]
+    greet([y_peer, x_peer, core_peer] + z_peers)
+
+    def copy(block, part, sem, peer):
+        view = held.at[block, pl.ds(part * half, half)]
+        return pltpu.make_async_remote_copy(
+            src_ref=view, dst_ref=view, send_sem=sem, recv_sem=arrive.at[block, part],
+            device_id=peer, device_id_type=MESH)
+
+    def arrived(block, part):
+        copy(block, part, to_core.at[0, 0, 0], core_peer).wait_recv()
+
+    def pick(block):
+        out_ref[block] = jnp.dot(
+            select_ref[block], held[block], preferred_element_type=jnp.float32
+        ).astype(out_ref.dtype)
+
+    mine = number(z, y, x, c)
+    held[mine] = x_ref[...]
+    for k in range(1, 4):
+        for part in range(2):
+            copy(mine, part, to_z.at[k - 1, part], z_peers[k - 1]).start()
+
+    def first(k):
+        return number((z + k) % 4, y, x, c)
+
+    def second_y(k):
+        return number((z + k) % 4, 1 - y, x, c)
+
+    def second_x(k):
+        return number((z + k) % 4, y, 1 - x, c)
+
+    def third(k):
+        return number((z + k) % 4, 1 - y, 1 - x, c)
+
+    def forward_first(k):
+        block = first(k)
+        copy(block, 0, to_y.at[0, k], y_peer).start()
+        copy(block, 1, to_x.at[0, k], x_peer).start()
+        copy(block, 0, to_x.at[1, k], x_peer).start()
+        copy(block, 1, to_y.at[1, k], y_peer).start()
+        copy(block, 0, to_core.at[0, 0, k], core_peer).start()
+        copy(block, 1, to_core.at[0, 1, k], core_peer).start()
+
+    forward_first(0)
+    pick(mine)
+
+    @pl.loop(1, 4)
+    def _(k):
+        arrived(first(k), 0)
+        arrived(first(k), 1)
+        forward_first(k)
+        pick(first(k))
+
+    @pl.loop(0, 4)
+    def _(k):
+        arrived(second_y(k), 0)
+        copy(second_y(k), 0, to_x.at[2, k], x_peer).start()
+        copy(second_y(k), 0, to_core.at[1, 0, k], core_peer).start()
+        arrived(second_x(k), 1)
+        copy(second_x(k), 1, to_y.at[2, k], y_peer).start()
+        copy(second_x(k), 1, to_core.at[2, 1, k], core_peer).start()
+        block = number((z + k) % 4, y, x, 1 - c)
+        arrived(block, 0)
+        arrived(block, 1)
+        pick(block)
+
+    @pl.loop(0, 4)
+    def _(k):
+        arrived(second_x(k), 0)
+        copy(second_x(k), 0, to_core.at[2, 0, k], core_peer).start()
+        arrived(second_y(k), 1)
+        copy(second_y(k), 1, to_core.at[1, 1, k], core_peer).start()
+        pick(second_x(k))
+        pick(second_y(k))
+
+    @pl.loop(0, 4)
+    def _(k):
+        arrived(third(k), 0)
+        copy(third(k), 0, to_core.at[3, 0, k], core_peer).start()
+        arrived(third(k), 1)
+        copy(third(k), 1, to_core.at[3, 1, k], core_peer).start()
+        pick(third(k))
+        for (yy, xx) in ((1 - y, x), (y, 1 - x)):
+            block = number((z + k) % 4, yy, xx, 1 - c)
+            arrived(block, 0)
+            arrived(block, 1)
+            pick(block)
+
+    @pl.loop(0, 4)
+    def _(k):
+        block = number((z + k) % 4, 1 - y, 1 - x, 1 - c)
+        arrived(block, 0)
+        arrived(block, 1)
+        pick(block)
+
+    for k in range(1, 4):
+        for part in range(2):
+            copy(mine, part, to_z.at[k - 1, part], z_peers[k - 1]).wait_send()
+
+    @pl.loop(0, 4)
+    def _(k):
+        for i in range(3):
+            copy(mine, 0, to_y.at[i, k], y_peer).wait_send()
+            copy(mine, 0, to_x.at[i, k], x_peer).wait_send()
+        for i in range(4):
+            for part in range(2):
+                copy(mine, part, to_core.at[i, part, k], core_peer).wait_send()
+
+
+def gather_pick(rows, select, collective_id):
+    count, width = rows.shape
+    blocks, kept = select.shape[:2]
+    return pl.pallas_call(
+        gather_kernel,
+        out_shape=jax.ShapeDtypeStruct((blocks, kept, width), rows.dtype),
+        in_specs=[pl.BlockSpec(memory_space=pltpu.VMEM)] * 2,
+        out_specs=pl.BlockSpec(memory_space=pltpu.VMEM),
+        scratch_shapes=[
+            pltpu.VMEM((blocks, count, width), rows.dtype),
+            pltpu.SemaphoreType.DMA((blocks, 2)),
+            pltpu.SemaphoreType.DMA((3, 2)),
+            pltpu.SemaphoreType.DMA((3, 4)),
+            pltpu.SemaphoreType.DMA((3, 4)),
+            pltpu.SemaphoreType.DMA((4, 2, 4)),
+        ],
+        compiler_params=pltpu.CompilerParams(
+            collective_id=collective_id, has_side_effects=True, vmem_limit_bytes=56 << 20),
+    )(rows, select)
+
+
+def scatter_kernel(spread_ref, rows_ref, extra_ref, out_ref, extra_out, outgoing, core_in, total,
+                   x_in, y_in, z_in, core_sent, core_got, x_sent, x_got, y_sent, y_got, z_sent, z_got):
+    z, y, x, c = spot()
+    width = rows_ref.shape[2]
+    half = out_ref.shape[0] // 2
+    y_peer, x_peer, core_peer = (
+        where_is(z, 1 - y, x, c), where_is(z, y, 1 - x, c), where_is(z, y, x, 1 - c))
+    greet([y_peer, x_peer, core_peer] + [where_is((z + k) % 4, y, x, c) for k in range(1, 4)])
+    groups = ((1, 1), (0, 1), (1, 0), (0, 0))
+
+    def part(block, place):
+        place[:, pl.ds(0, width)] = jnp.dot(
+            spread_ref[block], rows_ref[block], preferred_element_type=jnp.float32
+        ).astype(place.dtype)
+        place[:, pl.ds(width, 128)] = jnp.dot(
+            spread_ref[block], extra_ref[block], preferred_element_type=jnp.float32
+        ).astype(place.dtype)
+
+    def block_of(group, k, core):
+        other_y, other_x = groups[group]
+        return number((z + k) % 4, 1 - y if other_y else y, 1 - x if other_x else x, core)
+
+    def across(group, k):
+        return pltpu.make_async_remote_copy(
+            src_ref=outgoing.at[group, k], dst_ref=core_in.at[group, k],
+            send_sem=core_sent.at[group, k], recv_sem=core_got.at[group, k],
+            device_id=core_peer, device_id_type=MESH)
+
+    def along(group, k, side, sent, got, target, slot, peer):
+        return pltpu.make_async_remote_copy(
+            src_ref=total.at[group, k, pl.ds(side * half, half)], dst_ref=target.at[slot, k],
+            send_sem=sent.at[slot, k], recv_sem=got.at[slot, k],
+            device_id=peer, device_id_type=MESH)
+
+    def x_copy(group, k, side, slot):
+        return along(group, k, side, x_sent, x_got, x_in, slot, x_peer)
+
+    def y_copy(group, k, side, slot):
+        return along(group, k, side, y_sent, y_got, y_in, slot, y_peer)
+
+    def z_copy(k, side):
+        return pltpu.make_async_remote_copy(
+            src_ref=total.at[3, k, pl.ds(side * half, half)], dst_ref=z_in.at[k, side],
+            send_sem=z_sent.at[k, side], recv_sem=z_got.at[k, side],
+            device_id=where_is((z + k) % 4, y, x, c), device_id_type=MESH)
+
+    def add(group, k, side, source):
+        rows = pl.ds(side * half, half)
+        total[group, k, rows] = (
+            total[group, k, rows].astype(jnp.float32) + source.astype(jnp.float32)
+        ).astype(total.dtype)
+
+    order = (1, 2, 3, 0)
+    for group in range(4):
+        @pl.loop(0, 4)
+        def _(i):
+            k = (i + 1) % 4
+            part(block_of(group, k, 1 - c), outgoing.at[group, k])
+            across(group, k).start()
+        @pl.loop(0, 4)
+        def _(i):
+            k = (i + 1) % 4
+            part(block_of(group, k, c), total.at[group, k])
+            across(group, k).wait_recv()
+            total[group, k] = (
+                total[group, k].astype(jnp.float32) + core_in[group, k].astype(jnp.float32)
+            ).astype(total.dtype)
+            if group == 0:
+                x_copy(0, k, 0, 0).start()
+                y_copy(0, k, 1, 0).start()
+            if group == 1:
+                x_copy(1, k, 0, 1).start()
+            if group == 2:
+                y_copy(2, k, 1, 1).start()
+
+    @pl.loop(0, 4)
+    def _(i):
+        k = (i + 1) % 4
+        x_copy(0, k, 0, 0).wait_recv()
+        add(2, k, 0, x_in[0, k])
+        y_copy(2, k, 0, 2).start()
+        y_copy(0, k, 1, 0).wait_recv()
+        add(1, k, 1, y_in[0, k])
+        x_copy(1, k, 1, 2).start()
+
+    @pl.loop(0, 4)
+    def _(i):
+        k = (i + 1) % 4
+        x_copy(1, k, 0, 1).wait_recv()
+        add(3, k, 0, x_in[1, k])
+        y_copy(2, k, 1, 1).wait_recv()
+        add(3, k, 1, y_in[1, k])
+
+    @pl.loop(0, 4)
+    def _(i):
+        k = (i + 1) % 4
+        y_copy(2, k, 0, 2).wait_recv()
+        add(3, k, 0, y_in[2, k])
+        x_copy(1, k, 1, 2).wait_recv()
+        add(3, k, 1, x_in[2, k])
+
+        @pl.when(i < 3)
+        def _():
+            z_copy(k, 0).start()
+            z_copy(k, 1).start()
+
+    for k in range(1, 4):
+        for side in range(2):
+            z_copy(k, side).wait_recv()
+    for side in range(2):
+        rows = pl.ds(side * half, half)
+        sums = total[3, 0, rows].astype(jnp.float32)
+        for k in range(1, 4):
+            sums = sums + z_in[k, side].astype(jnp.float32)
+        out_ref[rows] = sums[:, :width]
+        extra_out[rows] = sums[:, width:]
+
+    for k in range(1, 4):
+        for side in range(2):
+            z_copy(k, side).wait_send()
+
+    @pl.loop(0, 4)
+    def _(k):
+        for group in range(4):
+            across(group, k).wait_send()
+        x_copy(0, k, 0, 0).wait_send()
+        x_copy(1, k, 0, 1).wait_send()
+        x_copy(1, k, 1, 2).wait_send()
+        y_copy(0, k, 1, 0).wait_send()
+        y_copy(2, k, 1, 1).wait_send()
+        y_copy(2, k, 0, 2).wait_send()
+
+
+def spread_scatter(spread, rows, extra, collective_id):
+    blocks, count, kept = spread.shape
+    width = rows.shape[2]
+    wide = width + 128
+    low = rows.dtype
+    return pl.pallas_call(
+        scatter_kernel,
+        out_shape=(jax.ShapeDtypeStruct((count, width), jnp.float32),
+                   jax.ShapeDtypeStruct((count, 128), jnp.float32)),
+        in_specs=[pl.BlockSpec(memory_space=pltpu.VMEM)] * 3,
+        out_specs=(pl.BlockSpec(memory_space=pltpu.VMEM), pl.BlockSpec(memory_space=pltpu.VMEM)),
+        scratch_shapes=[
+            pltpu.VMEM((4, 4, count, wide), low),
+            pltpu.VMEM((4, 4, count, wide), low),
+            pltpu.VMEM((4, 4, count, wide), low),
+            pltpu.VMEM((3, 4, count // 2, wide), low),
+            pltpu.VMEM((3, 4, count // 2, wide), low),
+            pltpu.VMEM((4, 2, count // 2, wide), low),
+            pltpu.SemaphoreType.DMA((4, 4)), pltpu.SemaphoreType.DMA((4, 4)),
+            pltpu.SemaphoreType.DMA((3, 4)), pltpu.SemaphoreType.DMA((3, 4)),
+            pltpu.SemaphoreType.DMA((3, 4)), pltpu.SemaphoreType.DMA((3, 4)),
+            pltpu.SemaphoreType.DMA((4, 2)), pltpu.SemaphoreType.DMA((4, 2)),
+        ],
+        compiler_params=pltpu.CompilerParams(
+            collective_id=collective_id, has_side_effects=True, vmem_limit_bytes=60 << 20),
+    )(spread, rows, extra)
+
+
+def reduce_kernel(part_ref, out_ref, held, y_in, z_in, final, gathered, y_sent, y_got, z_sent, z_got,
+                  back_sent, back_got, side_sent, side_got):
+    z, y, x, c = spot()
+    y_peer = where_is(z, 1 - y, x, c)
+    greet([y_peer] + [where_is((z + k) % 4, y, x, c) for k in range(1, 4)])
+
+    def y_copy(k):
+        spot_z = (z + k) % 4
+        return pltpu.make_async_remote_copy(
+            src_ref=part_ref.at[1 - y, spot_z], dst_ref=y_in.at[k],
+            send_sem=y_sent.at[k], recv_sem=y_got.at[k], device_id=y_peer, device_id_type=MESH)
+
+    def z_copy(k):
+        return pltpu.make_async_remote_copy(
+            src_ref=held.at[k], dst_ref=z_in.at[k],
+            send_sem=z_sent.at[k], recv_sem=z_got.at[k],
+            device_id=where_is((z + k) % 4, y, x, c), device_id_type=MESH)
+
+    def back_copy(k):
+        return pltpu.make_async_remote_copy(
+            src_ref=gathered.at[0, 0], dst_ref=gathered.at[0, (4 - k) % 4],
+            send_sem=back_sent.at[k], recv_sem=back_got.at[(4 - k) % 4],
+            device_id=where_is((z + k) % 4, y, x, c), device_id_type=MESH)
+
+    def back_arrived(k):
+        return pltpu.make_async_remote_copy(
+            src_ref=gathered.at[0, 0], dst_ref=gathered.at[0, k],
+            send_sem=back_sent.at[k], recv_sem=back_got.at[k],
+            device_id=where_is((z + k) % 4, y, x, c), device_id_type=MESH)
+
+    def side_copy(k):
+        return pltpu.make_async_remote_copy(
+            src_ref=gathered.at[0, k], dst_ref=gathered.at[1, k],
+            send_sem=side_sent.at[k], recv_sem=side_got.at[k], device_id=y_peer, device_id_type=MESH)
+
+    @pl.loop(0, 4)
+    def _(i):
+        y_copy((i + 1) % 4).start()
+
+    @pl.loop(0, 4)
+    def _(i):
+        k = (i + 1) % 4
+        y_copy(k).wait_recv()
+        held[k] = (part_ref[y, (z + k) % 4].astype(jnp.float32) + y_in[k].astype(jnp.float32)).astype(held.dtype)
+        @pl.when(i < 3)
+        def _():
+            z_copy(k).start()
+
+    for k in range(1, 4):
+        z_copy(k).wait_recv()
+    sums = held[0].astype(jnp.float32)
+    for k in range(1, 4):
+        sums = sums + z_in[k].astype(jnp.float32)
+    gathered[0, 0] = sums.astype(gathered.dtype)
+    for k in range(1, 4):
+        back_copy(k).start()
+    side_copy(0).start()
+    out_ref[y, z] = gathered[0, 0].astype(out_ref.dtype)
+
+    @pl.loop(1, 4)
+    def _(k):
+        back_arrived(k).wait_recv()
+        side_copy(k).start()
+        out_ref[y, (z + k) % 4] = gathered[0, k].astype(out_ref.dtype)
+
+    @pl.loop(0, 4)
+    def _(k):
+        side_copy(k).wait_recv()
+        out_ref[1 - y, (z + k) % 4] = gathered[1, k].astype(out_ref.dtype)
+
+    @pl.loop(0, 4)
+    def _(k):
+        y_copy(k).wait_send()
+        side_copy(k).wait_send()
+    for k in range(1, 4):
+        z_copy(k).wait_send()
+        back_copy(k).wait_send()
+
+
+def reduce_over_members(parts, collective_id):
+    shape = parts.shape[2:]
+    low = parts.dtype
+    return pl.pallas_call(
+        reduce_kernel,
+        out_shape=jax.ShapeDtypeStruct(parts.shape, jnp.bfloat16),
+        in_specs=[pl.BlockSpec(memory_space=pltpu.VMEM)],
+        out_specs=pl.BlockSpec(memory_space=pltpu.VMEM),
+        scratch_shapes=[
+            pltpu.VMEM((4, *shape), low),
+            pltpu.VMEM((4, *shape), low),
+            pltpu.VMEM((4, *shape), low),
+            pltpu.VMEM((8, 128), low),
+            pltpu.VMEM((2, 4, *shape), low),
+        ] + [pltpu.SemaphoreType.DMA((4,)) for _ in range(8)],
+        compiler_params=pltpu.CompilerParams(
+            collective_id=collective_id, has_side_effects=True, vmem_limit_bytes=60 << 20),
+    )(parts)
 
 
 def moe_gathered(normed, router, routes, capacity, cotangent, weights):
@@ -141,62 +551,62 @@
     rank = right_transposed(own.astype(jnp.bfloat16), before).astype(jnp.int32)
     places = jnp.arange(capacity, dtype=jnp.int32)
     select = (own[:, None, :] & (rank[:, None, :] == places[None, :, None])).astype(jnp.bfloat16)
+    spread = (own[:, :, None] & (rank[:, :, None] == places[None, None, :])).astype(jnp.bfloat16)
     grad_rows = contract(
         "bcj,bjd->bcd", select, all_grads.reshape(experts, token_count, MODEL_WIDTH)
     ).astype(jnp.bfloat16)
     grad_rows = grad_rows.reshape(experts * capacity, MODEL_WIDTH)
-
-    all_normed = lax.all_gather(normed, BOTH, axis=0, tiled=True)
-    logits = matrix_product(all_normed, router)
-    masked = jnp.where(named, logits, MASKED)
+    named_rows = contract(
+        "bcj,bje->bce", select, named.astype(jnp.bfloat16).reshape(experts, token_count, experts)
+    ).reshape(experts * capacity, experts)
+
+    arrived = gather_pick(normed, select, 1).reshape(experts * capacity, MODEL_WIDTH)
+    masked = jnp.where(named_rows > 0, matrix_product(arrived, router), MASKED)
     peak = jnp.max(masked, axis=1, keepdims=True)
     lifted = jnp.exp(masked - peak)
-    own_gate = jnp.sum(jnp.where(columns[None, :] == mine, lifted, 0.0), axis=1) / jnp.sum(
-        lifted, axis=1
-    )
     row_gate = jnp.sum(
-        jnp.where(select > 0, own_gate.reshape(experts, 1, token_count), 0.0), axis=2
-    ).reshape(experts * capacity, 1)
-    arrived = (
-        contract("bcj,bjd->bcd", select, all_normed.reshape(experts, token_count, MODEL_WIDTH))
+        jnp.where(columns[None, :] == mine, lifted, 0.0), axis=1, keepdims=True
+    ) / jnp.sum(lifted, axis=1, keepdims=True)
+    hidden = expert_forward(arrived, gate_w, up_w)
+    active = hidden[3]
+    out_rows = (row_gate * grad_rows.astype(jnp.float32)).astype(jnp.bfloat16)
+    rows_back, gate_pre_grad, up_pre_grad = expert_back(out_rows, hidden, gate_w, up_w, down_w)
+    produced = matrix_product(active, down_w).astype(jnp.bfloat16)
+    row_grad = jnp.sum(
+        produced.astype(jnp.float32) * grad_rows.astype(jnp.float32), axis=1, keepdims=True
+    )
+    weighted = (row_gate * produced.astype(jnp.float32)).astype(jnp.bfloat16)
+    high, low = two_halves(row_grad)
+    lanes = jnp.arange(128, dtype=jnp.int32)[None, :]
+    zero = jnp.zeros((), jnp.bfloat16)
+    extra = jnp.where(lanes == mine, high, jnp.where(lanes == experts + mine, low, zero))
+    summed, back = spread_scatter(
+        spread,
+        rows_back.reshape(experts, capacity, MODEL_WIDTH),
+        extra.reshape(experts, capacity, 128),
+        2,
+    )
+    full = (
+        contract("bjc,bcd->bjd", spread, weighted.reshape(experts, capacity, MODEL_WIDTH))
         .astype(jnp.bfloat16)
-        .reshape(experts * capacity, MODEL_WIDTH)
-    )
-    hidden = expert_forward(arrived, gate_w, up_w)
-    out_rows = (row_gate * grad_rows.astype(jnp.float32)).astype(jnp.bfloat16)
-    rows_back, gate_w_grad, up_w_grad, down_grad = expert_back(
-        arrived, out_rows, hidden, gate_w, up_w, down_w
-    )
-    produced = matrix_product(hidden[3], down_w).astype(jnp.bfloat16)
-    row_grad = jnp.sum(produced.astype(jnp.float32) * grad_rows.astype(jnp.float32), axis=1)
-    weighted = (row_gate * produced.astype(jnp.float32)).astype(jnp.bfloat16)
-
-    def spread(rows):
-        rows = rows.reshape(experts, capacity, rows.shape[1])
-        return (
-            contract("bcj,bcd->bjd", select, rows)
-            .astype(jnp.bfloat16)
-            .reshape(experts * token_count, rows.shape[2])
+        .reshape(experts * token_count, MODEL_WIDTH)
+    )
+    summed, back, full, arrived, gate_pre_grad, up_pre_grad, active, out_rows = (
+        lax.optimization_barrier(
+            (summed, back, full, arrived, gate_pre_grad, up_pre_grad, active, out_rows)
         )
-
-    own_grad = jnp.sum(
-        jnp.where(select > 0, row_grad.reshape(experts, capacity, 1), 0.0), axis=1
-    ).reshape(experts * token_count, 1)
-    placed = jnp.where(columns[None, :] == mine, own_grad, 0.0)
-    high, low = two_halves(placed)
-    back = lax.psum_scatter(
-        jnp.concatenate([spread(rows_back), high, low], axis=1),
-        BOTH,
-        scatter_dimension=0,
-        tiled=True,
-    )
-    mixed = lax.psum_scatter(spread(weighted), BOTH, scatter_dimension=0, tiled=True)
-    summed = back[:, :MODEL_WIDTH].astype(jnp.float32)
-    high = back[:, MODEL_WIDTH : MODEL_WIDTH + experts].astype(jnp.float32)
-    low = back[:, MODEL_WIDTH + experts :].astype(jnp.float32)
-    gate_grad = jnp.take_along_axis(high + low, routes, axis=1)
+    )
+    mixed = lax.psum_scatter(full, BOTH, scatter_dimension=0, tiled=True)
+    weight_grads = (
+        left_trans(arrived, gate_pre_grad),
+        left_trans(arrived, up_pre_grad),
+        left_trans(active, out_rows),
+    )
+    gate_grad = jnp.take_along_axis(
+        back[:, :experts] + back[:, experts : 2 * experts], routes, axis=1
+    )
     gates = gates_of(matrix_product(normed, router), routes, experts)
-    return mixed.astype(jnp.float32), summed, gates, gate_grad, gate_w_grad, up_w_grad, down_grad
+    return mixed.astype(jnp.float32), summed, gates, gate_grad, *weight_grads
 
 
 def moe_exchanged(normed, router, routes, capacity, cotangent, weights):
@@ -222,9 +632,10 @@
     hidden = expert_forward(arrived, gate_w, up_w)
     scaled = (gates[:, :, None] * cotangent.astype(jnp.float32)[:, None, :]).astype(jnp.bfloat16)
     out_rows = send(scaled.reshape(token_count * topk, MODEL_WIDTH))
-    rows_back, gate_w_grad, up_w_grad, down_grad = expert_back(
-        arrived, out_rows, hidden, gate_w, up_w, down_w
-    )
+    rows_back, gate_pre_grad, up_pre_grad = expert_back(out_rows, hidden, gate_w, up_w, down_w)
+    gate_w_grad = left_trans(arrived, gate_pre_grad)
+    up_w_grad = left_trans(arrived, up_pre_grad)
+    down_grad = left_trans(hidden[3], out_rows)
     returned = bring(matrix_product(hidden[3], down_w).astype(jnp.bfloat16))
     mixed = jnp.einsum("tk,tkd->td", gates, returned.astype(jnp.float32))
     gate_grad = jnp.einsum("td,tkd->tk", cotangent, returned, preferred_element_type=jnp.float32)
@@ -325,7 +736,8 @@
     scale_two = rms_scale(middle)
     normed = (middle * scale_two * gain_mlp).astype(jnp.bfloat16)
 
-    moe = moe_gathered if capacity * experts * 2 >= token_count * experts else moe_exchanged
+    dense = (members, shards) == (8, 4) and 2 * capacity >= token_count
+    moe = moe_gathered if dense else moe_exchanged
     mixed, summed, gates, gate_grad, gate_w_grad, up_w_grad, down_grad = moe(
         normed,
         router,
@@ -386,19 +798,26 @@
     joined_grad = contract("gk,ngc->nkc", hidden, head_grads).astype(jnp.bfloat16)
 
     out_sum = lax.psum(out_w_grad.astype(jnp.bfloat16), "exp").astype(jnp.float32)
-    joined_sum = lax.psum(joined_grad, "exp").astype(jnp.float32)
-    vectors = jnp.concatenate(
-        [router_grad.reshape(-1), attn_gain_grad, mlp_gain_grad, q_gain_grad, k_gain_grad]
-    )
-    vectors = lax.psum(vectors, BOTH)
-    sums, start = [], 0
-    for leaf in (w_router, attn_gain, mlp_gain, q_gain, k_gain):
-        sums.append(
-            lax.dynamic_slice_in_dim(vectors, start + place * leaf.size, leaf.size).reshape(
-                leaf.shape
-            )
-        )
-        start += leaf.size * shards
+    if dense:
+        joined_sum = reduce_over_members(joined_grad.reshape(2, 4, -1, wide + 2 * narrow), 3)
+        joined_sum = joined_sum.reshape(joined_grad.shape).astype(jnp.float32)
+    else:
+        joined_sum = lax.psum(joined_grad, "exp").astype(jnp.float32)
+
+    def all_summed(vectors, leaves):
+        vectors, cuts, start = lax.psum(vectors, BOTH), [], 0
+        for leaf in leaves:
+            cut = lax.dynamic_slice_in_dim(vectors, start + place * leaf.size, leaf.size)
+            cuts.append(cut.reshape(leaf.shape))
+            start += leaf.size * shards
+        return cuts
+
+    router_sum, mlp_sum = all_summed(
+        jnp.concatenate([router_grad.reshape(-1), mlp_gain_grad]), (w_router, mlp_gain)
+    )
+    attn_sum, q_sum, k_sum = all_summed(
+        jnp.concatenate([attn_gain_grad, q_gain_grad, k_gain_grad]), (attn_gain, q_gain, k_gain)
+    )
 
     def gather_heads(part):
         return part.transpose(1, 0, 2).reshape(depth, KEY_VALUE_HEADS, copies, HEAD_WIDTH).sum(
@@ -408,15 +827,15 @@
     return (
         layer_out,
         input_grad,
-        sums[1],
+        attn_sum,
         joined_sum[:, :, :wide].transpose(1, 0, 2).reshape(depth, QUERY_HEADS * HEAD_WIDTH),
         gather_heads(joined_sum[:, :, wide : wide + narrow]),
         gather_heads(joined_sum[:, :, wide + narrow :]),
-        sums[3],
-        sums[4],
+        q_sum,
+        k_sum,
         out_sum,
-        sums[2],
-        sums[0],
+        mlp_sum,
+        router_sum,
         gate_w_grad[None],
         up_w_grad[None],
         down_grad[None],

time: 1500 us -> 1280 us (0.85)
  waiting for transfers between devices: 1020 us -> 302 us
  Pallas kernels: 0 us -> 501 us
  blocking collectives: 40.1 us -> 116 us
  local copies, waits for them, and re-layouts: 124 us -> 83.1 us
  matrix products: 216 us -> 188 us
    pallas_call x0 -> x3, Pallas kernels: none -> 501 us  [the longest x1 236 us: reduce_over_members(): pl.pallas_call(reduce_kernel, out_shape=jax.ShapeDtypeStruct(parts.shape,...]
    reduce_scatter x2 -> x1, waiting for transfers between devices: 287 us -> 0.01 us  [moe_gathered(): mixed = lax.psum_scatter(full, BOTH, scatter_dimension=0, tiled=True)]
    psum x2, waiting for transfers between devices: 433 us -> 216 us  [the longest x1 155 us: local(): lax.psum(out_w_grad.astype(jnp.bfloat16), 'exp').astype(jnp.float32)]
    all_gather x1 -> x0, waiting for transfers between devices: 105 us -> none  [moe_gathered(): all_normed = lax.all_gather(normed, BOTH, axis=0, tiled=True)]
    psum x0 -> x1, blocking collectives: none -> 76.2 us  [all_summed(): vectors, cuts, start = (lax.psum(vectors, BOTH), [], 0)]
    all_gather x1, waiting for transfers between devices: 45.9 us -> 0.01 us  [moe_gathered(): all_grads = lax.all_gather(cotangent, BOTH, axis=0, tiled=True)]
    reduce_scatter x1, waiting for transfers between devices: 30.9 us -> 0.01 us  [local(): lax.psum_scatter(matrix_product(attended, w_out).astype(jnp.bfloat16), 'f...]
    dot_general x13 -> x12, matrix products: 82 us -> 56.1 us  [contract(): return jnp.einsum(spec, left, right, preferred_element_type=jnp.float32)]
  transfers between devices with their start and end apart: 13 -> 11, of which waited for: 12 -> 5; matrix products, arithmetic and copies ran while one was open for 9% -> 14% of each run, Pallas kernels for 0% -> 30%
where the time goes in v2:
time: 1280 us; the launch traced here: 1270 us
  Pallas kernels  501 us (39%)
  waiting for transfers between devices  302 us (24%)
  matrix products  188 us (15%)
  blocking collectives  116 us (9%)
  local copies, waits for them, and re-layouts  83.1 us (6%)
  other arithmetic  51.1 us (4%)
  between operations  17.8 us (1%)
    pallas_call x1, Pallas kernels, reduce_over_members(): pl.pallas_call(reduce_kernel, out_shape=jax.ShapeDtypeStruct(parts.shape,...  236 us
    psum x1, waiting for transfers between devices, local(): lax.psum(out_w_grad.astype(jnp.bfloat16), 'exp').astype(jnp.float32)  155 us
    pallas_call x1, Pallas kernels, gather_pick(): pl.pallas_call(gather_kernel, out_shape=jax.ShapeDtypeStruct((blocks, kep...  149 us
    pallas_call x1, Pallas kernels, spread_scatter(): pl.pallas_call(scatter_kernel, out_shape=(jax.ShapeDtypeStruct((count, wi...  117 us
    psum x1, blocking collectives, all_summed(): vectors, cuts, start = (lax.psum(vectors, BOTH), [], 0)  76.2 us
    psum x1, waiting for transfers between devices, all_summed(): vectors, cuts, start = (lax.psum(vectors, BOTH), [], 0)  61.6 us
    dot_general x12, matrix products, contract(): return jnp.einsum(spec, left, right, preferred_element_type=jnp.float32)  56.1 us
    dot_general x6, matrix products, matrix_product(): return jnp.dot(left, right, preferred_element_type=jnp.float32)  53.1 us
  transfers between devices with their start and end apart: 11, of which 5 were waited for; matrix products, arithmetic and copies ran while one was open for 14% of the time, Pallas kernels for 30%

profile of v2, /device:TPU:8, one launch (start us, length us, event | category | flops | bytes accessed | tf_op | source)
XLA Modules:
  0.0 1268.5 jit_solution(11726618668466689019)
XLA Ops:
  16.5 30.2 %all-reduce.9.cloned.1.call-done = bf16[69888]{0:T(1024)(128)(2,1)} async-done(((bf16[69888]{0:T(1024)(128)(2,1)}), bf16[69888]{0:T(1024)(128)(2,1)}) %all-reduce.9.cloned.1.call-update) | async-done | bytes 139792
  64.8 7.9 fusion.5
  79.3 46.3 %reduce-scatter.4.cloned.1.call-done = bf16[1,512,1280]{1,2,0:T(8,128)(2,1)} async-done(((bf16[4,512,1280]{1,2,0:T(8,128)(2,1)}), bf16[1,512,1280]{1,2,0:T(8,128)(2,1)}) %reduce-scatter.4.cloned.1.call-update) | async-done | bytes 1310736 | tf_op jit(solution)/shard_map/reduce_scatter | solution.py:703
  147.8 34.9 %all_gather.25 = s32[4096,8]{0,1:T(8,128)S(1)} all-gather(s32[128,8]{0,1:T(8,128)S(1)} %copy-done.52), channel_id=1, replica_groups=mesh['exp'=8,'fsdp'=4] {'exp','fsdp'}, dimensions={0}, use_global_device_ids=true | all-gather | bytes 135168 | tf_op jit(solution)/shard_map/all_gather | solution.py:545
  193.6 148.8 %shard_map.263 = bf16[32,64,2048]{2,1,0:T(8,128)(2,1)} custom-call(bf16[128,2048]{1,0:T(8,128)(2,1)} %multiply_convert_fusion.3.x_ref, bf16[32,64,128]{2,1,0:T(8,128)(2,1)} %fusion.60.select_ref), custom_call_target="tpu_custom_call" | custom-call | tf_op jit(solution)/shard_map/pallas_call | solution.py:262
  357.3 11.7 fusion.9
  369.0 11.4 fusion.2
  380.4 11.1 fusion.15
  391.5 13.9 %multiply_convert_fusion = (bf16[2048,768]{1,0:T(8,128)(2,1)}, bf16[2048,768]{1,0:T(8,128)(2,1)}, bf16[2048,768]{1,0:T(8,128)(2,1)}) fusion(f32[2048,768]{1,0:T(8,128)} %fusion.9, f32[2048,768]{1,0:T(8,128)} %fusion.15, bf16[2048,2048]{1,0:T(8,128)(2,1)S(1)} %bitcast.327, bf16[1,2048,768]{2,1,0:T(8,128)(2,1)S(1)} %copy-done.73), kind=kOutput, calls=%fused_computation.14 | convolution fusion | flops 6466043904 | bytes 33554432 | tf_op jit(solution)/shard_map/dot_general | solution.py:24
  405.3 12.7 %fusion.7 = f32[2048,2048]{1,0:T(8,128)} fusion(bf16[2048,768]{1,0:T(8,128)(2,1)} %get-tuple-element.31, bf16[1,2048,768]{2,1,0:T(8,128)(2,1)} %param.30), kind=kOutput, calls=%fused_computation.30 | convolution fusion | flops 6442450944 | bytes 23068672 | tf_op jit(solution)/shard_map/dot_general | solution.py:34
  418.1 13.9 %fusion.3 = (bf16[2048,2048]{1,0:T(8,128)(2,1)}, f32[2048]{0:T(1024)S(1)}, bf16[2048,2048]{1,0:T(8,128)(2,1)}) fusion(bf16[32,64,2048]{2,1,0:T(8,128)(2,1)S(1)} %copy-done.6, f32[2048]{0:T(1024)S(1)} %div.61, bf16[2048,768]{1,0:T(8,128)(2,1)} %get-tuple-element.33, bf16[1,768,2048]{2,1,0:T(8,128)(2,1)S(1)} %copy-done), kind=kOutput, calls=%fused_computation.9 | convolution fusion | flops 6480197632 | bytes 31473664 | tf_op jit(solution)/shard_map/dot_general | solution.py:24
  432.0 11.5 convolution_convert_fusion
  443.6 12.4 add_convert_fusion
  457.3 116.7 %shard_map.264 = (f32[128,2048]{1,0:T(8,128)}, f32[128,128]{1,0:T(8,128)}) custom-call(bf16[32,128,64]{2,1,0:T(8,128)(2,1)} %fusion.30.spread_ref, bf16[32,64,2048]{2,1,0:T(8,128)(2,1)} %bitcast.343, bf16[32,64,128]{2,1,0:T(8,128)(2,1)} %select_select_fusion.extra_ref), custom_call_target="tpu_custom_call" | custom-call | tf_op jit(solution)/shard_map/pallas_call | solution.py:418
  599.9 8.1 all-gather.8.cloned.1.call-done
  652.7 11.0 convolution_bitcast_fusion
  663.7 11.2 convolution_bitcast_fusion.2
  674.9 8.9 convolution_bitcast_fusion.1
  683.8 61.6 %all-reduce.7.cloned.1.call-done = f32[67584]{0:T(1024)} async-done(((f32[67584]{0:T(1024)}), f32[67584]{0:T(1024)}) %all-reduce.7.cloned.1.call-update) | async-done | bytes 270352 | tf_op jit(solution)/shard_map/psum | solution.py:808
  748.4 154.6 %all-reduce.5.cloned.1.call-done = bf16[1024,2048]{1,0:T(8,128)(2,1)} async-done(((bf16[1024,2048]{1,0:T(8,128)(2,1)}), bf16[1024,2048]{1,0:T(8,128)(2,1)}) %all-reduce.5.cloned.1.call-update) | async-done | bytes 4194320 | tf_op jit(solution)/shard_map/psum | solution.py:800
  909.7 7.8 fusion.39
  921.3 8.0 convolution_convert_fusion.2
  929.3 235.8 %shard_map.265 = bf16[2,4,256,1280]{3,2,1,0:T(8,128)(2,1)} custom-call(bf16[2,4,256,1280]{3,2,1,0:T(8,128)(2,1)} %bitcast.345), custom_call_target="tpu_custom_call" | custom-call | tf_op jit(solution)/shard_map/pallas_call | solution.py:523
  1179.5 76.2 %psum.21 = f32[2304]{0:T(1024)S(1)} all-reduce(f32[2304]{0:T(1024)S(1)} %pad_maximum_fusion.3), channel_id=1, replica_groups=mesh['exp'=8,'fsdp'=4] {'exp','fsdp'}, use_global_device_ids=true, to_apply=%region_30.32 | all-reduce | flops 2304 | bytes 18432 | tf_op jit(solution)/shard_map/psum | solution.py:808
  (337 shorter events, 184.4 us)
Async XLA Ops:
  8.0 372.3 %copy-start = (bf16[1,768,2048]{2,1,0:T(8,128)(2,1)S(1)}, bf16[1,768,2048]{2,1,0:T(8,128)(2,1)}, u32[]{:S(2)}) copy-start(bf16[1,768,2048]{2,1,0:T(8,128)(2,1)} %param.32) | copy-start | bytes 9437188
  8.0 38.7 %all-reduce.9.cloned.1.call-start = ((), (), s32[]{:S(2)}) async-start(), calls=%async_computation.13 | async-start | bytes 282624
  50.0 14.8 %all-to-all-start = ((bf16[128,4,512]{2,0,1:T(8,128)(2,1)}), bf16[128,4,512]{2,0,1:T(8,128)(2,1)}, u32[]{:S(2)}, u32[]{:S(2)}) async-start(bf16[128,4,512]{2,0,1:T(8,128)(2,1)} %bitcast.351), calls=%async_computation | async-start | bytes 1048576 | tf_op jit(solution)/shard_map/all_to_all | solution.py:701
  54.1 71.5 %reduce-scatter.4.cloned.1.call-start = ((), (), s32[]{:S(2)}) async-start(), calls=%async_computation.5 | async-start | bytes 6553600 | tf_op jit(solution)/shard_map/reduce_scatter | solution.py:703
  72.7 117.2 %reduce-scatter.6.cloned.1.call-start = ((), (), s32[]{:S(2)}) async-start(), calls=%async_computation.6 | async-start | bytes 2621440 | tf_op jit(solution)/shard_map/reduce_scatter | solution.py:732
  78.8 53.1 %copy-start.66 = (f32[128]{0:T(128)}, f32[128]{0:T(128)S(1)}, u32[]{:S(2)}) copy-start(f32[128]{0:T(128)S(1)} %fusion.99) | copy-start | bytes 1540
  79.0 53.0 %copy-start.53 = (f32[4,128]{1,0:T(4,128)}, f32[4,128]{1,0:T(4,128)S(1)}, u32[]{:S(2)}) copy-start(f32[4,128]{1,0:T(4,128)S(1)} %subtract_convert_fusion.1) | copy-start | bytes 6148
  79.3 53.9 %copy-start.56 = (f32[128]{0:T(128)}, f32[128]{0:T(128)S(1)}, u32[]{:S(2)}) copy-start(f32[128]{0:T(128)S(1)} %reshape.569) | copy-start | bytes 1540
  147.1 221.8 %all-gather.6.cloned.1.call-start = ((), (), s32[]{:S(2)}) async-start(), calls=%async_computation.7 | async-start | bytes 17301504 | tf_op jit(solution)/shard_map/all_gather | solution.py:546
  147.7 460.4 %all-gather.8.cloned.1.call-start = ((), (), s32[]{:S(2)}) async-start(), calls=%async_computation.9 | async-start | bytes 2621440 | tf_op jit(solution)/shard_map/all_gather | solution.py:761
  188.8 153.6 %copy-start.43 = (f32[1,4,4,128]{3,1,2,0:T(4,128)}, f32[1,4,4,128]{3,1,2,0:T(4,128)S(1)}, u32[]{:S(2)}) copy-start(f32[1,4,4,128]{3,1,2,0:T(4,128)S(1)} %copy.260) | copy-start | bytes 24580
  191.4 151.0 %copy-start.61 = (f32[128]{0:T(128)}, f32[128]{0:T(128)S(1)}, u32[]{:S(2)}) copy-start(f32[128]{0:T(128)S(1)} %add_rsqrt_fusion.2) | copy-start | bytes 1540
  193.6 148.8 %copy-start.21 = (bf16[2048,32]{1,0:T(8,128)(2,1)S(1)}, bf16[2048,32]{1,0:T(8,128)(2,1)}, u32[]{:S(2)}) copy-start(bf16[2048,32]{1,0:T(8,128)(2,1)} %reshape.550) | copy-start | bytes 393220
  587.1 158.3 %all-reduce.7.cloned.1.call-start = ((), (), s32[]{:S(2)}) async-start(), calls=%async_computation.12 | async-start | bytes 540672 | tf_op jit(solution)/shard_map/psum | solution.py:808
  599.9 303.2 %all-reduce.5.cloned.1.call-start = ((), (), s32[]{:S(2)}) async-start(), calls=%async_computation.11 | async-start | bytes 8388608 | tf_op jit(solution)/shard_map/psum | solution.py:800
  623.1 286.6 %all-gather.10.cloned.1.call-start = ((), (), s32[]{:S(2)}) async-start(), calls=%async_computation.10 | async-start | bytes 6553600 | tf_op jit(solution)/shard_map/all_gather | solution.py:789
  650.9 606.1 %reduce-scatter.8.cloned.1.call-start = ((), (), s32[]{:S(2)}) async-start(), calls=%async_computation.8 | async-start | bytes 17301504 | tf_op jit(solution)/shard_map/reduce_scatter | solution.py:599
  748.4 161.3 %copy-start.37 = (bf16[512,512]{0,1:T(8,128)(2,1)S(1)}, bf16[512,512]{0,1:T(8,128)(2,1)}, u32[]{:S(2)}) copy-start(bf16[512,512]{0,1:T(8,128)(2,1)} %copy.194) | copy-start | bytes 1572868
  748.4 161.3 %copy-start.38 = (bf16[512,512]{0,1:T(8,128)(2,1)S(1)}, bf16[512,512]{0,1:T(8,128)(2,1)}, u32[]{:S(2)}) copy-start(bf16[512,512]{0,1:T(8,128)(2,1)} %copy.193) | copy-start | bytes 1572868
  917.6 258.9 %all-to-all-start.1 = ((bf16[4,128,512]{2,1,0:T(8,128)(2,1)}), bf16[4,128,512]{2,1,0:T(8,128)(2,1)S(1)}, u32[]{:S(2)}, u32[]{:S(2)}) async-start(bf16[4,128,512]{2,1,0:T(8,128)(2,1)} %bitcast.65), calls=%async_computation.4 | async-start | bytes 1048576 | tf_op jit(solution)/shard_map/all_to_all | solution.py:791
  1176.5 80.5 %copy-start.45 = (f32[1,4,4,128]{3,1,2,0:T(4,128)S(1)}, f32[1,4,4,128]{3,1,2,0:T(4,128)}, u32[]{:S(2)}) copy-start(f32[1,4,4,128]{3,1,2,0:T(4,128)} %copy-done.43) | copy-start | bytes 24580
  1176.5 80.5 %copy-start.63 = (f32[128]{0:T(128)S(1)}, f32[128]{0:T(128)}, u32[]{:S(2)}) copy-start(f32[128]{0:T(128)} %copy-done.61) | copy-start | bytes 1540
  1176.5 80.5 %copy-start.69 = (f32[128]{0:T(128)S(1)}, f32[128]{0:T(128)}, u32[]{:S(2)}) copy-start(f32[128]{0:T(128)} %copy-done.68) | copy-start | bytes 1540
  1176.7 84.2 %copy-start.1 = (bf16[1,768,2048]{2,1,0:T(8,128)(2,1)S(1)}, bf16[1,768,2048]{2,1,0:T(8,128)(2,1)}, u32[]{:S(2)}) copy-start(bf16[1,768,2048]{2,1,0:T(8,128)(2,1)} %param.32) | copy-start | bytes 9437188
  (71 other events, 436.8 us)
Sparse Core Ops, SparseCore 0:
  15.4 31.2 all-reduce.8
  72.8 52.8 reduce-scatter.3
  147.3 31.8 reduce-scatter.5
  587.2 20.7 all-gather.7
  651.0 40.4 all-gather.9
Sparse Core Ops, SparseCore 1:
  150.9 169.3 all-gather.5
  600.0 145.4 all-reduce.6
  749.5 153.5 all-reduce.4
  905.4 275.3 reduce-scatter.7

commit v3 on v2

v3 whole, which is shorter than its diff:
```python
import math

import jax
import jax.numpy as jnp
from jax import lax
from jax.experimental import pallas as pl
from jax.experimental.pallas import tpu as pltpu
from jax.sharding import PartitionSpec as P

MODEL_WIDTH = 2048
QUERY_HEADS = 32
KEY_VALUE_HEADS = 4
HEAD_WIDTH = 128


EPSILON = 1e-06
THETA = 1000000.0
MASKED = -1e30
BOTH = ("exp", "fsdp")
MESH = pl.DeviceIdType.MESH


def matrix_product(left, right):
    return jnp.dot(left, right, preferred_element_type=jnp.float32)


def left_trans(left, right):
    return lax.dot_general(
        left, right, (((0,), (0,)), ((), ())), preferred_element_type=jnp.float32
    )


def right_transposed(left, right):
    return lax.dot_general(
        left, right, (((1,), (1,)), ((), ())), preferred_element_type=jnp.float32
    )


def contract(spec, left, right):
    return jnp.einsum(spec, left, right, preferred_element_type=jnp.float32)


def rms_scale(values):
    return lax.rsqrt(jnp.mean(values * values, axis=-1, keepdims=True) + EPSILON)


def rms_back(grad_hat, values, scale):
    normal = values * scale
    return scale * (grad_hat - normal * jnp.mean(grad_hat * normal, axis=-1, keepdims=True))


def seq_layout(length_row, token_count):
    ends = jnp.cumsum(length_row)
    starts = ends - length_row
    places = jnp.arange(token_count, dtype=jnp.int32)
    member = (places[:, None] >= starts[None, :]) & (places[:, None] < ends[None, :])
    numbers = jnp.arange(length_row.shape[0], dtype=jnp.int32)
    segment = jnp.sum(jnp.where(member, numbers[None, :], 0), axis=1)
    position = places - jnp.sum(jnp.where(member, starts[None, :], 0), axis=1)
    allowed = (segment[:, None] == segment[None, :]) & (places[None, :] <= places[:, None])
    return (position, allowed)


def rotary_tables(position, head_size):
    half = head_size // 2
    index = jnp.arange(head_size, dtype=jnp.int32) % half
    inverse = jnp.exp(index.astype(jnp.float32) * (-2.0 * math.log(THETA) / head_size))
    angles = position.astype(jnp.float32)[..., None] * inverse
    return (jnp.cos(angles)[..., None, :], jnp.sin(angles)[..., None, :])


def rotate(values, cosine, sine):
    half = values.shape[-1] // 2
    turned = jnp.concatenate([-values[..., half:], values[..., :half]], axis=-1)
    return values * cosine + turned * sine


def rotate_back(grads, cosine, sine):
    half = grads.shape[-1] // 2
    moved = grads * sine
    return grads * cosine + jnp.concatenate([moved[..., half:], -moved[..., :half]], axis=-1)


def slot_table(route_rows, experts, capacity):
    flat = route_rows.reshape(-1)
    onehot = (flat[:, None] == jnp.arange(experts, dtype=jnp.int32)[None, :]).astype(jnp.int32)
    ranks = jnp.cumsum(onehot, axis=0) - 1
    rank = jnp.sum(ranks * onehot, axis=1)
    return flat * capacity + rank


def exchange(buffer):
    return lax.all_to_all(buffer, BOTH, split_axis=0, concat_axis=0, tiled=True)


def two_halves(values):
    high = values.astype(jnp.bfloat16)
    low = (values - high.astype(jnp.float32)).astype(jnp.bfloat16)
    return high, low


def expert_forward(arrived, gate_w, up_w):
    gate_pre = matrix_product(arrived, gate_w)
    up_pre = matrix_product(arrived, up_w)
    sigma = jax.nn.sigmoid(gate_pre)
    active = (gate_pre * sigma * up_pre).astype(jnp.bfloat16)
    return gate_pre, up_pre, sigma, active


def expert_back(out_rows, hidden, gate_w, up_w, down_w):
    gate_pre, up_pre, sigma, _ = hidden
    active_grad = right_transposed(out_rows, down_w)
    gate_pre_grad = (active_grad * up_pre * (sigma * (1.0 + gate_pre * (1.0 - sigma)))).astype(
        jnp.bfloat16
    )
    up_pre_grad = (active_grad * (gate_pre * sigma)).astype(jnp.bfloat16)
    rows_back = right_transposed(gate_pre_grad, gate_w) + right_transposed(up_pre_grad, up_w)
    return rows_back.astype(jnp.bfloat16), gate_pre_grad, up_pre_grad


def gates_of(logits, routes, experts):
    picked = jnp.take_along_axis(logits, routes, axis=1)
    peak = jnp.max(picked, axis=1, keepdims=True)
    lifted = jnp.exp(picked - peak)
    return lifted / jnp.sum(lifted, axis=1, keepdims=True)


def spot():
    member, shard = lax.axis_index("exp"), lax.axis_index("fsdp")
    return member // 2, member % 2, shard // 2, shard % 2


def where_is(z, y, x, c):
    return (z * 2 + y, x * 2 + c)


def number(z, y, x, c):
    return z * 8 + y * 4 + x * 2 + c


def greet(peers):
    barrier = pltpu.get_barrier_semaphore()
    for peer in peers:
        pl.semaphore_signal(barrier, inc=1, device_id=peer, device_id_type=MESH)
    pl.semaphore_wait(barrier, len(peers))


def remote(source, target, sent, got, peer):
    return pltpu.make_async_remote_copy(
        src_ref=source,
        dst_ref=target,
        send_sem=sent,
        recv_sem=got,
        device_id=peer,
        device_id_type=MESH,
    )


def in_vmem(count):
    return [pl.BlockSpec(memory_space=pltpu.VMEM)] * count


def copies(*shape):
    return pltpu.SemaphoreType.DMA(shape)


def settings(collective_id):
    return pltpu.CompilerParams(
        collective_id=collective_id, has_side_effects=True, vmem_limit_bytes=60 << 20
    )


def gather_kernel(
    x_ref,
    select_ref,
    ahead_ref,
    named_ref,
    gate_ref,
    up_ref,
    router_ref,
    rows_out,
    active_out,
    gate_out,
    up_out,
    share_out,
    extra_out,
    held,
    picked,
    arrive,
    to_z,
    to_y,
    to_x,
    to_core,
):
    z, y, x, c = spot()
    half = x_ref.shape[0] // 2
    kept = select_ref.shape[1]
    y_peer, x_peer, core_peer = (
        where_is(z, 1 - y, x, c),
        where_is(z, y, 1 - x, c),
        where_is(z, y, x, 1 - c),
    )
    z_peers = [where_is((z + k) % 4, y, x, c) for k in range(1, 4)]
    greet([y_peer, x_peer, core_peer] + z_peers)
    mine = number(z, y, x, c)

    def copy(block, part, sem, peer):
        view = held.at[block, pl.ds(part * half, half)]
        return remote(view, view, sem, arrive.at[block, part], peer)

    def arrived(block, part):
        copy(block, part, to_core.at[0, 0, 0], core_peer).wait_recv()

    def block_of(group, k):
        other_y, other_x, other_core = group
        return number(
            (z + k) % 4,
            1 - y if other_y else y,
            1 - x if other_x else x,
            1 - c if other_core else c,
        )

    def work(group):
        blocks = [block_of(group, k) for k in range(4)]

        @pl.loop(0, 4)
        def _(k):
            block = block_of(group, k)
            rows = jnp.dot(
                select_ref[block], held[block], preferred_element_type=jnp.float32
            ).astype(picked.dtype)
            picked[pl.ds(k * kept, kept)] = rows
            rows_out[block] = rows

        rows = picked[...]
        gate_pre = jnp.dot(rows, gate_ref[...], preferred_element_type=jnp.float32)
        up_pre = jnp.dot(rows, up_ref[...], preferred_element_type=jnp.float32)
        logits = jnp.dot(rows, router_ref[...], preferred_element_type=jnp.float32)
        for k in range(4):
            part = slice(k * kept, (k + 1) * kept)
            block = blocks[k]
            masked = jnp.where(named_ref[block].astype(jnp.float32) > 0, logits[part], MASKED)
            lifted = jnp.exp(masked - jnp.max(masked, axis=1, keepdims=True))
            lanes = lax.broadcasted_iota(jnp.int32, lifted.shape, 1)
            share = jnp.sum(jnp.where(lanes == mine, lifted, 0.0), axis=1, keepdims=True)
            share = share / jnp.sum(lifted, axis=1, keepdims=True)
            gate, up, ahead = gate_pre[part], up_pre[part], ahead_ref[block]
            sigma = 1.0 / (1.0 + jnp.exp(-gate))
            silu = gate * sigma
            active = silu * up
            active_low = active.astype(active_out.dtype)
            grad = jnp.sum(active_low.astype(jnp.float32) * ahead, axis=1, keepdims=True)
            active_grad = share * ahead
            active_out[block] = active_low
            gate_out[block] = (active_grad * up * (sigma * (1.0 + gate * (1.0 - sigma)))).astype(
                gate_out.dtype
            )
            up_out[block] = (active_grad * silu).astype(up_out.dtype)
            share_out[block] = jnp.broadcast_to(share, share_out.shape[1:])
            high = grad.astype(extra_out.dtype).astype(jnp.float32)
            both = jnp.where(
                lanes == mine, high, jnp.where(lanes == 32 + mine, grad - high, 0.0)
            )
            extra_out[block] = both.astype(extra_out.dtype)

    held[mine] = x_ref[...]
    for k in range(1, 4):
        for part in range(2):
            copy(mine, part, to_z.at[k - 1, part], z_peers[k - 1]).start()

    def forward_first(k):
        block = block_of((0, 0, 0), k)
        copy(block, 0, to_y.at[0, k], y_peer).start()
        copy(block, 1, to_x.at[0, k], x_peer).start()
        copy(block, 0, to_x.at[1, k], x_peer).start()
        copy(block, 1, to_y.at[1, k], y_peer).start()
        copy(block, 0, to_core.at[0, 0, k], core_peer).start()
        copy(block, 1, to_core.at[0, 1, k], core_peer).start()

    forward_first(0)

    @pl.loop(1, 4)
    def _(k):
        block = block_of((0, 0, 0), k)
        arrived(block, 0)
        arrived(block, 1)
        forward_first(k)

    work((0, 0, 0))

    @pl.loop(0, 4)
    def _(k):
        block = block_of((1, 0, 0), k)
        arrived(block, 0)
        copy(block, 0, to_x.at[2, k], x_peer).start()
        copy(block, 0, to_core.at[1, 0, k], core_peer).start()
        block = block_of((0, 1, 0), k)
        arrived(block, 1)
        copy(block, 1, to_y.at[2, k], y_peer).start()
        copy(block, 1, to_core.at[2, 1, k], core_peer).start()
        block = block_of((0, 0, 1), k)
        arrived(block, 0)
        arrived(block, 1)

    work((0, 0, 1))

    @pl.loop(0, 4)
    def _(k):
        block = block_of((0, 1, 0), k)
        arrived(block, 0)
        copy(block, 0, to_core.at[2, 0, k], core_peer).start()
        block = block_of((1, 0, 0), k)
        arrived(block, 1)
        copy(block, 1, to_core.at[1, 1, k], core_peer).start()

    work((0, 1, 0))
    work((1, 0, 0))
    for group in ((0, 1, 1), (1, 0, 1)):

        @pl.loop(0, 4)
        def _(k):
            block = block_of(group, k)
            arrived(block, 0)
            arrived(block, 1)

        work(group)

    @pl.loop(0, 4)
    def _(k):
        block = block_of((1, 1, 0), k)
        arrived(block, 0)
        copy(block, 0, to_core.at[3, 0, k], core_peer).start()
        arrived(block, 1)
        copy(block, 1, to_core.at[3, 1, k], core_peer).start()

    work((1, 1, 0))

    @pl.loop(0, 4)
    def _(k):
        block = block_of((1, 1, 1), k)
        arrived(block, 0)
        arrived(block, 1)

    work((1, 1, 1))
    for k in range(1, 4):
        for part in range(2):
            copy(mine, part, to_z.at[k - 1, part], z_peers[k - 1]).wait_send()

    @pl.loop(0, 4)
    def _(k):
        for i in range(3):
            copy(mine, 0, to_y.at[i, k], y_peer).wait_send()
            copy(mine, 0, to_x.at[i, k], x_peer).wait_send()
        for i in range(4):
            for part in range(2):
                copy(mine, part, to_core.at[i, part, k], core_peer).wait_send()


def gather_experts(rows, select, ahead, named, gate_w, up_w, router):
    count, width = rows.shape
    blocks, kept = select.shape[:2]
    hidden = gate_w.shape[1]
    low = rows.dtype
    return pl.pallas_call(
        gather_kernel,
        out_shape=[
            jax.ShapeDtypeStruct((blocks, kept, width), low),
            jax.ShapeDtypeStruct((blocks, kept, hidden), low),
            jax.ShapeDtypeStruct((blocks, kept, hidden), low),
            jax.ShapeDtypeStruct((blocks, kept, hidden), low),
            jax.ShapeDtypeStruct((blocks, kept, 128), jnp.float32),
            jax.ShapeDtypeStruct((blocks, kept, 128), low),
        ],
        in_specs=in_vmem(7),
        out_specs=in_vmem(6),
        scratch_shapes=[
            pltpu.VMEM((blocks, count, width), low),
            pltpu.VMEM((4 * kept, width), low),
            copies(blocks, 2),
            copies(3, 2),
            copies(3, 4),
            copies(3, 4),
            copies(4, 2, 4),
        ],
        compiler_params=settings(1),
    )(rows, select, ahead, named, gate_w, up_w, router)


def scatter_kernel(
    spread_ref,
    gate_grad_ref,
    up_grad_ref,
    gate_ref,
    up_ref,
    extra_ref,
    out_ref,
    extra_out,
    outgoing,
    core_in,
    total,
    back,
    x_in,
    y_in,
    z_in,
    core_sent,
    core_got,
    x_sent,
    x_got,
    y_sent,
    y_got,
    z_sent,
    z_got,
):
    z, y, x, c = spot()
    width = out_ref.shape[1]
    half = out_ref.shape[0] // 2
    kept = spread_ref.shape[2]
    y_peer, x_peer, core_peer = (
        where_is(z, 1 - y, x, c),
        where_is(z, y, 1 - x, c),
        where_is(z, y, x, 1 - c),
    )
    greet([y_peer, x_peer, core_peer] + [where_is((z + k) % 4, y, x, c) for k in range(1, 4)])
    groups = ((1, 1), (0, 1), (1, 0), (0, 0))

    def block_of(group, k, core):
        other_y, other_x = groups[group]
        return number((z + k) % 4, 1 - y if other_y else y, 1 - x if other_x else x, core)

    def rows_back(group, core):
        gate_grads = jnp.concatenate(
            [gate_grad_ref[block_of(group, k, core)] for k in range(4)], axis=0
        )
        up_grads = jnp.concatenate(
            [up_grad_ref[block_of(group, k, core)] for k in range(4)], axis=0
        )
        sums = right_transposed(gate_grads, gate_ref[...])
        back[...] = (sums + right_transposed(up_grads, up_ref[...])).astype(back.dtype)

    def part(block, k, place):
        place[:, pl.ds(0, width)] = jnp.dot(
            spread_ref[block], back[pl.ds(k * kept, kept)], preferred_element_type=jnp.float32
        ).astype(place.dtype)
        place[:, pl.ds(width, 128)] = jnp.dot(
            spread_ref[block], extra_ref[block], preferred_element_type=jnp.float32
        ).astype(place.dtype)

    def across(group, k):
        return remote(
            outgoing.at[group, k],
            core_in.at[group, k],
            core_sent.at[group, k],
            core_got.at[group, k],
            core_peer,
        )

    def view(group, k, side):
        return total.at[group, k, pl.ds(side * half, half)]

    def x_copy(group, k, side, slot):
        return remote(
            view(group, k, side), x_in.at[slot, k], x_sent.at[slot, k], x_got.at[slot, k], x_peer
        )

    def y_copy(group, k, side, slot):
        return remote(
            view(group, k, side), y_in.at[slot, k], y_sent.at[slot, k], y_got.at[slot, k], y_peer
        )

    def z_copy(k, side):
        return remote(
            view(3, k, side),
            z_in.at[k, side],
            z_sent.at[k, side],
            z_got.at[k, side],
            where_is((z + k) % 4, y, x, c),
        )

    def add(group, k, side, source):
        rows = pl.ds(side * half, half)
        total[group, k, rows] = (
            total[group, k, rows].astype(jnp.float32) + source.astype(jnp.float32)
        ).astype(total.dtype)

    for group in range(4):
        rows_back(group, 1 - c)

        @pl.loop(0, 4)
        def _(i):
            k = (i + 1) % 4
            part(block_of(group, k, 1 - c), k, outgoing.at[group, k])
            across(group, k).start()

        rows_back(group, c)

        @pl.loop(0, 4)
        def _(i):
            k = (i + 1) % 4
            part(block_of(group, k, c), k, total.at[group, k])
            across(group, k).wait_recv()
            total[group, k] = (
                total[group, k].astype(jnp.float32) + core_in[group, k].astype(jnp.float32)
            ).astype(total.dtype)
            if group == 0:
                x_copy(0, k, 0, 0).start()
                y_copy(0, k, 1, 0).start()
            if group == 1:
                x_copy(1, k, 0, 1).start()
            if group == 2:
                y_copy(2, k, 1, 1).start()

    @pl.loop(0, 4)
    def _(i):
        k = (i + 1) % 4
        x_copy(0, k, 0, 0).wait_recv()
        add(2, k, 0, x_in[0, k])
        y_copy(2, k, 0, 2).start()
        y_copy(0, k, 1, 0).wait_recv()
        add(1, k, 1, y_in[0, k])
        x_copy(1, k, 1, 2).start()

    @pl.loop(0, 4)
    def _(i):
        k = (i + 1) % 4
        x_copy(1, k, 0, 1).wait_recv()
        add(3, k, 0, x_in[1, k])
        y_copy(2, k, 1, 1).wait_recv()
        add(3, k, 1, y_in[1, k])

    @pl.loop(0, 4)
    def _(i):
        k = (i + 1) % 4
        y_copy(2, k, 0, 2).wait_recv()
        add(3, k, 0, y_in[2, k])
        x_copy(1, k, 1, 2).wait_recv()
        add(3, k, 1, x_in[2, k])

        @pl.when(i < 3)
        def _():
            z_copy(k, 0).start()
            z_copy(k, 1).start()

    for k in range(1, 4):
        for side in range(2):
            z_copy(k, side).wait_recv()
    for side in range(2):
        rows = pl.ds(side * half, half)
        sums = total[3, 0, rows].astype(jnp.float32)
        for k in range(1, 4):
            sums = sums + z_in[k, side].astype(jnp.float32)
        out_ref[rows] = sums[:, :width]
        extra_out[rows] = sums[:, width:]

    for k in range(1, 4):
        for side in range(2):
            z_copy(k, side).wait_send()

    @pl.loop(0, 4)
    def _(k):
        for group in range(4):
            across(group, k).wait_send()
        x_copy(0, k, 0, 0).wait_send()
        x_copy(1, k, 0, 1).wait_send()
        x_copy(1, k, 1, 2).wait_send()
        y_copy(0, k, 1, 0).wait_send()
        y_copy(2, k, 1, 1).wait_send()
        y_copy(2, k, 0, 2).wait_send()


def scatter_experts(spread, gate_grad, up_grad, gate_w, up_w, extra):
    blocks, count, kept = spread.shape
    width = gate_w.shape[0]
    wide = width + 128
    low = gate_grad.dtype
    return pl.pallas_call(
        scatter_kernel,
        out_shape=(
            jax.ShapeDtypeStruct((count, width), jnp.float32),
            jax.ShapeDtypeStruct((count, 128), jnp.float32),
        ),
        in_specs=in_vmem(6),
        out_specs=tuple(in_vmem(2)),
        scratch_shapes=[
            pltpu.VMEM((4, 4, count, wide), low),
            pltpu.VMEM((4, 4, count, wide), low),
            pltpu.VMEM((4, 4, count, wide), low),
            pltpu.VMEM((4 * kept, width), low),
            pltpu.VMEM((3, 4, count // 2, wide), low),
            pltpu.VMEM((3, 4, count // 2, wide), low),
            pltpu.VMEM((4, 2, count // 2, wide), low),
            copies(4, 4),
            copies(4, 4),
            copies(3, 4),
            copies(3, 4),
            copies(3, 4),
            copies(3, 4),
            copies(4, 2),
            copies(4, 2),
        ],
        compiler_params=settings(2),
    )(spread, gate_grad, up_grad, gate_w, up_w, extra)


def reduce_kernel(
    first_ref,
    second_ref,
    vector_ref,
    first_out,
    second_out,
    vector_out,
    first_y,
    second_y,
    first_held,
    second_held,
    first_z,
    second_z,
    first_all,
    second_all,
    shard_in,
    member_own,
    member_in,
    y_sent,
    y_got,
    z_sent,
    z_got,
    back_sent,
    back_got,
    side_sent,
    side_got,
    shard_sent,
    shard_got,
    member_sent,
    member_got,
):
    z, y, x, c = spot()
    member, shard = lax.axis_index("exp"), lax.axis_index("fsdp")
    y_peer = where_is(z, 1 - y, x, c)
    members = [((member + j) % 8, shard) for j in range(8)]
    shards = [(member, (shard + j) % 4) for j in range(4)]
    greet(members[1:] + shards[1:])
    arrays = (
        (first_ref, first_out, first_y, first_held, first_z, first_all),
        (second_ref, second_out, second_y, second_held, second_z, second_all),
    )

    def shard_copy(j):
        return remote(
            vector_ref.at[(shard + j) % 4],
            shard_in.at[(4 - j) % 4],
            shard_sent.at[j],
            shard_got.at[(4 - j) % 4],
            shards[j],
        )

    def member_copy(j):
        return remote(
            member_own,
            member_in.at[(8 - j) % 8],
            member_sent.at[j],
            member_got.at[(8 - j) % 8],
            members[j],
        )

    def y_copy(which, k):
        source, _, target = arrays[which][:3]
        return remote(
            source.at[1 - y, (z + k) % 4],
            target.at[k],
            y_sent.at[which, k],
            y_got.at[which, k],
            y_peer,
        )

    def z_copy(which, k):
        return remote(
            arrays[which][3].at[k],
            arrays[which][4].at[k],
            z_sent.at[which, k],
            z_got.at[which, k],
            where_is((z + k) % 4, y, x, c),
        )

    def back_copy(which, k, slot):
        every = arrays[which][5]
        return remote(
            every.at[0, 0],
            every.at[0, slot],
            back_sent.at[which, k],
            back_got.at[which, slot],
            where_is((z + k) % 4, y, x, c),
        )

    def side_copy(which, k):
        every = arrays[which][5]
        return remote(
            every.at[0, k], every.at[1, k], side_sent.at[which, k], side_got.at[which, k], y_peer
        )

    for j in range(1, 4):
        shard_copy(j).start()

    @pl.loop(0, 4)
    def _(i):
        for which in range(2):
            y_copy(which, (i + 1) % 4).start()

    for j in range(1, 4):
        shard_copy(j).wait_recv()
    sums = vector_ref[shard]
    for j in range(1, 4):
        sums = sums + shard_in[j]
    member_own[...] = sums
    for j in range(1, 8):
        member_copy(j).start()

    @pl.loop(0, 4)
    def _(i):
        k = (i + 1) % 4
        for which in range(2):
            source, _, got, held = arrays[which][:4]
            y_copy(which, k).wait_recv()
            held[k] = (
                source[y, (z + k) % 4].astype(jnp.float32) + got[k].astype(jnp.float32)
            ).astype(held.dtype)

            @pl.when(i < 3)
            def _():
                z_copy(which, k).start()

    for which in range(2):
        _, out, _, held, got, every = arrays[which]
        for k in range(1, 4):
            z_copy(which, k).wait_recv()
        sums = held[0].astype(jnp.float32)
        for k in range(1, 4):
            sums = sums + got[k].astype(jnp.float32)
        every[0, 0] = sums.astype(every.dtype)
        for k in range(1, 4):
            back_copy(which, k, (4 - k) % 4).start()
        side_copy(which, 0).start()
        out[y, z] = every[0, 0]

    for j in range(1, 8):
        member_copy(j).wait_recv()
    sums = member_own[...]
    for j in range(1, 8):
        sums = sums + member_in[j]
    vector_out[...] = sums

    @pl.loop(1, 4)
    def _(k):
        for which in range(2):
            _, out, _, _, _, every = arrays[which]
            back_copy(which, k, k).wait_recv()
            side_copy(which, k).start()
            out[y, (z + k) % 4] = every[0, k]

    @pl.loop(0, 4)
    def _(k):
        for which in range(2):
            _, out, _, _, _, every = arrays[which]
            side_copy(which, k).wait_recv()
            out[1 - y, (z + k) % 4] = every[1, k]

    @pl.loop(0, 4)
    def _(k):
        for which in range(2):
            y_copy(which, k).wait_send()
            side_copy(which, k).wait_send()

    for k in range(1, 4):
        for which in range(2):
            z_copy(which, k).wait_send()
            back_copy(which, k, (4 - k) % 4).wait_send()
    for j in range(1, 4):
        shard_copy(j).wait_send()
    for j in range(1, 8):
        member_copy(j).wait_send()


def reduce_over_members(first, second, vectors):
    low = first.dtype

    def quarter(array, *lead):
        return pltpu.VMEM((*lead, *array.shape[2:]), low)

    return pl.pallas_call(
        reduce_kernel,
        out_shape=[
            jax.ShapeDtypeStruct(first.shape, low),
            jax.ShapeDtypeStruct(second.shape, low),
            jax.ShapeDtypeStruct(vectors.shape[1:], vectors.dtype),
        ],
        in_specs=in_vmem(3),
        out_specs=in_vmem(3),
        scratch_shapes=[
            quarter(first, 4),
            quarter(second, 4),
            quarter(first, 4),
            quarter(second, 4),
            quarter(first, 4),
            quarter(second, 4),
            quarter(first, 2, 4),
            quarter(second, 2, 4),
            pltpu.VMEM(vectors.shape, vectors.dtype),
            pltpu.VMEM(vectors.shape[1:], vectors.dtype),
            pltpu.VMEM((8, *vectors.shape[1:]), vectors.dtype),
        ]
        + [copies(2, 4)] * 8
        + [copies(4)] * 2
        + [copies(8)] * 2,
        compiler_params=settings(3),
    )(first, second, vectors)


def project_kernel(
    x_ref,
    routes_ref,
    gain_ref,
    query_ref,
    key_ref,
    value_ref,
    raw_out,
    hidden_out,
    routes_out,
    scale,
    x_in,
    scale_in,
    outgoing,
    core_in,
    across_x,
    x_sums,
    slice_sent,
    slice_got,
    scale_sent,
    scale_got,
    core_sent,
    core_got,
    x_sent,
    x_got,
    route_sent,
    route_got,
):
    z, y, x, c = spot()
    member, shard = lax.axis_index("exp"), lax.axis_index("fsdp")
    mine = number(z, y, x, c)
    count, depth = hidden_out.shape[1:]
    wide, narrow = query_ref.shape[1] // 4, key_ref.shape[1] // 4

    def everyone(j):
        other = (mine + j) % 32
        return (other // 4, other % 4)

    barrier = pltpu.get_barrier_semaphore()

    @pl.loop(1, 32)
    def _(j):
        pl.semaphore_signal(barrier, inc=1, device_id=everyone(j), device_id_type=MESH)

    pl.semaphore_wait(barrier, 31)

    def slice_copy(j):
        place = (shard + j) % 4
        return remote(
            x_ref.at[:, pl.ds(pl.multiple_of(place * depth, depth), depth)],
            x_in.at[(4 - j) % 4],
            slice_sent.at[j],
            slice_got.at[(4 - j) % 4],
            (member, place),
        )

    def scale_copy(j):
        return remote(
            scale,
            scale_in.at[(4 - j) % 4],
            scale_sent.at[j],
            scale_got.at[(4 - j) % 4],
            (member, (shard + j) % 4),
        )

    def route_copy(j):
        return remote(
            routes_ref, routes_out.at[mine], route_sent.at[j], route_got.at[(32 - j) % 32], everyone(j)
        )

    for j in range(1, 4):
        slice_copy(j).start()
    values = x_ref[...].astype(jnp.float32)
    scale[...] = jnp.broadcast_to(
        lax.rsqrt(jnp.mean(values * values, axis=1, keepdims=True) + EPSILON), scale.shape
    )
    for j in range(1, 4):
        scale_copy(j).start()
    routes_out[mine] = routes_ref[...]

    @pl.loop(1, 32)
    def _(j):
        route_copy(j).start()

    def hide(owner, piece, factor):
        gain = gain_ref[...].astype(jnp.float32)
        hidden = piece.astype(jnp.float32) * factor[:, :1] * gain
        hidden_out[owner] = hidden.astype(hidden_out.dtype)

    hide(shard, x_ref[:, pl.ds(pl.multiple_of(shard * depth, depth), depth)], scale[...])

    def take(owner):
        slot = (owner - shard + 4) % 4
        remote(x_in.at[slot], x_in.at[slot], slice_sent.at[slot], slice_got.at[slot], (member, owner)).wait_recv()
        remote(scale, scale_in.at[slot], scale_sent.at[slot], scale_got.at[slot], (member, owner)).wait_recv()
        hide(owner, x_in[slot], scale_in[slot])

    def partial(side, target):
        rows = jnp.concatenate([hidden_out[side * 2], hidden_out[side * 2 + 1]], axis=0)
        parts = []
        for weight, size in ((query_ref, wide), (key_ref, narrow), (value_ref, narrow)):
            columns = pl.ds(pl.multiple_of(target * size, size), size)
            parts.append(jnp.dot(rows, weight[:, columns], preferred_element_type=jnp.float32))
        return jnp.concatenate(parts, axis=1)

    core_peer, x_peer = where_is(z, y, x, 1 - c), where_is(z, y, 1 - x, c)

    def core_copy(turn, far):
        return remote(
            outgoing.at[turn, far],
            core_in.at[turn, far],
            core_sent.at[turn, far],
            core_got.at[turn, far],
            core_peer,
        )

    def x_copy(turn):
        return remote(across_x.at[turn], x_sums.at[turn], x_sent.at[turn], x_got.at[turn], x_peer)

    low = outgoing.dtype
    for turn in range(2):
        side = x if turn == 0 else 1 - x
        if turn == 0:
            take(side * 2 + 1 - c)
        else:
            take(side * 2 + c)
            take(side * 2 + 1 - c)
        outgoing[turn, 1] = partial(side, (1 - x) * 2 + 1 - c).astype(low)
        core_copy(turn, 1).start()
        sums = partial(side, (1 - x) * 2 + c)
        core_copy(turn, 1).wait_recv()
        across_x[turn] = (sums + core_in[turn, 1].astype(jnp.float32)).astype(low)
        x_copy(turn).start()
        outgoing[turn, 0] = partial(side, x * 2 + 1 - c).astype(low)
        core_copy(turn, 0).start()

    for turn in range(2):
        side = x if turn == 0 else 1 - x
        sums = partial(side, x * 2 + c)
        core_copy(turn, 0).wait_recv()
        sums = sums + core_in[turn, 0].astype(jnp.float32)
        raw_out[side * 2] = sums[:count]
        raw_out[side * 2 + 1] = sums[count:]

    for turn in range(2):
        side = 1 - x if turn == 0 else x
        x_copy(turn).wait_recv()
        raw_out[side * 2] += x_sums[turn, :count].astype(jnp.float32)
        raw_out[side * 2 + 1] += x_sums[turn, count:].astype(jnp.float32)

    @pl.loop(1, 32)
    def _(j):
        remote(
            routes_ref, routes_out.at[(mine + j) % 32], route_sent.at[j], route_got.at[j], everyone(j)
        ).wait_recv()

    @pl.loop(1, 32)
    def _(j):
        route_copy(j).wait_send()

    for j in range(1, 4):
        slice_copy(j).wait_send()
        scale_copy(j).wait_send()
    for turn in range(2):
        x_copy(turn).wait_send()
        for far in range(2):
            core_copy(turn, far).wait_send()


def project_tokens(tokens, routes, gain, w_query, key_weight, value_weight):
    count = tokens.shape[0]
    depth = w_query.shape[0]
    own = (w_query.shape[1] + key_weight.shape[1] + value_weight.shape[1]) // 4
    low = tokens.dtype
    return pl.pallas_call(
        project_kernel,
        out_shape=[
            jax.ShapeDtypeStruct((4, count, own), jnp.float32),
            jax.ShapeDtypeStruct((4, count, depth), low),
            jax.ShapeDtypeStruct((32, *routes.shape), routes.dtype),
        ],
        in_specs=in_vmem(6),
        out_specs=in_vmem(3),
        scratch_shapes=[
            pltpu.VMEM((count, 128), jnp.float32),
            pltpu.VMEM((4, count, depth), low),
            pltpu.VMEM((4, count, 128), jnp.float32),
            pltpu.VMEM((2, 2, 2 * count, own), low),
            pltpu.VMEM((2, 2, 2 * count, own), low),
            pltpu.VMEM((2, 2 * count, own), low),
            pltpu.VMEM((2, 2 * count, own), low),
            copies(4),
            copies(4),
            copies(4),
            copies(4),
            copies(2, 2),
            copies(2, 2),
            copies(2),
            copies(2),
            copies(32),
            copies(32),
        ],
        compiler_params=settings(4),
    )(tokens, routes, gain, w_query, key_weight, value_weight)


def finish_kernel(
    attended_ref,
    weight_ref,
    x_ref,
    gain_ref,
    middle_out,
    normed_out,
    outgoing,
    core_in,
    across_x,
    x_sums,
    core_sent,
    core_got,
    x_sent,
    x_got,
):
    z, y, x, c = spot()
    count = x_ref.shape[0]
    core_peer, x_peer = where_is(z, y, x, 1 - c), where_is(z, y, 1 - x, c)
    greet([core_peer, x_peer])

    def core_copy(far):
        return remote(
            outgoing.at[far], core_in.at[far], core_sent.at[far], core_got.at[far], core_peer
        )

    def x_copy():
        return remote(across_x, x_sums, x_sent, x_got, x_peer)

    def partial(side, core):
        return jnp.dot(
            attended_ref[side * 2 + core], weight_ref[...], preferred_element_type=jnp.float32
        )

    outgoing[1] = partial(1 - x, 1 - c).astype(outgoing.dtype)
    core_copy(1).start()
    sums = partial(1 - x, c)
    core_copy(1).wait_recv()
    across_x[...] = (sums + core_in[1].astype(jnp.float32)).astype(across_x.dtype)
    x_copy().start()
    outgoing[0] = partial(x, 1 - c).astype(outgoing.dtype)
    core_copy(0).start()
    sums = partial(x, c) + x_ref[...].astype(jnp.float32)
    core_copy(0).wait_recv()
    sums = sums + core_in[0].astype(jnp.float32)
    x_copy().wait_recv()
    middle = sums + x_sums[...].astype(jnp.float32)
    middle_out[...] = middle
    scale = lax.rsqrt(jnp.mean(middle * middle, axis=1, keepdims=True) + EPSILON)
    normed_out[...] = (middle * scale * gain_ref[...]).astype(normed_out.dtype)
    x_copy().wait_send()
    core_copy(0).wait_send()
    core_copy(1).wait_send()


def finish_attention(attended, w_out, tokens, gain):
    count, width = tokens.shape
    low = tokens.dtype
    return pl.pallas_call(
        finish_kernel,
        out_shape=[
            jax.ShapeDtypeStruct((count, width), jnp.float32),
            jax.ShapeDtypeStruct((count, width), low),
        ],
        in_specs=in_vmem(4),
        out_specs=in_vmem(2),
        scratch_shapes=[
            pltpu.VMEM((2, count, width), low),
            pltpu.VMEM((2, count, width), low),
            pltpu.VMEM((count, width), low),
            pltpu.VMEM((count, width), low),
            copies(2),
            copies(2),
            copies(),
            copies(),
        ],
        compiler_params=settings(5),
    )(attended, w_out, tokens, gain)


def branch_kernel(
    branch_ref, weight_ref, grad_out, every_out, x_sent, x_got, core_sent, core_got
):
    z, y, x, c = spot()
    mine = x * 2 + c
    core_peer, x_peer = where_is(z, y, x, 1 - c), where_is(z, y, 1 - x, c)
    greet([core_peer, x_peer])
    every_out[mine] = branch_ref[...]

    def x_copy():
        return remote(branch_ref, every_out.at[mine], x_sent, x_got, x_peer)

    def core_copy(far):
        place = (1 - x if far else x) * 2 + c
        return remote(
            every_out.at[place], every_out.at[place], core_sent.at[far], core_got.at[far], core_peer
        )

    def back(place):
        grad_out[place] = right_transposed(every_out[place], weight_ref[...]).astype(grad_out.dtype)

    x_copy().start()
    core_copy(0).start()
    back(mine)
    core_copy(0).wait_recv()
    back(x * 2 + 1 - c)
    x_copy().wait_recv()
    core_copy(1).start()
    back((1 - x) * 2 + c)
    core_copy(1).wait_recv()
    back((1 - x) * 2 + 1 - c)
    x_copy().wait_send()
    core_copy(0).wait_send()
    core_copy(1).wait_send()


def branch_back(branch, w_out):
    count, width = branch.shape
    low = branch.dtype
    return pl.pallas_call(
        branch_kernel,
        out_shape=[
            jax.ShapeDtypeStruct((4, count, w_out.shape[0]), low),
            jax.ShapeDtypeStruct((4, count, width), low),
        ],
        in_specs=in_vmem(2),
        out_specs=in_vmem(2),
        scratch_shapes=[copies(), copies(), copies(2), copies(2)],
        compiler_params=settings(6),
    )(branch, w_out)


def heads_kernel(
    grad_ref,
    hidden_ref,
    query_ref,
    key_ref,
    value_ref,
    weight_out,
    first_out,
    every,
    outgoing,
    x_sent,
    x_got,
    core_sent,
    core_got,
    back_sent,
    back_got,
):
    z, y, x, c = spot()
    member, shard = lax.axis_index("exp"), lax.axis_index("fsdp")
    core_peer, x_peer = where_is(z, y, x, 1 - c), where_is(z, y, 1 - x, c)
    peers = [(member, (shard + j) % 4) for j in range(1, 4)]
    greet(peers)
    rows = grad_ref.shape[0]
    half = rows // 2
    count = rows // 4
    depth = hidden_ref.shape[1]
    wide, narrow = query_ref.shape[1] // 4, key_ref.shape[1] // 4
    every[shard] = grad_ref[...]

    def x_copy(part):
        piece = pl.ds(part * half, half)
        return remote(
            grad_ref.at[piece], every.at[shard, piece], x_sent.at[part], x_got.at[part], x_peer
        )

    def core_copy(far, part):
        view = every.at[(1 - x if far else x) * 2 + c, pl.ds(part * half, half)]
        return remote(view, view, core_sent.at[far, part], core_got.at[far, part], core_peer)

    for part in range(2):
        x_copy(part).start()
    for part in range(2):
        core_copy(0, part).start()

    def weigh(place):
        weight_out[place] = left_trans(hidden_ref[...], every[place]).astype(weight_out.dtype)

    def back(place):
        grads = every[place]
        sums = None
        for weight, size, start in (
            (query_ref, wide, 0),
            (key_ref, narrow, wide),
            (value_ref, narrow, wide + narrow),
        ):
            columns = pl.ds(pl.multiple_of(place * size, size), size)
            term = right_transposed(grads[:, start : start + size], weight[:, columns])
            sums = term if sums is None else sums + term
        return sums

    total = back(shard)
    weigh(shard)
    near = x * 2 + 1 - c
    for part in range(2):
        core_copy(0, part).wait_recv()
    total = total + back(near)
    weigh(near)
    for part in range(2):
        x_copy(part).wait_recv()
        core_copy(1, part).start()
    far = (1 - x) * 2 + c
    total = total + back(far)
    for part in range(2):
        core_copy(1, part).wait_recv()
    total = total + back((1 - x) * 2 + 1 - c)
    for owner in range(4):
        outgoing[owner] = total[owner * count : (owner + 1) * count].astype(outgoing.dtype)

    def back_copy(j):
        place = (shard + j) % 4
        return remote(
            outgoing.at[place],
            first_out.at[shard],
            back_sent.at[j],
            back_got.at[(4 - j) % 4],
            (member, place),
        )

    for j in range(1, 4):
        back_copy(j).start()
    first_out[shard] = outgoing[shard]
    weigh(far)
    weigh((1 - x) * 2 + 1 - c)
    for j in range(1, 4):
        place = (shard + j) % 4
        remote(
            outgoing.at[place], first_out.at[place], back_sent.at[j], back_got.at[j], (member, place)
        ).wait_recv()
    for j in range(1, 4):
        back_copy(j).wait_send()
    for part in range(2):
        x_copy(part).wait_send()
        for far in range(2):
            core_copy(far, part).wait_send()


def heads_back(grads, hidden, w_query, key_weight, value_weight):
    rows, own = grads.shape
    depth = hidden.shape[1]
    low = grads.dtype
    return pl.pallas_call(
        heads_kernel,
        out_shape=[
            jax.ShapeDtypeStruct((4, depth, own), low),
            jax.ShapeDtypeStruct((4, rows // 4, depth), low),
        ],
        in_specs=in_vmem(5),
        out_specs=in_vmem(2),
        scratch_shapes=[
            pltpu.VMEM((4, rows, own), low),
            pltpu.VMEM((4, rows // 4, depth), low),
            copies(2),
            copies(2),
            copies(2, 2),
            copies(2, 2),
            copies(4),
            copies(4),
        ],
        compiler_params=settings(7),
    )(grads, hidden, w_query, key_weight, value_weight)


def moe_gathered(normed, router, routes, capacity, cotangent, weights, notes):
    gate_w, up_w, down_w = weights
    token_count, topk = routes.shape
    experts = router.shape[1]
    mine = lax.axis_index("exp") * lax.axis_size("fsdp") + lax.axis_index("fsdp")
    all_routes = notes[:, :topk]
    all_grads = lax.all_gather(cotangent, BOTH, axis=0, tiled=True)
    columns = jnp.arange(experts, dtype=jnp.int32)
    named = jnp.any(all_routes[:, :, None, :] == columns[None, None, :, None], axis=1)
    own = jnp.any(all_routes == mine, axis=1)
    before = jnp.tril(jnp.ones((token_count, token_count), jnp.bfloat16), -1)
    rank = right_transposed(own.astype(jnp.bfloat16), before).astype(jnp.int32)
    places = jnp.arange(capacity, dtype=jnp.int32)
    select = (own[:, None, :] & (rank[:, None, :] == places[None, :, None])).astype(jnp.bfloat16)
    spread = (own[:, :, None] & (rank[:, :, None] == places[None, None, :])).astype(jnp.bfloat16)
    grad_rows = contract(
        "bcj,bjd->bcd", select, all_grads.reshape(experts, token_count, MODEL_WIDTH)
    ).astype(jnp.bfloat16)
    named_rows = contract("bcj,bej->bce", select, named.astype(jnp.bfloat16))
    named_rows = jnp.pad(named_rows.astype(jnp.bfloat16), ((0, 0), (0, 0), (0, 128 - experts)))
    flat_grads = grad_rows.reshape(experts * capacity, MODEL_WIDTH)
    ahead = right_transposed(flat_grads, down_w).reshape(experts, capacity, -1)

    padded = jnp.pad(router, ((0, 0), (0, 128 - experts)))
    arrived, active, gate_pre_grad, up_pre_grad, share, extra = gather_experts(
        normed, select, ahead, named_rows, gate_w, up_w, padded
    )
    summed, back = scatter_experts(spread, gate_pre_grad, up_pre_grad, gate_w, up_w, extra)

    summed, back, arrived, gate_pre_grad, up_pre_grad, active, share = lax.optimization_barrier(
        (summed, back, arrived, gate_pre_grad, up_pre_grad, active, share)
    )

    def flat(rows):
        return rows.reshape(experts * capacity, rows.shape[2])

    share = flat(share)[:, :1]
    out_rows = (share * flat_grads.astype(jnp.float32)).astype(jnp.bfloat16)
    produced = matrix_product(flat(active), down_w).astype(jnp.bfloat16)
    weighted = (share * produced.astype(jnp.float32)).astype(jnp.bfloat16)
    full = contract("bjc,bcd->bjd", spread, weighted.reshape(experts, capacity, MODEL_WIDTH))
    full = full.astype(jnp.bfloat16).reshape(experts * token_count, MODEL_WIDTH)
    mixed = lax.psum_scatter(full, BOTH, scatter_dimension=0, tiled=True)
    weight_grads = (
        left_trans(flat(arrived), flat(gate_pre_grad)),
        left_trans(flat(arrived), flat(up_pre_grad)),
        left_trans(flat(active), out_rows),
    )
    gate_grad = back[:, :experts] + back[:, experts : 2 * experts]
    picks = jnp.any(routes[:, :, None] == columns[None, None, :], axis=1)
    gates = jax.nn.softmax(jnp.where(picks, matrix_product(normed, router), MASKED), axis=1)
    logit_grad = gates * (gate_grad - jnp.sum(gates * gate_grad, axis=1, keepdims=True))
    return mixed.astype(jnp.float32), summed, logit_grad.astype(jnp.bfloat16), *weight_grads


def moe_exchanged(normed, router, routes, capacity, cotangent, weights, notes):
    gate_w, up_w, down_w = weights
    token_count, topk = routes.shape
    experts = router.shape[1]
    gates = gates_of(matrix_product(normed, router), routes, experts)
    slots = slot_table(routes, experts, capacity)

    def send(rows):
        packed = jnp.zeros((experts * capacity, MODEL_WIDTH), jnp.bfloat16).at[slots].set(rows)
        return exchange(packed.reshape(experts, capacity, MODEL_WIDTH)).reshape(
            experts * capacity, MODEL_WIDTH
        )

    def bring(rows):
        rows = exchange(rows.reshape(experts, capacity, MODEL_WIDTH))
        return rows.reshape(experts * capacity, MODEL_WIDTH)[slots].reshape(
            token_count, topk, MODEL_WIDTH
        )

    arrived = send(jnp.repeat(normed, topk, axis=0))
    hidden = expert_forward(arrived, gate_w, up_w)
    scaled = (gates[:, :, None] * cotangent.astype(jnp.float32)[:, None, :]).astype(jnp.bfloat16)
    out_rows = send(scaled.reshape(token_count * topk, MODEL_WIDTH))
    rows_back, gate_pre_grad, up_pre_grad = expert_back(out_rows, hidden, gate_w, up_w, down_w)
    gate_w_grad = left_trans(arrived, gate_pre_grad)
    up_w_grad = left_trans(arrived, up_pre_grad)
    down_grad = left_trans(hidden[3], out_rows)
    returned = bring(matrix_product(hidden[3], down_w).astype(jnp.bfloat16))
    mixed = jnp.einsum("tk,tkd->td", gates, returned.astype(jnp.float32))
    gate_grad = jnp.einsum("td,tkd->tk", cotangent, returned, preferred_element_type=jnp.float32)
    summed = jnp.sum(bring(rows_back), axis=1, dtype=jnp.float32)
    picked_grad = gates * (gate_grad - jnp.sum(gates * gate_grad, axis=1, keepdims=True))
    onehot = routes[:, :, None] == jnp.arange(experts, dtype=jnp.int32)[None, None, :]
    logit_grad = jnp.sum(jnp.where(onehot, picked_grad[:, :, None], 0.0), axis=1)
    return mixed, summed, logit_grad.astype(jnp.bfloat16), gate_w_grad, up_w_grad, down_grad


def local(
    tokens,
    lengths,
    routes,
    attn_gain,
    w_query,
    key_weight,
    value_weight,
    q_gain,
    k_gain,
    w_out,
    mlp_gain,
    w_router,
    expert_gate,
    expert_up,
    expert_down,
    cotangent,
):
    shards, members = lax.axis_size("fsdp"), lax.axis_size("exp")
    experts = shards * members
    token_count, topk = routes.shape
    capacity = 2 * token_count * topk // experts
    group = shards * token_count
    depth = w_query.shape[0]
    heads = QUERY_HEADS // shards
    kv_heads = max(1, KEY_VALUE_HEADS // shards)
    copies_of = shards * kv_heads // KEY_VALUE_HEADS
    head_group = heads // kv_heads
    wide, narrow = heads * HEAD_WIDTH, kv_heads * HEAD_WIDTH
    place = lax.axis_index("fsdp")

    gathered = lax.all_gather(
        jnp.concatenate([w_router.reshape(-1), attn_gain, mlp_gain, q_gain, k_gain]), "fsdp"
    )
    cuts, start = [], 0
    for leaf in (w_router, attn_gain, mlp_gain, q_gain, k_gain):
        cuts.append(gathered[:, start : start + leaf.size])
        start += leaf.size
    router = cuts[0].reshape(MODEL_WIDTH, experts)
    gain_attn, gain_mlp, gain_query, gain_key = [
        cut.reshape(-1).astype(jnp.float32) for cut in cuts[1:]
    ]
    dense = (members, shards) == (8, 4) and 2 * capacity >= token_count
    inputs = tokens.astype(jnp.float32)
    scale_one = rms_scale(inputs)
    if dense:
        notes = jnp.pad(
            jnp.concatenate(
                [routes.T, jnp.pad(lengths, ((0, 0), (0, token_count - lengths.shape[1])))], axis=0
            ),
            ((0, 15 - topk), (0, 0)),
        )
        raw, hidden, notes = project_tokens(
            tokens, notes, attn_gain[None], w_query, key_weight, value_weight
        )
        hidden = hidden.reshape(group, depth)
        first = lax.axis_index("exp") * shards
        all_lengths = lax.dynamic_slice_in_dim(notes, first, shards)[:, topk, : lengths.shape[1]]
    else:
        notes = None
        all_lengths = lax.all_gather(lengths[0], "fsdp")

        def by_shard(weight):
            weight = weight.reshape(depth, KEY_VALUE_HEADS, HEAD_WIDTH)
            return jnp.repeat(weight, copies_of, axis=1).reshape(depth, shards, narrow)

        joined = jnp.concatenate(
            [w_query.reshape(depth, shards, wide), by_shard(key_weight), by_shard(value_weight)],
            axis=2,
        ).transpose(1, 0, 2)
        first_normed = (inputs * scale_one * gain_attn).astype(jnp.bfloat16)
        hidden = lax.all_to_all(first_normed, "fsdp", split_axis=1, concat_axis=0, tiled=True)
        partial = contract("gk,nkc->ngc", hidden, joined).astype(jnp.bfloat16)
        raw = lax.psum_scatter(partial, "fsdp", scatter_dimension=0, tiled=True)[0]
        raw = raw.astype(jnp.float32)
    raw = raw.reshape(shards, token_count, wide + 2 * narrow)
    query_raw = raw[:, :, :wide].reshape(shards, token_count, heads, HEAD_WIDTH)
    key_raw = raw[:, :, wide : wide + narrow].reshape(shards, token_count, kv_heads, HEAD_WIDTH)
    value = (
        raw[:, :, wide + narrow :]
        .astype(jnp.bfloat16)
        .reshape(shards, token_count, kv_heads, HEAD_WIDTH)
    )
    position, allowed = jax.vmap(lambda row: seq_layout(row, token_count))(all_lengths)
    cosine, sine = rotary_tables(position, HEAD_WIDTH)
    query_scale = rms_scale(query_raw)
    query_hat = query_raw * query_scale
    key_scale = rms_scale(key_raw)
    key_hat = key_raw * key_scale
    query = (
        rotate(query_hat * gain_query, cosine, sine)
        .astype(jnp.bfloat16)
        .reshape(shards, token_count, kv_heads, head_group, HEAD_WIDTH)
    )
    key = rotate(key_hat * gain_key, cosine, sine).astype(jnp.bfloat16)
    scores = contract("bqkgd,bpkd->bkgqp", query, key) * HEAD_WIDTH ** (-0.5)
    scores = jnp.where(allowed[:, None, None], scores, MASKED)
    top = jnp.max(scores, axis=-1, keepdims=True)
    raised = jnp.exp(scores - top)
    probs = raised / jnp.sum(raised, axis=-1, keepdims=True)
    probs_low = probs.astype(jnp.bfloat16)
    attended = contract("bkgqp,bpkd->bqkgd", probs_low, value).astype(jnp.bfloat16)
    attended = attended.reshape(group, wide)
    if dense:
        middle, normed = finish_attention(
            attended.reshape(shards, token_count, wide), w_out, tokens, gain_mlp[None]
        )
        scale_two = rms_scale(middle)
    else:
        mixed_heads = lax.psum_scatter(
            matrix_product(attended, w_out).astype(jnp.bfloat16),
            "fsdp",
            scatter_dimension=0,
            tiled=True,
        )
        middle = inputs + mixed_heads.astype(jnp.float32)
        scale_two = rms_scale(middle)
        normed = (middle * scale_two * gain_mlp).astype(jnp.bfloat16)

    moe = moe_gathered if dense else moe_exchanged
    mixed, summed, logit_grad, gate_w_grad, up_w_grad, down_grad = moe(
        normed,
        router,
        routes,
        capacity,
        cotangent,
        (expert_gate[0], expert_up[0], expert_down[0]),
        notes,
    )
    layer_out = (middle + mixed).astype(jnp.bfloat16)

    upstream = cotangent.astype(jnp.float32)
    normed_grad = summed + right_transposed(logit_grad, router)
    mlp_gain_grad = jnp.sum(normed_grad * middle * scale_two, axis=0)
    router_grad = left_trans(normed, logit_grad)
    middle_grad = upstream + rms_back(normed_grad * gain_mlp, middle, scale_two)
    branch_low = middle_grad.astype(jnp.bfloat16)
    if dense:
        attended_grad, branch_grad = branch_back(branch_low, w_out)
        branch_grad = branch_grad.reshape(group, MODEL_WIDTH)
    else:
        branch_grad = lax.all_gather(branch_low, "fsdp", axis=0, tiled=True)
        attended_grad = right_transposed(branch_grad, w_out).astype(jnp.bfloat16)
    out_w_grad = left_trans(attended, branch_grad)
    attended_grad = attended_grad.reshape(shards, token_count, kv_heads, head_group, HEAD_WIDTH)
    prob_grad = contract("bqkgd,bpkd->bkgqp", attended_grad, value)
    value_grad = contract("bkgqp,bqkgd->bpkd", probs_low, attended_grad)
    balance = jnp.sum(probs * prob_grad, axis=-1, keepdims=True)
    score_grad = (probs * (prob_grad - balance)).astype(jnp.bfloat16)
    query_norm_grad = contract("bkgqp,bpkd->bqkgd", score_grad, key) * HEAD_WIDTH ** (-0.5)
    query_norm_grad = query_norm_grad.reshape(shards, token_count, heads, HEAD_WIDTH)
    key_norm_grad = contract("bkgqp,bqkgd->bpkd", score_grad, query) * HEAD_WIDTH ** (-0.5)
    query_norm_grad = rotate_back(query_norm_grad, cosine, sine)
    key_norm_grad = rotate_back(key_norm_grad, cosine, sine)
    q_gain_grad = jnp.sum(query_norm_grad * query_hat, axis=(0, 1, 2))
    k_gain_grad = jnp.sum(key_norm_grad * key_hat, axis=(0, 1, 2))
    query_grad = rms_back(query_norm_grad * gain_query, query_raw, query_scale)
    key_grad = rms_back(key_norm_grad * gain_key, key_raw, key_scale)
    head_grads = jnp.concatenate(
        [
            query_grad.reshape(group, wide),
            key_grad.reshape(group, narrow),
            value_grad.reshape(group, narrow),
        ],
        axis=1,
    ).astype(jnp.bfloat16)
    if dense:
        joined_grad, first_grad = heads_back(head_grads, hidden, w_query, key_weight, value_weight)
        first_grad = first_grad.transpose(1, 0, 2).reshape(token_count, MODEL_WIDTH)
    else:
        head_grads = lax.all_gather(head_grads, "fsdp")
        hidden_grad = contract("ngc,nkc->gk", head_grads, joined).astype(jnp.bfloat16)
        first_grad = lax.all_to_all(
            hidden_grad, "fsdp", split_axis=0, concat_axis=1, tiled=True
        )
        joined_grad = contract("gk,ngc->nkc", hidden, head_grads).astype(jnp.bfloat16)
    first_grad = first_grad.astype(jnp.float32)
    attn_gain_grad = jnp.sum(first_grad * inputs * scale_one, axis=0)
    input_grad = (middle_grad + rms_back(first_grad * gain_attn, inputs, scale_one)).astype(
        jnp.bfloat16
    )

    out_w_grad = out_w_grad.astype(jnp.bfloat16)
    vectors = jnp.concatenate(
        [
            grad.reshape(shards, -1)
            for grad in (router_grad, attn_gain_grad, mlp_gain_grad, q_gain_grad, k_gain_grad)
        ],
        axis=1,
    )
    if dense:
        rows = -(-vectors.shape[1] // 1024) * 8
        padded = jnp.pad(vectors, ((0, 0), (0, rows * 128 - vectors.shape[1])))
        joined_sum, out_sum, vectors = reduce_over_members(
            joined_grad.reshape(2, 4, -1, wide + 2 * narrow),
            out_w_grad.reshape(2, 4, -1, MODEL_WIDTH),
            padded.reshape(shards, rows, 128),
        )
        joined_sum, out_sum = joined_sum.reshape(joined_grad.shape), out_sum.reshape(w_out.shape)
        vectors = vectors.reshape(-1)
    else:
        out_sum, joined_sum = lax.psum(out_w_grad, "exp"), lax.psum(joined_grad, "exp")
        vectors = lax.psum(vectors, BOTH)[place]
    out_sum, joined_sum = out_sum.astype(jnp.float32), joined_sum.astype(jnp.float32)
    sums, start = [], 0
    for leaf in (w_router, attn_gain, mlp_gain, q_gain, k_gain):
        sums.append(vectors[start : start + leaf.size].reshape(leaf.shape))
        start += leaf.size

    def gather_heads(part):
        return part.transpose(1, 0, 2).reshape(depth, KEY_VALUE_HEADS, copies_of, HEAD_WIDTH).sum(
            axis=2
        ).reshape(depth, KEY_VALUE_HEADS * HEAD_WIDTH)

    return (
        layer_out,
        input_grad,
        sums[1],
        joined_sum[:, :, :wide].transpose(1, 0, 2).reshape(depth, QUERY_HEADS * HEAD_WIDTH),
        gather_heads(joined_sum[:, :, wide : wide + narrow]),
        gather_heads(joined_sum[:, :, wide + narrow :]),
        sums[3],
        sums[4],
        out_sum,
        sums[2],
        sums[0],
        gate_w_grad[None],
        up_w_grad[None],
        down_grad[None],
    )


def solution(mesh):
    in_specs = (
        P(("exp", "fsdp"), None),
        P(("exp", "fsdp"), None),
        P(("exp", "fsdp"), None),
        P("fsdp"),
        P("fsdp", None),
        P("fsdp", None),
        P("fsdp", None),
        P("fsdp"),
        P("fsdp"),
        P("fsdp", None),
        P("fsdp"),
        P("fsdp", None),
        P(("exp", "fsdp"), None, None),
        P(("exp", "fsdp"), None, None),
        P(("exp", "fsdp"), None, None),
        P(("exp", "fsdp"), None),
    )
    out_specs = (
        P(("exp", "fsdp"), None),
        P(("exp", "fsdp"), None),
        P("fsdp"),
        P("fsdp", None),
        P("fsdp", None),
        P("fsdp", None),
        P("fsdp"),
        P("fsdp"),
        P("fsdp", None),
        P("fsdp"),
        P("fsdp", None),
        P(("exp", "fsdp"), None, None),
        P(("exp", "fsdp"), None, None),
        P(("exp", "fsdp"), None, None),
    )
    return jax.shard_map(local, mesh=mesh, in_specs=in_specs, out_specs=out_specs, check_vma=False)
```

time: 1280 us -> 1020 us (0.80)
  waiting for transfers between devices: 302 us -> 0.58 us
  Pallas kernels: 501 us -> 767 us
  blocking collectives: 116 us -> 0 us
  matrix products: 188 us -> 88.3 us
    pallas_call x3 -> x7, Pallas kernels: 501 us -> 767 us  [the longest x1 317 us: reduce_over_members(): pl.pallas_call(reduce_kernel, out_shape=[jax.ShapeDtypeStruct(first.shape...]
    psum x2 -> x0, waiting for transfers between devices: 216 us -> none  [the longest x1 155 us: local(): lax.psum(out_w_grad.astype(jnp.bfloat16), 'exp').astype(jnp.float32)]
    psum x1 -> x0, blocking collectives: 76.2 us -> none  [all_summed(): vectors, cuts, start = (lax.psum(vectors, BOTH), [], 0)]
    reduce_scatter x2 -> x0, waiting for transfers between devices: 46.3 us -> none  [the longest x1 46.3 us: local(): lax.psum_scatter(partial, 'fsdp', scatter_dimension=0, tiled=True)[0]]
    dot_general x6 -> x2, matrix products: 53.1 us -> 10.3 us  [matrix_product(): return jnp.dot(left, right, preferred_element_type=jnp.float32)]
    all_gather x2 -> x0, blocking collectives: 40.2 us -> none  [the longest x1 34.9 us: moe_gathered(): all_routes = lax.all_gather(routes, BOTH, axis=0, tiled=True)]
    unnamed x10 -> x4, waiting for transfers between devices: 31.3 us -> 0.56 us
    dot_general x6 -> x3, matrix products: 42.3 us -> 12.1 us  [right_transposed(): lax.dot_general(left, right, (((1,), (1,)), ((), ())), preferred_element_...]
  transfers between devices with their start and end apart: 11 -> 3, of which waited for: 5 -> 0; matrix products, arithmetic and copies ran while one was open for 14% -> 16% of each run, Pallas kernels for 30% -> 52%
where the time goes in v3:
time: 1020 us; the launch traced here: 1010 us
  Pallas kernels  767 us (75%)
  matrix products  88.3 us (9%)
  local copies, waits for them, and re-layouts  81.9 us (8%)
  other arithmetic  53.2 us (5%)
  between operations  17.4 us (2%)
    pallas_call x1, Pallas kernels, reduce_over_members(): pl.pallas_call(reduce_kernel, out_shape=[jax.ShapeDtypeStruct(first.shape...  317 us
    pallas_call x1, Pallas kernels, gather_experts(): pl.pallas_call(gather_kernel, out_shape=[jax.ShapeDtypeStruct((blocks, ke...  125 us
    pallas_call x1, Pallas kernels, scatter_experts(): pl.pallas_call(scatter_kernel, out_shape=(jax.ShapeDtypeStruct((count, wi...  116 us
    pallas_call x1, Pallas kernels, heads_back(): pl.pallas_call(heads_kernel, out_shape=[jax.ShapeDtypeStruct((4, depth, o...  82.2 us
    pallas_call x1, Pallas kernels, project_tokens(): pl.pallas_call(project_kernel, out_shape=[jax.ShapeDtypeStruct((4, count,...  71.5 us
    dot_general x5, matrix products, left_trans(): lax.dot_general(left, right, (((0,), (0,)), ((), ())), preferred_element_...  36.6 us
    pallas_call x1, Pallas kernels, branch_back(): pl.pallas_call(branch_kernel, out_shape=[jax.ShapeDtypeStruct((4, count,...  32.6 us
    dot_general x9, matrix products, contract(): return jnp.einsum(spec, left, right, preferred_element_type=jnp.float32)  29.3 us
  transfers between devices with their start and end apart: 3, of which 0 were waited for; matrix products, arithmetic and copies ran while one was open for 16% of the time, Pallas kernels for 52%

profile of v3, /device:TPU:8, one launch (start us, length us, event | category | flops | bytes accessed | tf_op | source)
XLA Modules:
  0.0 1008.5 jit_solution(3626631317975353162)
XLA Ops:
  18.5 71.5 %shard_map.263 = (f32[4,128,1280]{2,1,0:T(8,128)}, bf16[4,128,512]{2,1,0:T(8,128)(2,1)}, s32[32,16,128]{2,1,0:T(8,128)}) custom-call(bf16[128,2048]{1,0:T(8,128)(2,1)} %x_ref.3, s32[16,128]{1,0:T(8,128)} %pad.21.routes_ref, bf16[1,512]{1,0:T(2,128)(2,1)} %broadcast_in_dim.48.gain_ref, bf16[512,4096]{1,0:T(8,128)(2,1)} %query_ref.3, ...), custom_call_target="tpu_custom_call" | custom-call | tf_op jit(solution)/shard_map/pallas_call | solution.py:990
  102.8 3.1 copy.200
  121.3 3.3 fusion.57
  138.4 21.9 %shard_map.264 = (f32[128,2048]{1,0:T(8,128)}, bf16[128,2048]{1,0:T(8,128)(2,1)}) custom-call(bf16[4,128,1024]{2,1,0:T(8,128)(2,1)} %copy.247.attended_ref, bf16[1024,2048]{1,0:T(8,128)(2,1)} %weight_ref.3, bf16[128,2048]{1,0:T(8,128)(2,1)} %x_ref.3, f32[1,2048]{1,0:T(1,128)} %bitcast.316), custom_call_target="tpu_custom_call" | custom-call | tf_op jit(solution)/shard_map/pallas_call | solution.py:1080
  160.3 11.4 %convolution_convert_fusion.1 = bf16[32,64,2048]{2,1,0:T(8,128)(2,1)} fusion(bf16[32,128,2048]{2,1,0:T(8,128)(2,1)} %bitcast.277, s32[32,128]{1,0:T(8,128)S(1)} %convolution_convert_fusion.5, pred[32,128]{1,0:T(8,128)(4,1)} %copy-done.46), kind=kOutput, calls=%fused_computation.6 | convolution fusion | flops 1078460416 | bytes 25186304 | tf_op jit(solution)/shard_map/bcj,bjd->bcd/dot_general | solution.py:40
  171.7 10.8 %fusion.4.ahead_ref = f32[32,64,768]{2,1,0:T(8,128)} fusion(bf16[32,64,2048]{2,1,0:T(8,128)(2,1)} %convolution_convert_fusion.1, bf16[1,768,2048]{2,1,0:T(8,128)(2,1)S(1)} %copy-done), kind=kOutput, calls=%fused_computation.14 | convolution fusion | flops 6442450944 | bytes 17825792 | tf_op jit(solution)/shard_map/dot_general | solution.py:34
  182.5 124.9 %shard_map.265 = (bf16[32,64,2048]{2,1,0:T(8,128)(2,1)}, bf16[32,64,768]{2,1,0:T(8,128)(2,1)}, bf16[32,64,768]{2,1,0:T(8,128)(2,1)}, bf16[32,64,768]{2,1,0:T(8,1...) custom-call(bf16[128,2048]{1,0:T(8,128)(2,1)} %get-tuple-element.44.x_ref, ...), custom_call_target="tpu_custom_call" | custom-call | tf_op jit(solution)/shard_map/pallas_call | solution.py:364
  307.4 116.5 %shard_map.266 = (f32[128,2048]{1,0:T(8,128)}, f32[128,128]{1,0:T(8,128)}) custom-call(bf16[32,128,64]{2,1,0:T(8,128)(2,1)} %fusion.19.spread_ref, bf16[32,64,768]{2,1,0:T(8,128)(2,1)} %get-tuple-element.66.gate_grad_ref, bf16[32,64,768]{2,1,0:T(8,128)(2,1)} %get-tuple-element.67.up_grad_ref, bf16[2048,768]{1,0:T(8,128)(2,1)} %bitcast.284, ...), custom_call_target="tpu_custom_call" | custom-call | tf_op jit(solution)/shard_map/pallas_call | solution.py:575
  429.0 8.8 multiply_convert_fusion.1
  437.9 7.9 convolution_convert_fusion
  469.5 32.6 %shard_map.267 = (bf16[4,128,1024]{2,1,0:T(8,128)(2,1)}, bf16[4,128,2048]{2,1,0:T(8,128)(2,1)}) custom-call(bf16[128,2048]{1,0:T(8,128)(2,1)} %fusion.82.branch_ref, bf16[1024,2048]{1,0:T(8,128)(2,1)} %weight_ref.3), custom_call_target="tpu_custom_call" | custom-call | tf_op jit(solution)/shard_map/pallas_call | solution.py:1141
  509.3 3.2 fusion.61
  513.2 3.0 bitcast_multiply_fusion.4
  526.5 3.2 copy.218
  537.8 82.2 %shard_map.268 = (bf16[4,512,1280]{2,1,0:T(8,128)(2,1)}, bf16[4,128,512]{2,1,0:T(8,128)(2,1)}) custom-call(bf16[512,1280]{1,0:T(8,128)(2,1)} %pad_maximum_fusion.1.grad_ref, bf16[512,512]{1,0:T(8,128)(2,1)} %bitcast.307, bf16[512,4096]{1,0:T(8,128)(2,1)} %query_ref.3, bf16[512,512]{1,0:T(8,128)(2,1)} %key_ref.3, bf16[512,512]{1,0:T(8,128)(2,1)} %value_ref.3), custom_call_target="tpu_custom_call" | custom-call | tf_op jit(solution)/shard_map/pallas_call | solution.py:1264
  623.4 6.8 convolution_convert_fusion.2
  630.2 317.5 %shard_map.269 = (bf16[2,4,256,1280]{3,2,1,0:T(8,128)(2,1)}, bf16[2,4,128,2048]{3,2,1,0:T(8,128)(2,1)}, f32[144,128]{1,0:T(8,128)}) custom-call(bf16[2,4,256,1280]{3,2,1,0:T(8,128)(2,1)} %bitcast.296, bf16[2,4,128,2048]{3,2,1,0:T(8,128)(2,1)} %bitcast.298, f32[4,144,128]{2,1,0:T(8,128)} %bitcast.301), custom_call_target="tpu_custom_call" | custom-call | tf_op jit(solution)/shard_map/pallas_call | solution.py:787
  949.4 3.4 convert.29
  954.1 4.3 copy.256
  964.1 5.5 bitcast_convert_fusion
  969.6 9.3 fusion.3
  978.9 9.1 convolution_bitcast_fusion.1
  988.1 9.0 convolution_bitcast_fusion
  997.1 3.8 fusion.31
  (291 shorter events, 118.2 us)
Async XLA Ops:
  8.0 163.7 %copy-start = (bf16[1,768,2048]{2,1,0:T(8,128)(2,1)S(1)}, bf16[1,768,2048]{2,1,0:T(8,128)(2,1)}, u32[]{:S(2)}) copy-start(bf16[1,768,2048]{2,1,0:T(8,128)(2,1)} %param.30) | copy-start | bytes 9437188
  8.0 105.8 %all-reduce.8.cloned.1.call-start = ((), (), s32[]{:S(2)}) async-start(), calls=%async_computation.3 | async-start | bytes 282624
  15.3 145.1 %all-gather.3.cloned.1.call-start = ((), (), s32[]{:S(2)}) async-start(), calls=%async_computation.1 | async-start | bytes 17301504 | tf_op jit(solution)/shard_map/all_gather | solution.py:1292
  15.8 981.3 %reduce-scatter.2.cloned.1.call-start = ((), (), s32[]{:S(2)}) async-start(), calls=%async_computation.2 | async-start | bytes 17301504 | tf_op jit(solution)/shard_map/reduce_scatter | solution.py:1328
  92.8 18.6 %copy-start.46 = (pred[32,128]{1,0:T(8,128)(4,1)}, pred[32,128]{1,0:T(8,128)(4,1)S(1)}, u32[]{:S(2)}) copy-start(pred[32,128]{1,0:T(8,128)(4,1)S(1)} %compare_reduce_fusion) | copy-start | bytes 12292
  109.0 12.1 %copy-start.52 = (f32[4,128]{1,0:T(4,128)}, f32[4,128]{1,0:T(4,128)S(1)}, u32[]{:S(2)}) copy-start(f32[4,128]{1,0:T(4,128)S(1)} %add_rsqrt_fusion.1) | copy-start | bytes 6148
  115.2 6.1 copy-start.61
  429.0 8.8 copy-start.47
  446.4 6.4 copy-start.17
  459.0 10.6 %copy-start.20 = (f32[128,2048]{1,0:T(8,128)}, f32[128,2048]{1,0:T(8,128)S(1)}, u32[]{:S(2)}) copy-start(f32[128,2048]{1,0:T(8,128)S(1)} %get-tuple-element.194) | copy-start | bytes 3145732
  459.0 8.7 copy-start.24
  469.5 35.3 %copy-start.44 = (f32[4,8,128]{2,1,0:T(8,128)S(1)}, f32[4,8,128]{2,1,0:T(8,128)}, u32[]{:S(2)}) copy-start(f32[4,8,128]{2,1,0:T(8,128)} %copy-done.43) | copy-start | bytes 49156
  469.5 35.3 %copy-start.49 = (f32[4,8,128]{2,1,0:T(8,128)S(1)}, f32[4,8,128]{2,1,0:T(8,128)}, u32[]{:S(2)}) copy-start(f32[4,8,128]{2,1,0:T(8,128)} %copy-done.48) | copy-start | bytes 49156
  621.9 8.4 copy-start.19
  958.5 11.1 %slice-start = ((s8[8388608]{0:T(1024)(128)(4,1)}), s8[4194304]{0:T(1024)(128)(4,1)S(1)}, s32[]{:S(2)}) async-start(s8[8388608]{0:T(1024)(128)(4,1)} %bitcast.278), calls=%async_computation.4 | async-start | bytes 8388608
  959.6 9.9 copy-start.76
  964.1 14.8 %slice-start.2 = ((s8[8388608]{0:T(1024)(128)(4,1)}), s8[4194304]{0:T(1024)(128)(4,1)S(1)}, s32[]{:S(2)}) async-start(s8[8388608]{0:T(1024)(128)(4,1)} %bitcast.322), calls=%async_computation.6 | async-start | bytes 8388608
  969.6 9.3 copy-start.29
  969.6 9.3 slice-start.3
  978.9 9.2 copy-start.28
  988.1 9.0 copy-start.51
  988.1 9.0 copy-start.70
  988.1 9.0 copy-start.75
  988.1 12.8 %copy-start.1 = (bf16[1,768,2048]{2,1,0:T(8,128)(2,1)S(1)}, bf16[1,768,2048]{2,1,0:T(8,128)(2,1)}, u32[]{:S(2)}) copy-start(bf16[1,768,2048]{2,1,0:T(8,128)(2,1)} %param.30) | copy-start | bytes 9437188
  (60 other events, 145.8 us)
Sparse Core Ops, SparseCore 0:
  15.4 32.9 all-reduce.7
Sparse Core Ops, SparseCore 1:
  19.0 133.6 all-gather.2
  445.8 229.0 reduce-scatter.1

commit v4 on v3

--- a/solution.py
+++ b/solution.py
@@ -1,3 +1,4 @@
+import functools
 import math
 
 import jax
@@ -138,6 +139,10 @@
     return z * 8 + y * 4 + x * 2 + c
 
 
+def along_z(z, q):
+    return (z // 2 + q // 2) % 2 * 2 + (z % 2 + q % 2) % 2
+
+
 def greet(peers):
     barrier = pltpu.get_barrier_semaphore()
     for peer in peers:
@@ -173,10 +178,10 @@
 def gather_kernel(
     x_ref,
     select_ref,
-    ahead_ref,
+    ahead_hbm,
     named_ref,
-    gate_ref,
-    up_ref,
+    gate_hbm,
+    up_hbm,
     router_ref,
     rows_out,
     active_out,
@@ -185,7 +190,13 @@
     share_out,
     extra_out,
     held,
+    ahead_ref,
+    gate_ref,
+    up_ref,
     picked,
+    results,
+    loaded,
+    stored,
     arrive,
     to_z,
     to_y,
@@ -200,8 +211,16 @@
         where_is(z, y, 1 - x, c),
         where_is(z, y, x, 1 - c),
     )
-    z_peers = [where_is((z + k) % 4, y, x, c) for k in range(1, 4)]
-    greet([y_peer, x_peer, core_peer] + z_peers)
+    near_z, far_z = where_is(along_z(z, 1), y, x, c), where_is(along_z(z, 2), y, x, c)
+    loads = [
+        pltpu.make_async_copy(source, target, loaded.at[i])
+        for i, (source, target) in enumerate(
+            ((gate_hbm, gate_ref), (up_hbm, up_ref), (ahead_hbm, ahead_ref))
+        )
+    ]
+    for load in loads:
+        load.start()
+    greet([y_peer, x_peer, core_peer, near_z, far_z])
     mine = number(z, y, x, c)
 
     def copy(block, part, sem, peer):
@@ -211,28 +230,41 @@
     def arrived(block, part):
         copy(block, part, to_core.at[0, 0, 0], core_peer).wait_recv()
 
-    def block_of(group, k):
-        other_y, other_x, other_core = group
+    def block_of(q, other_y, other_x, core):
         return number(
-            (z + k) % 4,
-            1 - y if other_y else y,
-            1 - x if other_x else x,
-            1 - c if other_core else c,
-        )
-
-    def work(group):
-        blocks = [block_of(group, k) for k in range(4)]
-
-        @pl.loop(0, 4)
-        def _(k):
-            block = block_of(group, k)
+            along_z(z, q), 1 - y if other_y else y, 1 - x if other_x else x, core
+        )
+
+    combos = ((0, 0), (0, 1), (1, 0), (1, 1))
+
+    def stores(turn, blocks):
+        slot = turn % 2
+        made = []
+        for k in range(4):
+            part = pl.ds(k * kept, kept)
+            made.append((picked.at[slot, part], rows_out.at[blocks[k]]))
+            for i, out in enumerate((active_out, gate_out, up_out)):
+                made.append((results.at[slot, i, part], out.at[blocks[k]]))
+        return [
+            pltpu.make_async_copy(source, target, stored.at[slot, i])
+            for i, (source, target) in enumerate(made)
+        ]
+
+    def blocks_of(turn):
+        q, other = turn // 2, turn % 2
+        return [block_of(q, *combo, 1 - c if other else c) for combo in combos]
+
+    def work(turn):
+        blocks, slot = blocks_of(turn), turn % 2
+        if turn >= 2:
+            for store in stores(turn - 2, blocks_of(turn - 2)):
+                store.wait()
+        for k in range(4):
             rows = jnp.dot(
-                select_ref[block], held[block], preferred_element_type=jnp.float32
-            ).astype(picked.dtype)
-            picked[pl.ds(k * kept, kept)] = rows
-            rows_out[block] = rows
-
-        rows = picked[...]
+                select_ref[blocks[k]], held[blocks[k]], preferred_element_type=jnp.float32
+            )
+            picked[slot, k * kept : (k + 1) * kept] = rows.astype(picked.dtype)
+        rows = picked[slot]
         gate_pre = jnp.dot(rows, gate_ref[...], preferred_element_type=jnp.float32)
         up_pre = jnp.dot(rows, up_ref[...], preferred_element_type=jnp.float32)
         logits = jnp.dot(rows, router_ref[...], preferred_element_type=jnp.float32)
@@ -247,113 +279,111 @@
             gate, up, ahead = gate_pre[part], up_pre[part], ahead_ref[block]
             sigma = 1.0 / (1.0 + jnp.exp(-gate))
             silu = gate * sigma
-            active = silu * up
-            active_low = active.astype(active_out.dtype)
+            active_low = (silu * up).astype(results.dtype)
             grad = jnp.sum(active_low.astype(jnp.float32) * ahead, axis=1, keepdims=True)
             active_grad = share * ahead
-            active_out[block] = active_low
-            gate_out[block] = (active_grad * up * (sigma * (1.0 + gate * (1.0 - sigma)))).astype(
-                gate_out.dtype
-            )
-            up_out[block] = (active_grad * silu).astype(up_out.dtype)
+            gate_grad = active_grad * up * (sigma * (1.0 + gate * (1.0 - sigma)))
+            results[slot, 0, part] = active_low
+            results[slot, 1, part] = gate_grad.astype(results.dtype)
+            results[slot, 2, part] = (active_grad * silu).astype(results.dtype)
             share_out[block] = jnp.broadcast_to(share, share_out.shape[1:])
             high = grad.astype(extra_out.dtype).astype(jnp.float32)
-            both = jnp.where(
-                lanes == mine, high, jnp.where(lanes == 32 + mine, grad - high, 0.0)
-            )
+            both = jnp.where(lanes == mine, high, jnp.where(lanes == 32 + mine, grad - high, 0.0))
             extra_out[block] = both.astype(extra_out.dtype)
-
-    held[mine] = x_ref[...]
-    for k in range(1, 4):
-        for part in range(2):
-            copy(mine, part, to_z.at[k - 1, part], z_peers[k - 1]).start()
-
-    def forward_first(k):
-        block = block_of((0, 0, 0), k)
-        copy(block, 0, to_y.at[0, k], y_peer).start()
-        copy(block, 1, to_x.at[0, k], x_peer).start()
-        copy(block, 0, to_x.at[1, k], x_peer).start()
-        copy(block, 1, to_y.at[1, k], y_peer).start()
-        copy(block, 0, to_core.at[0, 0, k], core_peer).start()
-        copy(block, 1, to_core.at[0, 1, k], core_peer).start()
-
-    forward_first(0)
-
-    @pl.loop(1, 4)
-    def _(k):
-        block = block_of((0, 0, 0), k)
-        arrived(block, 0)
-        arrived(block, 1)
-        forward_first(k)
-
-    work((0, 0, 0))
-
-    @pl.loop(0, 4)
-    def _(k):
-        block = block_of((1, 0, 0), k)
-        arrived(block, 0)
-        copy(block, 0, to_x.at[2, k], x_peer).start()
-        copy(block, 0, to_core.at[1, 0, k], core_peer).start()
-        block = block_of((0, 1, 0), k)
-        arrived(block, 1)
-        copy(block, 1, to_y.at[2, k], y_peer).start()
-        copy(block, 1, to_core.at[2, 1, k], core_peer).start()
-        block = block_of((0, 0, 1), k)
-        arrived(block, 0)
-        arrived(block, 1)
-
-    work((0, 0, 1))
-
-    @pl.loop(0, 4)
-    def _(k):
-        block = block_of((0, 1, 0), k)
-        arrived(block, 0)
-        copy(block, 0, to_core.at[2, 0, k], core_peer).start()
-        block = block_of((1, 0, 0), k)
-        arrived(block, 1)
-        copy(block, 1, to_core.at[1, 1, k], core_peer).start()
-
-    work((0, 1, 0))
-    work((1, 0, 0))
-    for group in ((0, 1, 1), (1, 0, 1)):
-
-        @pl.loop(0, 4)
-        def _(k):
-            block = block_of(group, k)
+        for store in stores(turn, blocks):
+            store.start()
+
+    def forward(q):
+        block = block_of(q, 0, 0, c)
+        if q:
             arrived(block, 0)
             arrived(block, 1)
-
-        work(group)
+        if q == 2:
+            copy(block, 0, to_z.at[2, 0], near_z).start()
+            copy(block, 1, to_z.at[2, 1], near_z).start()
+        copy(block, 0, to_y.at[0, q], y_peer).start()
+        copy(block, 1, to_x.at[0, q], x_peer).start()
+        copy(block, 0, to_x.at[1, q], x_peer).start()
+        copy(block, 1, to_y.at[1, q], y_peer).start()
+        copy(block, 0, to_core.at[0, 0, q], core_peer).start()
+        copy(block, 1, to_core.at[0, 1, q], core_peer).start()
+
+    def second(q):
+        block = block_of(q, 1, 0, c)
+        arrived(block, 0)
+        copy(block, 0, to_x.at[2, q], x_peer).start()
+        copy(block, 0, to_core.at[1, 0, q], core_peer).start()
+        block = block_of(q, 0, 1, c)
+        arrived(block, 1)
+        copy(block, 1, to_y.at[2, q], y_peer).start()
+        copy(block, 1, to_core.at[2, 1, q], core_peer).start()
+
+    def last(q):
+        block = block_of(q, 0, 1, c)
+        arrived(block, 0)
+        copy(block, 0, to_core.at[2, 0, q], core_peer).start()
+        block = block_of(q, 1, 0, c)
+        arrived(block, 1)
+        copy(block, 1, to_core.at[1, 1, q], core_peer).start()
+        block = block_of(q, 1, 1, c)
+        arrived(block, 0)
+        copy(block, 0, to_core.at[3, 0, q], core_peer).start()
+        arrived(block, 1)
+        copy(block, 1, to_core.at[3, 1, q], core_peer).start()
+
+    def others(q):
+        for combo in combos:
+            block = block_of(q, *combo, 1 - c)
+            arrived(block, 0)
+            arrived(block, 1)
+
+    held[mine] = x_ref[...]
+    for part in range(2):
+        copy(mine, part, to_z.at[0, part], near_z).start()
+    for part in range(2):
+        copy(mine, part, to_z.at[1, part], far_z).start()
+    forward(0)
+    for load in loads:
+        load.wait()
+    forward(1)
+    second(0)
+    forward(2)
+    second(1)
+    last(0)
+    work(0)
+    others(0)
+    work(1)
+    forward(3)
+    second(2)
+    last(1)
+    work(2)
+    others(1)
+    work(3)
+    second(3)
+    last(2)
+    work(4)
+    others(2)
+    work(5)
+    last(3)
+    work(6)
+    others(3)
+    work(7)
+    for turn in (6, 7):
+        for store in stores(turn, blocks_of(turn)):
+            store.wait()
+    for part in range(2):
+        copy(mine, part, to_z.at[0, part], near_z).wait_send()
+        copy(mine, part, to_z.at[1, part], far_z).wait_send()
+        copy(mine, part, to_z.at[2, part], near_z).wait_send()
 
     @pl.loop(0, 4)
-    def _(k):
-        block = block_of((1, 1, 0), k)
-        arrived(block, 0)
-        copy(block, 0, to_core.at[3, 0, k], core_peer).start()
-        arrived(block, 1)
-        copy(block, 1, to_core.at[3, 1, k], core_peer).start()
-
-    work((1, 1, 0))
-
-    @pl.loop(0, 4)
-    def _(k):
-        block = block_of((1, 1, 1), k)
-        arrived(block, 0)
-        arrived(block, 1)
-
-    work((1, 1, 1))
-    for k in range(1, 4):
-        for part in range(2):
-            copy(mine, part, to_z.at[k - 1, part], z_peers[k - 1]).wait_send()
-
-    @pl.loop(0, 4)
-    def _(k):
+    def _(q):
         for i in range(3):
-            copy(mine, 0, to_y.at[i, k], y_peer).wait_send()
-            copy(mine, 0, to_x.at[i, k], x_peer).wait_send()
+            copy(mine, 0, to_y.at[i, q], y_peer).wait_send()
+            copy(mine, 0, to_x.at[i, q], x_peer).wait_send()
         for i in range(4):
             for part in range(2):
-                copy(mine, part, to_core.at[i, part, k], core_peer).wait_send()
+                copy(mine, part, to_core.at[i, part, q], core_peer).wait_send()
 
 
 def gather_experts(rows, select, ahead, named, gate_w, up_w, router):
@@ -361,6 +391,8 @@
     blocks, kept = select.shape[:2]
     hidden = gate_w.shape[1]
     low = rows.dtype
+    anywhere = pl.BlockSpec(memory_space=pl.ANY)
+    vmem = pl.BlockSpec(memory_space=pltpu.VMEM)
     return pl.pallas_call(
         gather_kernel,
         out_shape=[
@@ -371,11 +403,17 @@
             jax.ShapeDtypeStruct((blocks, kept, 128), jnp.float32),
             jax.ShapeDtypeStruct((blocks, kept, 128), low),
         ],
-        in_specs=in_vmem(7),
-        out_specs=in_vmem(6),
+        in_specs=[vmem, vmem, anywhere, vmem, anywhere, anywhere, vmem],
+        out_specs=[anywhere] * 4 + [vmem] * 2,
         scratch_shapes=[
             pltpu.VMEM((blocks, count, width), low),
-            pltpu.VMEM((4 * kept, width), low),
+            pltpu.VMEM(ahead.shape, ahead.dtype),
+            pltpu.VMEM(gate_w.shape, low),
+            pltpu.VMEM(up_w.shape, low),
+            pltpu.VMEM((2, 4 * kept, width), low),
+            pltpu.VMEM((2, 3, 4 * kept, hidden), low),
+            copies(3),
+            copies(2, 16),
             copies(blocks, 2),
             copies(3, 2),
             copies(3, 4),
@@ -387,30 +425,18 @@
 
 
 def scatter_kernel(
+    extended,
     spread_ref,
-    gate_grad_ref,
-    up_grad_ref,
-    gate_ref,
-    up_ref,
-    extra_ref,
-    out_ref,
-    extra_out,
-    outgoing,
-    core_in,
-    total,
-    back,
-    x_in,
-    y_in,
-    z_in,
-    core_sent,
-    core_got,
-    x_sent,
-    x_got,
-    y_sent,
-    y_got,
-    z_sent,
-    z_got,
+    *refs,
 ):
+    if extended:
+        gate_grad_ref, up_grad_ref, gate_ref, up_ref, extra_ref, out_ref, extra_out = refs[:7]
+        refs = refs[7:]
+    else:
+        active_ref, down_ref, share_ref, out_ref = refs[:4]
+        refs = refs[4:]
+    outgoing, core_in, total, back, x_in, y_in, z_in = refs[:7]
+    core_sent, core_got, x_sent, x_got, y_sent, y_got, z_sent, z_got = refs[7:]
     z, y, x, c = spot()
     width = out_ref.shape[1]
     half = out_ref.shape[0] // 2
@@ -420,166 +446,168 @@
         where_is(z, y, 1 - x, c),
         where_is(z, y, x, 1 - c),
     )
-    greet([y_peer, x_peer, core_peer] + [where_is((z + k) % 4, y, x, c) for k in range(1, 4)])
+    near_z, far_z = where_is(along_z(z, 1), y, x, c), where_is(along_z(z, 2), y, x, c)
+    greet([y_peer, x_peer, core_peer, near_z, far_z])
     groups = ((1, 1), (0, 1), (1, 0), (0, 0))
 
-    def block_of(group, k, core):
+    def block_of(group, q, core):
         other_y, other_x = groups[group]
-        return number((z + k) % 4, 1 - y if other_y else y, 1 - x if other_x else x, core)
-
-    def rows_back(group, core):
-        gate_grads = jnp.concatenate(
-            [gate_grad_ref[block_of(group, k, core)] for k in range(4)], axis=0
-        )
-        up_grads = jnp.concatenate(
-            [up_grad_ref[block_of(group, k, core)] for k in range(4)], axis=0
-        )
-        sums = right_transposed(gate_grads, gate_ref[...])
-        back[...] = (sums + right_transposed(up_grads, up_ref[...])).astype(back.dtype)
-
-    def part(block, k, place):
-        place[:, pl.ds(0, width)] = jnp.dot(
-            spread_ref[block], back[pl.ds(k * kept, kept)], preferred_element_type=jnp.float32
-        ).astype(place.dtype)
-        place[:, pl.ds(width, 128)] = jnp.dot(
-            spread_ref[block], extra_ref[block], preferred_element_type=jnp.float32
-        ).astype(place.dtype)
-
-    def across(group, k):
+        return number(along_z(z, q), 1 - y if other_y else y, 1 - x if other_x else x, core)
+
+    def rows_of(ref, q, core):
+        return jnp.concatenate([ref[block_of(group, q, core)] for group in range(4)], axis=0)
+
+    def rows_back(q, core):
+        if extended:
+            sums = right_transposed(rows_of(gate_grad_ref, q, core), gate_ref[...])
+            sums = sums + right_transposed(rows_of(up_grad_ref, q, core), up_ref[...])
+        else:
+            sums = jnp.dot(
+                rows_of(active_ref, q, core), down_ref[...], preferred_element_type=jnp.float32
+            )
+            sums = sums.astype(back.dtype).astype(jnp.float32)
+            sums = sums * rows_of(share_ref, q, core)[:, :1]
+        back[...] = sums.astype(back.dtype)
+
+    def part(block, group):
+        rows = jnp.dot(
+            spread_ref[block],
+            back[group * kept : (group + 1) * kept],
+            preferred_element_type=jnp.float32,
+        )
+        if not extended:
+            return rows
+        more = jnp.dot(spread_ref[block], extra_ref[block], preferred_element_type=jnp.float32)
+        return jnp.concatenate([rows, more], axis=1)
+
+    def across(group, q):
         return remote(
-            outgoing.at[group, k],
-            core_in.at[group, k],
-            core_sent.at[group, k],
-            core_got.at[group, k],
+            outgoing.at[q, group],
+            core_in.at[q, group],
+            core_sent.at[q, group],
+            core_got.at[q, group],
             core_peer,
         )
 
-    def view(group, k, side):
-        return total.at[group, k, pl.ds(side * half, half)]
-
-    def x_copy(group, k, side, slot):
+    def view(group, q, side):
+        return total.at[q, group, pl.ds(side * half, half)]
+
+    def x_copy(group, q, side, slot):
         return remote(
-            view(group, k, side), x_in.at[slot, k], x_sent.at[slot, k], x_got.at[slot, k], x_peer
-        )
-
-    def y_copy(group, k, side, slot):
+            view(group, q, side), x_in.at[slot, q], x_sent.at[slot, q], x_got.at[slot, q], x_peer
+        )
+
+    def y_copy(group, q, side, slot):
         return remote(
-            view(group, k, side), y_in.at[slot, k], y_sent.at[slot, k], y_got.at[slot, k], y_peer
-        )
-
-    def z_copy(k, side):
+            view(group, q, side), y_in.at[slot, q], y_sent.at[slot, q], y_got.at[slot, q], y_peer
+        )
+
+    def z_copy(q):
         return remote(
-            view(3, k, side),
-            z_in.at[k, side],
-            z_sent.at[k, side],
-            z_got.at[k, side],
-            where_is((z + k) % 4, y, x, c),
-        )
-
-    def add(group, k, side, source):
+            total.at[q, 3], z_in.at[q - 1], z_sent.at[q - 1], z_got.at[q - 1],
+            far_z if q == 2 else near_z,
+        )
+
+    def add(group, q, side, source):
         rows = pl.ds(side * half, half)
-        total[group, k, rows] = (
-            total[group, k, rows].astype(jnp.float32) + source.astype(jnp.float32)
+        total[q, group, rows] = (
+            total[q, group, rows].astype(jnp.float32) + source.astype(jnp.float32)
         ).astype(total.dtype)
 
-    for group in range(4):
-        rows_back(group, 1 - c)
-
-        @pl.loop(0, 4)
-        def _(i):
-            k = (i + 1) % 4
-            part(block_of(group, k, 1 - c), k, outgoing.at[group, k])
-            across(group, k).start()
-
-        rows_back(group, c)
-
-        @pl.loop(0, 4)
-        def _(i):
-            k = (i + 1) % 4
-            part(block_of(group, k, c), k, total.at[group, k])
-            across(group, k).wait_recv()
-            total[group, k] = (
-                total[group, k].astype(jnp.float32) + core_in[group, k].astype(jnp.float32)
-            ).astype(total.dtype)
+    def begin(q):
+        rows_back(q, 1 - c)
+        for group in range(4):
+            outgoing[q, group] = part(block_of(group, q, 1 - c), group).astype(total.dtype)
+            across(group, q).start()
+        rows_back(q, c)
+        for group in range(4):
+            sums = part(block_of(group, q, c), group)
+            across(group, q).wait_recv()
+            total[q, group] = (sums + core_in[q, group].astype(jnp.float32)).astype(total.dtype)
             if group == 0:
-                x_copy(0, k, 0, 0).start()
-                y_copy(0, k, 1, 0).start()
+                x_copy(0, q, 0, 0).start()
+                y_copy(0, q, 1, 0).start()
             if group == 1:
-                x_copy(1, k, 0, 1).start()
+                x_copy(1, q, 0, 1).start()
             if group == 2:
-                y_copy(2, k, 1, 1).start()
+                y_copy(2, q, 1, 1).start()
+
+    def middle(q):
+        x_copy(0, q, 0, 0).wait_recv()
+        add(2, q, 0, x_in[0, q])
+        y_copy(2, q, 0, 2).start()
+        y_copy(0, q, 1, 0).wait_recv()
+        add(1, q, 1, y_in[0, q])
+        x_copy(1, q, 1, 2).start()
+
+    def close(q):
+        for side, arrivals in ((0, ((x_copy(1, q, 0, 1), x_in, 1), (y_copy(2, q, 0, 2), y_in, 2))),
+                               (1, ((y_copy(2, q, 1, 1), y_in, 1), (x_copy(1, q, 1, 2), x_in, 2)))):
+            for arrival, _, _ in arrivals:
+                arrival.wait_recv()
+            rows = pl.ds(side * half, half)
+            sums = total[q, 3, rows].astype(jnp.float32)
+            for _, source, slot in arrivals:
+                sums = sums + source[slot, q].astype(jnp.float32)
+            if q == 2:
+                if side == 0:
+                    z_copy(3).wait_recv()
+                sums = sums + z_in[2, rows].astype(jnp.float32)
+            if q:
+                total[q, 3, rows] = sums.astype(total.dtype)
+            else:
+                if side == 0:
+                    z_copy(1).wait_recv()
+                    z_copy(2).wait_recv()
+                for i in range(2):
+                    sums = sums + z_in[i, rows].astype(jnp.float32)
+                out_ref[rows] = sums[:, :width]
+                if extended:
+                    extra_out[rows] = sums[:, width:]
+        if q:
+            z_copy(q).start()
+
+    begin(3)
+    begin(2)
+    middle(3)
+    begin(1)
+    middle(2)
+    close(3)
+    begin(0)
+    middle(1)
+    close(2)
+    middle(0)
+    close(1)
+    close(0)
+    for q in range(1, 4):
+        z_copy(q).wait_send()
 
     @pl.loop(0, 4)
-    def _(i):
-        k = (i + 1) % 4
-        x_copy(0, k, 0, 0).wait_recv()
-        add(2, k, 0, x_in[0, k])
-        y_copy(2, k, 0, 2).start()
-        y_copy(0, k, 1, 0).wait_recv()
-        add(1, k, 1, y_in[0, k])
-        x_copy(1, k, 1, 2).start()
-
-    @pl.loop(0, 4)
-    def _(i):
-        k = (i + 1) % 4
-        x_copy(1, k, 0, 1).wait_recv()
-        add(3, k, 0, x_in[1, k])
-        y_copy(2, k, 1, 1).wait_recv()
-        add(3, k, 1, y_in[1, k])
-
-    @pl.loop(0, 4)
-    def _(i):
-        k = (i + 1) % 4
-        y_copy(2, k, 0, 2).wait_recv()
-        add(3, k, 0, y_in[2, k])
-        x_copy(1, k, 1, 2).wait_recv()
-        add(3, k, 1, x_in[2, k])
-
-        @pl.when(i < 3)
-        def _():
-            z_copy(k, 0).start()
-            z_copy(k, 1).start()
-
-    for k in range(1, 4):
-        for side in range(2):
-            z_copy(k, side).wait_recv()
-    for side in range(2):
-        rows = pl.ds(side * half, half)
-        sums = total[3, 0, rows].astype(jnp.float32)
-        for k in range(1, 4):
-            sums = sums + z_in[k, side].astype(jnp.float32)
-        out_ref[rows] = sums[:, :width]
-        extra_out[rows] = sums[:, width:]
-
-    for k in range(1, 4):
-        for side in range(2):
-            z_copy(k, side).wait_send()
-
-    @pl.loop(0, 4)
-    def _(k):
+    def _(q):
         for group in range(4):
-            across(group, k).wait_send()
-        x_copy(0, k, 0, 0).wait_send()
-        x_copy(1, k, 0, 1).wait_send()
-        x_copy(1, k, 1, 2).wait_send()
-        y_copy(0, k, 1, 0).wait_send()
-        y_copy(2, k, 1, 1).wait_send()
-        y_copy(2, k, 0, 2).wait_send()
-
-
-def scatter_experts(spread, gate_grad, up_grad, gate_w, up_w, extra):
+            across(group, q).wait_send()
+        x_copy(0, q, 0, 0).wait_send()
+        x_copy(1, q, 0, 1).wait_send()
+        x_copy(1, q, 1, 2).wait_send()
+        y_copy(0, q, 1, 0).wait_send()
+        y_copy(2, q, 1, 1).wait_send()
+        y_copy(2, q, 0, 2).wait_send()
+
+
+def scatter_rows(spread, *operands):
     blocks, count, kept = spread.shape
-    width = gate_w.shape[0]
-    wide = width + 128
-    low = gate_grad.dtype
+    extended = len(operands) == 5
+    width = operands[2].shape[0] if extended else operands[1].shape[1]
+    wide = width + 128 if extended else width
+    low = operands[0].dtype
+    outs = [jax.ShapeDtypeStruct((count, width), jnp.float32)]
+    if extended:
+        outs.append(jax.ShapeDtypeStruct((count, 128), jnp.float32))
     return pl.pallas_call(
-        scatter_kernel,
-        out_shape=(
-            jax.ShapeDtypeStruct((count, width), jnp.float32),
-            jax.ShapeDtypeStruct((count, 128), jnp.float32),
-        ),
-        in_specs=in_vmem(6),
-        out_specs=tuple(in_vmem(2)),
+        functools.partial(scatter_kernel, extended),
+        out_shape=outs,
+        in_specs=in_vmem(1 + len(operands)),
+        out_specs=in_vmem(len(outs)),
         scratch_shapes=[
             pltpu.VMEM((4, 4, count, wide), low),
             pltpu.VMEM((4, 4, count, wide), low),
@@ -587,61 +615,53 @@
             pltpu.VMEM((4 * kept, width), low),
             pltpu.VMEM((3, 4, count // 2, wide), low),
             pltpu.VMEM((3, 4, count // 2, wide), low),
-            pltpu.VMEM((4, 2, count // 2, wide), low),
+            pltpu.VMEM((3, count, wide), low),
             copies(4, 4),
             copies(4, 4),
             copies(3, 4),
             copies(3, 4),
             copies(3, 4),
             copies(3, 4),
-            copies(4, 2),
-            copies(4, 2),
+            copies(3),
+            copies(3),
         ],
-        compiler_params=settings(2),
-    )(spread, gate_grad, up_grad, gate_w, up_w, extra)
+        compiler_params=settings(2 if extended else 8),
+    )(spread, *operands)
 
 
 def reduce_kernel(
-    first_ref,
-    second_ref,
+    cuts,
+    parts_ref,
     vector_ref,
-    first_out,
-    second_out,
+    sums_out,
     vector_out,
-    first_y,
-    second_y,
-    first_held,
-    second_held,
-    first_z,
-    second_z,
-    first_all,
-    second_all,
-    shard_in,
-    member_own,
-    member_in,
-    y_sent,
-    y_got,
-    z_sent,
-    z_got,
-    back_sent,
-    back_got,
-    side_sent,
-    side_got,
-    shard_sent,
-    shard_got,
-    member_sent,
-    member_got,
+    *refs,
 ):
     z, y, x, c = spot()
     member, shard = lax.axis_index("exp"), lax.axis_index("fsdp")
     y_peer = where_is(z, 1 - y, x, c)
+    near_z, far_z = where_is(along_z(z, 1), y, x, c), where_is(along_z(z, 2), y, x, c)
     members = [((member + j) % 8, shard) for j in range(8)]
     shards = [(member, (shard + j) % 4) for j in range(4)]
     greet(members[1:] + shards[1:])
-    arrays = (
-        (first_ref, first_out, first_y, first_held, first_z, first_all),
-        (second_ref, second_out, second_y, second_held, second_z, second_all),
-    )
+    pieces = len(cuts)
+    first_got, first_held, first_z = refs[:3]
+    y_got_in, y_held, y_z = refs[3:5], refs[5:7], refs[7:9]
+    shard_in, member_own, member_in = refs[3 * pieces : 3 * pieces + 3]
+    (
+        y_sent,
+        y_got,
+        z_sent,
+        z_got,
+        back_sent,
+        back_got,
+        side_sent,
+        side_got,
+        shard_sent,
+        shard_got,
+        member_sent,
+        member_got,
+    ) = refs[3 * pieces + 3 :]
 
     def shard_copy(j):
         return remote(
@@ -661,48 +681,58 @@
             members[j],
         )
 
-    def y_copy(which, k):
-        source, _, target = arrays[which][:3]
+    def rows(which):
+        return pl.ds(*cuts[which])
+
+    def z_peer(q):
+        return far_z if q == 2 else near_z
+
+    def y_copy(which, q):
         return remote(
-            source.at[1 - y, (z + k) % 4],
-            target.at[k],
-            y_sent.at[which, k],
-            y_got.at[which, k],
+            parts_ref.at[1 - y, along_z(z, q), rows(which)],
+            y_got_in[which - 1].at[q],
+            y_sent.at[which, q],
+            y_got.at[which, q],
             y_peer,
         )
 
-    def z_copy(which, k):
+    def z_copy(which, q):
+        if which:
+            source, target = y_held[which - 1].at[q], y_z[which - 1].at[q]
+        elif q == 2:
+            source, target = first_held, first_z.at[2]
+        else:
+            source, target = parts_ref.at[:, along_z(z, q), rows(0)], first_z.at[q]
+        return remote(source, target, z_sent.at[which, q], z_got.at[which, q], z_peer(q))
+
+    def first_y():
         return remote(
-            arrays[which][3].at[k],
-            arrays[which][4].at[k],
-            z_sent.at[which, k],
-            z_got.at[which, k],
-            where_is((z + k) % 4, y, x, c),
-        )
-
-    def back_copy(which, k, slot):
-        every = arrays[which][5]
-        return remote(
-            every.at[0, 0],
-            every.at[0, slot],
-            back_sent.at[which, k],
-            back_got.at[which, slot],
-            where_is((z + k) % 4, y, x, c),
-        )
-
-    def side_copy(which, k):
-        every = arrays[which][5]
-        return remote(
-            every.at[0, k], every.at[1, k], side_sent.at[which, k], side_got.at[which, k], y_peer
-        )
-
+            first_z.at[0, 1 - y], first_got, y_sent.at[0, 0], y_got.at[0, 0], y_peer
+        )
+
+    def place(side, q, which):
+        return sums_out.at[side, along_z(z, q), rows(which)]
+
+    def back_copy(which, q):
+        held = along_z(z, 2) if q == 3 else z
+        if which:
+            view = sums_out.at[y, held, rows(which)]
+        else:
+            view = sums_out.at[:, held, rows(0)]
+        return remote(view, view, back_sent.at[which, q], back_got.at[which, q], z_peer(q))
+
+    def side_copy(which, q):
+        view = place(y, q, which)
+        return remote(view, view, side_sent.at[which, q], side_got.at[which, q], y_peer)
+
+    later = range(1, pieces)
     for j in range(1, 4):
         shard_copy(j).start()
-
-    @pl.loop(0, 4)
-    def _(i):
-        for which in range(2):
-            y_copy(which, (i + 1) % 4).start()
+    z_copy(0, 3).start()
+    for q in (3, 2, 1, 0):
+        for which in later:
+            y_copy(which, q).start()
+    z_copy(0, 1).start()
 
     for j in range(1, 4):
         shard_copy(j).wait_recv()
@@ -713,32 +743,54 @@
     for j in range(1, 8):
         member_copy(j).start()
 
-    @pl.loop(0, 4)
-    def _(i):
-        k = (i + 1) % 4
-        for which in range(2):
-            source, _, got, held = arrays[which][:4]
-            y_copy(which, k).wait_recv()
-            held[k] = (
-                source[y, (z + k) % 4].astype(jnp.float32) + got[k].astype(jnp.float32)
-            ).astype(held.dtype)
-
-            @pl.when(i < 3)
-            def _():
-                z_copy(which, k).start()
-
-    for which in range(2):
-        _, out, _, held, got, every = arrays[which]
-        for k in range(1, 4):
-            z_copy(which, k).wait_recv()
-        sums = held[0].astype(jnp.float32)
-        for k in range(1, 4):
-            sums = sums + got[k].astype(jnp.float32)
-        every[0, 0] = sums.astype(every.dtype)
-        for k in range(1, 4):
-            back_copy(which, k, (4 - k) % 4).start()
+    def add_y(which, q):
+        y_copy(which, q).wait_recv()
+        sums = parts_ref[y, along_z(z, q), rows(which)].astype(jnp.float32)
+        sums = sums + y_got_in[which - 1][q].astype(jnp.float32)
+        held, z_in = y_held[which - 1], y_z[which - 1]
+        if q == 2:
+            z_copy(which, 3).wait_recv()
+            sums = sums + z_in[3].astype(jnp.float32)
+        if q:
+            held[q] = sums.astype(held.dtype)
+            z_copy(which, q).start()
+            return
+        for turn in (1, 2):
+            z_copy(which, turn).wait_recv()
+            sums = sums + z_in[turn].astype(jnp.float32)
+        sums_out[y, z, rows(which)] = sums.astype(sums_out.dtype)
         side_copy(which, 0).start()
-        out[y, z] = every[0, 0]
+        back_copy(which, 2).start()
+        back_copy(which, 1).start()
+
+    for which in later:
+        add_y(which, 3)
+    z_copy(0, 3).wait_recv()
+    first_held[...] = (
+        parts_ref[:, along_z(z, 2), rows(0)].astype(jnp.float32) + first_z[3].astype(jnp.float32)
+    ).astype(first_held.dtype)
+    z_copy(0, 2).start()
+    for which in later:
+        add_y(which, 2)
+    z_copy(0, 1).wait_recv()
+    z_copy(0, 2).wait_recv()
+    first_z[0] = (
+        parts_ref[:, z, rows(0)].astype(jnp.float32)
+        + first_z[1].astype(jnp.float32)
+        + first_z[2].astype(jnp.float32)
+    ).astype(first_z.dtype)
+    first_y().start()
+    for which in later:
+        add_y(which, 1)
+    first_y().wait_recv()
+    sums = first_z[0, y].astype(jnp.float32) + first_got[...].astype(jnp.float32)
+    sums_out[y, z, rows(0)] = sums.astype(sums_out.dtype)
+    side_copy(0, 0).start()
+    for which in later:
+        add_y(which, 0)
+    side_copy(0, 0).wait_recv()
+    back_copy(0, 2).start()
+    back_copy(0, 1).start()
 
     for j in range(1, 8):
         member_copy(j).wait_recv()
@@ -747,70 +799,69 @@
         sums = sums + member_in[j]
     vector_out[...] = sums
 
-    @pl.loop(1, 4)
-    def _(k):
-        for which in range(2):
-            _, out, _, _, _, every = arrays[which]
-            back_copy(which, k, k).wait_recv()
-            side_copy(which, k).start()
-            out[y, (z + k) % 4] = every[0, k]
-
-    @pl.loop(0, 4)
-    def _(k):
-        for which in range(2):
-            _, out, _, _, _, every = arrays[which]
-            side_copy(which, k).wait_recv()
-            out[1 - y, (z + k) % 4] = every[1, k]
-
-    @pl.loop(0, 4)
-    def _(k):
-        for which in range(2):
-            y_copy(which, k).wait_send()
-            side_copy(which, k).wait_send()
-
-    for k in range(1, 4):
-        for which in range(2):
-            z_copy(which, k).wait_send()
-            back_copy(which, k, (4 - k) % 4).wait_send()
+    for q in (1, 2, 3):
+        for which in later:
+            back_copy(which, q).wait_recv()
+            if q == 2:
+                back_copy(which, 3).start()
+            side_copy(which, q).start()
+        back_copy(0, q).wait_recv()
+        if q == 2:
+            back_copy(0, 3).start()
+
+    for which in later:
+        for q in range(4):
+            side_copy(which, q).wait_recv()
+    for which in range(pieces):
+        for q in range(4):
+            if which:
+                y_copy(which, q).wait_send()
+                side_copy(which, q).wait_send()
+            if q:
+                z_copy(which, q).wait_send()
+                back_copy(which, q).wait_send()
+    side_copy(0, 0).wait_send()
+    first_y().wait_send()
     for j in range(1, 4):
         shard_copy(j).wait_send()
     for j in range(1, 8):
         member_copy(j).wait_send()
 
 
-def reduce_over_members(first, second, vectors):
-    low = first.dtype
-
-    def quarter(array, *lead):
-        return pltpu.VMEM((*lead, *array.shape[2:]), low)
+def reduce_over_members(parts, vectors):
+    low = parts.dtype
+    depth, width = parts.shape[2:]
+    early = depth * 3 // 16 // 16 * 16
+    half = (depth - early) // 2 // 16 * 16
+    cuts = ((0, early), (early, half), (early + half, depth - early - half))
+
+    def quarters(*lead):
+        return [pltpu.VMEM((*lead, size, width), low) for _, size in cuts[1:]]
 
     return pl.pallas_call(
-        reduce_kernel,
+        functools.partial(reduce_kernel, cuts),
         out_shape=[
-            jax.ShapeDtypeStruct(first.shape, low),
-            jax.ShapeDtypeStruct(second.shape, low),
+            jax.ShapeDtypeStruct(parts.shape, low),
             jax.ShapeDtypeStruct(vectors.shape[1:], vectors.dtype),
         ],
-        in_specs=in_vmem(3),
-        out_specs=in_vmem(3),
+        in_specs=in_vmem(2),
+        out_specs=in_vmem(2),
         scratch_shapes=[
-            quarter(first, 4),
-            quarter(second, 4),
-            quarter(first, 4),
-            quarter(second, 4),
-            quarter(first, 4),
-            quarter(second, 4),
-            quarter(first, 2, 4),
-            quarter(second, 2, 4),
+            pltpu.VMEM((early, width), low),
+            pltpu.VMEM((2, early, width), low),
+            pltpu.VMEM((4, 2, early, width), low),
+            *quarters(4),
+            *quarters(4),
+            *quarters(4),
             pltpu.VMEM(vectors.shape, vectors.dtype),
             pltpu.VMEM(vectors.shape[1:], vectors.dtype),
             pltpu.VMEM((8, *vectors.shape[1:]), vectors.dtype),
         ]
-        + [copies(2, 4)] * 8
+        + [copies(3, 4)] * 8
         + [copies(4)] * 2
         + [copies(8)] * 2,
         compiler_params=settings(3),
-    )(first, second, vectors)
+    )(parts, vectors)
 
 
 def project_kernel(
@@ -1310,22 +1361,15 @@
     arrived, active, gate_pre_grad, up_pre_grad, share, extra = gather_experts(
         normed, select, ahead, named_rows, gate_w, up_w, padded
     )
-    summed, back = scatter_experts(spread, gate_pre_grad, up_pre_grad, gate_w, up_w, extra)
-
-    summed, back, arrived, gate_pre_grad, up_pre_grad, active, share = lax.optimization_barrier(
-        (summed, back, arrived, gate_pre_grad, up_pre_grad, active, share)
-    )
+    summed, back = scatter_rows(spread, gate_pre_grad, up_pre_grad, gate_w, up_w, extra)
+    (mixed,) = scatter_rows(spread, active, down_w, share)
+    summed, back, mixed = lax.optimization_barrier((summed, back, mixed))
 
     def flat(rows):
         return rows.reshape(experts * capacity, rows.shape[2])
 
     share = flat(share)[:, :1]
     out_rows = (share * flat_grads.astype(jnp.float32)).astype(jnp.bfloat16)
-    produced = matrix_product(flat(active), down_w).astype(jnp.bfloat16)
-    weighted = (share * produced.astype(jnp.float32)).astype(jnp.bfloat16)
-    full = contract("bjc,bcd->bjd", spread, weighted.reshape(experts, capacity, MODEL_WIDTH))
-    full = full.astype(jnp.bfloat16).reshape(experts * token_count, MODEL_WIDTH)
-    mixed = lax.psum_scatter(full, BOTH, scatter_dimension=0, tiled=True)
     weight_grads = (
         left_trans(flat(arrived), flat(gate_pre_grad)),
         left_trans(flat(arrived), flat(up_pre_grad)),
@@ -1335,7 +1379,7 @@
     picks = jnp.any(routes[:, :, None] == columns[None, None, :], axis=1)
     gates = jax.nn.softmax(jnp.where(picks, matrix_product(normed, router), MASKED), axis=1)
     logit_grad = gates * (gate_grad - jnp.sum(gates * gate_grad, axis=1, keepdims=True))
-    return mixed.astype(jnp.float32), summed, logit_grad.astype(jnp.bfloat16), *weight_grads
+    return mixed, summed, logit_grad.astype(jnp.bfloat16), *weight_grads
 
 
 def moe_exchanged(normed, router, routes, capacity, cotangent, weights, notes):
@@ -1518,7 +1562,8 @@
     else:
         branch_grad = lax.all_gather(branch_low, "fsdp", axis=0, tiled=True)
         attended_grad = right_transposed(branch_grad, w_out).astype(jnp.bfloat16)
-    out_w_grad = left_trans(attended, branch_grad)
+    out_w_grad = left_trans(attended, branch_grad).astype(jnp.bfloat16)
+    attended_grad, out_w_grad = lax.optimization_barrier((attended_grad, out_w_grad))
     attended_grad = attended_grad.reshape(shards, token_count, kv_heads, head_group, HEAD_WIDTH)
     prob_grad = contract("bqkgd,bpkd->bkgqp", attended_grad, value)
     value_grad = contract("bkgqp,bqkgd->bpkd", probs_low, attended_grad)
@@ -1557,7 +1602,12 @@
         jnp.bfloat16
     )
 
-    out_w_grad = out_w_grad.astype(jnp.bfloat16)
+    if dense:
+        out_sum = lax.psum_scatter(out_w_grad, "exp", scatter_dimension=0, tiled=True)
+        joined_grad, out_sum = lax.optimization_barrier((joined_grad, out_sum))
+        out_sum = lax.all_gather(out_sum, "exp", axis=0, tiled=True)
+    else:
+        out_sum = lax.psum(out_w_grad, "exp")
     vectors = jnp.concatenate(
         [
             grad.reshape(shards, -1)
@@ -1566,17 +1616,17 @@
         axis=1,
     )
     if dense:
+        joined_grad, out_sum, gate_w_grad, up_w_grad, down_grad = lax.optimization_barrier(
+            (joined_grad, out_sum, gate_w_grad, up_w_grad, down_grad)
+        )
         rows = -(-vectors.shape[1] // 1024) * 8
         padded = jnp.pad(vectors, ((0, 0), (0, rows * 128 - vectors.shape[1])))
-        joined_sum, out_sum, vectors = reduce_over_members(
-            joined_grad.reshape(2, 4, -1, wide + 2 * narrow),
-            out_w_grad.reshape(2, 4, -1, MODEL_WIDTH),
-            padded.reshape(shards, rows, 128),
-        )
-        joined_sum, out_sum = joined_sum.reshape(joined_grad.shape), out_sum.reshape(w_out.shape)
-        vectors = vectors.reshape(-1)
+        joined_sum, vectors = reduce_over_members(
+            joined_grad.reshape(2, 4, -1, wide + 2 * narrow), padded.reshape(shards, rows, 128)
+        )
+        joined_sum, vectors = joined_sum.reshape(joined_grad.shape), vectors.reshape(-1)
     else:
-        out_sum, joined_sum = lax.psum(out_w_grad, "exp"), lax.psum(joined_grad, "exp")
+        joined_sum = lax.psum(joined_grad, "exp")
         vectors = lax.psum(vectors, BOTH)[place]
     out_sum, joined_sum = out_sum.astype(jnp.float32), joined_sum.astype(jnp.float32)
     sums, start = [], 0

time: 1020 us -> 853 us (0.84)
  Pallas kernels: 767 us -> 574 us
  waiting for transfers between devices: 0.58 us -> 53.4 us
  local copies, waits for them, and re-layouts: 81.9 us -> 69 us
    pallas_call x2 -> x3, Pallas kernels: 434 us -> 329 us  [the longest x2 202 us: scatter_rows(): pl.pallas_call(functools.partial(scatter_kernel, extended), out_shape=out...]
    all_gather x0 -> x1, waiting for transfers between devices: none -> 52.8 us  [local(): out_sum = lax.all_gather(out_sum, 'exp', axis=0, tiled=True)]
    pallas_call x1, Pallas kernels: 125 us -> 85.4 us  [gather_experts(): pl.pallas_call(gather_kernel, out_shape=[jax.ShapeDtypeStruct((blocks, ke...]
    pallas_call x1, Pallas kernels: 82.2 us -> 45.8 us  [heads_back(): pl.pallas_call(heads_kernel, out_shape=[jax.ShapeDtypeStruct((4, depth, o...]
    pallas_call x1, Pallas kernels: 32.6 us -> 21 us  [branch_back(): pl.pallas_call(branch_kernel, out_shape=[jax.ShapeDtypeStruct((4, count,...]
    dot_general x9 -> x8, matrix products: 29.3 us -> 22.1 us  [contract(): return jnp.einsum(spec, left, right, preferred_element_type=jnp.float32)]
    unnamed x179 -> x166, local copies, waits for them, and re-layouts: 28.1 us -> 22.4 us
  transfers between devices with their start and end apart: 3 -> 4, of which waited for: 0 -> 1; matrix products, arithmetic and copies ran while one was open for 16% -> 15% of each run, Pallas kernels for 52% -> 17%
where the time goes in v4:
time: 853 us; the launch traced here: 842 us
  Pallas kernels  574 us (67%)
  matrix products  78.6 us (9%)
  local copies, waits for them, and re-layouts  69 us (8%)
  waiting for transfers between devices  53.4 us (6%)
  other arithmetic  49.2 us (6%)
  between operations  17.1 us (2%)
    pallas_call x2, Pallas kernels, scatter_rows(): pl.pallas_call(functools.partial(scatter_kernel, extended), out_shape=out...  202 us
    pallas_call x1, Pallas kernels, reduce_over_members(): pl.pallas_call(functools.partial(reduce_kernel, cuts), out_shape=[jax.Sha...  127 us
    pallas_call x1, Pallas kernels, gather_experts(): pl.pallas_call(gather_kernel, out_shape=[jax.ShapeDtypeStruct((blocks, ke...  85.4 us
    pallas_call x1, Pallas kernels, project_tokens(): pl.pallas_call(project_kernel, out_shape=[jax.ShapeDtypeStruct((4, count,...  71.6 us
    all_gather x1, waiting for transfers between devices, local(): out_sum = lax.all_gather(out_sum, 'exp', axis=0, tiled=True)  52.8 us
    pallas_call x1, Pallas kernels, heads_back(): pl.pallas_call(heads_kernel, out_shape=[jax.ShapeDtypeStruct((4, depth, o...  45.8 us
    dot_general x5, matrix products, left_trans(): lax.dot_general(left, right, (((0,), (0,)), ((), ())), preferred_element_...  41.4 us
    unnamed x166, local copies, waits for them, and re-layouts  22.4 us
  transfers between devices with their start and end apart: 4, of which 1 were waited for; matrix products, arithmetic and copies ran while one was open for 15% of the time, Pallas kernels for 17%

profile of v4, /device:TPU:8, one launch (start us, length us, event | category | flops | bytes accessed | tf_op | source)
XLA Modules:
  0.0 841.9 jit_solution(18047241889401821555)
XLA Ops:
  11.0 2.8 concatenate.36
  18.3 71.6 %shard_map.263 = (f32[4,128,1280]{2,1,0:T(8,128)}, bf16[4,128,512]{2,1,0:T(8,128)(2,1)}, s32[32,16,128]{2,1,0:T(8,128)}) custom-call(bf16[128,2048]{1,0:T(8,128)(2,1)} %x_ref.3, s32[16,128]{1,0:T(8,128)} %pad.21.routes_ref, bf16[1,512]{1,0:T(2,128)(2,1)} %broadcast_in_dim.48.gain_ref, bf16[512,4096]{1,0:T(8,128)(2,1)} %query_ref.3, ...), custom_call_target="tpu_custom_call" | custom-call | tf_op jit(solution)/shard_map/pallas_call | solution.py:1041
  136.0 21.6 %shard_map.264 = (f32[128,2048]{1,0:T(8,128)}, bf16[128,2048]{1,0:T(8,128)(2,1)}) custom-call(bf16[4,128,1024]{2,1,0:T(8,128)(2,1)} %copy.240.attended_ref, bf16[1024,2048]{1,0:T(8,128)(2,1)} %weight_ref.3, bf16[128,2048]{1,0:T(8,128)(2,1)} %x_ref.3, f32[1,2048]{1,0:T(1,128)} %bitcast.300), custom_call_target="tpu_custom_call" | custom-call | tf_op jit(solution)/shard_map/pallas_call | solution.py:1131
  162.8 11.6 %convolution_convert_fusion = bf16[32,64,2048]{2,1,0:T(8,128)(2,1)} fusion(bf16[32,128,2048]{2,1,0:T(8,128)(2,1)} %bitcast.264, s32[32,128]{1,0:T(8,128)S(1)} %copy-done.39, pred[32,128]{1,0:T(8,128)(4,1)S(1)} %copy-done.48), kind=kOutput, calls=%fused_computation.4 | convolution fusion | flops 1078460416 | bytes 25186304 | tf_op jit(solution)/shard_map/bcj,bjd->bcd/dot_general | solution.py:41
  174.4 11.1 %fusion.4.ahead_hbm = f32[32,64,768]{2,1,0:T(8,128)} fusion(bf16[32,64,2048]{2,1,0:T(8,128)(2,1)} %convolution_convert_fusion, bf16[1,768,2048]{2,1,0:T(8,128)(2,1)S(1)} %copy-done.26), kind=kOutput, calls=%fused_computation.11 | convolution fusion | flops 6442450944 | bytes 17825792 | tf_op jit(solution)/shard_map/dot_general | solution.py:35
  185.5 85.4 %shard_map.265 = (bf16[32,64,2048]{2,1,0:T(8,128)(2,1)}, bf16[32,64,768]{2,1,0:T(8,128)(2,1)}, bf16[32,64,768]{2,1,0:T(8,128)(2,1)}, bf16[32,64,768]{2,1,0:T(8,1...) custom-call(bf16[128,2048]{1,0:T(8,128)(2,1)} %get-tuple-element.48.x_ref, ...), custom_call_target="tpu_custom_call" | custom-call | tf_op jit(solution)/shard_map/pallas_call | solution.py:396
  270.9 109.2 %shard_map.266 = (f32[128,2048]{1,0:T(8,128)}, f32[128,128]{1,0:T(8,128)}) custom-call(bf16[32,128,64]{2,1,0:T(8,128)(2,1)} %fusion.17.spread_ref, bf16[32,64,768]{2,1,0:T(8,128)(2,1)} %get-tuple-element.49.refs_0_, bf16[32,64,768]{2,1,0:T(8,128)(2,1)} %get-tuple-element.50.refs_1_, bf16[2048,768]{1,0:T(8,128)(2,1)} %bitcast.269, ...), custom_call_target="tpu_custom_call" | custom-call | tf_op jit(solution)/shard_map/pallas_call | solution.py:606
  380.1 92.9 %shard_map.267 = f32[128,2048]{1,0:T(8,128)} custom-call(bf16[32,128,64]{2,1,0:T(8,128)(2,1)} %fusion.17.spread_ref, bf16[32,64,768]{2,1,0:T(8,128)(2,1)} %get-tuple-element.54.refs_0_, bf16[768,2048]{1,0:T(8,128)(2,1)} %bitcast.285, f32[32,64,128]{2,1,0:T(8,128)} %get-tuple-element.55.refs_2_), custom_call_target="tpu_custom_call" | custom-call | tf_op jit(solution)/shard_map/pallas_call | solution.py:606
  479.9 21.0 %shard_map.268 = (bf16[4,128,1024]{2,1,0:T(8,128)(2,1)}, bf16[4,128,2048]{2,1,0:T(8,128)(2,1)}) custom-call(bf16[128,2048]{1,0:T(8,128)(2,1)} %fusion.78.branch_ref, bf16[1024,2048]{1,0:T(8,128)(2,1)} %weight_ref.3), custom_call_target="tpu_custom_call" | custom-call | tf_op jit(solution)/shard_map/pallas_call | solution.py:1192
  500.9 6.3 convolution_convert_fusion.1
  507.2 4.5 fusion.13
  513.0 2.9 fusion.33
  521.2 3.1 copy.212
  525.8 3.2 copy.210
  540.7 45.8 %shard_map.269 = (bf16[4,512,1280]{2,1,0:T(8,128)(2,1)}, bf16[4,128,512]{2,1,0:T(8,128)(2,1)}) custom-call(bf16[512,1280]{1,0:T(8,128)(2,1)} %pad_maximum_fusion.1.grad_ref, bf16[512,512]{1,0:T(8,128)(2,1)} %bitcast.291, bf16[512,4096]{1,0:T(8,128)(2,1)} %query_ref.3, bf16[512,512]{1,0:T(8,128)(2,1)} %key_ref.3, bf16[512,512]{1,0:T(8,128)(2,1)} %value_ref.3), custom_call_target="tpu_custom_call" | custom-call | tf_op jit(solution)/shard_map/pallas_call | solution.py:1315
  599.1 3.2 fusion.29
  602.3 11.5 %fusion.3 = f32[768,2048]{1,0:T(8,128)} fusion(bf16[32,64,768]{2,1,0:T(8,128)(2,1)S(1)} %copy-done.27, bf16[32,64,2048]{2,1,0:T(8,128)(2,1)} %convolution_convert_fusion, f32[32,64]{1,0:T(8,128)S(1)} %mul.473), kind=kOutput, calls=%fused_computation.7 | convolution fusion | flops 6455033856 | bytes 17833984 | tf_op jit(solution)/shard_map/dot_general | solution.py:29
  613.8 11.0 %convolution_bitcast_fusion.1 = f32[2048,768]{1,0:T(8,128)} fusion(bf16[32,64,2048]{2,1,0:T(8,128)(2,1)} %get-tuple-element.68, bf16[32,64,768]{2,1,0:T(8,128)(2,1)S(1)} %copy-done.25), kind=kOutput, calls=%fused_computation.9 | convolution fusion | flops 6442450944 | bytes 17825792 | tf_op jit(solution)/shard_map/dot_general | solution.py:29
  624.8 11.3 %convolution_bitcast_fusion = f32[2048,768]{1,0:T(8,128)} fusion(bf16[32,64,2048]{2,1,0:T(8,128)(2,1)} %get-tuple-element.68, bf16[32,64,768]{2,1,0:T(8,128)(2,1)S(1)} %copy-done.24), kind=kOutput, calls=%fused_computation.8 | convolution fusion | flops 6442450944 | bytes 17825792 | tf_op jit(solution)/shard_map/dot_general | solution.py:29
  636.1 52.8 %all-gather.6.cloned.1.call-done = bf16[1024,2048]{1,0:T(8,128)(2,1)} async-done(((bf16[128,2048]{1,0:T(8,128)(2,1)}), bf16[1024,2048]{1,0:T(8,128)(2,1)}) %all-gather.6.cloned.1.call-update) | async-done | bytes 4194320 | tf_op jit(solution)/shard_map/all_gather | solution.py:1608
  688.9 126.9 %shard_map.270 = (bf16[2,4,256,1280]{3,2,1,0:T(8,128)(2,1)}, f32[144,128]{1,0:T(8,128)}) custom-call(bf16[2,4,256,1280]{3,2,1,0:T(8,128)(2,1)} %bitcast.280, f32[4,144,128]{2,1,0:T(8,128)} %bitcast.286), custom_call_target="tpu_custom_call" | custom-call | tf_op jit(solution)/shard_map/pallas_call | solution.py:841
  815.9 3.4 convert.28
  822.0 4.2 copy.249
  829.2 4.4 convert_element_type.200
  (278 shorter events, 103.0 us)
Async XLA Ops:
  8.0 102.1 %all-reduce.8.cloned.1.call-start = ((), (), s32[]{:S(2)}) async-start(), calls=%async_computation.4 | async-start | bytes 282624
  15.1 147.7 %all-gather.4.cloned.1.call-start = ((), (), s32[]{:S(2)}) async-start(), calls=%async_computation.1 | async-start | bytes 17301504 | tf_op jit(solution)/shard_map/all_gather | solution.py:1343
  15.7 598.1 %reduce-scatter.2.cloned.1.call-start = ((), (), s32[]{:S(2)}) async-start(), calls=%async_computation.2 | async-start | bytes 4718592 | tf_op jit(solution)/shard_map/reduce_scatter | solution.py:1606
  97.9 7.9 copy-start.6
  98.2 9.5 %copy-start.47 = (pred[32,128]{1,0:T(8,128)(4,1)}, pred[32,128]{1,0:T(8,128)(4,1)S(1)}, u32[]{:S(2)}) copy-start(pred[32,128]{1,0:T(8,128)(4,1)S(1)} %compare_reduce_fusion) | copy-start | bytes 12292
  99.7 8.1 copy-start.38
  104.6 8.9 %copy-start.68 = (f32[128]{0:T(128)}, f32[128]{0:T(128)S(1)}, u32[]{:S(2)}) copy-start(f32[128]{0:T(128)S(1)} %fusion.75) | copy-start | bytes 1540
  106.5 9.6 %copy-start.49 = (f32[4,128]{1,0:T(4,128)}, f32[4,128]{1,0:T(4,128)S(1)}, u32[]{:S(2)}) copy-start(f32[4,128]{1,0:T(4,128)S(1)} %add_rsqrt_fusion.1) | copy-start | bytes 6148
  106.5 9.6 %copy-start.54 = (f32[4,128]{1,0:T(4,128)}, f32[4,128]{1,0:T(4,128)S(1)}, u32[]{:S(2)}) copy-start(f32[4,128]{1,0:T(4,128)S(1)} %subtract_convert_fusion) | copy-start | bytes 6148
  124.4 8.8 %copy-start.12 = (bf16[4,128,8,128]{3,1,2,0:T(8,128)(2,1)S(1)}, bf16[4,128,8,128]{3,1,2,0:T(8,128)(2,1)}, u32[]{:S(2)}) copy-start(bf16[4,128,8,128]{3,1,2,0:T(8,128)(2,1)} %convolution_convert_fusion.2) | copy-start | bytes 3145732
  136.0 21.7 %copy-start.16 = (bf16[2048,32]{1,0:T(8,128)(2,1)S(1)}, bf16[2048,32]{1,0:T(8,128)(2,1)}, u32[]{:S(2)}) copy-start(bf16[2048,32]{1,0:T(8,128)(2,1)} %reshape.388) | copy-start | bytes 393220
  136.0 21.7 %copy-start.53 = (pred[128,32]{1,0:T(32,128)(4,1)S(1)}, pred[128,32]{1,0:T(32,128)(4,1)}, u32[]{:S(2)}) copy-start(pred[128,32]{1,0:T(32,128)(4,1)} %copy.203) | copy-start | bytes 12292
  159.1 15.3 %copy-start.32 = (f32[128,32]{1,0:T(8,128)}, f32[128,32]{1,0:T(8,128)S(1)}, u32[]{:S(2)}) copy-start(f32[128,32]{1,0:T(8,128)S(1)} %get-tuple-element.199) | copy-start | bytes 49156
  162.7 11.7 %copy-start.26 = (bf16[1,768,2048]{2,1,0:T(8,128)(2,1)S(1)}, bf16[1,768,2048]{2,1,0:T(8,128)(2,1)}, u32[]{:S(2)}) copy-start(bf16[1,768,2048]{2,1,0:T(8,128)(2,1)} %param.30) | copy-start | bytes 9437188
  380.1 93.0 %copy-start.65 = (f32[128]{0:T(128)S(1)}, f32[128]{0:T(128)}, u32[]{:S(2)}) copy-start(f32[128]{0:T(128)} %copy-done.64) | copy-start | bytes 1540
  380.1 93.0 %copy-start.70 = (f32[128]{0:T(128)S(1)}, f32[128]{0:T(128)}, u32[]{:S(2)}) copy-start(f32[128]{0:T(128)} %fusion.65) | copy-start | bytes 1540
  380.1 95.2 %copy-start.5 = (f32[128,2048]{1,0:T(8,128)S(1)}, f32[128,2048]{1,0:T(8,128)}, u32[]{:S(2)}) copy-start(f32[128,2048]{1,0:T(8,128)} %get-tuple-element.47) | copy-start | bytes 3145732
  380.1 95.2 %copy-start.17 = (bf16[2048,32]{1,0:T(8,128)(2,1)S(1)}, bf16[2048,32]{1,0:T(8,128)(2,1)}, u32[]{:S(2)}) copy-start(bf16[2048,32]{1,0:T(8,128)(2,1)} %reshape.388) | copy-start | bytes 393220
  380.1 95.2 %copy-start.45 = (f32[1,4,4,128]{3,1,2,0:T(4,128)S(1)}, f32[1,4,4,128]{3,1,2,0:T(4,128)}, u32[]{:S(2)}) copy-start(f32[1,4,4,128]{3,1,2,0:T(4,128)} %copy.254) | copy-start | bytes 24580
  380.1 95.2 %copy-start.66 = (f32[128]{0:T(128)S(1)}, f32[128]{0:T(128)}, u32[]{:S(2)}) copy-start(f32[128]{0:T(128)} %get-tuple-element.208) | copy-start | bytes 1540
  477.7 23.1 %copy-start.72 = (f32[128]{0:T(128)}, f32[128]{0:T(128)S(1)}, u32[]{:S(2)}) copy-start(f32[128]{0:T(128)S(1)} %broadcast_multiply_fusion.3) | copy-start | bytes 1540
  512.9 176.0 %all-gather.6.cloned.1.call-start = ((), (), s32[]{:S(2)}) async-start(), calls=%async_computation.3 | async-start | bytes 4718592 | tf_op jit(solution)/shard_map/all_gather | solution.py:1608
  602.3 11.5 %copy-start.25 = (bf16[32,64,768]{2,1,0:T(8,128)(2,1)S(1)}, bf16[32,64,768]{2,1,0:T(8,128)(2,1)}, u32[]{:S(2)}) copy-start(bf16[32,64,768]{2,1,0:T(8,128)(2,1)} %get-tuple-element.49.refs_0_) | copy-start | bytes 9437188
  613.8 11.0 %copy-start.24 = (bf16[32,64,768]{2,1,0:T(8,128)(2,1)S(1)}, bf16[32,64,768]{2,1,0:T(8,128)(2,1)}, u32[]{:S(2)}) copy-start(bf16[32,64,768]{2,1,0:T(8,128)(2,1)} %get-tuple-element.50.refs_1_) | copy-start | bytes 9437188
  (55 other events, 166.7 us)
Sparse Core Ops, SparseCore 0:
  15.2 32.9 all-reduce.7
  513.1 89.2 reduce-scatter.1
  613.9 74.9 all-gather.5
Sparse Core Ops, SparseCore 1:
  18.8 133.6 all-gather.3

commit v5 on v4

--- a/solution.py
+++ b/solution.py
@@ -178,7 +178,6 @@
 def gather_kernel(
     x_ref,
     select_ref,
-    ahead_hbm,
     named_ref,
     gate_hbm,
     up_hbm,
@@ -188,12 +187,11 @@
     gate_out,
     up_out,
     share_out,
-    extra_out,
     held,
-    ahead_ref,
     gate_ref,
     up_ref,
     picked,
+    lively,
     results,
     loaded,
     stored,
@@ -215,7 +213,7 @@
     loads = [
         pltpu.make_async_copy(source, target, loaded.at[i])
         for i, (source, target) in enumerate(
-            ((gate_hbm, gate_ref), (up_hbm, up_ref), (ahead_hbm, ahead_ref))
+            ((gate_hbm, gate_ref), (up_hbm, up_ref))
         )
     ]
     for load in loads:
@@ -237,28 +235,28 @@
 
     combos = ((0, 0), (0, 1), (1, 0), (1, 1))
 
-    def stores(turn, blocks):
-        slot = turn % 2
+    def stores(slot, blocks):
         made = []
         for k in range(4):
             part = pl.ds(k * kept, kept)
             made.append((picked.at[slot, part], rows_out.at[blocks[k]]))
-            for i, out in enumerate((active_out, gate_out, up_out)):
+            made.append((lively.at[slot, part], active_out.at[blocks[k]]))
+            for i, out in enumerate((gate_out, up_out)):
                 made.append((results.at[slot, i, part], out.at[blocks[k]]))
         return [
             pltpu.make_async_copy(source, target, stored.at[slot, i])
             for i, (source, target) in enumerate(made)
         ]
 
-    def blocks_of(turn):
-        q, other = turn // 2, turn % 2
-        return [block_of(q, *combo, 1 - c if other else c) for combo in combos]
-
-    def work(turn):
-        blocks, slot = blocks_of(turn), turn % 2
-        if turn >= 2:
-            for store in stores(turn - 2, blocks_of(turn - 2)):
+    def work(q, slot):
+        core = 1 - c if slot else c
+        blocks = [block_of(q, *combo, core) for combo in combos]
+
+        @pl.when(q > 0)
+        def _():
+            for store in stores(slot, [block_of(q - 1, *combo, core) for combo in combos]):
                 store.wait()
+
         for k in range(4):
             rows = jnp.dot(
                 select_ref[blocks[k]], held[blocks[k]], preferred_element_type=jnp.float32
@@ -268,6 +266,10 @@
         gate_pre = jnp.dot(rows, gate_ref[...], preferred_element_type=jnp.float32)
         up_pre = jnp.dot(rows, up_ref[...], preferred_element_type=jnp.float32)
         logits = jnp.dot(rows, router_ref[...], preferred_element_type=jnp.float32)
+        results[slot, 0] = gate_pre
+        results[slot, 1] = up_pre
+        active = gate_pre * (1.0 / (1.0 + jnp.exp(-gate_pre))) * up_pre
+        lively[slot] = active.astype(lively.dtype)
         for k in range(4):
             part = slice(k * kept, (k + 1) * kept)
             block = blocks[k]
@@ -276,21 +278,8 @@
             lanes = lax.broadcasted_iota(jnp.int32, lifted.shape, 1)
             share = jnp.sum(jnp.where(lanes == mine, lifted, 0.0), axis=1, keepdims=True)
             share = share / jnp.sum(lifted, axis=1, keepdims=True)
-            gate, up, ahead = gate_pre[part], up_pre[part], ahead_ref[block]
-            sigma = 1.0 / (1.0 + jnp.exp(-gate))
-            silu = gate * sigma
-            active_low = (silu * up).astype(results.dtype)
-            grad = jnp.sum(active_low.astype(jnp.float32) * ahead, axis=1, keepdims=True)
-            active_grad = share * ahead
-            gate_grad = active_grad * up * (sigma * (1.0 + gate * (1.0 - sigma)))
-            results[slot, 0, part] = active_low
-            results[slot, 1, part] = gate_grad.astype(results.dtype)
-            results[slot, 2, part] = (active_grad * silu).astype(results.dtype)
             share_out[block] = jnp.broadcast_to(share, share_out.shape[1:])
-            high = grad.astype(extra_out.dtype).astype(jnp.float32)
-            both = jnp.where(lanes == mine, high, jnp.where(lanes == 32 + mine, grad - high, 0.0))
-            extra_out[block] = both.astype(extra_out.dtype)
-        for store in stores(turn, blocks):
+        for store in stores(slot, blocks):
             store.start()
 
     def forward(q):
@@ -349,27 +338,26 @@
     second(0)
     forward(2)
     second(1)
-    last(0)
-    work(0)
-    others(0)
-    work(1)
-    forward(3)
-    second(2)
-    last(1)
-    work(2)
-    others(1)
-    work(3)
-    second(3)
-    last(2)
-    work(4)
-    others(2)
-    work(5)
-    last(3)
-    work(6)
-    others(3)
-    work(7)
-    for turn in (6, 7):
-        for store in stores(turn, blocks_of(turn)):
+
+    @pl.loop(0, 4)
+    def _(q):
+        last(q)
+        work(q, 0)
+        others(q)
+        work(q, 1)
+
+        @pl.when(q == 0)
+        def _():
+            forward(3)
+            second(2)
+
+        @pl.when(q == 1)
+        def _():
+            second(3)
+
+    for slot in range(2):
+        core = 1 - c if slot else c
+        for store in stores(slot, [block_of(3, *combo, core) for combo in combos]):
             store.wait()
     for part in range(2):
         copy(mine, part, to_z.at[0, part], near_z).wait_send()
@@ -386,7 +374,7 @@
                 copy(mine, part, to_core.at[i, part, q], core_peer).wait_send()
 
 
-def gather_experts(rows, select, ahead, named, gate_w, up_w, router):
+def gather_experts(rows, select, named, gate_w, up_w, router):
     count, width = rows.shape
     blocks, kept = select.shape[:2]
     hidden = gate_w.shape[1]
@@ -398,21 +386,20 @@
         out_shape=[
             jax.ShapeDtypeStruct((blocks, kept, width), low),
             jax.ShapeDtypeStruct((blocks, kept, hidden), low),
-            jax.ShapeDtypeStruct((blocks, kept, hidden), low),
-            jax.ShapeDtypeStruct((blocks, kept, hidden), low),
+            jax.ShapeDtypeStruct((blocks, kept, hidden), jnp.float32),
+            jax.ShapeDtypeStruct((blocks, kept, hidden), jnp.float32),
             jax.ShapeDtypeStruct((blocks, kept, 128), jnp.float32),
-            jax.ShapeDtypeStruct((blocks, kept, 128), low),
         ],
-        in_specs=[vmem, vmem, anywhere, vmem, anywhere, anywhere, vmem],
-        out_specs=[anywhere] * 4 + [vmem] * 2,
+        in_specs=[vmem, vmem, vmem, anywhere, anywhere, vmem],
+        out_specs=[anywhere] * 4 + [vmem],
         scratch_shapes=[
             pltpu.VMEM((blocks, count, width), low),
-            pltpu.VMEM(ahead.shape, ahead.dtype),
             pltpu.VMEM(gate_w.shape, low),
             pltpu.VMEM(up_w.shape, low),
             pltpu.VMEM((2, 4 * kept, width), low),
-            pltpu.VMEM((2, 3, 4 * kept, hidden), low),
-            copies(3),
+            pltpu.VMEM((2, 4 * kept, hidden), low),
+            pltpu.VMEM((2, 2, 4 * kept, hidden), jnp.float32),
+            copies(2),
             copies(2, 16),
             copies(blocks, 2),
             copies(3, 2),
@@ -421,7 +408,7 @@
             copies(4, 2, 4),
         ],
         compiler_params=settings(1),
-    )(rows, select, ahead, named, gate_w, up_w, router)
+    )(rows, select, named, gate_w, up_w, router)
 
 
 def scatter_kernel(
@@ -430,17 +417,21 @@
     *refs,
 ):
     if extended:
-        gate_grad_ref, up_grad_ref, gate_ref, up_ref, extra_ref, out_ref, extra_out = refs[:7]
-        refs = refs[7:]
+        gate_grad_ref, up_grad_ref, gate_ref, up_ref, extra_ref, rows_hbm = refs[:6]
+        out_ref, extra_out, gate_out, up_out = refs[6:10]
+        tiles, staged, loaded, stored = refs[10:14]
+        refs = refs[14:]
     else:
-        active_ref, down_ref, share_ref, out_ref = refs[:4]
-        refs = refs[4:]
+        active_ref, down_ref, share_ref, select_ref, grads_hbm, gate_hbm, up_hbm = refs[:7]
+        out_ref, rows_out, gate_out, up_out, extra_ref = refs[7:12]
+        grads_in, pre_in, rows_staged, staged, loaded, stored = refs[12:18]
+        refs = refs[18:]
     outgoing, core_in, total, back, x_in, y_in, z_in = refs[:7]
     core_sent, core_got, x_sent, x_got, y_sent, y_got, z_sent, z_got = refs[7:]
     z, y, x, c = spot()
     width = out_ref.shape[1]
     half = out_ref.shape[0] // 2
-    kept = spread_ref.shape[2]
+    blocks, _, kept = spread_ref.shape
     y_peer, x_peer, core_peer = (
         where_is(z, 1 - y, x, c),
         where_is(z, y, 1 - x, c),
@@ -469,6 +460,111 @@
             sums = sums * rows_of(share_ref, q, core)[:, :1]
         back[...] = sums.astype(back.dtype)
 
+    def turn_blocks(turn):
+        core = (c + turn) % 2
+        return [block_of(group, turn // 2, core) for group in range(4)]
+
+    def loads(turn):
+        slot, made = turn % 2, []
+        if extended:
+            columns = pl.ds(pl.multiple_of(turn * tiles.shape[3], tiles.shape[3]), tiles.shape[3])
+            made.append((rows_hbm.at[:, :, columns], tiles.at[slot]))
+        else:
+            for group, block in enumerate(turn_blocks(turn)):
+                rows = pl.ds(group * kept, kept)
+                made.append((grads_hbm.at[block], grads_in.at[slot, group]))
+                made.append((gate_hbm.at[block], pre_in.at[slot, 0, rows]))
+                made.append((up_hbm.at[block], pre_in.at[slot, 1, rows]))
+        return [
+            pltpu.make_async_copy(source, target, loaded.at[slot, i])
+            for i, (source, target) in enumerate(made)
+        ]
+
+    def stores(turn):
+        slot, made = turn % 2, []
+        if extended:
+            columns = tiles.shape[3]
+            rows = pl.ds(pl.multiple_of(turn * columns, columns), columns)
+            made.append((staged.at[slot, 0], gate_out.at[rows]))
+            made.append((staged.at[slot, 1], up_out.at[rows]))
+        else:
+            for group, block in enumerate(turn_blocks(turn)):
+                rows = pl.ds(group * kept, kept)
+                made.append((rows_staged.at[slot, rows], rows_out.at[block]))
+                made.append((staged.at[slot, 0, rows], gate_out.at[block]))
+                made.append((staged.at[slot, 1, rows], up_out.at[block]))
+        return [
+            pltpu.make_async_copy(source, target, stored.at[slot, i])
+            for i, (source, target) in enumerate(made)
+        ]
+
+    def begin_loads(turn):
+        for load in loads(turn):
+            load.start()
+
+    def fill(turn):
+        for load in loads(turn):
+            load.wait()
+
+        @pl.when(turn >= 2)
+        def _():
+            for store in stores(turn - 2):
+                store.wait()
+
+        if extended:
+            weigh(turn)
+        else:
+            prepare(turn)
+        for store in stores(turn):
+            store.start()
+
+        @pl.when(turn < 6)
+        def _():
+            begin_loads(turn + 2)
+
+    def weigh(turn):
+        slot = turn % 2
+        staged[slot] = jnp.zeros_like(staged[slot])
+
+        @pl.loop(0, blocks // 4)
+        def _(i):
+            span = pl.ds(i * 4, 4)
+            rows = tiles[slot, span].reshape(4 * kept, tiles.shape[3])
+            for which, grads in enumerate((gate_grad_ref, up_grad_ref)):
+                staged[slot, which] += left_trans(
+                    rows, grads[span].reshape(4 * kept, grads.shape[2])
+                )
+
+    def prepare(turn):
+        blocks, slot = turn_blocks(turn), turn % 2
+        mine = number(z, y, x, c)
+        parts = [
+            jnp.dot(
+                select_ref[blocks[group]],
+                grads_in[slot, group],
+                preferred_element_type=jnp.float32,
+            )
+            for group in range(4)
+        ]
+        share = jnp.concatenate([share_ref[block] for block in blocks], axis=0)[:, :1]
+        picked = jnp.concatenate(parts, axis=0)
+        rows_staged[slot] = (share * picked).astype(rows_staged.dtype)
+        ahead = right_transposed(picked.astype(rows_staged.dtype), down_ref[...])
+        gate, up = pre_in[slot, 0], pre_in[slot, 1]
+        active = jnp.concatenate([active_ref[block] for block in blocks], axis=0)
+        grad = jnp.sum(active.astype(jnp.float32) * ahead, axis=1, keepdims=True)
+        active_grad = share * ahead
+        sigma = 1.0 / (1.0 + jnp.exp(-gate))
+        gate_grad = active_grad * up * (sigma * (1.0 + gate * (1.0 - sigma)))
+        staged[slot, 0] = gate_grad.astype(staged.dtype)
+        staged[slot, 1] = (active_grad * (gate * sigma)).astype(staged.dtype)
+        lanes = lax.broadcasted_iota(jnp.int32, (4 * kept, 128), 1)
+        high = grad.astype(extra_ref.dtype).astype(jnp.float32)
+        both = jnp.where(lanes == mine, high, jnp.where(lanes == 32 + mine, grad - high, 0.0))
+        both = both.astype(extra_ref.dtype)
+        for group, block in enumerate(blocks):
+            extra_ref[block] = both[group * kept : (group + 1) * kept]
+
     def part(block, group):
         rows = jnp.dot(
             spread_ref[block],
@@ -505,7 +601,7 @@
     def z_copy(q):
         return remote(
             total.at[q, 3], z_in.at[q - 1], z_sent.at[q - 1], z_got.at[q - 1],
-            far_z if q == 2 else near_z,
+            where_is(along_z(z, 2 - q % 2), y, x, c),
         )
 
     def add(group, q, side, source):
@@ -541,44 +637,64 @@
         x_copy(1, q, 1, 2).start()
 
     def close(q):
-        for side, arrivals in ((0, ((x_copy(1, q, 0, 1), x_in, 1), (y_copy(2, q, 0, 2), y_in, 2))),
-                               (1, ((y_copy(2, q, 1, 1), y_in, 1), (x_copy(1, q, 1, 2), x_in, 2)))):
-            for arrival, _, _ in arrivals:
+        arrivals = (
+            ((x_copy(1, q, 0, 1), x_in, 1), (y_copy(2, q, 0, 2), y_in, 2)),
+            ((y_copy(2, q, 1, 1), y_in, 1), (x_copy(1, q, 1, 2), x_in, 2)),
+        )
+        for side in range(2):
+            for arrival, _, _ in arrivals[side]:
                 arrival.wait_recv()
             rows = pl.ds(side * half, half)
             sums = total[q, 3, rows].astype(jnp.float32)
-            for _, source, slot in arrivals:
+            for _, source, slot in arrivals[side]:
                 sums = sums + source[slot, q].astype(jnp.float32)
-            if q == 2:
-                if side == 0:
-                    z_copy(3).wait_recv()
-                sums = sums + z_in[2, rows].astype(jnp.float32)
-            if q:
-                total[q, 3, rows] = sums.astype(total.dtype)
-            else:
-                if side == 0:
-                    z_copy(1).wait_recv()
-                    z_copy(2).wait_recv()
-                for i in range(2):
-                    sums = sums + z_in[i, rows].astype(jnp.float32)
-                out_ref[rows] = sums[:, :width]
-                if extended:
-                    extra_out[rows] = sums[:, width:]
-        if q:
+            total[q, 3, rows] = sums.astype(total.dtype)
+
+        @pl.when(q == 2)
+        def _():
+            z_copy(3).wait_recv()
+            total[2, 3] = (
+                total[2, 3].astype(jnp.float32) + z_in[2].astype(jnp.float32)
+            ).astype(total.dtype)
+
+        @pl.when(q > 0)
+        def _():
             z_copy(q).start()
 
-    begin(3)
-    begin(2)
-    middle(3)
-    begin(1)
-    middle(2)
-    close(3)
-    begin(0)
-    middle(1)
-    close(2)
-    middle(0)
-    close(1)
-    close(0)
+    def done(i):
+        return jnp.maximum(i, 0) + jnp.maximum(i - 2, 0)
+
+    begin_loads(0)
+    begin_loads(1)
+
+    @pl.loop(0, 6)
+    def _(i):
+        @pl.when(i < 4)
+        def _():
+            begin(3 - i)
+
+        @pl.loop(done(i - 1), done(i))
+        def _(turn):
+            fill(turn)
+
+        @pl.when((i > 0) & (i < 5))
+        def _():
+            middle(4 - i)
+
+        @pl.when(i > 1)
+        def _():
+            close(5 - i)
+
+    for turn in (6, 7):
+        for store in stores(turn):
+            store.wait()
+    for q in (1, 2):
+        z_copy(q).wait_recv()
+    sums = total[0, 3].astype(jnp.float32)
+    sums = sums + z_in[0].astype(jnp.float32) + z_in[1].astype(jnp.float32)
+    out_ref[...] = sums[:, :width]
+    if extended:
+        extra_out[...] = sums[:, width:]
     for q in range(1, 4):
         z_copy(q).wait_send()
 
@@ -596,19 +712,49 @@
 
 def scatter_rows(spread, *operands):
     blocks, count, kept = spread.shape
-    extended = len(operands) == 5
+    extended = len(operands) == 6
     width = operands[2].shape[0] if extended else operands[1].shape[1]
     wide = width + 128 if extended else width
     low = operands[0].dtype
+    anywhere = pl.BlockSpec(memory_space=pl.ANY)
     outs = [jax.ShapeDtypeStruct((count, width), jnp.float32)]
     if extended:
         outs.append(jax.ShapeDtypeStruct((count, 128), jnp.float32))
+        hidden = operands[0].shape[2]
+        outs += [jax.ShapeDtypeStruct((width, hidden), jnp.float32)] * 2
+        in_specs = in_vmem(6) + [anywhere]
+        out_specs = in_vmem(2) + [anywhere] * 2
+        filler = [
+            pltpu.VMEM((2, blocks, kept, width // 8), low),
+            pltpu.VMEM((2, 2, width // 8, hidden), jnp.float32),
+            copies(2, 1),
+            copies(2, 2),
+        ]
+    else:
+        hidden = operands[0].shape[2]
+        outs += [
+            jax.ShapeDtypeStruct((blocks, kept, width), low),
+            jax.ShapeDtypeStruct((blocks, kept, hidden), low),
+            jax.ShapeDtypeStruct((blocks, kept, hidden), low),
+            jax.ShapeDtypeStruct((blocks, kept, 128), low),
+        ]
+        in_specs = in_vmem(5) + [anywhere] * 3
+        out_specs = in_vmem(1) + [anywhere] * 3 + in_vmem(1)
+        filler = [
+            pltpu.VMEM((2, 4, count, width), low),
+            pltpu.VMEM((2, 2, 4 * kept, hidden), jnp.float32),
+            pltpu.VMEM((2, 4 * kept, width), low),
+            pltpu.VMEM((2, 2, 4 * kept, hidden), low),
+            copies(2, 12),
+            copies(2, 12),
+        ]
     return pl.pallas_call(
         functools.partial(scatter_kernel, extended),
         out_shape=outs,
-        in_specs=in_vmem(1 + len(operands)),
-        out_specs=in_vmem(len(outs)),
-        scratch_shapes=[
+        in_specs=in_specs,
+        out_specs=out_specs,
+        scratch_shapes=filler
+        + [
             pltpu.VMEM((4, 4, count, wide), low),
             pltpu.VMEM((4, 4, count, wide), low),
             pltpu.VMEM((4, 4, count, wide), low),
@@ -1070,13 +1216,39 @@
     )(tokens, routes, gain, w_query, key_weight, value_weight)
 
 
+def turned(values):
+    return pltpu.roll(values, HEAD_WIDTH // 2, 1)
+
+
+def signed(sine):
+    lanes = lax.broadcasted_iota(jnp.int32, sine.shape, 1)
+    return jnp.where(lanes < HEAD_WIDTH // 2, -sine, sine)
+
+
+def nt_product(left, right):
+    return lax.dot_general(
+        left, right, (((1,), (1,)), ((), ())), preferred_element_type=jnp.float32
+    )
+
+
 def finish_kernel(
-    attended_ref,
+    row,
+    sequences,
+    raw_ref,
+    notes_ref,
+    query_gain_ref,
+    key_gain_ref,
     weight_ref,
     x_ref,
     gain_ref,
     middle_out,
     normed_out,
+    attended_out,
+    probs_out,
+    query_out,
+    key_out,
+    cosine_out,
+    sine_out,
     outgoing,
     core_in,
     across_x,
@@ -1090,6 +1262,54 @@
     count = x_ref.shape[0]
     core_peer, x_peer = where_is(z, y, x, 1 - c), where_is(z, y, 1 - x, c)
     greet([core_peer, x_peer])
+    heads = query_out.shape[2] // HEAD_WIDTH
+    wide = heads * HEAD_WIDTH
+
+    def place(block):
+        down = lax.broadcasted_iota(jnp.int32, (count, count), 0)
+        along = lax.broadcasted_iota(jnp.int32, (count, count), 1)
+        end = jnp.zeros((1, 1), jnp.int32)
+        start = jnp.zeros((count, count), jnp.int32)
+        own, other = start, start
+        for i in range(sequences - 1):
+            length = notes_ref[block, row : row + 1, i : i + 1]
+            end = end + length
+            own = own + jnp.where(down >= end, 1, 0)
+            other = other + jnp.where(along >= end, 1, 0)
+            start = start + jnp.where(down >= end, length, 0)
+        return down - start, (own == other) & (along <= down)
+
+    def attend(block):
+        position, allowed = place(block)
+        lanes = lax.broadcasted_iota(jnp.int32, position.shape, 1)
+        spin = lanes % (HEAD_WIDTH // 2)
+        inverse = jnp.exp(spin.astype(jnp.float32) * (-2.0 * math.log(THETA) / HEAD_WIDTH))
+        angles = position.astype(jnp.float32) * inverse
+        cosine, sine = jnp.cos(angles), jnp.sin(angles)
+        cosine_out[block] = cosine
+        sine_out[block] = sine
+        flipped = signed(sine)
+
+        def normal(values, gain):
+            scale = lax.rsqrt(jnp.mean(values * values, axis=1, keepdims=True) + EPSILON)
+            values = values * scale * gain
+            return (values * cosine + turned(values) * flipped).astype(query_out.dtype)
+
+        key = normal(raw_ref[block, :, wide : wide + HEAD_WIDTH], key_gain_ref[...])
+        key_out[block] = key
+        value = raw_ref[block, :, wide + HEAD_WIDTH :].astype(query_out.dtype)
+        for head in range(heads):
+            columns = slice(head * HEAD_WIDTH, (head + 1) * HEAD_WIDTH)
+            query = normal(raw_ref[block, :, columns], query_gain_ref[...])
+            query_out[block, :, columns] = query
+            scores = nt_product(query, key) * HEAD_WIDTH ** (-0.5)
+            scores = jnp.where(allowed, scores, MASKED)
+            raised = jnp.exp(scores - jnp.max(scores, axis=1, keepdims=True))
+            probs = raised / jnp.sum(raised, axis=1, keepdims=True)
+            probs_out[block, head] = probs
+            attended_out[block, :, columns] = jnp.dot(
+                probs.astype(value.dtype), value, preferred_element_type=jnp.float32
+            ).astype(attended_out.dtype)
 
     def core_copy(far):
         return remote(
@@ -1100,9 +1320,9 @@
         return remote(across_x, x_sums, x_sent, x_got, x_peer)
 
     def partial(side, core):
-        return jnp.dot(
-            attended_ref[side * 2 + core], weight_ref[...], preferred_element_type=jnp.float32
-        )
+        block = side * 2 + core
+        attend(block)
+        return jnp.dot(attended_out[block], weight_ref[...], preferred_element_type=jnp.float32)
 
     outgoing[1] = partial(1 - x, 1 - c).astype(outgoing.dtype)
     core_copy(1).start()
@@ -1125,17 +1345,25 @@
     core_copy(1).wait_send()
 
 
-def finish_attention(attended, w_out, tokens, gain):
+def finish_attention(raw, notes, row, sequences, q_gain, k_gain, w_out, tokens, gain):
     count, width = tokens.shape
     low = tokens.dtype
+    wide = w_out.shape[0]
+    heads = wide // HEAD_WIDTH
     return pl.pallas_call(
-        finish_kernel,
+        functools.partial(finish_kernel, row, sequences),
         out_shape=[
             jax.ShapeDtypeStruct((count, width), jnp.float32),
             jax.ShapeDtypeStruct((count, width), low),
+            jax.ShapeDtypeStruct((4, count, wide), low),
+            jax.ShapeDtypeStruct((4, heads, count, count), jnp.float32),
+            jax.ShapeDtypeStruct((4, count, wide), low),
+            jax.ShapeDtypeStruct((4, count, HEAD_WIDTH), low),
+            jax.ShapeDtypeStruct((4, count, HEAD_WIDTH), jnp.float32),
+            jax.ShapeDtypeStruct((4, count, HEAD_WIDTH), jnp.float32),
         ],
-        in_specs=in_vmem(4),
-        out_specs=in_vmem(2),
+        in_specs=in_vmem(7),
+        out_specs=in_vmem(8),
         scratch_shapes=[
             pltpu.VMEM((2, count, width), low),
             pltpu.VMEM((2, count, width), low),
@@ -1147,7 +1375,7 @@
             copies(),
         ],
         compiler_params=settings(5),
-    )(attended, w_out, tokens, gain)
+    )(raw, notes, q_gain, k_gain, w_out, tokens, gain)
 
 
 def branch_kernel(
@@ -1203,13 +1431,22 @@
 
 
 def heads_kernel(
-    grad_ref,
+    branch_ref,
+    raw_ref,
+    probs_ref,
+    rotated_ref,
+    rotated_key_ref,
+    cosine_ref,
+    sine_ref,
+    query_gain_ref,
+    key_gain_ref,
     hidden_ref,
     query_ref,
     key_ref,
     value_ref,
     weight_out,
     first_out,
+    gains_out,
     every,
     outgoing,
     x_sent,
@@ -1224,26 +1461,71 @@
     core_peer, x_peer = where_is(z, y, x, 1 - c), where_is(z, y, 1 - x, c)
     peers = [(member, (shard + j) % 4) for j in range(1, 4)]
     greet(peers)
-    rows = grad_ref.shape[0]
+    rows = every.shape[1]
     half = rows // 2
     count = rows // 4
     depth = hidden_ref.shape[1]
     wide, narrow = query_ref.shape[1] // 4, key_ref.shape[1] // 4
-    every[shard] = grad_ref[...]
+    low = every.dtype
+
+    def attention_back(block):
+        cosine = cosine_ref[block]
+        flipped = signed(sine_ref[block])
+
+        def unturn(grads):
+            return grads * cosine + turned(grads * flipped)
+
+        def normal_back(grads, values, gain, into):
+            scale = lax.rsqrt(jnp.mean(values * values, axis=1, keepdims=True) + EPSILON)
+            hat = values * scale
+            gains_out[into : into + 1] += jnp.sum(grads * hat, axis=0, keepdims=True)
+            grads = grads * gain
+            return scale * (grads - hat * jnp.mean(grads * hat, axis=1, keepdims=True))
+
+        rotated_key = rotated_key_ref[block]
+        value = raw_ref[block, :, wide + narrow :].astype(low)
+        place = pl.ds(block * count, count)
+        value_grad = key_grad = None
+        for head in range(wide // HEAD_WIDTH):
+            columns = slice(head * HEAD_WIDTH, (head + 1) * HEAD_WIDTH)
+            grads = branch_ref[block, :, columns]
+            probs = probs_ref[block, head]
+            prob_grad = nt_product(grads, value)
+            term = left_trans(probs.astype(low), grads)
+            value_grad = term if value_grad is None else value_grad + term
+            balance = jnp.sum(probs * prob_grad, axis=1, keepdims=True)
+            score_grad = (probs * (prob_grad - balance)).astype(low)
+            query_grad = jnp.dot(score_grad, rotated_key, preferred_element_type=jnp.float32)
+            term = left_trans(score_grad, rotated_ref[block, :, columns])
+            key_grad = term if key_grad is None else key_grad + term
+            query_grad = unturn(query_grad * HEAD_WIDTH ** (-0.5))
+            query_grad = normal_back(
+                query_grad, raw_ref[block, :, columns], query_gain_ref[...], 0
+            )
+            every[shard, place, columns] = query_grad.astype(low)
+        key_grad = unturn(key_grad * HEAD_WIDTH ** (-0.5))
+        key_grad = normal_back(
+            key_grad, raw_ref[block, :, wide : wide + narrow], key_gain_ref[...], 1
+        )
+        every[shard, place, wide : wide + narrow] = key_grad.astype(low)
+        every[shard, place, wide + narrow :] = value_grad.astype(low)
 
     def x_copy(part):
-        piece = pl.ds(part * half, half)
-        return remote(
-            grad_ref.at[piece], every.at[shard, piece], x_sent.at[part], x_got.at[part], x_peer
-        )
+        view = every.at[shard, pl.ds(part * half, half)]
+        return remote(view, view, x_sent.at[part], x_got.at[part], x_peer)
 
     def core_copy(far, part):
         view = every.at[(1 - x if far else x) * 2 + c, pl.ds(part * half, half)]
         return remote(view, view, core_sent.at[far, part], core_got.at[far, part], core_peer)
 
+    gains_out[...] = jnp.zeros_like(gains_out)
     for part in range(2):
+
+        @pl.loop(part * 2, part * 2 + 2)
+        def _(block):
+            attention_back(block)
+
         x_copy(part).start()
-    for part in range(2):
         core_copy(0, part).start()
 
     def weigh(place):
@@ -1308,18 +1590,21 @@
             core_copy(far, part).wait_send()
 
 
-def heads_back(grads, hidden, w_query, key_weight, value_weight):
-    rows, own = grads.shape
+def heads_back(branch, raw, probs, rotated, tables, gains, hidden, weights):
+    rows = 4 * raw.shape[1]
+    own = raw.shape[2]
     depth = hidden.shape[1]
-    low = grads.dtype
+    low = hidden.dtype
+    operands = (branch, raw, probs, *rotated, *tables, *gains, hidden, *weights)
     return pl.pallas_call(
         heads_kernel,
         out_shape=[
             jax.ShapeDtypeStruct((4, depth, own), low),
             jax.ShapeDtypeStruct((4, rows // 4, depth), low),
+            jax.ShapeDtypeStruct((8, HEAD_WIDTH), jnp.float32),
         ],
-        in_specs=in_vmem(5),
-        out_specs=in_vmem(2),
+        in_specs=in_vmem(len(operands)),
+        out_specs=in_vmem(3),
         scratch_shapes=[
             pltpu.VMEM((4, rows, own), low),
             pltpu.VMEM((4, rows // 4, depth), low),
@@ -1331,7 +1616,7 @@
             copies(4),
         ],
         compiler_params=settings(7),
-    )(grads, hidden, w_query, key_weight, value_weight)
+    )(*operands)
 
 
 def moe_gathered(normed, router, routes, capacity, cotangent, weights, notes):
@@ -1349,32 +1634,30 @@
     places = jnp.arange(capacity, dtype=jnp.int32)
     select = (own[:, None, :] & (rank[:, None, :] == places[None, :, None])).astype(jnp.bfloat16)
     spread = (own[:, :, None] & (rank[:, :, None] == places[None, None, :])).astype(jnp.bfloat16)
-    grad_rows = contract(
-        "bcj,bjd->bcd", select, all_grads.reshape(experts, token_count, MODEL_WIDTH)
-    ).astype(jnp.bfloat16)
     named_rows = contract("bcj,bej->bce", select, named.astype(jnp.bfloat16))
     named_rows = jnp.pad(named_rows.astype(jnp.bfloat16), ((0, 0), (0, 0), (0, 128 - experts)))
-    flat_grads = grad_rows.reshape(experts * capacity, MODEL_WIDTH)
-    ahead = right_transposed(flat_grads, down_w).reshape(experts, capacity, -1)
-
     padded = jnp.pad(router, ((0, 0), (0, 128 - experts)))
-    arrived, active, gate_pre_grad, up_pre_grad, share, extra = gather_experts(
-        normed, select, ahead, named_rows, gate_w, up_w, padded
+    arrived, active, gate_pre, up_pre, share = gather_experts(
+        normed, select, named_rows, gate_w, up_w, padded
     )
-    summed, back = scatter_rows(spread, gate_pre_grad, up_pre_grad, gate_w, up_w, extra)
-    (mixed,) = scatter_rows(spread, active, down_w, share)
-    summed, back, mixed = lax.optimization_barrier((summed, back, mixed))
+    mixed, out_rows, gate_pre_grad, up_pre_grad, extra = scatter_rows(
+        spread,
+        active,
+        down_w,
+        share,
+        select,
+        all_grads.reshape(experts, token_count, MODEL_WIDTH),
+        gate_pre,
+        up_pre,
+    )
+    summed, back, gate_w_grad, up_w_grad = scatter_rows(
+        spread, gate_pre_grad, up_pre_grad, gate_w, up_w, extra, arrived
+    )
 
     def flat(rows):
         return rows.reshape(experts * capacity, rows.shape[2])
 
-    share = flat(share)[:, :1]
-    out_rows = (share * flat_grads.astype(jnp.float32)).astype(jnp.bfloat16)
-    weight_grads = (
-        left_trans(flat(arrived), flat(gate_pre_grad)),
-        left_trans(flat(arrived), flat(up_pre_grad)),
-        left_trans(flat(active), out_rows),
-    )
+    weight_grads = (gate_w_grad, up_w_grad, left_trans(flat(active), flat(out_rows)))
     gate_grad = back[:, :experts] + back[:, experts : 2 * experts]
     picks = jnp.any(routes[:, :, None] == columns[None, None, :], axis=1)
     gates = jax.nn.softmax(jnp.where(picks, matrix_product(normed, router), MASKED), axis=1)
@@ -1476,7 +1759,7 @@
         )
         hidden = hidden.reshape(group, depth)
         first = lax.axis_index("exp") * shards
-        all_lengths = lax.dynamic_slice_in_dim(notes, first, shards)[:, topk, : lengths.shape[1]]
+        notes_own = lax.dynamic_slice_in_dim(notes, first, shards)
     else:
         notes = None
         all_lengths = lax.all_gather(lengths[0], "fsdp")
@@ -1494,40 +1777,42 @@
         partial = contract("gk,nkc->ngc", hidden, joined).astype(jnp.bfloat16)
         raw = lax.psum_scatter(partial, "fsdp", scatter_dimension=0, tiled=True)[0]
         raw = raw.astype(jnp.float32)
-    raw = raw.reshape(shards, token_count, wide + 2 * narrow)
-    query_raw = raw[:, :, :wide].reshape(shards, token_count, heads, HEAD_WIDTH)
-    key_raw = raw[:, :, wide : wide + narrow].reshape(shards, token_count, kv_heads, HEAD_WIDTH)
-    value = (
-        raw[:, :, wide + narrow :]
-        .astype(jnp.bfloat16)
-        .reshape(shards, token_count, kv_heads, HEAD_WIDTH)
-    )
-    position, allowed = jax.vmap(lambda row: seq_layout(row, token_count))(all_lengths)
-    cosine, sine = rotary_tables(position, HEAD_WIDTH)
-    query_scale = rms_scale(query_raw)
-    query_hat = query_raw * query_scale
-    key_scale = rms_scale(key_raw)
-    key_hat = key_raw * key_scale
-    query = (
-        rotate(query_hat * gain_query, cosine, sine)
-        .astype(jnp.bfloat16)
-        .reshape(shards, token_count, kv_heads, head_group, HEAD_WIDTH)
-    )
-    key = rotate(key_hat * gain_key, cosine, sine).astype(jnp.bfloat16)
-    scores = contract("bqkgd,bpkd->bkgqp", query, key) * HEAD_WIDTH ** (-0.5)
-    scores = jnp.where(allowed[:, None, None], scores, MASKED)
-    top = jnp.max(scores, axis=-1, keepdims=True)
-    raised = jnp.exp(scores - top)
-    probs = raised / jnp.sum(raised, axis=-1, keepdims=True)
-    probs_low = probs.astype(jnp.bfloat16)
-    attended = contract("bkgqp,bpkd->bqkgd", probs_low, value).astype(jnp.bfloat16)
-    attended = attended.reshape(group, wide)
     if dense:
-        middle, normed = finish_attention(
-            attended.reshape(shards, token_count, wide), w_out, tokens, gain_mlp[None]
-        )
+        gains = (gain_query[None], gain_key[None])
+        middle, normed, attended, probs, *rotated, cosine, sine = finish_attention(
+            raw, notes_own, topk, lengths.shape[1], *gains, w_out, tokens, gain_mlp[None]
+        )
+        attended = attended.reshape(group, wide)
         scale_two = rms_scale(middle)
     else:
+        raw = raw.reshape(shards, token_count, wide + 2 * narrow)
+        query_raw = raw[:, :, :wide].reshape(shards, token_count, heads, HEAD_WIDTH)
+        key_raw = raw[:, :, wide : wide + narrow].reshape(shards, token_count, kv_heads, HEAD_WIDTH)
+        value = (
+            raw[:, :, wide + narrow :]
+            .astype(jnp.bfloat16)
+            .reshape(shards, token_count, kv_heads, HEAD_WIDTH)
+        )
+        position, allowed = jax.vmap(lambda row: seq_layout(row, token_count))(all_lengths)
+        cosine, sine = rotary_tables(position, HEAD_WIDTH)
+        query_scale = rms_scale(query_raw)
+        query_hat = query_raw * query_scale
+        key_scale = rms_scale(key_raw)
+        key_hat = key_raw * key_scale
+        query = (
+            rotate(query_hat * gain_query, cosine, sine)
+            .astype(jnp.bfloat16)
+            .reshape(shards, token_count, kv_heads, head_group, HEAD_WIDTH)
+        )
+        key = rotate(key_hat * gain_key, cosine, sine).astype(jnp.bfloat16)
+        scores = contract("bqkgd,bpkd->bkgqp", query, key) * HEAD_WIDTH ** (-0.5)
+        scores = jnp.where(allowed[:, None, None], scores, MASKED)
+        top = jnp.max(scores, axis=-1, keepdims=True)
+        raised = jnp.exp(scores - top)
+        probs = raised / jnp.sum(raised, axis=-1, keepdims=True)
+        probs_low = probs.astype(jnp.bfloat16)
+        attended = contract("bkgqp,bpkd->bqkgd", probs_low, value).astype(jnp.bfloat16)
+        attended = attended.reshape(group, wide)
         mixed_heads = lax.psum_scatter(
             matrix_product(attended, w_out).astype(jnp.bfloat16),
             "fsdp",
@@ -1564,32 +1849,42 @@
         attended_grad = right_transposed(branch_grad, w_out).astype(jnp.bfloat16)
     out_w_grad = left_trans(attended, branch_grad).astype(jnp.bfloat16)
     attended_grad, out_w_grad = lax.optimization_barrier((attended_grad, out_w_grad))
-    attended_grad = attended_grad.reshape(shards, token_count, kv_heads, head_group, HEAD_WIDTH)
-    prob_grad = contract("bqkgd,bpkd->bkgqp", attended_grad, value)
-    value_grad = contract("bkgqp,bqkgd->bpkd", probs_low, attended_grad)
-    balance = jnp.sum(probs * prob_grad, axis=-1, keepdims=True)
-    score_grad = (probs * (prob_grad - balance)).astype(jnp.bfloat16)
-    query_norm_grad = contract("bkgqp,bpkd->bqkgd", score_grad, key) * HEAD_WIDTH ** (-0.5)
-    query_norm_grad = query_norm_grad.reshape(shards, token_count, heads, HEAD_WIDTH)
-    key_norm_grad = contract("bkgqp,bqkgd->bpkd", score_grad, query) * HEAD_WIDTH ** (-0.5)
-    query_norm_grad = rotate_back(query_norm_grad, cosine, sine)
-    key_norm_grad = rotate_back(key_norm_grad, cosine, sine)
-    q_gain_grad = jnp.sum(query_norm_grad * query_hat, axis=(0, 1, 2))
-    k_gain_grad = jnp.sum(key_norm_grad * key_hat, axis=(0, 1, 2))
-    query_grad = rms_back(query_norm_grad * gain_query, query_raw, query_scale)
-    key_grad = rms_back(key_norm_grad * gain_key, key_raw, key_scale)
-    head_grads = jnp.concatenate(
-        [
-            query_grad.reshape(group, wide),
-            key_grad.reshape(group, narrow),
-            value_grad.reshape(group, narrow),
-        ],
-        axis=1,
-    ).astype(jnp.bfloat16)
     if dense:
-        joined_grad, first_grad = heads_back(head_grads, hidden, w_query, key_weight, value_weight)
+        joined_grad, first_grad, gain_grads = heads_back(
+            attended_grad,
+            raw,
+            probs,
+            rotated,
+            (cosine, sine),
+            gains,
+            hidden,
+            (w_query, key_weight, value_weight),
+        )
         first_grad = first_grad.transpose(1, 0, 2).reshape(token_count, MODEL_WIDTH)
+        q_gain_grad, k_gain_grad = gain_grads[0], gain_grads[1]
     else:
+        attended_grad = attended_grad.reshape(shards, token_count, kv_heads, head_group, HEAD_WIDTH)
+        prob_grad = contract("bqkgd,bpkd->bkgqp", attended_grad, value)
+        value_grad = contract("bkgqp,bqkgd->bpkd", probs_low, attended_grad)
+        balance = jnp.sum(probs * prob_grad, axis=-1, keepdims=True)
+        score_grad = (probs * (prob_grad - balance)).astype(jnp.bfloat16)
+        query_norm_grad = contract("bkgqp,bpkd->bqkgd", score_grad, key) * HEAD_WIDTH ** (-0.5)
+        query_norm_grad = query_norm_grad.reshape(shards, token_count, heads, HEAD_WIDTH)
+        key_norm_grad = contract("bkgqp,bqkgd->bpkd", score_grad, query) * HEAD_WIDTH ** (-0.5)
+        query_norm_grad = rotate_back(query_norm_grad, cosine, sine)
+        key_norm_grad = rotate_back(key_norm_grad, cosine, sine)
+        q_gain_grad = jnp.sum(query_norm_grad * query_hat, axis=(0, 1, 2))
+        k_gain_grad = jnp.sum(key_norm_grad * key_hat, axis=(0, 1, 2))
+        query_grad = rms_back(query_norm_grad * gain_query, query_raw, query_scale)
+        key_grad = rms_back(key_norm_grad * gain_key, key_raw, key_scale)
+        head_grads = jnp.concatenate(
+            [
+                query_grad.reshape(group, wide),
+                key_grad.reshape(group, narrow),
+                value_grad.reshape(group, narrow),
+            ],
+            axis=1,
+        ).astype(jnp.bfloat16)
         head_grads = lax.all_gather(head_grads, "fsdp")
         hidden_grad = contract("ngc,nkc->gk", head_grads, joined).astype(jnp.bfloat16)
         first_grad = lax.all_to_all(
@@ -1602,12 +1897,6 @@
         jnp.bfloat16
     )
 
-    if dense:
-        out_sum = lax.psum_scatter(out_w_grad, "exp", scatter_dimension=0, tiled=True)
-        joined_grad, out_sum = lax.optimization_barrier((joined_grad, out_sum))
-        out_sum = lax.all_gather(out_sum, "exp", axis=0, tiled=True)
-    else:
-        out_sum = lax.psum(out_w_grad, "exp")
     vectors = jnp.concatenate(
         [
             grad.reshape(shards, -1)
@@ -1616,16 +1905,25 @@
         axis=1,
     )
     if dense:
-        joined_grad, out_sum, gate_w_grad, up_w_grad, down_grad = lax.optimization_barrier(
-            (joined_grad, out_sum, gate_w_grad, up_w_grad, down_grad)
-        )
         rows = -(-vectors.shape[1] // 1024) * 8
-        padded = jnp.pad(vectors, ((0, 0), (0, rows * 128 - vectors.shape[1])))
+        vectors = jnp.pad(vectors, ((0, 0), (0, rows * 128 - vectors.shape[1])))
+        started = lengths[0, 0] > 0
+        gate_w_grad, up_w_grad = (
+            jnp.where(started, grad, 0.0) for grad in (gate_w_grad, up_w_grad)
+        )
+        out_sum = lax.psum_scatter(out_w_grad, "exp", scatter_dimension=0, tiled=True)
+        joined_grad, vectors, out_sum, gate_w_grad, up_w_grad, down_grad = (
+            lax.optimization_barrier(
+                (joined_grad, vectors, out_sum, gate_w_grad, up_w_grad, down_grad)
+            )
+        )
+        out_sum = lax.all_gather(out_sum, "exp", axis=0, tiled=True)
         joined_sum, vectors = reduce_over_members(
-            joined_grad.reshape(2, 4, -1, wide + 2 * narrow), padded.reshape(shards, rows, 128)
+            joined_grad.reshape(2, 4, -1, wide + 2 * narrow), vectors.reshape(shards, rows, 128)
         )
         joined_sum, vectors = joined_sum.reshape(joined_grad.shape), vectors.reshape(-1)
     else:
+        out_sum = lax.psum(out_w_grad, "exp")
         joined_sum = lax.psum(joined_grad, "exp")
         vectors = lax.psum(vectors, BOTH)[place]
     out_sum, joined_sum = out_sum.astype(jnp.float32), joined_sum.astype(jnp.float32)

time: 853 us -> 786 us (0.921)
  Pallas kernels: 574 us -> 662 us
  matrix products: 78.6 us -> 21.7 us
  waiting for transfers between devices: 53.4 us -> 6.46 us
  local copies, waits for them, and re-layouts: 69 us -> 33.5 us
  other arithmetic: 49.2 us -> 35.5 us
    all_gather x1, waiting for transfers between devices: 52.8 us -> 0.01 us  [local(): out_sum = lax.all_gather(out_sum, 'exp', axis=0, tiled=True)]
    pallas_call x1, Pallas kernels: 127 us -> 178 us  [reduce_over_members(): pl.pallas_call(functools.partial(reduce_kernel, cuts), out_shape=[jax.Sha...]
    dot_general x5 -> x3, matrix products: 41.4 us -> 18.9 us  [left_trans(): lax.dot_general(left, right, (((0,), (0,)), ((), ())), preferred_element_...]
    dot_general x8 -> x1, matrix products: 22.1 us -> 0.41 us  [contract(): return jnp.einsum(spec, left, right, preferred_element_type=jnp.float32)]
    pallas_call x1, Pallas kernels: 21.6 us -> 39.9 us  [finish_attention(): pl.pallas_call(functools.partial(finish_kernel, row, sequences), out_shap...]
    unnamed x166 -> x35, local copies, waits for them, and re-layouts: 22.4 us -> 7.95 us
    dot_general x3 -> x2, matrix products: 13.7 us -> 1.98 us  [right_transposed(): lax.dot_general(left, right, (((1,), (1,)), ((), ())), preferred_element_...]
    select_n x0 -> x1, other arithmetic: none -> 10.3 us  [local(): jnp.where(started, grad, 0.0)]
  transfers between devices with their start and end apart: 4 -> 4, of which waited for: 1 -> 1; matrix products, arithmetic and copies ran while one was open for 15% -> 8% of each run, Pallas kernels for 17% -> 56%
where the time goes in v5:
time: 786 us; the launch traced here: 776 us
  Pallas kernels  662 us (84%)
  other arithmetic  35.5 us (5%)
  local copies, waits for them, and re-layouts  33.5 us (4%)
  matrix products  21.7 us (3%)
  between operations  16.8 us (2%)
    pallas_call x2, Pallas kernels, scatter_rows(): pl.pallas_call(functools.partial(scatter_kernel, extended), out_shape=out...  204 us
    pallas_call x1, Pallas kernels, reduce_over_members(): pl.pallas_call(functools.partial(reduce_kernel, cuts), out_shape=[jax.Sha...  178 us
    pallas_call x1, Pallas kernels, gather_experts(): pl.pallas_call(gather_kernel, out_shape=[jax.ShapeDtypeStruct((blocks, ke...  95 us
    pallas_call x1, Pallas kernels, project_tokens(): pl.pallas_call(project_kernel, out_shape=[jax.ShapeDtypeStruct((4, count,...  71.5 us
    pallas_call x1, Pallas kernels, heads_back(): pl.pallas_call(heads_kernel, out_shape=[jax.ShapeDtypeStruct((4, depth, o...  52.6 us
    pallas_call x1, Pallas kernels, finish_attention(): pl.pallas_call(functools.partial(finish_kernel, row, sequences), out_shap...  39.9 us
    pallas_call x1, Pallas kernels, branch_back(): pl.pallas_call(branch_kernel, out_shape=[jax.ShapeDtypeStruct((4, count,...  21 us
    dot_general x3, matrix products, left_trans(): lax.dot_general(left, right, (((0,), (0,)), ((), ())), preferred_element_...  18.9 us
  transfers between devices with their start and end apart: 4, of which 1 were waited for; matrix products, arithmetic and copies ran while one was open for 8% of the time, Pallas kernels for 56%

profile of v5, /device:TPU:8, one launch (start us, length us, event | category | flops | bytes accessed | tf_op | source)
XLA Modules:
  0.0 776.4 jit_solution(16797912155813296925)
XLA Ops:
  11.1 2.8 concatenate.10
  18.4 71.5 %shard_map.263 = (f32[4,128,1280]{2,1,0:T(8,128)}, bf16[4,128,512]{2,1,0:T(8,128)(2,1)}, s32[32,16,128]{2,1,0:T(8,128)}) custom-call(bf16[128,2048]{1,0:T(8,128)(2,1)} %x_ref.3, s32[16,128]{1,0:T(8,128)} %pad.21.routes_ref, bf16[1,512]{1,0:T(2,128)(2,1)} %broadcast_in_dim.22.gain_ref, bf16[512,4096]{1,0:T(8,128)(2,1)} %query_ref.3, ...), custom_call_target="tpu_custom_call" | custom-call | tf_op jit(solution)/shard_map/pallas_call | solution.py:1187
  95.0 1.4 constant_dynamic-slice_fusion.notes_ref
  97.5 2.6 fusion.2.spread_ref
  104.5 39.9 %shard_map.264 = (f32[128,2048]{1,0:T(8,128)}, bf16[128,2048]{1,0:T(8,128)(2,1)}, bf16[4,128,1024]{2,1,0:T(8,128)(2,1)}, f32[4,8,128,128]{3,2,1,0:T(8,128)}, bf1...) custom-call(f32[4,128,1280]{2,1,0:T(8,128)} %get-tuple-element.54.ra, ...), custom_call_target="tpu_custom_call" | custom-call | tf_op jit(solution)/shard_map/pallas_call | solution.py:1353
  144.5 95.0 %shard_map.265 = (bf16[32,64,2048]{2,1,0:T(8,128)(2,1)}, bf16[32,64,768]{2,1,0:T(8,128)(2,1)}, f32[32,64,768]{2,1,0:T(8,128)}, f32[32,64,768]{2,1,0:T(8,128)}, f32[32,64,128]{2,1,0:T(8,128)}) custom-call(bf16[128,2048]{1,0:T(8,128)(2,1)} %get-tuple-element.57.x_ref, bf16[32,64,128]{2,1,0:T(8,128)(2,1)} %fusion.15.select_ref.refs_3_, ...), custom_call_target="tpu_custom_call" | custom-call | tf_op jit(solution)/shard_map/pallas_call | solution.py:384
  240.2 103.2 %shard_map.266 = (f32[128,2048]{1,0:T(8,128)}, bf16[32,64,2048]{2,1,0:T(8,128)(2,1)}, bf16[32,64,768]{2,1,0:T(8,128)(2,1)}, bf16[32,64,768]{2,1,0:T(8,128)(2,1)}, bf16[32,64,128]{2,1,0:T(8,128)(2,1)}) custom-call(bf16[32,128,64]{2,1,0:T(8,128)(2,1)} %fusion.2.spread_ref, bf16[32,64,768]{2,1,0:T(8,128)(2,1)} %get-tuple-element.58.refs_0_, ...), custom_call_target="tpu_custom_call" | custom-call | tf_op jit(solution)/shard_map/pallas_call | solution.py:751
  343.4 101.2 %shard_map.267 = (f32[128,2048]{1,0:T(8,128)}, f32[128,128]{1,0:T(8,128)}, f32[2048,768]{1,0:T(8,128)}, f32[2048,768]{1,0:T(8,128)}) custom-call(bf16[32,128,64]{2,1,0:T(8,128)(2,1)} %fusion.2.spread_ref, bf16[32,64,768]{2,1,0:T(8,128)(2,1)} %get-tuple-element.63.refs_0_, bf16[32,64,768]{2,1,0:T(8,128)(2,1)} %get-tuple-element.64.refs_1_, ...), custom_call_target="tpu_custom_call" | custom-call | tf_op jit(solution)/shard_map/pallas_call | solution.py:751
  446.8 1.8 multiply_reduce_fusion
  450.7 21.0 %shard_map.268 = (bf16[4,128,1024]{2,1,0:T(8,128)(2,1)}, bf16[4,128,2048]{2,1,0:T(8,128)(2,1)}) custom-call(bf16[128,2048]{1,0:T(8,128)(2,1)} %fusion.28.branch_ref, bf16[1024,2048]{1,0:T(8,128)(2,1)} %weight_ref.3), custom_call_target="tpu_custom_call" | custom-call | tf_op jit(solution)/shard_map/pallas_call | solution.py:1420
  471.7 6.3 bitcast_convert_fusion
  478.2 52.6 %shard_map.269 = (bf16[4,512,1280]{2,1,0:T(8,128)(2,1)}, bf16[4,128,512]{2,1,0:T(8,128)(2,1)}, f32[8,128]{1,0:T(8,128)}) custom-call(bf16[4,128,1024]{2,1,0:T(8,128)(2,1)} %get-tuple-element.72.branch_ref, f32[4,128,1280]{2,1,0:T(8,128)} %get-tuple-element.54.raw_ref, f32[4,8,128,128]{3,2,1,0:T(8,128)} %get-tuple-element.73.probs_ref, ...), custom_call_target="tpu_custom_call" | custom-call | tf_op jit(solution)/shard_map/pallas_call | solution.py:1599
  532.0 1.3 copy.69
  533.3 1.6 copy.70
  536.3 1.3 fusion.31
  537.6 1.7 reshape.181
  539.6 10.3 %broadcast_select_fusion = (f32[2048,768]{1,0:T(8,128)}, f32[2048,768]{1,0:T(8,128)}) fusion(f32[2048,768]{1,0:T(8,128)} %get-tuple-element.84, pred[]{:T(512)} %bitcast.10, f32[2048,768]{1,0:T(8,128)} %get-tuple-element.83), kind=kLoop, calls=%fused_computation.5 | loop fusion | flops 3145728 | bytes 25165824 | tf_op jit(solution)/shard_map/jit(_where)/select_n | solution.py:1912
  549.9 11.3 %convolution_bitcast_fusion = f32[768,2048]{1,0:T(8,128)} fusion(bf16[32,64,768]{2,1,0:T(8,128)(2,1)S(1)} %copy-done.7, bf16[32,64,2048]{2,1,0:T(8,128)(2,1)} %get-tuple-element.85), kind=kOutput, calls=%fused_computation.4 | convolution fusion | flops 6442450944 | bytes 17825792 | tf_op jit(solution)/shard_map/dot_general | solution.py:29
  561.2 5.8 reduce-scatter.2.cloned.1.call-done
  567.1 3.0 fusion.9
  570.8 177.9 %shard_map.270 = (bf16[2,4,256,1280]{3,2,1,0:T(8,128)(2,1)}, f32[144,128]{1,0:T(8,128)}) custom-call(bf16[2,4,256,1280]{3,2,1,0:T(8,128)(2,1)} %bitcast.77, f32[4,144,128]{2,1,0:T(8,128)} %bitcast.82), custom_call_target="tpu_custom_call" | custom-call | tf_op jit(solution)/shard_map/pallas_call | solution.py:987
  748.8 3.4 convert.8
  753.5 4.3 copy.80
  762.2 6.7 convert_element_type.140
  (94 shorter events, 31.7 us)
Async XLA Ops:
  8.0 86.8 %copy-start.10 = (s32[128,8]{0,1:T(8,128)S(1)}, s32[128,8]{0,1:T(8,128)}, u32[]{:S(2)}) copy-start(s32[128,8]{0,1:T(8,128)} %param.18) | copy-start | bytes 12292
  8.0 88.3 %copy-start.1 = (bf16[128,2048]{1,0:T(8,128)(2,1)S(1)}, bf16[128,2048]{1,0:T(8,128)(2,1)}, u32[]{:S(2)}) copy-start(bf16[128,2048]{1,0:T(8,128)(2,1)} %x_ref.3) | copy-start | bytes 1572868
  8.0 92.2 %all-reduce.8.cloned.1.call-start = ((), (), s32[]{:S(2)}) async-start(), calls=%async_computation.4 | async-start | bytes 282624
  14.5 0.7 copy-start.8
  15.2 225.1 %all-gather.4.cloned.1.call-start = ((), (), s32[]{:S(2)}) async-start(), calls=%async_computation.1 | async-start | bytes 17301504 | tf_op jit(solution)/shard_map/all_gather | solution.py:1628
  15.7 551.3 %reduce-scatter.2.cloned.1.call-start = ((), (), s32[]{:S(2)}) async-start(), calls=%async_computation.2 | async-start | bytes 4718592 | tf_op jit(solution)/shard_map/reduce_scatter | solution.py:1914
  144.4 95.0 %copy-start.4 = (bf16[128,2048]{1,0:T(8,128)(2,1)S(1)}, bf16[128,2048]{1,0:T(8,128)(2,1)}, u32[]{:S(2)}) copy-start(bf16[128,2048]{1,0:T(8,128)(2,1)} %get-tuple-element.57.x_ref) | copy-start | bytes 1572868
  144.5 95.6 %copy-start = (f32[128,2048]{1,0:T(8,128)S(1)}, f32[128,2048]{1,0:T(8,128)}, u32[]{:S(2)}) copy-start(f32[128,2048]{1,0:T(8,128)} %get-tuple-element.56) | copy-start | bytes 3145732
  343.4 106.1 %copy-start.5 = (bf16[128,2048]{1,0:T(8,128)(2,1)S(1)}, bf16[128,2048]{1,0:T(8,128)(2,1)}, u32[]{:S(2)}) copy-start(bf16[128,2048]{1,0:T(8,128)(2,1)} %param.31) | copy-start | bytes 1572868
  448.6 1.0 copy-start.3
  471.7 6.4 copy-start.11
  478.1 284.1 %all-gather.6.cloned.1.call-start = ((), (), s32[]{:S(2)}) async-start(), calls=%async_computation.3 | async-start | bytes 4718592 | tf_op jit(solution)/shard_map/all_gather | solution.py:1920
  478.2 56.7 %copy-start.2 = (bf16[128,2048]{1,0:T(8,128)(2,1)S(1)}, bf16[128,2048]{1,0:T(8,128)(2,1)}, u32[]{:S(2)}) copy-start(bf16[128,2048]{1,0:T(8,128)(2,1)} %x_ref.3) | copy-start | bytes 1572868
  539.6 10.4 %copy-start.7 = (bf16[32,64,768]{2,1,0:T(8,128)(2,1)S(1)}, bf16[32,64,768]{2,1,0:T(8,128)(2,1)}, u32[]{:S(2)}) copy-start(bf16[32,64,768]{2,1,0:T(8,128)(2,1)} %get-tuple-element.58.refs_0_) | copy-start | bytes 9437188
  549.9 17.2 %copy-start.6 = (bf16[128,2048]{1,0:T(8,128)(2,1)S(1)}, bf16[128,2048]{1,0:T(8,128)(2,1)}, u32[]{:S(2)}) copy-start(bf16[128,2048]{1,0:T(8,128)(2,1)} %param.31) | copy-start | bytes 1572868
  757.7 2.4 copy-start.9
Sparse Core Ops, SparseCore 0:
  15.3 32.9 all-reduce.7
  478.2 88.8 reduce-scatter.1
  569.2 123.0 all-gather.5
Sparse Core Ops, SparseCore 1:
  18.9 157.7 all-gather.3

commit v6 on v5

--- a/solution.py
+++ b/solution.py
@@ -426,11 +426,14 @@
         out_ref, rows_out, gate_out, up_out, extra_ref = refs[7:12]
         grads_in, pre_in, rows_staged, staged, loaded, stored = refs[12:18]
         refs = refs[18:]
-    outgoing, core_in, total, back, x_in, y_in, z_in = refs[:7]
-    core_sent, core_got, x_sent, x_got, y_sent, y_got, z_sent, z_got = refs[7:]
+    outgoing, core_in, total, back, x_in, y_in, z_in, deep_in, deep_x, deep_y = refs[:10]
+    core_sent, core_got, x_sent, x_got, y_sent, y_got, z_sent, z_got = refs[10:18]
+    deep_sent, deep_got, corner_sent, corner_got = refs[18:]
     z, y, x, c = spot()
     width = out_ref.shape[1]
-    half = out_ref.shape[0] // 2
+    count = out_ref.shape[0]
+    half, thin = count * 3 // 8, count // 8
+    wide = 2 * half
     blocks, _, kept = spread_ref.shape
     y_peer, x_peer, core_peer = (
         where_is(z, 1 - y, x, c),
@@ -600,9 +603,77 @@
 
     def z_copy(q):
         return remote(
-            total.at[q, 3], z_in.at[q - 1], z_sent.at[q - 1], z_got.at[q - 1],
+            total.at[q, 3, pl.ds(0, wide)],
+            z_in.at[q - 1],
+            z_sent.at[q - 1],
+            z_got.at[q - 1],
             where_is(along_z(z, 2 - q % 2), y, x, c),
         )
+
+    def deep_copy(q):
+        return remote(
+            total.at[q, :, pl.ds(wide, 2 * thin)],
+            deep_in.at[q - 1],
+            deep_sent.at[q - 1],
+            deep_got.at[q - 1],
+            far_z if q == 2 else near_z,
+        )
+
+    def corner_copy(over_x, group, side, slot):
+        place, peer = (deep_x, x_peer) if over_x else (deep_y, y_peer)
+        return remote(
+            total.at[0, group, pl.ds(wide + side * thin, thin)],
+            place.at[slot],
+            corner_sent.at[over_x, slot],
+            corner_got.at[over_x, slot],
+            peer,
+        )
+
+    y_corners = [corner_copy(0, 0, 0, 0), corner_copy(0, 2, 0, 1), corner_copy(0, 2, 1, 2)]
+    x_corners = [corner_copy(1, 0, 1, 0), corner_copy(1, 1, 1, 1), corner_copy(1, 1, 0, 2)]
+
+    def add_deep(q, *arrivals):
+        rows = pl.ds(wide, 2 * thin)
+        sums = total[q, :, rows].astype(jnp.float32)
+        for arrival in arrivals:
+            deep_copy(arrival).wait_recv()
+            sums = sums + deep_in[arrival - 1].astype(jnp.float32)
+        total[q, :, rows] = sums.astype(total.dtype)
+
+    def add_corner(group, side, source):
+        rows = pl.ds(wide + side * thin, thin)
+        total[0, group, rows] = (
+            total[0, group, rows].astype(jnp.float32) + source.astype(jnp.float32)
+        ).astype(total.dtype)
+
+    def deep_step(i):
+        @pl.when(i == 0)
+        def _():
+            deep_copy(3).start()
+
+        @pl.when(i == 1)
+        def _():
+            add_deep(2, 3)
+            deep_copy(2).start()
+
+        @pl.when(i == 2)
+        def _():
+            deep_copy(1).start()
+
+        @pl.when(i == 3)
+        def _():
+            add_deep(0, 1, 2)
+            for corner in (*y_corners[:2], *x_corners[:2]):
+                corner.start()
+
+        @pl.when(i == 4)
+        def _():
+            y_corners[0].wait_recv()
+            add_corner(1, 0, deep_y[0])
+            x_corners[2].start()
+            x_corners[0].wait_recv()
+            add_corner(2, 1, deep_x[0])
+            y_corners[2].start()
 
     def add(group, q, side, source):
         rows = pl.ds(side * half, half)
@@ -653,8 +724,9 @@
         @pl.when(q == 2)
         def _():
             z_copy(3).wait_recv()
-            total[2, 3] = (
-                total[2, 3].astype(jnp.float32) + z_in[2].astype(jnp.float32)
+            rows = pl.ds(0, wide)
+            total[2, 3, rows] = (
+                total[2, 3, rows].astype(jnp.float32) + z_in[2].astype(jnp.float32)
             ).astype(total.dtype)
 
         @pl.when(q > 0)
@@ -677,6 +749,8 @@
         def _(turn):
             fill(turn)
 
+        deep_step(i)
+
         @pl.when((i > 0) & (i < 5))
         def _():
             middle(4 - i)
@@ -690,13 +764,27 @@
             store.wait()
     for q in (1, 2):
         z_copy(q).wait_recv()
-    sums = total[0, 3].astype(jnp.float32)
-    sums = sums + z_in[0].astype(jnp.float32) + z_in[1].astype(jnp.float32)
-    out_ref[...] = sums[:, :width]
-    if extended:
-        extra_out[...] = sums[:, width:]
+
+    def finish(start, size, *more):
+        rows = pl.ds(start, size)
+        sums = total[0, 3, rows].astype(jnp.float32)
+        for source in more:
+            sums = sums + source.astype(jnp.float32)
+        out_ref[rows] = sums[:, :width]
+        if extended:
+            extra_out[rows] = sums[:, width:]
+
+    finish(0, wide, z_in[0], z_in[1])
+    for slot in (1, 2):
+        y_corners[slot].wait_recv()
+        x_corners[slot].wait_recv()
+    finish(wide, thin, deep_y[1], deep_x[2])
+    finish(wide + thin, thin, deep_x[1], deep_y[2])
+    for corner in (*y_corners, *x_corners):
+        corner.wait_send()
     for q in range(1, 4):
         z_copy(q).wait_send()
+        deep_copy(q).wait_send()
 
     @pl.loop(0, 4)
     def _(q):
@@ -759,9 +847,12 @@
             pltpu.VMEM((4, 4, count, wide), low),
             pltpu.VMEM((4, 4, count, wide), low),
             pltpu.VMEM((4 * kept, width), low),
-            pltpu.VMEM((3, 4, count // 2, wide), low),
-            pltpu.VMEM((3, 4, count // 2, wide), low),
-            pltpu.VMEM((3, count, wide), low),
+            pltpu.VMEM((3, 4, count * 3 // 8, wide), low),
+            pltpu.VMEM((3, 4, count * 3 // 8, wide), low),
+            pltpu.VMEM((3, count * 3 // 4, wide), low),
+            pltpu.VMEM((3, 4, count // 4, wide), low),
+            pltpu.VMEM((3, count // 8, wide), low),
+            pltpu.VMEM((3, count // 8, wide), low),
             copies(4, 4),
             copies(4, 4),
             copies(3, 4),
@@ -770,6 +861,10 @@
             copies(3, 4),
             copies(3),
             copies(3),
+            copies(3),
+            copies(3),
+            copies(2, 3),
+            copies(2, 3),
         ],
         compiler_params=settings(2 if extended else 8),
     )(spread, *operands)
@@ -778,9 +873,19 @@
 def reduce_kernel(
     cuts,
     parts_ref,
+    own_ref,
     vector_ref,
+    query_out,
+    key_out,
+    value_out,
+    every_out,
+    vector_out,
     sums_out,
-    vector_out,
+    own_sent,
+    own_got,
+    own_side_sent,
+    own_side_got,
+    stored,
     *refs,
 ):
     z, y, x, c = spot()
@@ -871,14 +976,47 @@
         view = place(y, q, which)
         return remote(view, view, side_sent.at[which, q], side_got.at[which, q], y_peer)
 
+    def own_copy(q):
+        view = every_out.at[along_z(z, 2) if q == 3 else z, y]
+        return remote(view, view, own_sent.at[q], own_got.at[q], z_peer(q))
+
+    def own_side(q):
+        view = every_out.at[along_z(z, q), y]
+        return remote(view, view, own_side_sent.at[q], own_side_got.at[q], y_peer)
+
+    def pass_on(q):
+        own_copy(q).wait_recv()
+        if q == 2:
+            own_copy(3).start()
+        own_side(q).start()
+
+    def exports(side, q):
+        zone = along_z(z, q)
+        head, rows = side * 2 + zone // 2, zone % 2
+        made, start = [], 0
+        for i, out in enumerate((query_out, key_out, value_out)):
+            size, depth = out.shape[1] // 4, parts_ref.shape[2]
+            source = sums_out.at[side, zone, :, pl.ds(start, size)]
+            target = out.at[
+                pl.ds(pl.multiple_of(rows * depth, depth), depth),
+                pl.ds(pl.multiple_of(head * size, size), size),
+            ]
+            made.append(pltpu.make_async_copy(source, target, stored.at[side, q, i]))
+            start += size
+        return made
+
     later = range(1, pieces)
+    every_out[z, y] = own_ref[...]
     for j in range(1, 4):
         shard_copy(j).start()
     z_copy(0, 3).start()
+    own_copy(1).start()
+    own_copy(2).start()
     for q in (3, 2, 1, 0):
         for which in later:
             y_copy(which, q).start()
     z_copy(0, 1).start()
+    own_side(0).start()
 
     for j in range(1, 4):
         shard_copy(j).wait_recv()
@@ -916,8 +1054,10 @@
         parts_ref[:, along_z(z, 2), rows(0)].astype(jnp.float32) + first_z[3].astype(jnp.float32)
     ).astype(first_held.dtype)
     z_copy(0, 2).start()
+    pass_on(1)
     for which in later:
         add_y(which, 2)
+    pass_on(2)
     z_copy(0, 1).wait_recv()
     z_copy(0, 2).wait_recv()
     first_z[0] = (
@@ -928,6 +1068,7 @@
     first_y().start()
     for which in later:
         add_y(which, 1)
+    pass_on(3)
     first_y().wait_recv()
     sums = first_z[0, y].astype(jnp.float32) + first_got[...].astype(jnp.float32)
     sums_out[y, z, rows(0)] = sums.astype(sums_out.dtype)
@@ -955,9 +1096,24 @@
         if q == 2:
             back_copy(0, 3).start()
 
-    for which in later:
-        for q in range(4):
+    for q in range(4):
+        for export in exports(y, q):
+            export.start()
+    for q in range(4):
+        for which in later:
             side_copy(which, q).wait_recv()
+        for export in exports(1 - y, q):
+            export.start()
+    for q in range(4):
+        own_side(q).wait_recv()
+    for q in range(4):
+        for side in (y, 1 - y):
+            for export in exports(side, q):
+                export.wait()
+    for q in range(4):
+        own_side(q).wait_send()
+        if q:
+            own_copy(q).wait_send()
     for which in range(pieces):
         for q in range(4):
             if which:
@@ -974,25 +1130,33 @@
         member_copy(j).wait_send()
 
 
-def reduce_over_members(parts, vectors):
+def reduce_over_members(parts, own, vectors, widths):
     low = parts.dtype
     depth, width = parts.shape[2:]
-    early = depth * 3 // 16 // 16 * 16
+    early = depth // 4 // 16 * 16
     half = (depth - early) // 2 // 16 * 16
     cuts = ((0, early), (early, half), (early + half, depth - early - half))
+    anywhere = pl.BlockSpec(memory_space=pl.ANY)
 
     def quarters(*lead):
         return [pltpu.VMEM((*lead, size, width), low) for _, size in cuts[1:]]
 
     return pl.pallas_call(
         functools.partial(reduce_kernel, cuts),
-        out_shape=[
-            jax.ShapeDtypeStruct(parts.shape, low),
+        out_shape=[jax.ShapeDtypeStruct((2 * depth, size), low) for size in widths]
+        + [
+            jax.ShapeDtypeStruct((4, 2, *own.shape), low),
             jax.ShapeDtypeStruct(vectors.shape[1:], vectors.dtype),
         ],
-        in_specs=in_vmem(2),
-        out_specs=in_vmem(2),
+        in_specs=in_vmem(3),
+        out_specs=[anywhere] * 3 + in_vmem(2),
         scratch_shapes=[
+            pltpu.VMEM(parts.shape, low),
+            copies(4),
+            copies(4),
+            copies(4),
+            copies(4),
+            copies(2, 4, 3),
             pltpu.VMEM((early, width), low),
             pltpu.VMEM((2, early, width), low),
             pltpu.VMEM((4, 2, early, width), low),
@@ -1007,7 +1171,7 @@
         + [copies(4)] * 2
         + [copies(8)] * 2,
         compiler_params=settings(3),
-    )(parts, vectors)
+    )(parts, own, vectors)
 
 
 def project_kernel(
@@ -1917,36 +2081,44 @@
                 (joined_grad, vectors, out_sum, gate_w_grad, up_w_grad, down_grad)
             )
         )
-        out_sum = lax.all_gather(out_sum, "exp", axis=0, tiled=True)
-        joined_sum, vectors = reduce_over_members(
-            joined_grad.reshape(2, 4, -1, wide + 2 * narrow), vectors.reshape(shards, rows, 128)
-        )
-        joined_sum, vectors = joined_sum.reshape(joined_grad.shape), vectors.reshape(-1)
+        *joined_sum, out_sum, vectors = reduce_over_members(
+            joined_grad.reshape(2, 4, -1, wide + 2 * narrow),
+            out_sum,
+            vectors.reshape(shards, rows, 128),
+            (shards * wide, shards * narrow, shards * narrow),
+        )
+        out_sum, vectors = out_sum.reshape(w_out.shape), vectors.reshape(-1)
     else:
         out_sum = lax.psum(out_w_grad, "exp")
-        joined_sum = lax.psum(joined_grad, "exp")
+        joined_sum = lax.psum(joined_grad, "exp").astype(jnp.float32)
         vectors = lax.psum(vectors, BOTH)[place]
-    out_sum, joined_sum = out_sum.astype(jnp.float32), joined_sum.astype(jnp.float32)
+    if not dense:
+
+        def gather_heads(part):
+            part = part.transpose(1, 0, 2).reshape(depth, KEY_VALUE_HEADS, copies_of, HEAD_WIDTH)
+            return part.sum(axis=2).reshape(depth, KEY_VALUE_HEADS * HEAD_WIDTH)
+
+        joined_sum = (
+            joined_sum[:, :, :wide].transpose(1, 0, 2).reshape(depth, QUERY_HEADS * HEAD_WIDTH),
+            gather_heads(joined_sum[:, :, wide : wide + narrow]),
+            gather_heads(joined_sum[:, :, wide + narrow :]),
+        )
+    query_sum, key_sum, value_sum = (part.astype(jnp.float32) for part in joined_sum)
     sums, start = [], 0
     for leaf in (w_router, attn_gain, mlp_gain, q_gain, k_gain):
         sums.append(vectors[start : start + leaf.size].reshape(leaf.shape))
         start += leaf.size
 
-    def gather_heads(part):
-        return part.transpose(1, 0, 2).reshape(depth, KEY_VALUE_HEADS, copies_of, HEAD_WIDTH).sum(
-            axis=2
-        ).reshape(depth, KEY_VALUE_HEADS * HEAD_WIDTH)
-
     return (
         layer_out,
         input_grad,
         sums[1],
-        joined_sum[:, :, :wide].transpose(1, 0, 2).reshape(depth, QUERY_HEADS * HEAD_WIDTH),
-        gather_heads(joined_sum[:, :, wide : wide + narrow]),
-        gather_heads(joined_sum[:, :, wide + narrow :]),
+        query_sum,
+        key_sum,
+        value_sum,
         sums[3],
         sums[4],
-        out_sum,
+        out_sum.astype(jnp.float32),
         sums[2],
         sums[0],
         gate_w_grad[None],

time: 786 us -> 767 us (0.976)
  Pallas kernels: 662 us -> 651 us
    pallas_call x1, Pallas kernels: 178 us -> 165 us  [reduce_over_members(): pl.pallas_call(functools.partial(reduce_kernel, cuts), out_shape=[jax.Sha...]
  transfers between devices with their start and end apart: 4 -> 3, of which waited for: 1 -> 1; matrix products, arithmetic and copies ran while one was open for 8% -> 7% of each run, Pallas kernels for 56% -> 34%
where the time goes in v6:
time: 767 us; the launch traced here: 758 us
  Pallas kernels  651 us (85%)
  other arithmetic  39.5 us (5%)
  local copies, waits for them, and re-layouts  28.5 us (4%)
  matrix products  21.4 us (3%)
  between operations  17.1 us (2%)
    pallas_call x2, Pallas kernels, scatter_rows(): pl.pallas_call(functools.partial(scatter_kernel, extended), out_shape=out...  205 us
    pallas_call x1, Pallas kernels, reduce_over_members(): pl.pallas_call(functools.partial(reduce_kernel, cuts), out_shape=[jax.Sha...  165 us
    pallas_call x1, Pallas kernels, gather_experts(): pl.pallas_call(gather_kernel, out_shape=[jax.ShapeDtypeStruct((blocks, ke...  94.9 us
    pallas_call x1, Pallas kernels, project_tokens(): pl.pallas_call(project_kernel, out_shape=[jax.ShapeDtypeStruct((4, count,...  71.6 us
    pallas_call x1, Pallas kernels, heads_back(): pl.pallas_call(heads_kernel, out_shape=[jax.ShapeDtypeStruct((4, depth, o...  52.2 us
    pallas_call x1, Pallas kernels, finish_attention(): pl.pallas_call(functools.partial(finish_kernel, row, sequences), out_shap...  39.9 us
    pallas_call x1, Pallas kernels, branch_back(): pl.pallas_call(branch_kernel, out_shape=[jax.ShapeDtypeStruct((4, count,...  22.4 us
    dot_general x3, matrix products, left_trans(): lax.dot_general(left, right, (((0,), (0,)), ((), ())), preferred_element_...  18.6 us
  transfers between devices with their start and end apart: 3, of which 1 were waited for; matrix products, arithmetic and copies ran while one was open for 7% of the time, Pallas kernels for 34%

profile of v6, /device:TPU:8, one launch (start us, length us, event | category | flops | bytes accessed | tf_op | source)
XLA Modules:
  0.0 758.1 jit_solution(6850604044067053340)
XLA Ops:
  11.0 2.8 concatenate.10
  18.3 71.6 %shard_map.263 = (f32[4,128,1280]{2,1,0:T(8,128)}, bf16[4,128,512]{2,1,0:T(8,128)(2,1)}, s32[32,16,128]{2,1,0:T(8,128)}) custom-call(bf16[128,2048]{1,0:T(8,128)(2,1)} %x_ref.3, s32[16,128]{1,0:T(8,128)} %pad.21.routes_ref, bf16[1,512]{1,0:T(2,128)(2,1)} %broadcast_in_dim.22.gain_ref, bf16[512,4096]{1,0:T(8,128)(2,1)} %query_ref.3, ...), custom_call_target="tpu_custom_call" | custom-call | tf_op jit(solution)/shard_map/pallas_call | solution.py:1351
  94.9 1.4 constant_dynamic-slice_fusion.notes_ref
  97.5 2.6 fusion.2.spread_ref
  104.5 39.9 %shard_map.264 = (f32[128,2048]{1,0:T(8,128)}, bf16[128,2048]{1,0:T(8,128)(2,1)}, bf16[4,128,1024]{2,1,0:T(8,128)(2,1)}, f32[4,8,128,128]{3,2,1,0:T(8,128)}, bf1...) custom-call(f32[4,128,1280]{2,1,0:T(8,128)} %get-tuple-element.57.ra, ...), custom_call_target="tpu_custom_call" | custom-call | tf_op jit(solution)/shard_map/pallas_call | solution.py:1517
  144.5 94.9 %shard_map.265 = (bf16[32,64,2048]{2,1,0:T(8,128)(2,1)}, bf16[32,64,768]{2,1,0:T(8,128)(2,1)}, f32[32,64,768]{2,1,0:T(8,128)}, f32[32,64,768]{2,1,0:T(8,128)}, f32[32,64,128]{2,1,0:T(8,128)}) custom-call(bf16[128,2048]{1,0:T(8,128)(2,1)} %get-tuple-element.60.x_ref, bf16[32,64,128]{2,1,0:T(8,128)(2,1)} %fusion.15.select_ref.refs_3_, ...), custom_call_target="tpu_custom_call" | custom-call | tf_op jit(solution)/shard_map/pallas_call | solution.py:384
  240.2 103.6 %shard_map.266 = (f32[128,2048]{1,0:T(8,128)}, bf16[32,64,2048]{2,1,0:T(8,128)(2,1)}, bf16[32,64,768]{2,1,0:T(8,128)(2,1)}, bf16[32,64,768]{2,1,0:T(8,128)(2,1)}, bf16[32,64,128]{2,1,0:T(8,128)(2,1)}) custom-call(bf16[32,128,64]{2,1,0:T(8,128)(2,1)} %fusion.2.spread_ref, bf16[32,64,768]{2,1,0:T(8,128)(2,1)} %get-tuple-element.61.refs_0_, ...), custom_call_target="tpu_custom_call" | custom-call | tf_op jit(solution)/shard_map/pallas_call | solution.py:839
  343.8 101.2 %shard_map.267 = (f32[128,2048]{1,0:T(8,128)}, f32[128,128]{1,0:T(8,128)}, f32[2048,768]{1,0:T(8,128)}, f32[2048,768]{1,0:T(8,128)}) custom-call(bf16[32,128,64]{2,1,0:T(8,128)(2,1)} %fusion.2.spread_ref, bf16[32,64,768]{2,1,0:T(8,128)(2,1)} %get-tuple-element.66.refs_0_, bf16[32,64,768]{2,1,0:T(8,128)(2,1)} %get-tuple-element.67.refs_1_, ...), custom_call_target="tpu_custom_call" | custom-call | tf_op jit(solution)/shard_map/pallas_call | solution.py:839
  447.2 1.8 multiply_reduce_fusion
  451.1 22.4 %shard_map.268 = (bf16[4,128,1024]{2,1,0:T(8,128)(2,1)}, bf16[4,128,2048]{2,1,0:T(8,128)(2,1)}) custom-call(bf16[128,2048]{1,0:T(8,128)(2,1)} %fusion.28.branch_ref, bf16[1024,2048]{1,0:T(8,128)(2,1)} %weight_ref.3), custom_call_target="tpu_custom_call" | custom-call | tf_op jit(solution)/shard_map/pallas_call | solution.py:1584
  473.5 6.0 bitcast_convert_fusion
  480.2 52.2 %shard_map.269 = (bf16[4,512,1280]{2,1,0:T(8,128)(2,1)}, bf16[4,128,512]{2,1,0:T(8,128)(2,1)}, f32[8,128]{1,0:T(8,128)}) custom-call(bf16[4,128,1024]{2,1,0:T(8,128)(2,1)} %get-tuple-element.75.branch_ref, f32[4,128,1280]{2,1,0:T(8,128)} %get-tuple-element.57.raw_ref, f32[4,8,128,128]{3,2,1,0:T(8,128)} %get-tuple-element.76.probs_ref, ...), custom_call_target="tpu_custom_call" | custom-call | tf_op jit(solution)/shard_map/pallas_call | solution.py:1763
  533.7 1.3 copy.60
  535.0 1.6 copy.61
  537.9 1.3 fusion.31
  539.2 1.7 reshape.164
  541.2 3.2 fusion.9
  544.4 10.7 %broadcast_select_fusion = (f32[2048,768]{1,0:T(8,128)}, f32[2048,768]{1,0:T(8,128)}) fusion(f32[2048,768]{1,0:T(8,128)} %get-tuple-element.87, pred[]{:T(512)} %bitcast.10, f32[2048,768]{1,0:T(8,128)} %get-tuple-element.86), kind=kLoop, calls=%fused_computation.5 | loop fusion | flops 3145728 | bytes 25165824 | tf_op jit(solution)/shard_map/jit(_where)/select_n | solution.py:2076
  555.1 11.3 %convolution_bitcast_fusion = f32[768,2048]{1,0:T(8,128)} fusion(bf16[32,64,768]{2,1,0:T(8,128)(2,1)S(1)} %copy-done.7, bf16[32,64,2048]{2,1,0:T(8,128)(2,1)} %get-tuple-element.88), kind=kOutput, calls=%fused_computation.4 | convolution fusion | flops 6442450944 | bytes 17825792 | tf_op jit(solution)/shard_map/dot_general | solution.py:29
  567.3 165.0 %shard_map.270 = (bf16[512,4096]{1,0:T(8,128)(2,1)}, bf16[512,512]{1,0:T(8,128)(2,1)}, bf16[512,512]{1,0:T(8,128)(2,1)}, bf16[4,2,128,2048]{3,2,1,0:T(8,128)(2,1)}, f32[144,128]{1,0:T(8,128)}) custom-call(bf16[2,4,256,1280]{3,2,1,0:T(8,128)(2,1)} %bitcast.61, bf16[128,2048]{1,0:T(8,128)(2,1)} %reduce-scatter.2.cloned.1.call-done.own_ref, f32[4,144,128]{2,1,0:T(8,128)} %bitcast.64), custom_call_target="tpu_custom_call" | custom-call | tf_op jit(solution)/shard_map/pallas_call | solution.py:1144
  733.1 1.3 slice_bitcast_fusion
  734.5 6.8 bitcast_convert_fusion.1
  741.3 4.5 convert_element_type.144
  748.8 1.3 fusion.29
  (92 shorter events, 30.6 us)
Async XLA Ops:
  8.0 92.2 %all-reduce.8.cloned.1.call-start = ((), (), s32[]{:S(2)}) async-start(), calls=%async_computation.3 | async-start | bytes 282624
  14.4 0.7 copy-start.8
  15.1 225.1 %all-gather.3.cloned.1.call-start = ((), (), s32[]{:S(2)}) async-start(), calls=%async_computation.1 | async-start | bytes 17301504 | tf_op jit(solution)/shard_map/all_gather | solution.py:1792
  15.7 550.9 %reduce-scatter.2.cloned.1.call-start = ((), (), s32[]{:S(2)}) async-start(), calls=%async_computation.2 | async-start | bytes 4718592 | tf_op jit(solution)/shard_map/reduce_scatter | solution.py:2078
  18.3 76.5 %copy-start.11 = (s32[128,8]{0,1:T(8,128)S(1)}, s32[128,8]{0,1:T(8,128)}, u32[]{:S(2)}) copy-start(s32[128,8]{0,1:T(8,128)} %param.18) | copy-start | bytes 12292
  18.3 78.0 %copy-start.1 = (bf16[128,2048]{1,0:T(8,128)(2,1)S(1)}, bf16[128,2048]{1,0:T(8,128)(2,1)}, u32[]{:S(2)}) copy-start(bf16[128,2048]{1,0:T(8,128)(2,1)} %x_ref.3) | copy-start | bytes 1572868
  144.4 94.9 %copy-start.4 = (bf16[128,2048]{1,0:T(8,128)(2,1)S(1)}, bf16[128,2048]{1,0:T(8,128)(2,1)}, u32[]{:S(2)}) copy-start(bf16[128,2048]{1,0:T(8,128)(2,1)} %get-tuple-element.60.x_ref) | copy-start | bytes 1572868
  144.5 95.5 %copy-start = (f32[128,2048]{1,0:T(8,128)S(1)}, f32[128,2048]{1,0:T(8,128)}, u32[]{:S(2)}) copy-start(f32[128,2048]{1,0:T(8,128)} %get-tuple-element.59) | copy-start | bytes 3145732
  445.0 5.0 copy-start.5
  449.0 1.0 copy-start.3
  449.0 24.5 %copy-start.13 = (bf16[4,128,1024]{2,1,0:T(8,128)(2,1)S(1)}, bf16[4,128,1024]{2,1,0:T(8,128)(2,1)}, u32[]{:S(2)}) copy-start(bf16[4,128,1024]{2,1,0:T(8,128)(2,1)} %get-tuple-element.73) | copy-start | bytes 3145732
  479.5 0.7 copy-start.12
  532.4 4.1 copy-start.2
  544.4 10.7 %copy-start.7 = (bf16[32,64,768]{2,1,0:T(8,128)(2,1)S(1)}, bf16[32,64,768]{2,1,0:T(8,128)(2,1)}, u32[]{:S(2)}) copy-start(bf16[32,64,768]{2,1,0:T(8,128)(2,1)} %get-tuple-element.61.refs_0_) | copy-start | bytes 9437188
  734.5 6.8 copy-start.6
  741.3 4.5 copy-start.10
  741.3 5.6 copy-start.9
Sparse Core Ops, SparseCore 0:
  15.2 32.9 all-reduce.7
  479.6 86.8 reduce-scatter.1
Sparse Core Ops, SparseCore 1:
  18.8 157.7 all-gather.2

commit v7 on v6

--- a/solution.py
+++ b/solution.py
@@ -176,9 +176,9 @@
 
 
 def gather_kernel(
+    topk,
     x_ref,
-    select_ref,
-    named_ref,
+    notes_ref,
     gate_hbm,
     up_hbm,
     router_ref,
@@ -187,6 +187,8 @@
     gate_out,
     up_out,
     share_out,
+    select_out,
+    spread_out,
     held,
     gate_ref,
     up_ref,
@@ -200,10 +202,15 @@
     to_y,
     to_x,
     to_core,
+    corners,
+    deep_z,
+    deep_core,
 ):
     z, y, x, c = spot()
-    half = x_ref.shape[0] // 2
-    kept = select_ref.shape[1]
+    count = x_ref.shape[0]
+    half, thin = count * 3 // 8, count // 8
+    cuts = ((0, half), (half, half), (2 * half, thin), (2 * half + thin, thin), (2 * half, 2 * thin))
+    kept = select_out.shape[1]
     y_peer, x_peer, core_peer = (
         where_is(z, 1 - y, x, c),
         where_is(z, y, 1 - x, c),
@@ -222,8 +229,8 @@
     mine = number(z, y, x, c)
 
     def copy(block, part, sem, peer):
-        view = held.at[block, pl.ds(part * half, half)]
-        return remote(view, view, sem, arrive.at[block, part], peer)
+        view = held.at[block, pl.ds(*cuts[part])]
+        return remote(view, view, sem, arrive.at[block, 2 if part == 4 else part], peer)
 
     def arrived(block, part):
         copy(block, part, to_core.at[0, 0, 0], core_peer).wait_recv()
@@ -248,6 +255,29 @@
             for i, (source, target) in enumerate(made)
         ]
 
+    def choose(block):
+        notes = notes_ref[block]
+        own = jnp.zeros((1, count), jnp.float32)
+        lines = lax.broadcasted_iota(jnp.int32, (128, count), 0)
+        names = jnp.zeros((128, count), jnp.float32)
+        for k in range(topk):
+            line = notes[k : k + 1]
+            own = own + jnp.where(line == mine, 1.0, 0.0)
+            names = names + jnp.where(lines == line, 1.0, 0.0)
+        before = lax.broadcasted_iota(jnp.int32, (count, count), 0)
+        before = before < lax.broadcasted_iota(jnp.int32, (count, count), 1)
+        rank = jnp.dot(
+            jnp.broadcast_to(own, (8, count)).astype(x_ref.dtype),
+            jnp.where(before, 1.0, 0.0).astype(x_ref.dtype),
+            preferred_element_type=jnp.float32,
+        )[:1]
+        places = lax.broadcasted_iota(jnp.int32, (kept, count), 0).astype(jnp.float32)
+        chosen = jnp.where((rank == places) & (own > 0), 1.0, 0.0)
+        spread_out[block] = jnp.transpose(chosen).astype(spread_out.dtype)
+        chosen = chosen.astype(select_out.dtype)
+        select_out[block] = chosen
+        return chosen, right_transposed(chosen, names.astype(chosen.dtype))
+
     def work(q, slot):
         core = 1 - c if slot else c
         blocks = [block_of(q, *combo, core) for combo in combos]
@@ -257,10 +287,11 @@
             for store in stores(slot, [block_of(q - 1, *combo, core) for combo in combos]):
                 store.wait()
 
+        named = []
         for k in range(4):
-            rows = jnp.dot(
-                select_ref[blocks[k]], held[blocks[k]], preferred_element_type=jnp.float32
-            )
+            chosen, names = choose(blocks[k])
+            named.append(names)
+            rows = jnp.dot(chosen, held[blocks[k]], preferred_element_type=jnp.float32)
             picked[slot, k * kept : (k + 1) * kept] = rows.astype(picked.dtype)
         rows = picked[slot]
         gate_pre = jnp.dot(rows, gate_ref[...], preferred_element_type=jnp.float32)
@@ -273,7 +304,7 @@
         for k in range(4):
             part = slice(k * kept, (k + 1) * kept)
             block = blocks[k]
-            masked = jnp.where(named_ref[block].astype(jnp.float32) > 0, logits[part], MASKED)
+            masked = jnp.where(named[k] > 0, logits[part], MASKED)
             lifted = jnp.exp(masked - jnp.max(masked, axis=1, keepdims=True))
             lanes = lax.broadcasted_iota(jnp.int32, lifted.shape, 1)
             share = jnp.sum(jnp.where(lanes == mine, lifted, 0.0), axis=1, keepdims=True)
@@ -323,19 +354,58 @@
     def others(q):
         for combo in combos:
             block = block_of(q, *combo, 1 - c)
-            arrived(block, 0)
-            arrived(block, 1)
+            for part in (0, 1, 4):
+                arrived(block, part)
+
+    beside_x, beside_y, across = (block_of(0, *combo, c) for combo in combos[1:])
+
+    def corner(i):
+        block = (mine, mine, mine, mine, beside_x, beside_y)[i]
+        part, peer = ((2, x_peer), (3, y_peer), (2, y_peer), (3, x_peer), (2, y_peer), (3, x_peer))[i]
+        return copy(block, part, corners.at[i], peer)
+
+    def deep_copy(kind, i, block):
+        return copy(block, 4, deep_z.at[kind, i], far_z if kind == 1 else near_z)
+
+    def deep_core_copy(q, i, block):
+        return copy(block, 4, deep_core.at[q, i], core_peer)
+
+    def deep_first():
+        arrived(beside_x, 3)
+        arrived(beside_y, 2)
+        arrived(across, 2)
+        arrived(across, 3)
+        for i, combo in enumerate(combos):
+            block = block_of(0, *combo, c)
+            deep_copy(0, i, block).start()
+            deep_copy(1, i, block).start()
+            deep_core_copy(0, i, block).start()
+
+    def deep_next(q):
+        for i, combo in enumerate(combos):
+            block = block_of(q, *combo, c)
+            arrived(block, 4)
+            if q == 2:
+                deep_copy(2, i, block).start()
+            deep_core_copy(q, i, block).start()
 
     held[mine] = x_ref[...]
     for part in range(2):
         copy(mine, part, to_z.at[0, part], near_z).start()
     for part in range(2):
         copy(mine, part, to_z.at[1, part], far_z).start()
+    for i in range(4):
+        corner(i).start()
     forward(0)
     for load in loads:
         load.wait()
+    arrived(beside_x, 2)
+    corner(4).start()
+    arrived(beside_y, 3)
+    corner(5).start()
     forward(1)
     second(0)
+    deep_first()
     forward(2)
     second(1)
 
@@ -349,11 +419,14 @@
         @pl.when(q == 0)
         def _():
             forward(3)
+            deep_next(1)
             second(2)
+            deep_next(2)
 
         @pl.when(q == 1)
         def _():
             second(3)
+            deep_next(3)
 
     for slot in range(2):
         core = 1 - c if slot else c
@@ -364,8 +437,16 @@
         copy(mine, part, to_z.at[1, part], far_z).wait_send()
         copy(mine, part, to_z.at[2, part], near_z).wait_send()
 
+    for i in range(6):
+        corner(i).wait_send()
+    for i in range(4):
+        for kind in range(3):
+            deep_copy(kind, i, mine).wait_send()
+
     @pl.loop(0, 4)
     def _(q):
+        for i in range(4):
+            deep_core_copy(q, i, mine).wait_send()
         for i in range(3):
             copy(mine, 0, to_y.at[i, q], y_peer).wait_send()
             copy(mine, 0, to_x.at[i, q], x_peer).wait_send()
@@ -374,24 +455,26 @@
                 copy(mine, part, to_core.at[i, part, q], core_peer).wait_send()
 
 
-def gather_experts(rows, select, named, gate_w, up_w, router):
+def gather_experts(rows, notes, topk, kept, gate_w, up_w, router):
     count, width = rows.shape
-    blocks, kept = select.shape[:2]
+    blocks = notes.shape[0]
     hidden = gate_w.shape[1]
     low = rows.dtype
     anywhere = pl.BlockSpec(memory_space=pl.ANY)
     vmem = pl.BlockSpec(memory_space=pltpu.VMEM)
     return pl.pallas_call(
-        gather_kernel,
+        functools.partial(gather_kernel, topk),
         out_shape=[
             jax.ShapeDtypeStruct((blocks, kept, width), low),
             jax.ShapeDtypeStruct((blocks, kept, hidden), low),
             jax.ShapeDtypeStruct((blocks, kept, hidden), jnp.float32),
             jax.ShapeDtypeStruct((blocks, kept, hidden), jnp.float32),
             jax.ShapeDtypeStruct((blocks, kept, 128), jnp.float32),
+            jax.ShapeDtypeStruct((blocks, kept, count), low),
+            jax.ShapeDtypeStruct((blocks, count, kept), low),
         ],
-        in_specs=[vmem, vmem, vmem, anywhere, anywhere, vmem],
-        out_specs=[anywhere] * 4 + [vmem],
+        in_specs=[vmem, vmem, anywhere, anywhere, vmem],
+        out_specs=[anywhere] * 4 + [vmem] * 3,
         scratch_shapes=[
             pltpu.VMEM((blocks, count, width), low),
             pltpu.VMEM(gate_w.shape, low),
@@ -401,14 +484,17 @@
             pltpu.VMEM((2, 2, 4 * kept, hidden), jnp.float32),
             copies(2),
             copies(2, 16),
-            copies(blocks, 2),
+            copies(blocks, 4),
             copies(3, 2),
             copies(3, 4),
             copies(3, 4),
             copies(4, 2, 4),
+            copies(6),
+            copies(3, 4),
+            copies(4, 4),
         ],
         compiler_params=settings(1),
-    )(rows, select, named, gate_w, up_w, router)
+    )(rows, notes, gate_w, up_w, router)
 
 
 def scatter_kernel(
@@ -1389,12 +1475,6 @@
     return jnp.where(lanes < HEAD_WIDTH // 2, -sine, sine)
 
 
-def nt_product(left, right):
-    return lax.dot_general(
-        left, right, (((1,), (1,)), ((), ())), preferred_element_type=jnp.float32
-    )
-
-
 def finish_kernel(
     row,
     sequences,
@@ -1466,7 +1546,7 @@
             columns = slice(head * HEAD_WIDTH, (head + 1) * HEAD_WIDTH)
             query = normal(raw_ref[block, :, columns], query_gain_ref[...])
             query_out[block, :, columns] = query
-            scores = nt_product(query, key) * HEAD_WIDTH ** (-0.5)
+            scores = right_transposed(query, key) * HEAD_WIDTH ** (-0.5)
             scores = jnp.where(allowed, scores, MASKED)
             raised = jnp.exp(scores - jnp.max(scores, axis=1, keepdims=True))
             probs = raised / jnp.sum(raised, axis=1, keepdims=True)
@@ -1483,24 +1563,32 @@
     def x_copy():
         return remote(across_x, x_sums, x_sent, x_got, x_peer)
 
-    def partial(side, core):
-        block = side * 2 + core
+    @pl.loop(0, 4)
+    def _(i):
+        block = (1 - x + i // 2) % 2 * 2 + (1 - c + i) % 2
+        far = 1 - i // 2
         attend(block)
-        return jnp.dot(attended_out[block], weight_ref[...], preferred_element_type=jnp.float32)
-
-    outgoing[1] = partial(1 - x, 1 - c).astype(outgoing.dtype)
-    core_copy(1).start()
-    sums = partial(1 - x, c)
-    core_copy(1).wait_recv()
-    across_x[...] = (sums + core_in[1].astype(jnp.float32)).astype(across_x.dtype)
-    x_copy().start()
-    outgoing[0] = partial(x, 1 - c).astype(outgoing.dtype)
-    core_copy(0).start()
-    sums = partial(x, c) + x_ref[...].astype(jnp.float32)
-    core_copy(0).wait_recv()
-    sums = sums + core_in[0].astype(jnp.float32)
+        product = jnp.dot(attended_out[block], weight_ref[...], preferred_element_type=jnp.float32)
+
+        @pl.when(i % 2 == 0)
+        def _():
+            outgoing[far] = product.astype(outgoing.dtype)
+            core_copy(far).start()
+
+        @pl.when(i == 1)
+        def _():
+            core_copy(1).wait_recv()
+            across_x[...] = (product + core_in[1].astype(jnp.float32)).astype(across_x.dtype)
+            x_copy().start()
+
+        @pl.when(i == 3)
+        def _():
+            core_copy(0).wait_recv()
+            sums = product + x_ref[...].astype(jnp.float32)
+            middle_out[...] = sums + core_in[0].astype(jnp.float32)
+
     x_copy().wait_recv()
-    middle = sums + x_sums[...].astype(jnp.float32)
+    middle = middle_out[...] + x_sums[...].astype(jnp.float32)
     middle_out[...] = middle
     scale = lax.rsqrt(jnp.mean(middle * middle, axis=1, keepdims=True) + EPSILON)
     normed_out[...] = (middle * scale * gain_ref[...]).astype(normed_out.dtype)
@@ -1548,34 +1636,41 @@
     z, y, x, c = spot()
     mine = x * 2 + c
     core_peer, x_peer = where_is(z, y, x, 1 - c), where_is(z, y, 1 - x, c)
+    half = branch_ref.shape[0] // 2
     greet([core_peer, x_peer])
     every_out[mine] = branch_ref[...]
 
-    def x_copy():
-        return remote(branch_ref, every_out.at[mine], x_sent, x_got, x_peer)
-
-    def core_copy(far):
-        place = (1 - x if far else x) * 2 + c
+    def x_copy(part):
+        rows = pl.ds(part * half, half)
         return remote(
-            every_out.at[place], every_out.at[place], core_sent.at[far], core_got.at[far], core_peer
-        )
+            branch_ref.at[rows], every_out.at[mine, rows], x_sent.at[part], x_got.at[part], x_peer
+        )
+
+    def core_copy(far, part):
+        view = every_out.at[(1 - x if far else x) * 2 + c, pl.ds(part * half, half)]
+        return remote(view, view, core_sent.at[far, part], core_got.at[far, part], core_peer)
 
     def back(place):
         grad_out[place] = right_transposed(every_out[place], weight_ref[...]).astype(grad_out.dtype)
 
-    x_copy().start()
-    core_copy(0).start()
+    for part in range(2):
+        x_copy(part).start()
+        core_copy(0, part).start()
     back(mine)
-    core_copy(0).wait_recv()
+    for part in range(2):
+        core_copy(0, part).wait_recv()
     back(x * 2 + 1 - c)
-    x_copy().wait_recv()
-    core_copy(1).start()
+    for part in range(2):
+        x_copy(part).wait_recv()
+        core_copy(1, part).start()
     back((1 - x) * 2 + c)
-    core_copy(1).wait_recv()
+    for part in range(2):
+        core_copy(1, part).wait_recv()
     back((1 - x) * 2 + 1 - c)
-    x_copy().wait_send()
-    core_copy(0).wait_send()
-    core_copy(1).wait_send()
+    for part in range(2):
+        x_copy(part).wait_send()
+        core_copy(0, part).wait_send()
+        core_copy(1, part).wait_send()
 
 
 def branch_back(branch, w_out):
@@ -1589,7 +1684,7 @@
         ],
         in_specs=in_vmem(2),
         out_specs=in_vmem(2),
-        scratch_shapes=[copies(), copies(), copies(2), copies(2)],
+        scratch_shapes=[copies(2), copies(2), copies(2, 2), copies(2, 2)],
         compiler_params=settings(6),
     )(branch, w_out)
 
@@ -1613,6 +1708,7 @@
     gains_out,
     every,
     outgoing,
+    total,
     x_sent,
     x_got,
     core_sent,
@@ -1626,7 +1722,6 @@
     peers = [(member, (shard + j) % 4) for j in range(1, 4)]
     greet(peers)
     rows = every.shape[1]
-    half = rows // 2
     count = rows // 4
     depth = hidden_ref.shape[1]
     wide, narrow = query_ref.shape[1] // 4, key_ref.shape[1] // 4
@@ -1654,7 +1749,7 @@
             columns = slice(head * HEAD_WIDTH, (head + 1) * HEAD_WIDTH)
             grads = branch_ref[block, :, columns]
             probs = probs_ref[block, head]
-            prob_grad = nt_product(grads, value)
+            prob_grad = right_transposed(grads, value)
             term = left_trans(probs.astype(low), grads)
             value_grad = term if value_grad is None else value_grad + term
             balance = jnp.sum(probs * prob_grad, axis=1, keepdims=True)
@@ -1675,22 +1770,20 @@
         every[shard, place, wide + narrow :] = value_grad.astype(low)
 
     def x_copy(part):
-        view = every.at[shard, pl.ds(part * half, half)]
+        view = every.at[shard, pl.ds(part * count, count)]
         return remote(view, view, x_sent.at[part], x_got.at[part], x_peer)
 
     def core_copy(far, part):
-        view = every.at[(1 - x if far else x) * 2 + c, pl.ds(part * half, half)]
+        view = every.at[(1 - x if far else x) * 2 + c, pl.ds(part * count, count)]
         return remote(view, view, core_sent.at[far, part], core_got.at[far, part], core_peer)
 
     gains_out[...] = jnp.zeros_like(gains_out)
-    for part in range(2):
-
-        @pl.loop(part * 2, part * 2 + 2)
-        def _(block):
-            attention_back(block)
-
-        x_copy(part).start()
-        core_copy(0, part).start()
+
+    @pl.loop(0, 4)
+    def _(block):
+        attention_back(block)
+        x_copy(block).start()
+        core_copy(0, block).start()
 
     def weigh(place):
         weight_out[place] = left_trans(hidden_ref[...], every[place]).astype(weight_out.dtype)
@@ -1708,21 +1801,41 @@
             sums = term if sums is None else sums + term
         return sums
 
-    total = back(shard)
-    weigh(shard)
-    near = x * 2 + 1 - c
-    for part in range(2):
-        core_copy(0, part).wait_recv()
-    total = total + back(near)
-    weigh(near)
-    for part in range(2):
-        x_copy(part).wait_recv()
-        core_copy(1, part).start()
-    far = (1 - x) * 2 + c
-    total = total + back(far)
-    for part in range(2):
-        core_copy(1, part).wait_recv()
-    total = total + back((1 - x) * 2 + 1 - c)
+    def place_of(i):
+        return (x + i // 2) % 2 * 2 + (c + i) % 2
+
+    @pl.loop(0, 4)
+    def _(i):
+        @pl.when(i == 1)
+        def _():
+            for part in range(4):
+                core_copy(0, part).wait_recv()
+
+        @pl.when(i == 2)
+        def _():
+            for part in range(4):
+                x_copy(part).wait_recv()
+                core_copy(1, part).start()
+
+        @pl.when(i == 3)
+        def _():
+            for part in range(4):
+                core_copy(1, part).wait_recv()
+
+        sums = back(place_of(i))
+
+        @pl.when(i == 0)
+        def _():
+            total[...] = sums
+
+        @pl.when(i > 0)
+        def _():
+            total[...] += sums
+
+        @pl.when(i < 2)
+        def _():
+            weigh(place_of(i))
+
     for owner in range(4):
         outgoing[owner] = total[owner * count : (owner + 1) * count].astype(outgoing.dtype)
 
@@ -1739,8 +1852,11 @@
     for j in range(1, 4):
         back_copy(j).start()
     first_out[shard] = outgoing[shard]
-    weigh(far)
-    weigh((1 - x) * 2 + 1 - c)
+
+    @pl.loop(2, 4)
+    def _(i):
+        weigh(place_of(i))
+
     for j in range(1, 4):
         place = (shard + j) % 4
         remote(
@@ -1748,7 +1864,7 @@
         ).wait_recv()
     for j in range(1, 4):
         back_copy(j).wait_send()
-    for part in range(2):
+    for part in range(4):
         x_copy(part).wait_send()
         for far in range(2):
             core_copy(far, part).wait_send()
@@ -1772,10 +1888,11 @@
         scratch_shapes=[
             pltpu.VMEM((4, rows, own), low),
             pltpu.VMEM((4, rows // 4, depth), low),
-            copies(2),
-            copies(2),
-            copies(2, 2),
-            copies(2, 2),
+            pltpu.VMEM((rows, depth), jnp.float32),
+            copies(4),
+            copies(4),
+            copies(2, 4),
+            copies(2, 4),
             copies(4),
             copies(4),
         ],
@@ -1787,22 +1904,10 @@
     gate_w, up_w, down_w = weights
     token_count, topk = routes.shape
     experts = router.shape[1]
-    mine = lax.axis_index("exp") * lax.axis_size("fsdp") + lax.axis_index("fsdp")
-    all_routes = notes[:, :topk]
     all_grads = lax.all_gather(cotangent, BOTH, axis=0, tiled=True)
-    columns = jnp.arange(experts, dtype=jnp.int32)
-    named = jnp.any(all_routes[:, :, None, :] == columns[None, None, :, None], axis=1)
-    own = jnp.any(all_routes == mine, axis=1)
-    before = jnp.tril(jnp.ones((token_count, token_count), jnp.bfloat16), -1)
-    rank = right_transposed(own.astype(jnp.bfloat16), before).astype(jnp.int32)
-    places = jnp.arange(capacity, dtype=jnp.int32)
-    select = (own[:, None, :] & (rank[:, None, :] == places[None, :, None])).astype(jnp.bfloat16)
-    spread = (own[:, :, None] & (rank[:, :, None] == places[None, None, :])).astype(jnp.bfloat16)
-    named_rows = contract("bcj,bej->bce", select, named.astype(jnp.bfloat16))
-    named_rows = jnp.pad(named_rows.astype(jnp.bfloat16), ((0, 0), (0, 0), (0, 128 - experts)))
     padded = jnp.pad(router, ((0, 0), (0, 128 - experts)))
-    arrived, active, gate_pre, up_pre, share = gather_experts(
-        normed, select, named_rows, gate_w, up_w, padded
+    arrived, active, gate_pre, up_pre, share, select, spread = gather_experts(
+        normed, notes, topk, capacity, gate_w, up_w, padded
     )
     mixed, out_rows, gate_pre_grad, up_pre_grad, extra = scatter_rows(
         spread,
@@ -1822,6 +1927,7 @@
         return rows.reshape(experts * capacity, rows.shape[2])
 
     weight_grads = (gate_w_grad, up_w_grad, left_trans(flat(active), flat(out_rows)))
+    columns = jnp.arange(experts, dtype=jnp.int32)
     gate_grad = back[:, :experts] + back[:, experts : 2 * experts]
     picks = jnp.any(routes[:, :, None] == columns[None, None, :], axis=1)
     gates = jax.nn.softmax(jnp.where(picks, matrix_product(normed, router), MASKED), axis=1)

time: 767 us -> 756 us (0.986)
    pallas_call x2, Pallas kernels: 205 us -> 194 us  [scatter_rows(): pl.pallas_call(functools.partial(scatter_kernel, extended), out_shape=out...]
  transfers between devices with their start and end apart: 3 -> 3, of which waited for: 1 -> 1; matrix products, arithmetic and copies ran while one was open for 7% -> 6% of each run, Pallas kernels for 34% -> 35%
where the time goes in v7:
time: 756 us; the launch traced here: 747 us
  Pallas kernels  645 us (85%)
  other arithmetic  34.2 us (5%)
  local copies, waits for them, and re-layouts  27.5 us (4%)
  matrix products  21.6 us (3%)
  between operations  17 us (2%)
    pallas_call x2, Pallas kernels, scatter_rows(): pl.pallas_call(functools.partial(scatter_kernel, extended), out_shape=out...  194 us
    pallas_call x1, Pallas kernels, reduce_over_members(): pl.pallas_call(functools.partial(reduce_kernel, cuts), out_shape=[jax.Sha...  166 us
    pallas_call x1, Pallas kernels, gather_experts(): pl.pallas_call(functools.partial(gather_kernel, topk), out_shape=[jax.Sha...  102 us
    pallas_call x1, Pallas kernels, project_tokens(): pl.pallas_call(project_kernel, out_shape=[jax.ShapeDtypeStruct((4, count,...  71.4 us
    pallas_call x1, Pallas kernels, heads_back(): pl.pallas_call(heads_kernel, out_shape=[jax.ShapeDtypeStruct((4, depth, o...  49.9 us
    pallas_call x1, Pallas kernels, finish_attention(): pl.pallas_call(functools.partial(finish_kernel, row, sequences), out_shap...  39.7 us
    pallas_call x1, Pallas kernels, branch_back(): pl.pallas_call(branch_kernel, out_shape=[jax.ShapeDtypeStruct((4, count,...  21.9 us
    dot_general x3, matrix products, left_trans(): lax.dot_general(left, right, (((0,), (0,)), ((), ())), preferred_element_...  19.4 us
  transfers between devices with their start and end apart: 3, of which 1 were waited for; matrix products, arithmetic and copies ran while one was open for 6% of the time, Pallas kernels for 35%

profile of v7, /device:TPU:8, one launch (start us, length us, event | category | flops | bytes accessed | tf_op | source)
XLA Modules:
  0.0 746.8 jit_solution(5594415363382986237)
XLA Ops:
  11.0 2.8 concatenate.10
  15.8 1.3 broadcast_in_dim.16.gain_ref
  19.2 71.4 %shard_map.263 = (f32[4,128,1280]{2,1,0:T(8,128)}, bf16[4,128,512]{2,1,0:T(8,128)(2,1)}, s32[32,16,128]{2,1,0:T(8,128)}) custom-call(bf16[128,2048]{1,0:T(8,128)(2,1)} %x_ref.3, s32[16,128]{1,0:T(8,128)} %pad.17.routes_ref, bf16[1,512]{1,0:T(2,128)(2,1)} %broadcast_in_dim.16.gain_ref, bf16[512,4096]{1,0:T(8,128)(2,1)} %query_ref.3, ...), custom_call_target="tpu_custom_call" | custom-call | tf_op jit(solution)/shard_map/pallas_call | solution.py:1437
  90.6 1.4 constant_dynamic-slice_fusion.notes_ref
  96.4 39.7 %shard_map.264 = (f32[128,2048]{1,0:T(8,128)}, bf16[128,2048]{1,0:T(8,128)(2,1)}, bf16[4,128,1024]{2,1,0:T(8,128)(2,1)}, f32[4,8,128,128]{3,2,1,0:T(8,128)}, bf1...) custom-call(f32[4,128,1280]{2,1,0:T(8,128)} %get-tuple-element.59.ra, ...), custom_call_target="tpu_custom_call" | custom-call | tf_op jit(solution)/shard_map/pallas_call | solution.py:1605
  136.2 102.4 %shard_map.265 = (bf16[32,64,2048]{2,1,0:T(8,128)(2,1)}, bf16[32,64,768]{2,1,0:T(8,128)(2,1)}, f32[32,64,768]{2,1,0:T(8,128)}, f32[32,64,768]{2,1,0:T(8,128)}, f...) custom-call(bf16[128,2048]{1,0:T(8,128)(2,1)} %get-tuple-element.62.x_ref, ...), custom_call_target="tpu_custom_call" | custom-call | tf_op jit(solution)/shard_map/pallas_call | solution.py:465
  239.3 92.0 %shard_map.266 = (f32[128,2048]{1,0:T(8,128)}, bf16[32,64,2048]{2,1,0:T(8,128)(2,1)}, bf16[32,64,768]{2,1,0:T(8,128)(2,1)}, bf16[32,64,768]{2,1,0:T(8,128)(2,1)}, bf16[32,64,128]{2,1,0:T(8,128)(2,1)}) custom-call(bf16[32,128,64]{2,1,0:T(8,128)(2,1)} %get-tuple-element.63.spread_ref, bf16[32,64,768]{2,1,0:T(8,128)(2,1)} %get-tuple-element.64.refs_0_, ...), custom_call_target="tpu_custom_call" | custom-call | tf_op jit(solution)/shard_map/pallas_call | solution.py:925
  331.4 101.7 %shard_map.267 = (f32[128,2048]{1,0:T(8,128)}, f32[128,128]{1,0:T(8,128)}, f32[2048,768]{1,0:T(8,128)}, f32[2048,768]{1,0:T(8,128)}) custom-call(bf16[32,128,64]{2,1,0:T(8,128)(2,1)} %get-tuple-element.63.spread_ref, bf16[32,64,768]{2,1,0:T(8,128)(2,1)} %get-tuple-element.70.refs_0_, bf16[32,64,768]{2,1,0:T(8,128)(2,1)} %get-tuple-element.71.refs_1_, ...), custom_call_target="tpu_custom_call" | custom-call | tf_op jit(solution)/shard_map/pallas_call | solution.py:925
  435.3 1.9 multiply_reduce_fusion
  439.3 21.9 %shard_map.268 = (bf16[4,128,1024]{2,1,0:T(8,128)(2,1)}, bf16[4,128,2048]{2,1,0:T(8,128)(2,1)}) custom-call(bf16[128,2048]{1,0:T(8,128)(2,1)} %fusion.13.branch_ref, bf16[1024,2048]{1,0:T(8,128)(2,1)} %weight_ref.3), custom_call_target="tpu_custom_call" | custom-call | tf_op jit(solution)/shard_map/pallas_call | solution.py:1679
  461.3 6.0 bitcast_convert_fusion
  467.3 49.9 %shard_map.269 = (bf16[4,512,1280]{2,1,0:T(8,128)(2,1)}, bf16[4,128,512]{2,1,0:T(8,128)(2,1)}, f32[8,128]{1,0:T(8,128)}) custom-call(bf16[4,128,1024]{2,1,0:T(8,128)(2,1)} %get-tuple-element.79.branch_ref, f32[4,128,1280]{2,1,0:T(8,128)} %get-tuple-element.59.raw_ref, f32[4,8,128,128]{3,2,1,0:T(8,128)} %get-tuple-element.80.probs_ref, ...), custom_call_target="tpu_custom_call" | custom-call | tf_op jit(solution)/shard_map/pallas_call | solution.py:1879
  518.5 1.3 copy.47
  519.8 1.6 copy.48
  522.7 2.3 fusion.16
  525.1 1.7 reshape.159
  528.7 3.0 fusion.6
  531.7 10.7 %broadcast_select_fusion = (f32[2048,768]{1,0:T(8,128)}, f32[2048,768]{1,0:T(8,128)}) fusion(f32[2048,768]{1,0:T(8,128)} %get-tuple-element.91, pred[]{:T(512)} %bitcast.10, f32[2048,768]{1,0:T(8,128)} %get-tuple-element.90), kind=kLoop, calls=%fused_computation.3 | loop fusion | flops 3145728 | bytes 25165824 | tf_op jit(solution)/shard_map/jit(_where)/select_n | solution.py:2182
  542.4 11.0 %convolution_bitcast_fusion = f32[768,2048]{1,0:T(8,128)} fusion(bf16[32,64,768]{2,1,0:T(8,128)(2,1)S(1)} %copy-done.7, bf16[32,64,2048]{2,1,0:T(8,128)(2,1)} %get-tuple-element.92), kind=kOutput, calls=%fused_computation.2 | convolution fusion | flops 6442450944 | bytes 17825792 | tf_op jit(solution)/shard_map/dot_general | solution.py:29
  555.2 165.9 %shard_map.270 = (bf16[512,4096]{1,0:T(8,128)(2,1)}, bf16[512,512]{1,0:T(8,128)(2,1)}, bf16[512,512]{1,0:T(8,128)(2,1)}, bf16[4,2,128,2048]{3,2,1,0:T(8,128)(2,1)}, f32[144,128]{1,0:T(8,128)}) custom-call(bf16[2,4,256,1280]{3,2,1,0:T(8,128)(2,1)} %bitcast.59, bf16[128,2048]{1,0:T(8,128)(2,1)} %reduce-scatter.2.cloned.1.call-done.own_ref, f32[4,144,128]{2,1,0:T(8,128)} %bitcast.62), custom_call_target="tpu_custom_call" | custom-call | tf_op jit(solution)/shard_map/pallas_call | solution.py:1230
  721.9 1.3 slice_bitcast_fusion
  723.3 6.8 bitcast_convert_fusion.1
  730.1 4.5 convert_element_type.124
  737.6 1.3 fusion.14
  (80 shorter events, 26.0 us)
Async XLA Ops:
  8.0 83.9 %copy-start.1 = (bf16[128,2048]{1,0:T(8,128)(2,1)S(1)}, bf16[128,2048]{1,0:T(8,128)(2,1)}, u32[]{:S(2)}) copy-start(bf16[128,2048]{1,0:T(8,128)(2,1)} %x_ref.3) | copy-start | bytes 1572868
  8.0 84.1 %all-reduce.7.cloned.1.call-start = ((), (), s32[]{:S(2)}) async-start(), calls=%async_computation.3 | async-start | bytes 282624
  14.5 0.7 copy-start.8
  15.1 224.2 %all-gather.3.cloned.1.call-start = ((), (), s32[]{:S(2)}) async-start(), calls=%async_computation.1 | async-start | bytes 17301504 | tf_op jit(solution)/shard_map/all_gather | solution.py:1907
  15.7 538.8 %reduce-scatter.2.cloned.1.call-start = ((), (), s32[]{:S(2)}) async-start(), calls=%async_computation.2 | async-start | bytes 4718592 | tf_op jit(solution)/shard_map/reduce_scatter | solution.py:2184
  136.2 102.4 %copy-start.5 = (bf16[128,2048]{1,0:T(8,128)(2,1)S(1)}, bf16[128,2048]{1,0:T(8,128)(2,1)}, u32[]{:S(2)}) copy-start(bf16[128,2048]{1,0:T(8,128)(2,1)} %get-tuple-element.62.x_ref) | copy-start | bytes 1572868
  136.2 102.9 %copy-start = (f32[128,2048]{1,0:T(8,128)S(1)}, f32[128,2048]{1,0:T(8,128)}, u32[]{:S(2)}) copy-start(f32[128,2048]{1,0:T(8,128)} %get-tuple-element.61) | copy-start | bytes 3145732
  331.4 106.8 %copy-start.4 = (bf16[128,2048]{1,0:T(8,128)(2,1)S(1)}, bf16[128,2048]{1,0:T(8,128)(2,1)}, u32[]{:S(2)}) copy-start(bf16[128,2048]{1,0:T(8,128)(2,1)} %param.31) | copy-start | bytes 1572868
  435.3 25.9 %copy-start.12 = (bf16[4,128,1024]{2,1,0:T(8,128)(2,1)S(1)}, bf16[4,128,1024]{2,1,0:T(8,128)(2,1)}, u32[]{:S(2)}) copy-start(bf16[4,128,1024]{2,1,0:T(8,128)(2,1)} %get-tuple-element.77) | copy-start | bytes 3145732
  437.2 1.0 copy-start.3
  461.3 6.0 copy-start.11
  517.2 4.1 copy-start.2
  531.7 10.7 %copy-start.7 = (bf16[32,64,768]{2,1,0:T(8,128)(2,1)S(1)}, bf16[32,64,768]{2,1,0:T(8,128)(2,1)}, u32[]{:S(2)}) copy-start(bf16[32,64,768]{2,1,0:T(8,128)(2,1)} %get-tuple-element.64.refs_0_) | copy-start | bytes 9437188
  723.3 6.8 copy-start.6
  730.1 4.5 copy-start.10
  730.1 5.6 copy-start.9
Sparse Core Ops, SparseCore 0:
  15.3 33.3 all-reduce.6
  467.4 87.0 reduce-scatter.1
Sparse Core Ops, SparseCore 1:
  18.9 163.7 all-gather.2

commit v8 on v7

--- a/solution.py
+++ b/solution.py
@@ -499,22 +499,36 @@
 
 def scatter_kernel(
     extended,
-    spread_ref,
     *refs,
 ):
+    resident = 6 if extended else 5
+    streamed = 1 if extended else 3
+    given, refs = refs[:resident], refs[resident:]
+    sources, refs = refs[:streamed], refs[streamed:]
     if extended:
-        gate_grad_ref, up_grad_ref, gate_ref, up_ref, extra_ref, rows_hbm = refs[:6]
-        out_ref, extra_out, gate_out, up_out = refs[6:10]
-        tiles, staged, loaded, stored = refs[10:14]
-        refs = refs[14:]
+        (rows_hbm,) = sources
+        out_ref, extra_out, gate_out, up_out = refs[:4]
+        tiles, staged, loaded, stored = refs[4:8]
+        refs = refs[8:]
     else:
-        active_ref, down_ref, share_ref, select_ref, grads_hbm, gate_hbm, up_hbm = refs[:7]
-        out_ref, rows_out, gate_out, up_out, extra_ref = refs[7:12]
-        grads_in, pre_in, rows_staged, staged, loaded, stored = refs[12:18]
-        refs = refs[18:]
+        grads_hbm, gate_hbm, up_hbm = sources
+        out_ref, rows_out, gate_out, up_out, extra_ref = refs[:5]
+        grads_in, pre_in, rows_staged, staged, loaded, stored = refs[5:11]
+        refs = refs[11:]
+    held, (fetched, *refs) = refs[:resident], refs[resident:]
+    if extended:
+        spread_ref, gate_grad_ref, up_grad_ref, gate_ref, up_ref, extra_ref = held
+    else:
+        spread_ref, active_ref, down_ref, share_ref, select_ref = held
     outgoing, core_in, total, back, x_in, y_in, z_in, deep_in, deep_x, deep_y = refs[:10]
     core_sent, core_got, x_sent, x_got, y_sent, y_got, z_sent, z_got = refs[10:18]
     deep_sent, deep_got, corner_sent, corner_got = refs[18:]
+    fetches = [
+        pltpu.make_async_copy(source, target, fetched.at[i])
+        for i, (source, target) in enumerate(zip(given, held))
+    ]
+    for fetch in fetches:
+        fetch.start()
     z, y, x, c = spot()
     width = out_ref.shape[1]
     count = out_ref.shape[0]
@@ -528,6 +542,8 @@
     )
     near_z, far_z = where_is(along_z(z, 1), y, x, c), where_is(along_z(z, 2), y, x, c)
     greet([y_peer, x_peer, core_peer, near_z, far_z])
+    for fetch in fetches:
+        fetch.wait()
     groups = ((1, 1), (0, 1), (1, 0), (0, 0))
 
     def block_of(group, q, core):
@@ -891,12 +907,12 @@
     wide = width + 128 if extended else width
     low = operands[0].dtype
     anywhere = pl.BlockSpec(memory_space=pl.ANY)
+    resident = (spread, *operands[: 5 if extended else 4])
     outs = [jax.ShapeDtypeStruct((count, width), jnp.float32)]
     if extended:
         outs.append(jax.ShapeDtypeStruct((count, 128), jnp.float32))
         hidden = operands[0].shape[2]
         outs += [jax.ShapeDtypeStruct((width, hidden), jnp.float32)] * 2
-        in_specs = in_vmem(6) + [anywhere]
         out_specs = in_vmem(2) + [anywhere] * 2
         filler = [
             pltpu.VMEM((2, blocks, kept, width // 8), low),
@@ -912,7 +928,6 @@
             jax.ShapeDtypeStruct((blocks, kept, hidden), low),
             jax.ShapeDtypeStruct((blocks, kept, 128), low),
         ]
-        in_specs = in_vmem(5) + [anywhere] * 3
         out_specs = in_vmem(1) + [anywhere] * 3 + in_vmem(1)
         filler = [
             pltpu.VMEM((2, 4, count, width), low),
@@ -925,10 +940,12 @@
     return pl.pallas_call(
         functools.partial(scatter_kernel, extended),
         out_shape=outs,
-        in_specs=in_specs,
+        in_specs=[anywhere] * (1 + len(operands)),
         out_specs=out_specs,
         scratch_shapes=filler
+        + [pltpu.VMEM(operand.shape, operand.dtype) for operand in resident]
         + [
+            copies(len(resident)),
             pltpu.VMEM((4, 4, count, wide), low),
             pltpu.VMEM((4, 4, count, wide), low),
             pltpu.VMEM((4, 4, count, wide), low),

time: 756 us -> 749 us (level)
    pallas_call x2, Pallas kernels: 194 us -> 177 us  [scatter_rows(): pl.pallas_call(functools.partial(scatter_kernel, extended), out_shape=out...]
    pallas_call x1, Pallas kernels: 21.9 us -> 31 us  [branch_back(): pl.pallas_call(branch_kernel, out_shape=[jax.ShapeDtypeStruct((4, count,...]
  transfers between devices with their start and end apart: 3 -> 3, of which waited for: 1 -> 1; matrix products, arithmetic and copies ran while one was open for 6% -> 6% of each run, Pallas kernels for 35% -> 36%
where the time goes in v8:
time: 749 us; the launch traced here: 740 us
  Pallas kernels  638 us (85%)
  other arithmetic  34.2 us (5%)
  local copies, waits for them, and re-layouts  27.5 us (4%)
  matrix products  21.6 us (3%)
  between operations  17 us (2%)
    pallas_call x2, Pallas kernels, scatter_rows(): pl.pallas_call(functools.partial(scatter_kernel, extended), out_shape=out...  177 us
    pallas_call x1, Pallas kernels, reduce_over_members(): pl.pallas_call(functools.partial(reduce_kernel, cuts), out_shape=[jax.Sha...  166 us
    pallas_call x1, Pallas kernels, gather_experts(): pl.pallas_call(functools.partial(gather_kernel, topk), out_shape=[jax.Sha...  102 us
    pallas_call x1, Pallas kernels, project_tokens(): pl.pallas_call(project_kernel, out_shape=[jax.ShapeDtypeStruct((4, count,...  71.4 us
    pallas_call x1, Pallas kernels, heads_back(): pl.pallas_call(heads_kernel, out_shape=[jax.ShapeDtypeStruct((4, depth, o...  49.9 us
    pallas_call x1, Pallas kernels, finish_attention(): pl.pallas_call(functools.partial(finish_kernel, row, sequences), out_shap...  39.7 us
    pallas_call x1, Pallas kernels, branch_back(): pl.pallas_call(branch_kernel, out_shape=[jax.ShapeDtypeStruct((4, count,...  31 us
    dot_general x3, matrix products, left_trans(): lax.dot_general(left, right, (((0,), (0,)), ((), ())), preferred_element_...  19.4 us
  transfers between devices with their start and end apart: 3, of which 1 were waited for; matrix products, arithmetic and copies ran while one was open for 6% of the time, Pallas kernels for 36%

profile of v8, /device:TPU:8, one launch (start us, length us, event | category | flops | bytes accessed | tf_op | source)
XLA Modules:
  0.0 739.8 jit_solution(14900211420649719940)
XLA Ops:
  11.0 2.8 concatenate.10
  15.8 1.3 broadcast_in_dim.16.gain_ref
  19.2 71.4 %shard_map.263 = (f32[4,128,1280]{2,1,0:T(8,128)}, bf16[4,128,512]{2,1,0:T(8,128)(2,1)}, s32[32,16,128]{2,1,0:T(8,128)}) custom-call(bf16[128,2048]{1,0:T(8,128)(2,1)} %x_ref.3, s32[16,128]{1,0:T(8,128)} %pad.17.routes_ref, bf16[1,512]{1,0:T(2,128)(2,1)} %broadcast_in_dim.16.gain_ref, bf16[512,4096]{1,0:T(8,128)(2,1)} %query_ref.3, ...), custom_call_target="tpu_custom_call" | custom-call | tf_op jit(solution)/shard_map/pallas_call | solution.py:1454
  90.6 1.4 constant_dynamic-slice_fusion.notes_ref
  96.4 39.7 %shard_map.264 = (f32[128,2048]{1,0:T(8,128)}, bf16[128,2048]{1,0:T(8,128)(2,1)}, bf16[4,128,1024]{2,1,0:T(8,128)(2,1)}, f32[4,8,128,128]{3,2,1,0:T(8,128)}, bf1...) custom-call(f32[4,128,1280]{2,1,0:T(8,128)} %get-tuple-element.59.ra, ...), custom_call_target="tpu_custom_call" | custom-call | tf_op jit(solution)/shard_map/pallas_call | solution.py:1622
  136.2 102.4 %shard_map.265 = (bf16[32,64,2048]{2,1,0:T(8,128)(2,1)}, bf16[32,64,768]{2,1,0:T(8,128)(2,1)}, f32[32,64,768]{2,1,0:T(8,128)}, f32[32,64,768]{2,1,0:T(8,128)}, f...) custom-call(bf16[128,2048]{1,0:T(8,128)(2,1)} %get-tuple-element.62.x_ref, ...), custom_call_target="tpu_custom_call" | custom-call | tf_op jit(solution)/shard_map/pallas_call | solution.py:465
  239.3 89.5 %shard_map.266 = (f32[128,2048]{1,0:T(8,128)}, bf16[32,64,2048]{2,1,0:T(8,128)(2,1)}, bf16[32,64,768]{2,1,0:T(8,128)(2,1)}, bf16[32,64,768]{2,1,0:T(8,128)(2,1)}, bf16[32,64,128]{2,1,0:T(8,128)(2,1)}) custom-call(bf16[32,128,64]{2,1,0:T(8,128)(2,1)} %get-tuple-element.63.refs_0_, bf16[32,64,768]{2,1,0:T(8,128)(2,1)} %get-tuple-element.64.refs_1_, ...), custom_call_target="tpu_custom_call" | custom-call | tf_op jit(solution)/shard_map/pallas_call | solution.py:940
  328.8 87.9 %shard_map.267 = (f32[128,2048]{1,0:T(8,128)}, f32[128,128]{1,0:T(8,128)}, f32[2048,768]{1,0:T(8,128)}, f32[2048,768]{1,0:T(8,128)}) custom-call(bf16[32,128,64]{2,1,0:T(8,128)(2,1)} %get-tuple-element.63.refs_0_, bf16[32,64,768]{2,1,0:T(8,128)(2,1)} %get-tuple-element.70.refs_1_, bf16[32,64,768]{2,1,0:T(8,128)(2,1)} %get-tuple-element.71.refs_2_, ...), custom_call_target="tpu_custom_call" | custom-call | tf_op jit(solution)/shard_map/pallas_call | solution.py:940
  418.9 1.9 multiply_reduce_fusion
  422.9 31.0 %shard_map.268 = (bf16[4,128,1024]{2,1,0:T(8,128)(2,1)}, bf16[4,128,2048]{2,1,0:T(8,128)(2,1)}) custom-call(bf16[128,2048]{1,0:T(8,128)(2,1)} %fusion.13.branch_ref, bf16[1024,2048]{1,0:T(8,128)(2,1)} %weight_ref.3), custom_call_target="tpu_custom_call" | custom-call | tf_op jit(solution)/shard_map/pallas_call | solution.py:1696
  454.0 6.0 bitcast_convert_fusion
  460.0 49.9 %shard_map.269 = (bf16[4,512,1280]{2,1,0:T(8,128)(2,1)}, bf16[4,128,512]{2,1,0:T(8,128)(2,1)}, f32[8,128]{1,0:T(8,128)}) custom-call(bf16[4,128,1024]{2,1,0:T(8,128)(2,1)} %get-tuple-element.79.branch_ref, f32[4,128,1280]{2,1,0:T(8,128)} %get-tuple-element.59.raw_ref, f32[4,8,128,128]{3,2,1,0:T(8,128)} %get-tuple-element.80.probs_ref, ...), custom_call_target="tpu_custom_call" | custom-call | tf_op jit(solution)/shard_map/pallas_call | solution.py:1896
  511.2 1.3 copy.47
  512.5 1.6 copy.48
  515.4 2.3 fusion.16
  517.8 1.7 reshape.159
  521.4 3.0 fusion.6
  524.4 10.7 %broadcast_select_fusion = (f32[2048,768]{1,0:T(8,128)}, f32[2048,768]{1,0:T(8,128)}) fusion(f32[2048,768]{1,0:T(8,128)} %get-tuple-element.91, pred[]{:T(512)} %bitcast.10, f32[2048,768]{1,0:T(8,128)} %get-tuple-element.90), kind=kLoop, calls=%fused_computation.3 | loop fusion | flops 3145728 | bytes 25165824 | tf_op jit(solution)/shard_map/jit(_where)/select_n | solution.py:2199
  535.1 11.0 %convolution_bitcast_fusion = f32[768,2048]{1,0:T(8,128)} fusion(bf16[32,64,768]{2,1,0:T(8,128)(2,1)S(1)} %copy-done.7, bf16[32,64,2048]{2,1,0:T(8,128)(2,1)} %get-tuple-element.92), kind=kOutput, calls=%fused_computation.2 | convolution fusion | flops 6442450944 | bytes 17825792 | tf_op jit(solution)/shard_map/dot_general | solution.py:29
  548.1 165.9 %shard_map.270 = (bf16[512,4096]{1,0:T(8,128)(2,1)}, bf16[512,512]{1,0:T(8,128)(2,1)}, bf16[512,512]{1,0:T(8,128)(2,1)}, bf16[4,2,128,2048]{3,2,1,0:T(8,128)(2,1)}, f32[144,128]{1,0:T(8,128)}) custom-call(bf16[2,4,256,1280]{3,2,1,0:T(8,128)(2,1)} %bitcast.59, bf16[128,2048]{1,0:T(8,128)(2,1)} %reduce-scatter.2.cloned.1.call-done.own_ref, f32[4,144,128]{2,1,0:T(8,128)} %bitcast.62), custom_call_target="tpu_custom_call" | custom-call | tf_op jit(solution)/shard_map/pallas_call | solution.py:1247
  714.9 1.3 slice_bitcast_fusion
  716.2 6.8 bitcast_convert_fusion.1
  723.1 4.5 convert_element_type.124
  730.6 1.3 fusion.14
  (80 shorter events, 26.2 us)
Async XLA Ops:
  8.0 83.9 %copy-start.1 = (bf16[128,2048]{1,0:T(8,128)(2,1)S(1)}, bf16[128,2048]{1,0:T(8,128)(2,1)}, u32[]{:S(2)}) copy-start(bf16[128,2048]{1,0:T(8,128)(2,1)} %x_ref.3) | copy-start | bytes 1572868
  8.0 84.1 %all-reduce.7.cloned.1.call-start = ((), (), s32[]{:S(2)}) async-start(), calls=%async_computation.3 | async-start | bytes 282624
  14.5 0.7 copy-start.8
  15.1 224.2 %all-gather.3.cloned.1.call-start = ((), (), s32[]{:S(2)}) async-start(), calls=%async_computation.1 | async-start | bytes 17301504 | tf_op jit(solution)/shard_map/all_gather | solution.py:1924
  15.7 531.7 %reduce-scatter.2.cloned.1.call-start = ((), (), s32[]{:S(2)}) async-start(), calls=%async_computation.2 | async-start | bytes 4718592 | tf_op jit(solution)/shard_map/reduce_scatter | solution.py:2201
  136.2 102.4 %copy-start.5 = (bf16[128,2048]{1,0:T(8,128)(2,1)S(1)}, bf16[128,2048]{1,0:T(8,128)(2,1)}, u32[]{:S(2)}) copy-start(bf16[128,2048]{1,0:T(8,128)(2,1)} %get-tuple-element.62.x_ref) | copy-start | bytes 1572868
  136.2 102.9 %copy-start = (f32[128,2048]{1,0:T(8,128)S(1)}, f32[128,2048]{1,0:T(8,128)}, u32[]{:S(2)}) copy-start(f32[128,2048]{1,0:T(8,128)} %get-tuple-element.61) | copy-start | bytes 3145732
  328.8 92.9 %copy-start.4 = (bf16[128,2048]{1,0:T(8,128)(2,1)S(1)}, bf16[128,2048]{1,0:T(8,128)(2,1)}, u32[]{:S(2)}) copy-start(bf16[128,2048]{1,0:T(8,128)(2,1)} %param.31) | copy-start | bytes 1572868
  418.9 35.1 %copy-start.12 = (bf16[4,128,1024]{2,1,0:T(8,128)(2,1)S(1)}, bf16[4,128,1024]{2,1,0:T(8,128)(2,1)}, u32[]{:S(2)}) copy-start(bf16[4,128,1024]{2,1,0:T(8,128)(2,1)} %get-tuple-element.77) | copy-start | bytes 3145732
  420.7 1.0 copy-start.3
  453.9 6.0 copy-start.11
  509.9 4.1 copy-start.2
  524.4 10.7 %copy-start.7 = (bf16[32,64,768]{2,1,0:T(8,128)(2,1)S(1)}, bf16[32,64,768]{2,1,0:T(8,128)(2,1)}, u32[]{:S(2)}) copy-start(bf16[32,64,768]{2,1,0:T(8,128)(2,1)} %get-tuple-element.64.refs_1_) | copy-start | bytes 9437188
  716.2 6.8 copy-start.6
  723.1 4.5 copy-start.10
  723.1 5.6 copy-start.9
Sparse Core Ops, SparseCore 0:
  15.3 33.3 all-reduce.6
  460.1 87.2 reduce-scatter.1
Sparse Core Ops, SparseCore 1:
  18.9 163.7 all-gather.2

commit v9 on v8

--- a/solution.py
+++ b/solution.py
@@ -173,6 +173,35 @@
     return pltpu.CompilerParams(
         collective_id=collective_id, has_side_effects=True, vmem_limit_bytes=60 << 20
     )
+
+
+def fetching(kernel, count):
+    def run(*refs):
+        given, refs = refs[:count], refs[count:]
+        refs, held, fetched = refs[: -count - 1], refs[-count - 1 : -1], refs[-1]
+        fetches = [
+            pltpu.make_async_copy(source, target, fetched.at[i])
+            for i, (source, target) in enumerate(zip(given, held))
+        ]
+        for fetch in fetches:
+            fetch.start()
+        kernel(fetches, *held, *refs)
+
+    return run
+
+
+def anywhere(count):
+    return [pl.BlockSpec(memory_space=pl.ANY)] * count
+
+
+def room_for(operands):
+    held = [pltpu.VMEM(operand.shape, operand.dtype) for operand in operands]
+    return held + [copies(len(operands))]
+
+
+def wait_all(fetches):
+    for fetch in fetches:
+        fetch.wait()
 
 
 def gather_kernel(
@@ -975,6 +1004,7 @@
 
 def reduce_kernel(
     cuts,
+    fetches,
     parts_ref,
     own_ref,
     vector_ref,
@@ -998,6 +1028,7 @@
     members = [((member + j) % 8, shard) for j in range(8)]
     shards = [(member, (shard + j) % 4) for j in range(4)]
     greet(members[1:] + shards[1:])
+    wait_all(fetches)
     pieces = len(cuts)
     first_got, first_held, first_z = refs[:3]
     y_got_in, y_held, y_z = refs[3:5], refs[5:7], refs[7:9]
@@ -1245,13 +1276,13 @@
         return [pltpu.VMEM((*lead, size, width), low) for _, size in cuts[1:]]
 
     return pl.pallas_call(
-        functools.partial(reduce_kernel, cuts),
+        fetching(functools.partial(reduce_kernel, cuts), 3),
         out_shape=[jax.ShapeDtypeStruct((2 * depth, size), low) for size in widths]
         + [
             jax.ShapeDtypeStruct((4, 2, *own.shape), low),
             jax.ShapeDtypeStruct(vectors.shape[1:], vectors.dtype),
         ],
-        in_specs=in_vmem(3),
+        in_specs=[anywhere] * 3,
         out_specs=[anywhere] * 3 + in_vmem(2),
         scratch_shapes=[
             pltpu.VMEM(parts.shape, low),
@@ -1272,7 +1303,8 @@
         ]
         + [copies(3, 4)] * 8
         + [copies(4)] * 2
-        + [copies(8)] * 2,
+        + [copies(8)] * 2
+        + room_for((parts, own, vectors)),
         compiler_params=settings(3),
     )(parts, own, vectors)
 
@@ -1495,6 +1527,7 @@
 def finish_kernel(
     row,
     sequences,
+    fetches,
     raw_ref,
     notes_ref,
     query_gain_ref,
@@ -1523,6 +1556,7 @@
     count = x_ref.shape[0]
     core_peer, x_peer = where_is(z, y, x, 1 - c), where_is(z, y, 1 - x, c)
     greet([core_peer, x_peer])
+    wait_all(fetches)
     heads = query_out.shape[2] // HEAD_WIDTH
     wide = heads * HEAD_WIDTH
 
@@ -1619,8 +1653,9 @@
     low = tokens.dtype
     wide = w_out.shape[0]
     heads = wide // HEAD_WIDTH
+    operands = (raw, notes, q_gain, k_gain, w_out, tokens, gain)
     return pl.pallas_call(
-        functools.partial(finish_kernel, row, sequences),
+        fetching(functools.partial(finish_kernel, row, sequences), len(operands)),
         out_shape=[
             jax.ShapeDtypeStruct((count, width), jnp.float32),
             jax.ShapeDtypeStruct((count, width), low),
@@ -1631,7 +1666,7 @@
             jax.ShapeDtypeStruct((4, count, HEAD_WIDTH), jnp.float32),
             jax.ShapeDtypeStruct((4, count, HEAD_WIDTH), jnp.float32),
         ],
-        in_specs=in_vmem(7),
+        in_specs=anywhere(len(operands)),
         out_specs=in_vmem(8),
         scratch_shapes=[
             pltpu.VMEM((2, count, width), low),
@@ -1642,19 +1677,21 @@
             copies(2),
             copies(),
             copies(),
-        ],
+        ]
+        + room_for(operands),
         compiler_params=settings(5),
-    )(raw, notes, q_gain, k_gain, w_out, tokens, gain)
+    )(*operands)
 
 
 def branch_kernel(
-    branch_ref, weight_ref, grad_out, every_out, x_sent, x_got, core_sent, core_got
+    fetches, branch_ref, weight_ref, grad_out, every_out, x_sent, x_got, core_sent, core_got
 ):
     z, y, x, c = spot()
     mine = x * 2 + c
     core_peer, x_peer = where_is(z, y, x, 1 - c), where_is(z, y, 1 - x, c)
     half = branch_ref.shape[0] // 2
     greet([core_peer, x_peer])
+    wait_all(fetches)
     every_out[mine] = branch_ref[...]
 
     def x_copy(part):
@@ -1694,19 +1731,21 @@
     count, width = branch.shape
     low = branch.dtype
     return pl.pallas_call(
-        branch_kernel,
+        fetching(branch_kernel, 2),
         out_shape=[
             jax.ShapeDtypeStruct((4, count, w_out.shape[0]), low),
             jax.ShapeDtypeStruct((4, count, width), low),
         ],
-        in_specs=in_vmem(2),
+        in_specs=anywhere(2),
         out_specs=in_vmem(2),
-        scratch_shapes=[copies(2), copies(2), copies(2, 2), copies(2, 2)],
+        scratch_shapes=[copies(2), copies(2), copies(2, 2), copies(2, 2)]
+        + room_for((branch, w_out)),
         compiler_params=settings(6),
     )(branch, w_out)
 
 
 def heads_kernel(
+    fetches,
     branch_ref,
     raw_ref,
     probs_ref,
@@ -1738,6 +1777,7 @@
     core_peer, x_peer = where_is(z, y, x, 1 - c), where_is(z, y, 1 - x, c)
     peers = [(member, (shard + j) % 4) for j in range(1, 4)]
     greet(peers)
+    wait_all(fetches)
     rows = every.shape[1]
     count = rows // 4
     depth = hidden_ref.shape[1]
@@ -1894,13 +1934,13 @@
     low = hidden.dtype
     operands = (branch, raw, probs, *rotated, *tables, *gains, hidden, *weights)
     return pl.pallas_call(
-        heads_kernel,
+        fetching(heads_kernel, len(operands)),
         out_shape=[
             jax.ShapeDtypeStruct((4, depth, own), low),
             jax.ShapeDtypeStruct((4, rows // 4, depth), low),
             jax.ShapeDtypeStruct((8, HEAD_WIDTH), jnp.float32),
         ],
-        in_specs=in_vmem(len(operands)),
+        in_specs=anywhere(len(operands)),
         out_specs=in_vmem(3),
         scratch_shapes=[
             pltpu.VMEM((4, rows, own), low),
@@ -1912,7 +1952,8 @@
             copies(2, 4),
             copies(4),
             copies(4),
-        ],
+        ]
+        + room_for(operands),
         compiler_params=settings(7),
     )(*operands)
 

time: 749 us -> 744 us (level)
    pallas_call x4, Pallas kernels: 287 us -> 269 us  [the longest x1 163 us: reduce_over_members(): pl.pallas_call(fetching(functools.partial(reduce_kernel, cuts), 3), out_s...]
    pallas_call x2, Pallas kernels: 177 us -> 189 us  [scatter_rows(): pl.pallas_call(functools.partial(scatter_kernel, extended), out_shape=out...]
where the time goes in v9:
time: 744 us; the launch traced here: 734 us
  Pallas kernels  631 us (85%)
  other arithmetic  34.2 us (5%)
  local copies, waits for them, and re-layouts  27.5 us (4%)
  matrix products  21.6 us (3%)
  between operations  17 us (2%)
    pallas_call x2, Pallas kernels, scatter_rows(): pl.pallas_call(functools.partial(scatter_kernel, extended), out_shape=out...  189 us
    pallas_call x1, Pallas kernels, reduce_over_members(): pl.pallas_call(fetching(functools.partial(reduce_kernel, cuts), 3), out_s...  163 us
    pallas_call x1, Pallas kernels, gather_experts(): pl.pallas_call(functools.partial(gather_kernel, topk), out_shape=[jax.Sha...  102 us
    pallas_call x1, Pallas kernels, project_tokens(): pl.pallas_call(project_kernel, out_shape=[jax.ShapeDtypeStruct((4, count,...  71.4 us
    pallas_call x1, Pallas kernels, heads_back(): pl.pallas_call(fetching(heads_kernel, len(operands)), out_shape=[jax.Shap...  49.6 us
    pallas_call x1, Pallas kernels, finish_attention(): pl.pallas_call(fetching(functools.partial(finish_kernel, row, sequences),...  38.9 us
    dot_general x3, matrix products, left_trans(): lax.dot_general(left, right, (((0,), (0,)), ((), ())), preferred_element_...  19.4 us
    pallas_call x1, Pallas kernels, branch_back(): pl.pallas_call(fetching(branch_kernel, 2), out_shape=[jax.ShapeDtypeStruc...  17.7 us
  transfers between devices with their start and end apart: 3, of which 1 were waited for; matrix products, arithmetic and copies ran while one was open for 6% of the time, Pallas kernels for 36%

profile of v9, /device:TPU:8, one launch (start us, length us, event | category | flops | bytes accessed | tf_op | source)
XLA Modules:
  0.0 733.6 jit_solution(6799960666204389232)
XLA Ops:
  11.0 2.8 concatenate.10
  19.2 71.4 %shard_map.263 = (f32[4,128,1280]{2,1,0:T(8,128)}, bf16[4,128,512]{2,1,0:T(8,128)(2,1)}, s32[32,16,128]{2,1,0:T(8,128)}) custom-call(bf16[128,2048]{1,0:T(8,128)(2,1)} %refs_5_.1, s32[16,128]{1,0:T(8,128)} %pad.17.routes_ref, bf16[1,512]{1,0:T(2,128)(2,1)} %broadcast_in_dim.16.gain_ref, bf16[512,4096]{1,0:T(8,128)(2,1)} %refs_10_.1, ...), custom_call_target="tpu_custom_call" | custom-call | tf_op jit(solution)/shard_map/pallas_call | solution.py:1486
  90.6 1.4 constant_dynamic-slice_fusion.refs_1_
  96.4 38.9 %shard_map.264 = (f32[128,2048]{1,0:T(8,128)}, bf16[128,2048]{1,0:T(8,128)(2,1)}, bf16[4,128,1024]{2,1,0:T(8,128)(2,1)}, f32[4,8,128,128]{3,2,1,0:T(8,128)}, bf1...) custom-call(f32[4,128,1280]{2,1,0:T(8,128)} %get-tuple-element.59.re, ...), custom_call_target="tpu_custom_call" | custom-call | tf_op jit(solution)/shard_map/pallas_call | solution.py:1657
  135.3 102.2 %shard_map.265 = (bf16[32,64,2048]{2,1,0:T(8,128)(2,1)}, bf16[32,64,768]{2,1,0:T(8,128)(2,1)}, f32[32,64,768]{2,1,0:T(8,128)}, f32[32,64,768]{2,1,0:T(8,128)}, f...) custom-call(bf16[128,2048]{1,0:T(8,128)(2,1)} %get-tuple-element.62.x_ref, ...), custom_call_target="tpu_custom_call" | custom-call | tf_op jit(solution)/shard_map/pallas_call | solution.py:494
  238.3 91.6 %shard_map.266 = (f32[128,2048]{1,0:T(8,128)}, bf16[32,64,2048]{2,1,0:T(8,128)(2,1)}, bf16[32,64,768]{2,1,0:T(8,128)(2,1)}, bf16[32,64,768]{2,1,0:T(8,128)(2,1)}, bf16[32,64,128]{2,1,0:T(8,128)(2,1)}) custom-call(bf16[32,128,64]{2,1,0:T(8,128)(2,1)} %get-tuple-element.63.refs_0_, bf16[32,64,768]{2,1,0:T(8,128)(2,1)} %get-tuple-element.64.refs_1_, ...), custom_call_target="tpu_custom_call" | custom-call | tf_op jit(solution)/shard_map/pallas_call | solution.py:969
  329.9 97.0 %shard_map.267 = (f32[128,2048]{1,0:T(8,128)}, f32[128,128]{1,0:T(8,128)}, f32[2048,768]{1,0:T(8,128)}, f32[2048,768]{1,0:T(8,128)}) custom-call(bf16[32,128,64]{2,1,0:T(8,128)(2,1)} %get-tuple-element.63.refs_0_, bf16[32,64,768]{2,1,0:T(8,128)(2,1)} %get-tuple-element.70.refs_1_, bf16[32,64,768]{2,1,0:T(8,128)(2,1)} %get-tuple-element.71.refs_2_, ...), custom_call_target="tpu_custom_call" | custom-call | tf_op jit(solution)/shard_map/pallas_call | solution.py:969
  429.1 1.9 multiply_reduce_fusion
  433.1 17.7 %shard_map.268 = (bf16[4,128,1024]{2,1,0:T(8,128)(2,1)}, bf16[4,128,2048]{2,1,0:T(8,128)(2,1)}) custom-call(bf16[128,2048]{1,0:T(8,128)(2,1)} %fusion.13.refs_0_, bf16[1024,2048]{1,0:T(8,128)(2,1)} %refs_1_.1), custom_call_target="tpu_custom_call" | custom-call | tf_op jit(solution)/shard_map/pallas_call | solution.py:1733
  450.9 6.0 bitcast_convert_fusion
  456.9 49.6 %shard_map.269 = (bf16[4,512,1280]{2,1,0:T(8,128)(2,1)}, bf16[4,128,512]{2,1,0:T(8,128)(2,1)}, f32[8,128]{1,0:T(8,128)}) custom-call(bf16[4,128,1024]{2,1,0:T(8,128)(2,1)} %get-tuple-element.79.refs_0_, f32[4,128,1280]{2,1,0:T(8,128)} %get-tuple-element.59.refs_0_.refs_1_, f32[4,8,128,128]{3,2,1,0:T(8,128)} %get-tuple-element.80.refs_2_, ...), custom_call_target="tpu_custom_call" | custom-call | tf_op jit(solution)/shard_map/pallas_call | solution.py:1936
  507.8 1.3 copy.47
  509.1 1.6 copy.48
  512.1 2.3 fusion.16
  514.5 1.7 reshape.159
  518.1 3.0 fusion.6
  521.1 10.7 %broadcast_select_fusion = (f32[2048,768]{1,0:T(8,128)}, f32[2048,768]{1,0:T(8,128)}) fusion(f32[2048,768]{1,0:T(8,128)} %get-tuple-element.91, pred[]{:T(512)} %bitcast.10, f32[2048,768]{1,0:T(8,128)} %get-tuple-element.90), kind=kLoop, calls=%fused_computation.3 | loop fusion | flops 3145728 | bytes 25165824 | tf_op jit(solution)/shard_map/jit(_where)/select_n | solution.py:2240
  531.8 11.0 %convolution_bitcast_fusion = f32[768,2048]{1,0:T(8,128)} fusion(bf16[32,64,768]{2,1,0:T(8,128)(2,1)S(1)} %copy-done.7, bf16[32,64,2048]{2,1,0:T(8,128)(2,1)} %get-tuple-element.92), kind=kOutput, calls=%fused_computation.2 | convolution fusion | flops 6442450944 | bytes 17825792 | tf_op jit(solution)/shard_map/dot_general | solution.py:29
  542.9 1.7 reduce-scatter.2.cloned.1.call-done.refs_1_
  545.3 162.5 %shard_map.270 = (bf16[512,4096]{1,0:T(8,128)(2,1)}, bf16[512,512]{1,0:T(8,128)(2,1)}, bf16[512,512]{1,0:T(8,128)(2,1)}, bf16[4,2,128,2048]{3,2,1,0:T(8,128)(2,1)}, f32[144,128]{1,0:T(8,128)}) custom-call(bf16[2,4,256,1280]{3,2,1,0:T(8,128)(2,1)} %bitcast.59, bf16[128,2048]{1,0:T(8,128)(2,1)} %reduce-scatter.2.cloned.1.call-done.refs_1_, f32[4,144,128]{2,1,0:T(8,128)} %bitcast.62), custom_call_target="tpu_custom_call" | custom-call | tf_op jit(solution)/shard_map/pallas_call | solution.py:1278
  708.7 1.3 slice_bitcast_fusion
  710.0 6.8 bitcast_convert_fusion.1
  716.8 4.5 convert_element_type.124
  724.4 1.3 fusion.14
  (80 shorter events, 26.3 us)
Async XLA Ops:
  8.0 83.9 %copy-start.1 = (bf16[128,2048]{1,0:T(8,128)(2,1)S(1)}, bf16[128,2048]{1,0:T(8,128)(2,1)}, u32[]{:S(2)}) copy-start(bf16[128,2048]{1,0:T(8,128)(2,1)} %refs_5_.1) | copy-start | bytes 1572868
  8.0 84.1 %all-reduce.7.cloned.1.call-start = ((), (), s32[]{:S(2)}) async-start(), calls=%async_computation.3 | async-start | bytes 282624
  14.5 0.7 copy-start.8
  15.1 223.1 %all-gather.3.cloned.1.call-start = ((), (), s32[]{:S(2)}) async-start(), calls=%async_computation.1 | async-start | bytes 17301504 | tf_op jit(solution)/shard_map/all_gather | solution.py:1965
  15.7 528.9 %reduce-scatter.2.cloned.1.call-start = ((), (), s32[]{:S(2)}) async-start(), calls=%async_computation.2 | async-start | bytes 4718592 | tf_op jit(solution)/shard_map/reduce_scatter | solution.py:2242
  135.3 102.2 %copy-start.5 = (bf16[128,2048]{1,0:T(8,128)(2,1)S(1)}, bf16[128,2048]{1,0:T(8,128)(2,1)}, u32[]{:S(2)}) copy-start(bf16[128,2048]{1,0:T(8,128)(2,1)} %get-tuple-element.62.x_ref) | copy-start | bytes 1572868
  135.3 102.8 %copy-start = (f32[128,2048]{1,0:T(8,128)S(1)}, f32[128,2048]{1,0:T(8,128)}, u32[]{:S(2)}) copy-start(f32[128,2048]{1,0:T(8,128)} %get-tuple-element.61) | copy-start | bytes 3145732
  329.9 102.1 %copy-start.4 = (bf16[128,2048]{1,0:T(8,128)(2,1)S(1)}, bf16[128,2048]{1,0:T(8,128)(2,1)}, u32[]{:S(2)}) copy-start(bf16[128,2048]{1,0:T(8,128)(2,1)} %param.31) | copy-start | bytes 1572868
  429.1 21.7 %copy-start.12 = (bf16[4,128,1024]{2,1,0:T(8,128)(2,1)S(1)}, bf16[4,128,1024]{2,1,0:T(8,128)(2,1)}, u32[]{:S(2)}) copy-start(bf16[4,128,1024]{2,1,0:T(8,128)(2,1)} %get-tuple-element.77) | copy-start | bytes 3145732
  431.0 1.0 copy-start.3
  450.8 6.0 copy-start.11
  506.6 4.1 copy-start.2
  521.1 10.7 %copy-start.7 = (bf16[32,64,768]{2,1,0:T(8,128)(2,1)S(1)}, bf16[32,64,768]{2,1,0:T(8,128)(2,1)}, u32[]{:S(2)}) copy-start(bf16[32,64,768]{2,1,0:T(8,128)(2,1)} %get-tuple-element.64.refs_1_) | copy-start | bytes 9437188
  710.0 6.8 copy-start.6
  716.8 4.5 copy-start.10
  716.8 5.6 copy-start.9
Sparse Core Ops, SparseCore 0:
  15.3 33.3 all-reduce.6
  457.0 87.5 reduce-scatter.1
Sparse Core Ops, SparseCore 1:
  18.9 163.1 all-gather.2

commit v10 on v9

--- a/solution.py
+++ b/solution.py
@@ -1310,6 +1310,7 @@
 
 
 def project_kernel(
+    fetches,
     x_ref,
     routes_ref,
     gain_ref,
@@ -1354,6 +1355,7 @@
         pl.semaphore_signal(barrier, inc=1, device_id=everyone(j), device_id_type=MESH)
 
     pl.semaphore_wait(barrier, 31)
+    wait_all(fetches)
 
     def slice_copy(j):
         place = (shard + j) % 4
@@ -1484,13 +1486,13 @@
     own = (w_query.shape[1] + key_weight.shape[1] + value_weight.shape[1]) // 4
     low = tokens.dtype
     return pl.pallas_call(
-        project_kernel,
+        fetching(project_kernel, 6),
         out_shape=[
             jax.ShapeDtypeStruct((4, count, own), jnp.float32),
             jax.ShapeDtypeStruct((4, count, depth), low),
             jax.ShapeDtypeStruct((32, *routes.shape), routes.dtype),
         ],
-        in_specs=in_vmem(6),
+        in_specs=anywhere(6),
         out_specs=in_vmem(3),
         scratch_shapes=[
             pltpu.VMEM((count, 128), jnp.float32),
@@ -1510,7 +1512,8 @@
             copies(2),
             copies(32),
             copies(32),
-        ],
+        ]
+        + room_for((tokens, routes, gain, w_query, key_weight, value_weight)),
         compiler_params=settings(4),
     )(tokens, routes, gain, w_query, key_weight, value_weight)
 

time: 744 us -> 742 us (level)
  no operation moved by 1% of the time
where the time goes in v10:
time: 742 us; the launch traced here: 732 us
  Pallas kernels  629 us (85%)
  other arithmetic  34.2 us (5%)
  local copies, waits for them, and re-layouts  27.5 us (4%)
  matrix products  21.6 us (3%)
  between operations  17 us (2%)
    pallas_call x2, Pallas kernels, scatter_rows(): pl.pallas_call(functools.partial(scatter_kernel, extended), out_shape=out...  188 us
    pallas_call x1, Pallas kernels, reduce_over_members(): pl.pallas_call(fetching(functools.partial(reduce_kernel, cuts), 3), out_s...  162 us
    pallas_call x1, Pallas kernels, gather_experts(): pl.pallas_call(functools.partial(gather_kernel, topk), out_shape=[jax.Sha...  103 us
    pallas_call x1, Pallas kernels, project_tokens(): pl.pallas_call(fetching(project_kernel, 6), out_shape=[jax.ShapeDtypeStru...  69.5 us
    pallas_call x1, Pallas kernels, heads_back(): pl.pallas_call(fetching(heads_kernel, len(operands)), out_shape=[jax.Shap...  49 us
    pallas_call x1, Pallas kernels, finish_attention(): pl.pallas_call(fetching(functools.partial(finish_kernel, row, sequences),...  39 us
    dot_general x3, matrix products, left_trans(): lax.dot_general(left, right, (((0,), (0,)), ((), ())), preferred_element_...  19.4 us
    pallas_call x1, Pallas kernels, branch_back(): pl.pallas_call(fetching(branch_kernel, 2), out_shape=[jax.ShapeDtypeStruc...  18.4 us
  transfers between devices with their start and end apart: 3, of which 1 were waited for; matrix products, arithmetic and copies ran while one was open for 6% of the time, Pallas kernels for 36%

profile of v10, /device:TPU:8, one launch (start us, length us, event | category | flops | bytes accessed | tf_op | source)
XLA Modules:
  0.0 731.7 jit_solution(4299566790390937714)
XLA Ops:
  11.0 2.8 concatenate.10
  19.2 69.5 %shard_map.263 = (f32[4,128,1280]{2,1,0:T(8,128)}, bf16[4,128,512]{2,1,0:T(8,128)(2,1)}, s32[32,16,128]{2,1,0:T(8,128)}) custom-call(bf16[128,2048]{1,0:T(8,128)(2,1)} %refs_5_.3, s32[16,128]{1,0:T(8,128)} %pad.17.refs_1_, bf16[1,512]{1,0:T(2,128)(2,1)} %broadcast_in_dim.16.refs_2_, bf16[512,4096]{1,0:T(8,128)(2,1)} %refs_10_.1, bf16[512,512]{1,0:T(8,128)(2,1)} %refs_11_.1, ...), custom_call_target="tpu_custom_call" | custom-call | tf_op jit(solution)/shard_map/pallas_call | solution.py:1488
  88.7 1.4 constant_dynamic-slice_fusion.refs_1_
  94.5 39.0 %shard_map.264 = (f32[128,2048]{1,0:T(8,128)}, bf16[128,2048]{1,0:T(8,128)(2,1)}, bf16[4,128,1024]{2,1,0:T(8,128)(2,1)}, f32[4,8,128,128]{3,2,1,0:T(8,128)}, bf1...) custom-call(f32[4,128,1280]{2,1,0:T(8,128)} %get-tuple-element.59.re, ...), custom_call_target="tpu_custom_call" | custom-call | tf_op jit(solution)/shard_map/pallas_call | solution.py:1660
  133.6 102.9 %shard_map.265 = (bf16[32,64,2048]{2,1,0:T(8,128)(2,1)}, bf16[32,64,768]{2,1,0:T(8,128)(2,1)}, f32[32,64,768]{2,1,0:T(8,128)}, f32[32,64,768]{2,1,0:T(8,128)}, f...) custom-call(bf16[128,2048]{1,0:T(8,128)(2,1)} %get-tuple-element.62.x_ref, ...), custom_call_target="tpu_custom_call" | custom-call | tf_op jit(solution)/shard_map/pallas_call | solution.py:494
  237.2 90.8 %shard_map.266 = (f32[128,2048]{1,0:T(8,128)}, bf16[32,64,2048]{2,1,0:T(8,128)(2,1)}, bf16[32,64,768]{2,1,0:T(8,128)(2,1)}, bf16[32,64,768]{2,1,0:T(8,128)(2,1)}, bf16[32,64,128]{2,1,0:T(8,128)(2,1)}) custom-call(bf16[32,128,64]{2,1,0:T(8,128)(2,1)} %get-tuple-element.63.refs_0_, bf16[32,64,768]{2,1,0:T(8,128)(2,1)} %get-tuple-element.64.refs_1_, ...), custom_call_target="tpu_custom_call" | custom-call | tf_op jit(solution)/shard_map/pallas_call | solution.py:969
  328.1 97.0 %shard_map.267 = (f32[128,2048]{1,0:T(8,128)}, f32[128,128]{1,0:T(8,128)}, f32[2048,768]{1,0:T(8,128)}, f32[2048,768]{1,0:T(8,128)}) custom-call(bf16[32,128,64]{2,1,0:T(8,128)(2,1)} %get-tuple-element.63.refs_0_, bf16[32,64,768]{2,1,0:T(8,128)(2,1)} %get-tuple-element.70.refs_1_, bf16[32,64,768]{2,1,0:T(8,128)(2,1)} %get-tuple-element.71.refs_2_, ...), custom_call_target="tpu_custom_call" | custom-call | tf_op jit(solution)/shard_map/pallas_call | solution.py:969
  427.3 1.9 multiply_reduce_fusion
  431.3 18.4 %shard_map.268 = (bf16[4,128,1024]{2,1,0:T(8,128)(2,1)}, bf16[4,128,2048]{2,1,0:T(8,128)(2,1)}) custom-call(bf16[128,2048]{1,0:T(8,128)(2,1)} %fusion.13.refs_0_, bf16[1024,2048]{1,0:T(8,128)(2,1)} %refs_1_.1), custom_call_target="tpu_custom_call" | custom-call | tf_op jit(solution)/shard_map/pallas_call | solution.py:1736
  449.7 6.0 bitcast_convert_fusion
  455.8 49.0 %shard_map.269 = (bf16[4,512,1280]{2,1,0:T(8,128)(2,1)}, bf16[4,128,512]{2,1,0:T(8,128)(2,1)}, f32[8,128]{1,0:T(8,128)}) custom-call(bf16[4,128,1024]{2,1,0:T(8,128)(2,1)} %get-tuple-element.79.refs_0_, f32[4,128,1280]{2,1,0:T(8,128)} %get-tuple-element.59.refs_0_.refs_1_, f32[4,8,128,128]{3,2,1,0:T(8,128)} %get-tuple-element.80.refs_2_, ...), custom_call_target="tpu_custom_call" | custom-call | tf_op jit(solution)/shard_map/pallas_call | solution.py:1939
  506.0 1.3 copy.47
  507.4 1.6 copy.48
  510.3 2.3 fusion.16
  512.7 1.7 reshape.159
  516.3 3.0 fusion.6
  519.3 10.7 %broadcast_select_fusion = (f32[2048,768]{1,0:T(8,128)}, f32[2048,768]{1,0:T(8,128)}) fusion(f32[2048,768]{1,0:T(8,128)} %get-tuple-element.91, pred[]{:T(512)} %bitcast.10, f32[2048,768]{1,0:T(8,128)} %get-tuple-element.90), kind=kLoop, calls=%fused_computation.3 | loop fusion | flops 3145728 | bytes 25165824 | tf_op jit(solution)/shard_map/jit(_where)/select_n | solution.py:2243
  530.0 11.0 %convolution_bitcast_fusion = f32[768,2048]{1,0:T(8,128)} fusion(bf16[32,64,768]{2,1,0:T(8,128)(2,1)S(1)} %copy-done.7, bf16[32,64,2048]{2,1,0:T(8,128)(2,1)} %get-tuple-element.92), kind=kOutput, calls=%fused_computation.2 | convolution fusion | flops 6442450944 | bytes 17825792 | tf_op jit(solution)/shard_map/dot_general | solution.py:29
  541.1 1.6 reduce-scatter.2.cloned.1.call-done.refs_1_
  543.4 162.5 %shard_map.270 = (bf16[512,4096]{1,0:T(8,128)(2,1)}, bf16[512,512]{1,0:T(8,128)(2,1)}, bf16[512,512]{1,0:T(8,128)(2,1)}, bf16[4,2,128,2048]{3,2,1,0:T(8,128)(2,1)}, f32[144,128]{1,0:T(8,128)}) custom-call(bf16[2,4,256,1280]{3,2,1,0:T(8,128)(2,1)} %bitcast.59, bf16[128,2048]{1,0:T(8,128)(2,1)} %reduce-scatter.2.cloned.1.call-done.refs_1_, f32[4,144,128]{2,1,0:T(8,128)} %bitcast.62), custom_call_target="tpu_custom_call" | custom-call | tf_op jit(solution)/shard_map/pallas_call | solution.py:1278
  706.8 1.3 slice_bitcast_fusion
  708.1 6.8 bitcast_convert_fusion.1
  714.9 4.5 convert_element_type.124
  722.5 1.3 fusion.14
  (80 shorter events, 26.3 us)
Async XLA Ops:
  8.0 82.0 %copy-start.1 = (bf16[128,2048]{1,0:T(8,128)(2,1)S(1)}, bf16[128,2048]{1,0:T(8,128)(2,1)}, u32[]{:S(2)}) copy-start(bf16[128,2048]{1,0:T(8,128)(2,1)} %refs_5_.3) | copy-start | bytes 1572868
  8.0 82.2 %all-reduce.7.cloned.1.call-start = ((), (), s32[]{:S(2)}) async-start(), calls=%async_computation.3 | async-start | bytes 282624
  14.5 0.7 copy-start.8
  15.1 222.1 %all-gather.3.cloned.1.call-start = ((), (), s32[]{:S(2)}) async-start(), calls=%async_computation.1 | async-start | bytes 17301504 | tf_op jit(solution)/shard_map/all_gather | solution.py:1968
  15.7 527.0 %reduce-scatter.2.cloned.1.call-start = ((), (), s32[]{:S(2)}) async-start(), calls=%async_computation.2 | async-start | bytes 4718592 | tf_op jit(solution)/shard_map/reduce_scatter | solution.py:2245
  133.5 102.9 %copy-start.5 = (bf16[128,2048]{1,0:T(8,128)(2,1)S(1)}, bf16[128,2048]{1,0:T(8,128)(2,1)}, u32[]{:S(2)}) copy-start(bf16[128,2048]{1,0:T(8,128)(2,1)} %get-tuple-element.62.x_ref) | copy-start | bytes 1572868
  133.6 103.5 %copy-start = (f32[128,2048]{1,0:T(8,128)S(1)}, f32[128,2048]{1,0:T(8,128)}, u32[]{:S(2)}) copy-start(f32[128,2048]{1,0:T(8,128)} %get-tuple-element.61) | copy-start | bytes 3145732
  328.1 102.1 %copy-start.4 = (bf16[128,2048]{1,0:T(8,128)(2,1)S(1)}, bf16[128,2048]{1,0:T(8,128)(2,1)}, u32[]{:S(2)}) copy-start(bf16[128,2048]{1,0:T(8,128)(2,1)} %param.31) | copy-start | bytes 1572868
  427.3 22.4 %copy-start.12 = (bf16[4,128,1024]{2,1,0:T(8,128)(2,1)S(1)}, bf16[4,128,1024]{2,1,0:T(8,128)(2,1)}, u32[]{:S(2)}) copy-start(bf16[4,128,1024]{2,1,0:T(8,128)(2,1)} %get-tuple-element.77) | copy-start | bytes 3145732
  429.2 1.0 copy-start.3
  449.7 6.0 copy-start.11
  504.8 4.2 copy-start.2
  519.3 10.7 %copy-start.7 = (bf16[32,64,768]{2,1,0:T(8,128)(2,1)S(1)}, bf16[32,64,768]{2,1,0:T(8,128)(2,1)}, u32[]{:S(2)}) copy-start(bf16[32,64,768]{2,1,0:T(8,128)(2,1)} %get-tuple-element.64.refs_1_) | copy-start | bytes 9437188
  708.1 6.8 copy-start.6
  714.9 4.5 copy-start.10
  714.9 5.6 copy-start.9
Sparse Core Ops, SparseCore 0:
  15.3 33.9 all-reduce.6
  455.8 86.8 reduce-scatter.1
Sparse Core Ops, SparseCore 1:
  18.9 162.8 all-gather.2
